TPU v7x, 32 devices: a whole 2x2x4 slice. The times are simulated.
32 devices in a mesh: groups: 2 (over y), blk: 16 (over z, x, core), sp: 1.
Axes of the slice: x: 2, y: 2, z: 4, core: 2. Of those that a mesh axis runs over, the one named last changes fastest.
Arguments:
- out_grad: bfloat16 [8192, 1024], P(('groups', 'blk', 'sp')), parts along dimension 0, may hold values from -48 to 48
- query_act: bfloat16 [8192, 1024], P(('groups', 'blk'), 'sp'), parts along dimension 0, may hold values from -54 to 54
- key_act: bfloat16 [8192, 1024], P(('groups', 'blk'), 'sp'), parts along dimension 0, may hold values from -6 to 6
- value_act: bfloat16 [8192, 1024], P(('groups', 'blk'), 'sp'), parts along dimension 0, may hold values from -6 to 6
- out_weight: bfloat16 [1024, 1024], P('sp'), may hold values from -0.1875 to 0.1875
- query_weight: bfloat16 [1024, 1024], P(None, 'sp'), may hold values from -0.1875 to 0.1875
- key_weight: bfloat16 [1024, 1024], P(None, 'sp'), may hold values from -0.1875 to 0.1875
- value_weight: bfloat16 [1024, 1024], P(None, 'sp'), may hold values from -0.1875 to 0.1875
- neighbours: int32 [64, 8], P('groups'), parts along dimension 0, may hold values from 0 to 31, as said below
- block_counts: int32 [64], P('groups'), parts along dimension 0, may hold values from 1 to 8, as said below
Outputs:
- input_grad: bfloat16 [8192, 1024], P(('groups', 'blk', 'sp')), parts along dimension 0
There are 2 independent parts, one for each index of `groups`. A program takes and returns all parts, laid end to end along the dimension named above; an argument that names none is the same for every part. Nothing has to cross between parts.
Inputs may be any that keep to these rules, and one draw needn't show every extreme that they name: `neighbours`: entry 0 of each row is the query block itself; the live entries of a row are distinct blocks within 8 blocks of it, counted cyclically over 32 blocks; entries at or beyond the row's count hold the block itself. `block_counts`: in every draw at least one index of blk has both of its 2 blocks (starting at a multiple of 2) with 8 live slots; other blocks may have any count from 1 to 8.
All inputs are finite; a program needn't handle non-finite values.
Results may differ from a plain program's by a relative error of at most 0.009.
Values may be sent and summed in bfloat16 or wider, within the bound.
No kernel may reach another device: no remote copies, remote signals or barrier semaphores. Data moves between devices by JAX's collectives and lax.ppermute only.
A program may use at most 128 MiB of HBM per device.

v0:
```python
import math

import jax
import jax.numpy as jnp
from jax import lax
from jax.sharding import PartitionSpec as P

HD = 128
BLOCK = 128
NBR = 8
WIN = 8


def passed_along(shard, axis, by):
    size = lax.axis_size(axis)
    return lax.ppermute(shard, axis, [(i, (i + by) % size) for i in range(size)])


def body(
    out_grad,
    query_act,
    key_act,
    value_act,
    out_weight,
    query_weight,
    key_weight,
    value_weight,
    neighbours,
    block_counts,
):
    cycle_size = lax.axis_size("blk")
    my_index = lax.axis_index("blk")
    tokens = query_act.shape[0]
    features = query_act.shape[1]
    head_count = features // HD
    query_blocks = tokens // BLOCK
    reach_dev = (WIN + query_blocks - 1) // query_blocks
    total_blocks = query_blocks * cycle_size
    window_blocks = (2 * reach_dev + 1) * query_blocks
    softmax_scale = 1.0 / math.sqrt(HD)
    contract = (((1,), (1,)), ((), ()))
    attn_grad = lax.dot_general(
        lax.all_gather(out_grad, "sp", axis=0, tiled=True),
        out_weight,
        contract,
        preferred_element_type=jnp.float32,
    ).astype(jnp.bfloat16)
    key_value = jnp.stack((key_act, value_act))
    window = {0: key_value}
    current = passed_along(key_value, "blk", -reach_dev)
    window[reach_dev] = current
    for offset in range(reach_dev - 1, -reach_dev - 1, -1):
        current = passed_along(current, "blk", 1)
        if offset != 0:
            window[offset] = current
    gathered = jnp.concatenate(
        [window[offset] for offset in range(-reach_dev, reach_dev + 1)], axis=1
    )
    gathered = gathered.reshape(2, window_blocks, BLOCK, features)
    anchor = (my_index - reach_dev) * query_blocks
    own_lists = lax.dynamic_slice_in_dim(neighbours, my_index * query_blocks, query_blocks, 0)
    own_counts = lax.dynamic_slice_in_dim(block_counts, my_index * query_blocks, query_blocks, 0)
    window_index = (own_lists - anchor) % total_blocks
    picked = jnp.take(gathered, window_index, axis=1).reshape(
        2, query_blocks, NBR, BLOCK, head_count, HD
    )
    query_heads = query_act.reshape(query_blocks, BLOCK, head_count, HD)
    grad_heads = attn_grad.reshape(query_blocks, BLOCK, head_count, HD)
    scores = softmax_scale * jnp.einsum(
        "bihd,bsjhd->bhisj", query_heads, picked[0], preferred_element_type=jnp.float32
    )
    live_slots = jnp.arange(NBR)[None, :] < own_counts[:, None]
    scores = jnp.where(live_slots[:, None, None, :, None], scores, -jnp.inf)
    row_peak = jnp.max(scores, axis=(3, 4), keepdims=True)
    log_total = row_peak + jnp.log(jnp.sum(jnp.exp(scores - row_peak), axis=(3, 4), keepdims=True))
    soft_probs = jnp.exp(scores - log_total)
    probs_half = soft_probs.astype(jnp.bfloat16)
    outputs = jnp.einsum(
        "bhisj,bsjhd->bihd", probs_half, picked[1], preferred_element_type=jnp.float32
    )
    row_delta = jnp.transpose(jnp.sum(grad_heads.astype(jnp.float32) * outputs, axis=3), (0, 2, 1))
    prob_grad = jnp.einsum(
        "bihd,bsjhd->bhisj", grad_heads, picked[1], preferred_element_type=jnp.float32
    )
    dscore_half = (soft_probs * (prob_grad - row_delta[:, :, :, None, None])).astype(jnp.bfloat16)
    query_grad = softmax_scale * jnp.einsum(
        "bhisj,bsjhd->bihd", dscore_half, picked[0], preferred_element_type=jnp.float32
    )
    query_grad = query_grad.astype(jnp.bfloat16).reshape(tokens, features)
    key_slots = softmax_scale * jnp.einsum(
        "bhisj,bihd->bsjhd", dscore_half, query_heads, preferred_element_type=jnp.float32
    )
    value_slots = jnp.einsum(
        "bhisj,bihd->bsjhd", probs_half, grad_heads, preferred_element_type=jnp.float32
    )
    slot_grads = jnp.stack((key_slots, value_slots)).reshape(
        2, query_blocks * NBR, BLOCK * features
    )
    selector = (jnp.arange(window_blocks)[:, None] == window_index.reshape(1, -1)).astype(
        jnp.float32
    )
    window_grads = jnp.einsum("wn,gnc->gwc", selector, slot_grads, precision=lax.Precision.HIGHEST)
    summed = window_grads[:, reach_dev * query_blocks : (reach_dev + 1) * query_blocks]
    for offset in range(-reach_dev, reach_dev + 1):
        if offset != 0:
            portion = window_grads[
                :, (offset + reach_dev) * query_blocks : (offset + reach_dev + 1) * query_blocks
            ]
            summed = summed + passed_along(portion, "blk", offset)
    own_grads = summed.reshape(2, tokens, features).astype(jnp.bfloat16)
    key_grad = own_grads[0]
    value_grad = own_grads[1]
    summed_rows = lax.dot_general(
        query_grad, query_weight, contract, preferred_element_type=jnp.float32
    )
    summed_rows = summed_rows + lax.dot_general(
        key_grad, key_weight, contract, preferred_element_type=jnp.float32
    )
    summed_rows = summed_rows + lax.dot_general(
        value_grad, value_weight, contract, preferred_element_type=jnp.float32
    )
    input_grad = lax.psum_scatter(summed_rows, "sp", scatter_dimension=0, tiled=True)
    return input_grad.astype(jnp.bfloat16)


def solution(mesh):
    return jax.shard_map(
        body,
        mesh=mesh,
        in_specs=(
            P(("groups", "blk", "sp"), None),
            P(("groups", "blk"), "sp"),
            P(("groups", "blk"), "sp"),
            P(("groups", "blk"), "sp"),
            P("sp", None),
            P(None, "sp"),
            P(None, "sp"),
            P(None, "sp"),
            P("groups", None),
            P("groups"),
        ),
        out_specs=P(("groups", "blk", "sp"), None),
        check_vma=False,
    )
```

profile of v0, /device:TPU:0, one launch (start us, length us, event | category | flops | bytes accessed | tf_op | source)
XLA Modules:
  0.0 579.0 jit_solution(13881855419978878257)
XLA Ops:
  1.5 5.1 collective-permute-start
  6.6 22.4 %collective-permute-done = bf16[2,256,1024]{2,1,0:T(8,128)(2,1)S(1)} collective-permute-done((bf16[2,256,1024]{2,1,0:T(8,128)(2,1)S(1)}, bf16[2,256,1024]{2,1,0:T(8,128)(2,1)S(1)}, u32[]{:S(2)}, u32[]{:S(2)}) %collective-permute-start) | collective-permute-done | bytes 1048608 | tf_op jit(solution)/shard_map/ppermute | solution.py:16
  30.0 16.9 %collective-permute-done.1 = bf16[2,256,1024]{2,1,0:T(8,128)(2,1)S(1)} collective-permute-done((bf16[2,256,1024]{2,1,0:T(8,128)(2,1)S(1)}, bf16[2,256,1024]{2,1,0:T(8,128)(2,1)S(1)}, u32[]{:S(2)}, u32[]{:S(2)}) %collective-permute-start.1) | collective-permute-done | bytes 1048608 | tf_op jit(solution)/shard_map/ppermute | solution.py:16
  47.9 16.9 %collective-permute-done.2 = bf16[2,256,1024]{2,1,0:T(8,128)(2,1)S(1)} collective-permute-done((bf16[2,256,1024]{2,1,0:T(8,128)(2,1)S(1)}, bf16[2,256,1024]{2,1,0:T(8,128)(2,1)S(1)}, u32[]{:S(2)}, u32[]{:S(2)}) %collective-permute-start.2) | collective-permute-done | bytes 1048608 | tf_op jit(solution)/shard_map/ppermute | solution.py:16
  65.8 16.9 %collective-permute-done.3 = bf16[2,256,1024]{2,1,0:T(8,128)(2,1)S(1)} collective-permute-done((bf16[2,256,1024]{2,1,0:T(8,128)(2,1)S(1)}, bf16[2,256,1024]{2,1,0:T(8,128)(2,1)S(1)}, u32[]{:S(2)}, u32[]{:S(2)}) %collective-permute-start.3) | collective-permute-done | bytes 1048608 | tf_op jit(solution)/shard_map/ppermute | solution.py:16
  83.7 16.9 %collective-permute-done.4 = bf16[2,256,1024]{2,1,0:T(8,128)(2,1)S(1)} collective-permute-done((bf16[2,256,1024]{2,1,0:T(8,128)(2,1)S(1)}, bf16[2,256,1024]{2,1,0:T(8,128)(2,1)S(1)}, u32[]{:S(2)}, u32[]{:S(2)}) %collective-permute-start.4) | collective-permute-done | bytes 1048608 | tf_op jit(solution)/shard_map/ppermute | solution.py:16
  100.7 16.9 %collective-permute-done.5 = bf16[2,256,1024]{2,1,0:T(8,128)(2,1)S(1)} collective-permute-done((bf16[2,256,1024]{2,1,0:T(8,128)(2,1)S(1)}, bf16[2,256,1024]{2,1,0:T(8,128)(2,1)S(1)}, u32[]{:S(2)}, u32[]{:S(2)}) %collective-permute-start.5) | collective-permute-done | bytes 1048608 | tf_op jit(solution)/shard_map/ppermute | solution.py:16
  118.6 17.0 %collective-permute-done.6 = bf16[2,256,1024]{2,1,0:T(8,128)(2,1)} collective-permute-done((bf16[2,256,1024]{2,1,0:T(8,128)(2,1)S(1)}, bf16[2,256,1024]{2,1,0:T(8,128)(2,1)}, u32[]{:S(2)}, u32[]{:S(2)}) %collective-permute-start.6) | collective-permute-done | bytes 1048608 | tf_op jit(solution)/shard_map/ppermute | solution.py:16
  137.5 15.3 %collective-permute-done.7 = bf16[2,256,1024]{2,1,0:T(8,128)(2,1)} collective-permute-done((bf16[2,256,1024]{2,1,0:T(8,128)(2,1)}, bf16[2,256,1024]{2,1,0:T(8,128)(2,1)}, u32[]{:S(2)}, u32[]{:S(2)}) %collective-permute-start.7) | collective-permute-done | bytes 1048608 | tf_op jit(solution)/shard_map/ppermute | solution.py:16
  152.8 1.8 fusion.38
  157.7 12.4 %collective-permute-done.8 = bf16[2,256,1024]{2,1,0:T(8,128)(2,1)} collective-permute-done((bf16[2,256,1024]{2,1,0:T(8,128)(2,1)}, bf16[2,256,1024]{2,1,0:T(8,128)(2,1)}, u32[]{:S(2)}, u32[]{:S(2)}) %collective-permute-start.8) | collective-permute-done | bytes 1048608 | tf_op jit(solution)/shard_map/ppermute | solution.py:16
  170.1 2.3 constant_dynamic-update-slice_fusion.8
  172.3 2.3 constant_dynamic-update-slice_fusion.7
  174.6 2.3 constant_dynamic-update-slice_fusion.6
  179.1 2.3 constant_dynamic-update-slice_fusion.3
  181.3 2.3 constant_dynamic-update-slice_fusion.2
  185.8 9.1 %gather_fusion = bf16[16,2,128,1024]{3,2,1,0:T(8,128)(2,1)} fusion(bf16[2,18,128,1024]{3,2,1,0:T(8,128)(2,1)} %bitcast.2, s32[1024]{0:T(1024)S(1)} %pad_clamp_fusion), kind=kCustom, calls=%fused_computation | custom fusion | bytes 16777280 | tf_op jit(solution)/shard_map/jit(_take)/gather | solution.py:64
  194.9 11.4 %copy.46 = bf16[2,8,2,128,1024]{3,4,1,0,2:T(8,128)(2,1)} copy(bf16[2,8,2,128,1024]{4,3,2,1,0:T(8,128)(2,1)} %bitcast.91) | data formatting | bytes 16777216 | tf_op jit(solution)/shard_map/jit(_take)/gather | solution.py:64
  206.4 7.5 %select_bitcast_fusion = bf16[2,2,8,128,1024]{3,4,2,1,0:T(8,128)(2,1)} fusion(bf16[2,8,2,128,1024]{3,4,1,0,2:T(8,128)(2,1)} %copy.46, pred[2,8]{1,0:T(4,128)(4,1)S(1)} %copy.44), kind=kLoop, calls=%fused_computation.11 | loop fusion | flops 4194304 | bytes 16777232 | tf_op jit(solution)/shard_map/jit(_take)/select_n | solution.py:64
  213.9 3.8 fusion.62
  217.7 2.0 bitcast_reduce_fusion
  219.7 1.7 fusion.4
  221.4 5.4 convolution_bitcast_fusion.1
  226.8 2.9 fusion.42
  229.7 4.6 multiply_convert_fusion
  234.3 8.7 %copy.62 = f32[2,8,128,8,128]{4,3,2,1,0:T(8,128)} copy(f32[2,8,128,8,128]{2,4,1,3,0:T(8,128)} %convolution_bitcast_fusion.1) | data formatting | bytes 16777216 | tf_op jit(solution)/shard_map/bhisj,bihd->bsjhd/transpose | solution.py:93
  243.0 6.3 %stack.22 = f32[1,16,131072]{2,1,0:T(8,128)} reshape(f32[2,8,128,8,128]{4,3,2,1,0:T(8,128)} %copy.62) | data formatting | bytes 16777216 | tf_op jit(solution)/shard_map/stack | solution.py:96
  249.4 3.4 multiply_bitcast_fusion
  252.8 9.8 %copy.59 = f32[2,8,128,8,128]{4,3,2,1,0:T(8,128)} copy(f32[2,8,128,8,128]{4,2,1,3,0:T(8,128)S(1)} %multiply_bitcast_fusion) | data formatting | bytes 16777216 | tf_op jit(solution)/shard_map/mul | solution.py:90
  262.6 6.2 %stack.21 = f32[1,16,131072]{2,1,0:T(8,128)} reshape(f32[2,8,128,8,128]{4,3,2,1,0:T(8,128)} %copy.59) | data formatting | bytes 16777216 | tf_op jit(solution)/shard_map/stack | solution.py:96
  268.9 19.1 %convolution_bitcast_fusion = f32[2,18,131072]{2,1,0:T(8,128)} fusion(f32[1,16,131072]{2,1,0:T(8,128)} %stack.22, f32[1,16,131072]{2,1,0:T(8,128)} %stack.21, s32[16]{0:T(128)S(1)} %eq.18), kind=kOutput, calls=%fused_computation.1 | convolution fusion | flops 910164224 | bytes 35651648 | tf_op jit(solution)/shard_map/wn,gnc->gwc/dot_general | solution.py:102
  287.9 29.0 %fusion.61 = (f32[2,2,131072]{2,1,0:T(2,128)}, f32[2,2,131072]{2,1,0:T(2,128)}, f32[2,2,131072]{2,1,0:T(2,128)}, f32[2,2,131072]{2,1,0:T(2,128)}, f32[2,2,131072...) fusion(f32[2,18,131072]{2,1,0:T(8,128)} %convolution_bitcast_fusion), kind=kLoop, calls=%fused_computation.78 | loop fusion | bytes 33554432 | tf_op jit(solution)/shard_map/slice | solution.py:106
  317.0 2.0 collective-permute-start.16
  319.2 90.6 %collective-permute-done.9 = f32[2,2,131072]{2,1,0:T(2,128)S(1)} collective-permute-done((f32[2,2,131072]{2,1,0:T(2,128)}, f32[2,2,131072]{2,1,0:T(2,128)S(1)}, u32[]{:S(2)}, u32[]{:S(2)}) %collective-permute-start.9) | collective-permute-done | bytes 2097184 | tf_op jit(solution)/shard_map/ppermute | solution.py:16
  409.9 16.2 %collective-permute-done.15 = f32[2,2,131072]{2,1,0:T(2,128)} collective-permute-done((f32[2,2,131072]{2,1,0:T(2,128)}, f32[2,2,131072]{2,1,0:T(2,128)}, u32[]{:S(2)}, u32[]{:S(2)}) %collective-permute-start.15) | collective-permute-done | bytes 2097184 | tf_op jit(solution)/shard_map/ppermute | solution.py:16
  426.1 14.6 %collective-permute-start.10 = (f32[2,2,131072]{2,1,0:T(2,128)}, f32[2,2,131072]{2,1,0:T(2,128)}, u32[]{:S(2)}, u32[]{:S(2)}) collective-permute-start(f32[2,2,131072]{2,1,0:T(2,128)} %get-tuple-element.14), channel_id=1, source_target_pairs={{0,13},{1,14},{2,15},{3,0},{4,1},{5,2},{6,3},{7,4},{8,5},{9,6},{10... | collective-permute-start | bytes 6291464 | tf_op jit(solution)/shard_map/ppermute | solution.py:16
  440.6 4.7 fusion.39
  446.4 2.5 fusion.45
  448.9 25.6 %collective-permute-done.14 = f32[2,2,131072]{2,1,0:T(2,128)} collective-permute-done((f32[2,2,131072]{2,1,0:T(2,128)}, f32[2,2,131072]{2,1,0:T(2,128)}, u32[]{:S(2)}, u32[]{:S(2)}) %collective-permute-start.14) | collective-permute-done | bytes 2097184 | tf_op jit(solution)/shard_map/ppermute | solution.py:16
  474.6 56.5 %collective-permute-done.13 = f32[2,2,131072]{2,1,0:T(2,128)} collective-permute-done((f32[2,2,131072]{2,1,0:T(2,128)}, f32[2,2,131072]{2,1,0:T(2,128)}, u32[]{:S(2)}, u32[]{:S(2)}) %collective-permute-start.13) | collective-permute-done | bytes 2097184 | tf_op jit(solution)/shard_map/ppermute | solution.py:16
  531.1 2.8 collective-permute-done.11
  533.9 22.2 %collective-permute-done.10 = f32[2,2,131072]{2,1,0:T(2,128)} collective-permute-done((f32[2,2,131072]{2,1,0:T(2,128)}, f32[2,2,131072]{2,1,0:T(2,128)}, u32[]{:S(2)}, u32[]{:S(2)}) %collective-permute-start.10) | collective-permute-done | bytes 2097184 | tf_op jit(solution)/shard_map/ppermute | solution.py:16
  556.2 10.4 %add_convert_fusion = bf16[2,2,131072]{2,1,0:T(2,128)(2,1)S(1)} fusion(f32[2,2,131072]{2,1,0:T(2,128)} %collective-permute-done.16, f32[2,2,131072]{2,1,0:T(2,128)} %collective-permute-done.15, f32[2,2,131072]{2,1,0:T(2,128)} %collective-permute-done.14, f32[2,2,131072]{2,1,0:T(2,128)} %collective-permute-done.13, ...), kind=kLoop, calls=%fused_computation.31 | loop fusion | flops 4718592 | bytes 19922944 | tf_op jit(solution)/shard_map/convert_element_type | solution.py:110
  566.6 1.7 fusion.63
  568.3 2.3 squeeze.17
  570.6 2.3 squeeze.16
  572.9 2.5 convolution_add_fusion.1
  575.4 3.3 fusion.37
  (69 shorter events, 17.1 us)
Async XLA Ops:
  0.0 152.8 %copy-start = (bf16[1024,1024]{1,0:T(8,128)(2,1)S(1)}, bf16[1024,1024]{1,0:T(8,128)(2,1)}, u32[]{:S(2)}) copy-start(bf16[1024,1024]{1,0:T(8,128)(2,1)} %param.14) | copy-start | bytes 6291460
  1.5 27.5 %collective-permute-start = (bf16[2,256,1024]{2,1,0:T(8,128)(2,1)S(1)}, bf16[2,256,1024]{2,1,0:T(8,128)(2,1)S(1)}, u32[]{:S(2)}, u32[]{:S(2)}) collective-permute-start(bf16[2,256,1024]{2,1,0:T(8,128)(2,1)S(1)} %pad_maximum_fusion), channel_id=1, source_target_pairs={{0,12},{1,13},{2,14},{3,15},{4,0},{5,1},{6,2},{7,3},{8,4},{9,5},{1... | collective-permute-start | bytes 3145736 | tf_op jit(solution)/shard_map/ppermute | solution.py:16
  29.0 1.0 copy-start.6
  30.0 16.9 %collective-permute-start.1 = (bf16[2,256,1024]{2,1,0:T(8,128)(2,1)S(1)}, bf16[2,256,1024]{2,1,0:T(8,128)(2,1)S(1)}, u32[]{:S(2)}, u32[]{:S(2)}) collective-permute-start(bf16[2,256,1024]{2,1,0:T(8,128)(2,1)S(1)} %collective-permute-done), channel_id=1, source_target_pairs={{0,1},{1,2},{2,3},{3,4},{4,5},{5,6},{6,7},{7,8},{8,9},{9,10},{10,1... | collective-permute-start | bytes 3145736 | tf_op jit(solution)/shard_map/ppermute | solution.py:16
  46.9 1.0 copy-start.8
  47.9 16.9 %collective-permute-start.2 = (bf16[2,256,1024]{2,1,0:T(8,128)(2,1)S(1)}, bf16[2,256,1024]{2,1,0:T(8,128)(2,1)S(1)}, u32[]{:S(2)}, u32[]{:S(2)}) collective-permute-start(bf16[2,256,1024]{2,1,0:T(8,128)(2,1)S(1)} %collective-permute-done.1), channel_id=1, source_target_pairs={{0,1},{1,2},{2,3},{3,4},{4,5},{5,6},{6,7},{7,8},{8,9},{9,10},{10,1... | collective-permute-start | bytes 3145736 | tf_op jit(solution)/shard_map/ppermute | solution.py:16
  64.8 1.0 copy-start.10
  65.8 16.9 %collective-permute-start.3 = (bf16[2,256,1024]{2,1,0:T(8,128)(2,1)S(1)}, bf16[2,256,1024]{2,1,0:T(8,128)(2,1)S(1)}, u32[]{:S(2)}, u32[]{:S(2)}) collective-permute-start(bf16[2,256,1024]{2,1,0:T(8,128)(2,1)S(1)} %collective-permute-done.2), channel_id=1, source_target_pairs={{0,1},{1,2},{2,3},{3,4},{4,5},{5,6},{6,7},{7,8},{8,9},{9,10},{10,1... | collective-permute-start | bytes 3145736 | tf_op jit(solution)/shard_map/ppermute | solution.py:16
  82.7 1.0 copy-start.11
  83.7 16.9 %collective-permute-start.4 = (bf16[2,256,1024]{2,1,0:T(8,128)(2,1)S(1)}, bf16[2,256,1024]{2,1,0:T(8,128)(2,1)S(1)}, u32[]{:S(2)}, u32[]{:S(2)}) collective-permute-start(bf16[2,256,1024]{2,1,0:T(8,128)(2,1)S(1)} %collective-permute-done.3), channel_id=1, source_target_pairs={{0,1},{1,2},{2,3},{3,4},{4,5},{5,6},{6,7},{7,8},{8,9},{9,10},{10,1... | collective-permute-start | bytes 3145736 | tf_op jit(solution)/shard_map/ppermute | solution.py:16
  100.7 16.9 %collective-permute-start.5 = (bf16[2,256,1024]{2,1,0:T(8,128)(2,1)S(1)}, bf16[2,256,1024]{2,1,0:T(8,128)(2,1)S(1)}, u32[]{:S(2)}, u32[]{:S(2)}) collective-permute-start(bf16[2,256,1024]{2,1,0:T(8,128)(2,1)S(1)} %collective-permute-done.4), channel_id=1, source_target_pairs={{0,1},{1,2},{2,3},{3,4},{4,5},{5,6},{6,7},{7,8},{8,9},{9,10},{10,1... | collective-permute-start | bytes 3145736 | tf_op jit(solution)/shard_map/ppermute | solution.py:16
  117.6 1.0 copy-start.12
  118.5 17.0 %collective-permute-start.6 = (bf16[2,256,1024]{2,1,0:T(8,128)(2,1)S(1)}, bf16[2,256,1024]{2,1,0:T(8,128)(2,1)}, u32[]{:S(2)}, u32[]{:S(2)}) collective-permute-start(bf16[2,256,1024]{2,1,0:T(8,128)(2,1)S(1)} %collective-permute-done.5), channel_id=1, source_target_pairs={{0,1},{1,2},{2,3},{3,4},{4,5},{5,6},{6,7},{7,8},{8,9},{9,10},{10,1... | collective-permute-start | bytes 3145736 | tf_op jit(solution)/shard_map/ppermute | solution.py:16
  135.6 17.2 %collective-permute-start.7 = (bf16[2,256,1024]{2,1,0:T(8,128)(2,1)}, bf16[2,256,1024]{2,1,0:T(8,128)(2,1)}, u32[]{:S(2)}, u32[]{:S(2)}) collective-permute-start(bf16[2,256,1024]{2,1,0:T(8,128)(2,1)} %collective-permute-done.6), channel_id=1, source_target_pairs={{0,1},{1,2},{2,3},{3,4},{4,5},{5,6},{6,7},{7,8},{8,9},{9,10},{10,1... | collective-permute-start | bytes 3145736 | tf_op jit(solution)/shard_map/ppermute | solution.py:16
  137.5 40.5 %copy-start.4 = (bf16[256,1024]{1,0:T(8,128)(2,1)S(1)}, bf16[256,1024]{1,0:T(8,128)(2,1)}, u32[]{:S(2)}) copy-start(bf16[256,1024]{1,0:T(8,128)(2,1)} %param.13) | copy-start | bytes 1572868
  137.5 40.5 %copy-start.5 = (bf16[256,1024]{1,0:T(8,128)(2,1)S(1)}, bf16[256,1024]{1,0:T(8,128)(2,1)}, u32[]{:S(2)}) copy-start(bf16[256,1024]{1,0:T(8,128)(2,1)} %param.12) | copy-start | bytes 1572868
  152.8 17.2 %collective-permute-start.8 = (bf16[2,256,1024]{2,1,0:T(8,128)(2,1)}, bf16[2,256,1024]{2,1,0:T(8,128)(2,1)}, u32[]{:S(2)}, u32[]{:S(2)}) collective-permute-start(bf16[2,256,1024]{2,1,0:T(8,128)(2,1)} %collective-permute-done.7), channel_id=1, source_target_pairs={{0,1},{1,2},{2,3},{3,4},{4,5},{5,6},{6,7},{7,8},{8,9},{9,10},{10,1... | collective-permute-start | bytes 3145736 | tf_op jit(solution)/shard_map/ppermute | solution.py:16
  156.2 20.7 %copy-start.13 = (bf16[2,256,1024]{2,1,0:T(8,128)(2,1)S(1)}, bf16[2,256,1024]{2,1,0:T(8,128)(2,1)}, u32[]{:S(2)}) copy-start(bf16[2,256,1024]{2,1,0:T(8,128)(2,1)} %copy-done.12) | copy-start | bytes 3145732
  156.3 27.4 %copy-start.9 = (bf16[2,256,1024]{2,1,0:T(8,128)(2,1)S(1)}, bf16[2,256,1024]{2,1,0:T(8,128)(2,1)}, u32[]{:S(2)}) copy-start(bf16[2,256,1024]{2,1,0:T(8,128)(2,1)} %copy-done.8) | copy-start | bytes 3145732
  157.7 27.1 %copy-start.7 = (bf16[2,256,1024]{2,1,0:T(8,128)(2,1)S(1)}, bf16[2,256,1024]{2,1,0:T(8,128)(2,1)}, u32[]{:S(2)}) copy-start(bf16[2,256,1024]{2,1,0:T(8,128)(2,1)} %copy-done.6) | copy-start | bytes 3145732
  217.7 3.7 copy-start.2
  221.4 5.4 copy-start.14
  317.0 92.9 %collective-permute-start.9 = (f32[2,2,131072]{2,1,0:T(2,128)}, f32[2,2,131072]{2,1,0:T(2,128)S(1)}, u32[]{:S(2)}, u32[]{:S(2)}) collective-permute-start(f32[2,2,131072]{2,1,0:T(2,128)} %get-tuple-element.7), channel_id=1, source_target_pairs={{0,12},{1,13},{2,14},{3,15},{4,0},{5,1},{6,2},{7,3},{8,4},{9,5},{1... | collective-permute-start | bytes 6291464 | tf_op jit(solution)/shard_map/ppermute | solution.py:16
  317.0 92.8 %collective-permute-start.16 = (f32[2,2,131072]{2,1,0:T(2,128)}, f32[2,2,131072]{2,1,0:T(2,128)}, u32[]{:S(2)}, u32[]{:S(2)}) collective-permute-start(f32[2,2,131072]{2,1,0:T(2,128)} %get-tuple-element.8), channel_id=1, source_target_pairs={{0,4},{1,5},{2,6},{3,7},{4,8},{5,9},{6,10},{7,11},{8,12},{9,13},{1... | collective-permute-start | bytes 6291464 | tf_op jit(solution)/shard_map/ppermute | solution.py:16
  319.0 107.0 %collective-permute-start.15 = (f32[2,2,131072]{2,1,0:T(2,128)}, f32[2,2,131072]{2,1,0:T(2,128)}, u32[]{:S(2)}, u32[]{:S(2)}) collective-permute-start(f32[2,2,131072]{2,1,0:T(2,128)} %get-tuple-element.9), channel_id=1, source_target_pairs={{0,3},{1,4},{2,5},{3,6},{4,7},{5,8},{6,9},{7,10},{8,11},{9,12},{10... | collective-permute-start | bytes 6291464 | tf_op jit(solution)/shard_map/ppermute | solution.py:16
  319.0 155.5 %collective-permute-start.14 = (f32[2,2,131072]{2,1,0:T(2,128)}, f32[2,2,131072]{2,1,0:T(2,128)}, u32[]{:S(2)}, u32[]{:S(2)}) collective-permute-start(f32[2,2,131072]{2,1,0:T(2,128)} %get-tuple-element.10), channel_id=1, source_target_pairs={{0,2},{1,3},{2,4},{3,5},{4,6},{5,7},{6,8},{7,9},{8,10},{9,11},{10,... | collective-permute-start | bytes 6291464 | tf_op jit(solution)/shard_map/ppermute | solution.py:16
  319.0 212.1 %collective-permute-start.13 = (f32[2,2,131072]{2,1,0:T(2,128)}, f32[2,2,131072]{2,1,0:T(2,128)}, u32[]{:S(2)}, u32[]{:S(2)}) collective-permute-start(f32[2,2,131072]{2,1,0:T(2,128)} %get-tuple-element.11), channel_id=1, source_target_pairs={{0,1},{1,2},{2,3},{3,4},{4,5},{5,6},{6,7},{7,8},{8,9},{9,10},{10,1... | collective-permute-start | bytes 6291464 | tf_op jit(solution)/shard_map/ppermute | solution.py:16
  409.8 124.1 %copy-start.3 = (f32[2,2,131072]{2,1,0:T(2,128)}, f32[2,2,131072]{2,1,0:T(2,128)S(1)}, u32[]{:S(2)}) copy-start(f32[2,2,131072]{2,1,0:T(2,128)S(1)} %collective-permute-done.9) | copy-start | bytes 6291460
  409.8 121.3 %collective-permute-start.12 = (f32[2,2,131072]{2,1,0:T(2,128)}, f32[2,2,131072]{2,1,0:T(2,128)}, u32[]{:S(2)}, u32[]{:S(2)}) collective-permute-start(f32[2,2,131072]{2,1,0:T(2,128)} %get-tuple-element.12), channel_id=1, source_target_pairs={{0,15},{1,0},{2,1},{3,2},{4,3},{5,4},{6,5},{7,6},{8,7},{9,8},{10,9... | collective-permute-start | bytes 6291464 | tf_op jit(solution)/shard_map/ppermute | solution.py:16
  409.8 124.1 %collective-permute-start.11 = (f32[2,2,131072]{2,1,0:T(2,128)}, f32[2,2,131072]{2,1,0:T(2,128)}, u32[]{:S(2)}, u32[]{:S(2)}) collective-permute-start(f32[2,2,131072]{2,1,0:T(2,128)} %get-tuple-element.13), channel_id=1, source_target_pairs={{0,14},{1,15},{2,0},{3,1},{4,2},{5,3},{6,4},{7,5},{8,6},{9,7},{10,... | collective-permute-start | bytes 6291464 | tf_op jit(solution)/shard_map/ppermute | solution.py:16
  426.1 130.1 %collective-permute-start.10 = (f32[2,2,131072]{2,1,0:T(2,128)}, f32[2,2,131072]{2,1,0:T(2,128)}, u32[]{:S(2)}, u32[]{:S(2)}) collective-permute-start(f32[2,2,131072]{2,1,0:T(2,128)} %get-tuple-element.14), channel_id=1, source_target_pairs={{0,13},{1,14},{2,15},{3,0},{4,1},{5,2},{6,3},{7,4},{8,5},{9,6},{10... | collective-permute-start | bytes 6291464 | tf_op jit(solution)/shard_map/ppermute | solution.py:16
  556.2 22.6 %copy-start.1 = (bf16[1024,1024]{1,0:T(8,128)(2,1)S(1)}, bf16[1024,1024]{1,0:T(8,128)(2,1)}, u32[]{:S(2)}) copy-start(bf16[1024,1024]{1,0:T(8,128)(2,1)} %param.14) | copy-start | bytes 6291460
where the time goes:
time: 583 us; the launch traced here: 579 us
  waiting for transfers between devices  366 us (63%)
  local copies, waits for them, and re-layouts  116 us (20%)
  matrix products  52.2 us (9%)
  other arithmetic  23 us (4%)
  starting transfers between devices  22 us (4%)
    ppermute x17, waiting for transfers between devices, passed_along(): lax.ppermute(shard, axis, [(i, (i + by) % size) for i in range(size)])  366 us
    slice x1, local copies, waits for them, and re-layouts, body(): window_grads[:, (offset + reach_dev) * query_blocks:(offset + reach_dev +...  29 us
    ppermute x17, starting transfers between devices, passed_along(): lax.ppermute(shard, axis, [(i, (i + by) % size) for i in range(size)])  22 us
    gather x2, local copies, waits for them, and re-layouts, body(): jnp.take(gathered, window_index, axis=1)  20.5 us
    unnamed x39, local copies, waits for them, and re-layouts  20 us
    dot_general x1, matrix products, body(): jnp.einsum('wn,gnc->gwc', selector, slot_grads, precision=lax.Precision.H...  19.1 us
    another operation x2, local copies, waits for them, and re-layouts, body(): jnp.stack((key_slots, value_slots))  12.6 us
  transfers between devices with their start and end apart: 17, of which 15 were waited for; matrix products, arithmetic and copies ran while one was open for 3% of the time, Pallas kernels for 0%

commit v1 on v0

v1 whole, which is shorter than its diff:
```python
import functools
import math

import jax
import jax.numpy as jnp
from jax import lax
from jax.experimental import pallas as pl
from jax.experimental.pallas import tpu as pltpu
from jax.sharding import PartitionSpec as P

HD = 128
BLOCK = 128
NBR = 8
WIN = 8
CORES = 2
WIDTHS = (2, 4, 6, 8)
CONTRACT = (((1,), (1,)), ((), ()))
ANY = pl.BlockSpec(memory_space=pl.ANY)
VMEM = pl.BlockSpec(memory_space=pltpu.VMEM)
SMEM = pl.BlockSpec(memory_space=pltpu.SMEM)
LIMIT = pltpu.CompilerParams(vmem_limit_bytes=48 << 20)


def passed_along(shard, axis, by):
    size = lax.axis_size(axis)
    return lax.ppermute(shard, axis, [(i, (i + by) % size) for i in range(size)])


def rotated(chip, step, chips):
    return lax.rem(chip + step, chips)


def columns(head):
    return pl.ds(pl.multiple_of(head * HD, HD), HD)


def rows_of(block, size):
    return pl.ds(pl.multiple_of(block * size, size), size)


def pack_kernel(chips, chip_ref, *refs):
    sources, outs, sem = refs[:3], refs[3 : 3 + chips], refs[-1]
    copies = []
    for step in range(chips):
        head = rotated(chip_ref[0], step, chips)
        for place, source in enumerate(sources):
            copies.append(
                pltpu.make_async_copy(
                    source.at[:, columns(head)],
                    outs[step].at[place],
                    sem.at[step * 3 + place],
                )
            )
    for copy in copies:
        copy.start()
    for copy in copies:
        copy.wait()


def grad_kernel(chips, chip_ref, grad_ref, weight_ref, *outs):
    for step in range(chips):
        head = rotated(chip_ref[0], step, chips)
        outs[step][...] = lax.dot_general(
            grad_ref[...],
            weight_ref[rows_of(head, HD), :],
            CONTRACT,
            preferred_element_type=jnp.float32,
        ).astype(jnp.bfloat16)


def assemble_kernel(chips, tokens, chip_ref, *refs):
    pieces, (query_ref, pair_ref), sem = refs[:chips], refs[chips:-1], refs[-1]
    copies = []
    for step in range(chips):
        source = rotated(chip_ref[0], chips - step, chips)
        for place in range(3):
            target = query_ref if place == 0 else pair_ref.at[place - 1]
            copies.append(
                pltpu.make_async_copy(
                    pieces[step].at[place],
                    target.at[rows_of(source, tokens)],
                    sem.at[step * 3 + place],
                )
            )
    for copy in copies:
        copy.start()
    for copy in copies:
        copy.wait()


def attention_kernel(
    chips, tokens, scale, chip_ref, table_ref, count_ref, query_ref, own_ref, other_ref, *refs
):
    grads = refs[:chips]
    dq_ref, own_out, other_out = refs[chips : chips + 3]
    grad_buf, key_buf, value_buf, dk_buf, dv_buf, sem = refs[chips + 3 :]
    blocks = chips * tokens // BLOCK
    copies = [
        pltpu.make_async_copy(
            grads[step],
            grad_buf.at[rows_of(rotated(chip_ref[0], chips - step, chips), tokens)],
            sem.at[step],
        )
        for step in range(chips)
    ]
    half = blocks * BLOCK
    for place, buf in ((0, key_buf), (1, value_buf)):
        for side, source in ((0, own_ref), (1, other_ref)):
            copies.append(
                pltpu.make_async_copy(
                    source.at[place],
                    buf.at[pl.ds(side * half, half)],
                    sem.at[chips + 2 * place + side],
                )
            )
    for copy in copies:
        copy.start()
    dk_buf[...] = jnp.zeros_like(dk_buf)
    dv_buf[...] = jnp.zeros_like(dv_buf)
    for copy in copies:
        copy.wait()

    def attend(block, count, width):
        slots = [rows_of(table_ref[block * NBR + slot], BLOCK) for slot in range(width)]
        query = query_ref[rows_of(block, BLOCK), :]
        grad = grad_buf[rows_of(block, BLOCK), :]
        keys = jnp.concatenate([key_buf[slot, :] for slot in slots], axis=0)
        values = jnp.concatenate([value_buf[slot, :] for slot in slots], axis=0)
        scores = lax.dot_general(keys, query, CONTRACT, preferred_element_type=jnp.float32)
        live = lax.broadcasted_iota(jnp.int32, scores.shape, 0) < count * BLOCK
        scores = jnp.where(live, scores, -jnp.inf)
        peak = jnp.max(scores, axis=0, keepdims=True)
        weights = jnp.exp((scores - peak) * scale)
        probs = weights * (1.0 / jnp.sum(weights, axis=0, keepdims=True))
        half_probs = probs.astype(jnp.bfloat16)
        prob_grad = lax.dot_general(values, grad, CONTRACT, preferred_element_type=jnp.float32)
        delta = jnp.sum(half_probs.astype(jnp.float32) * prob_grad, axis=0, keepdims=True)
        dscore = (probs * (prob_grad - delta)).astype(jnp.bfloat16)
        dv = jnp.dot(half_probs, grad, preferred_element_type=jnp.float32)
        dk = jnp.dot(dscore, query, preferred_element_type=jnp.float32)
        dq = lax.dot_general(
            dscore, keys, (((0,), (0,)), ((), ())), preferred_element_type=jnp.float32
        )
        dq_ref[rows_of(block, BLOCK), :] = (dq * scale).astype(jnp.bfloat16)
        for place, slot in enumerate(slots):
            part = slice(place * BLOCK, (place + 1) * BLOCK)
            dk_buf[slot, :] += dk[part]
            dv_buf[slot, :] += dv[part]

    def one_block(block, carry):
        count = count_ref[block]
        below = 0
        for width in WIDTHS:
            pl.when((count > below) & (count <= width))(
                functools.partial(attend, block, count, width)
            )
            below = width
        return carry

    lax.fori_loop(0, blocks, one_block, 0)
    for place, buf, factor in ((0, dk_buf, scale), (1, dv_buf, 1.0)):
        own_out[place] = buf[:half] * factor
        other_out[place] = (buf[half:] * factor).astype(jnp.bfloat16)


def combine_kernel(chips, tokens, chip_ref, dq_ref, own_ref, other_ref, *outs):
    for step in range(chips):
        rows = rows_of(rotated(chip_ref[0], chips - step, chips), tokens)
        outs[step][0] = dq_ref[rows, :]
        for place in range(2):
            outs[step][place + 1] = (
                own_ref[place, rows, :] + other_ref[place, rows, :].astype(jnp.float32)
            ).astype(jnp.bfloat16)


def project_kernel(chips, chip_ref, *refs):
    pieces, weights = refs[:chips], refs[chips : chips + 3]
    out_ref, rows_buf, sem = refs[chips + 3 :]

    @pl.when(pl.program_id(0) == 0)
    def _():
        copies = []
        for step in range(chips):
            head = rotated(chip_ref[0], step, chips)
            for place in range(3):
                copies.append(
                    pltpu.make_async_copy(
                        pieces[step].at[place],
                        rows_buf.at[place, :, columns(head)],
                        sem.at[step * 3 + place],
                    )
                )
        for copy in copies:
            copy.start()
        for copy in copies:
            copy.wait()

    total = None
    for place in range(3):
        part = lax.dot_general(
            rows_buf[place],
            weights[place][...],
            CONTRACT,
            preferred_element_type=jnp.float32,
        )
        total = part if total is None else total + part
    out_ref[...] = total.astype(jnp.bfloat16)


def head_per_chip(
    out_grad, query_act, key_act, value_act, out_weight, weights, neighbours, block_counts
):
    my_index = lax.axis_index("blk")
    chips = lax.axis_size("blk") // CORES
    tokens, features = query_act.shape
    scale = 1.0 / math.sqrt(HD)
    chip = (my_index // CORES).astype(jnp.int32).reshape(1)
    core = my_index % CORES
    per_device = tokens // BLOCK
    blocks = chips * per_device
    bf16 = functools.partial(jax.ShapeDtypeStruct, dtype=jnp.bfloat16)

    def by_chips(shard, step):
        pairs = [
            (CORES * c + k, CORES * ((c + step) % chips) + k)
            for c in range(chips)
            for k in range(CORES)
        ]
        return lax.ppermute(shard, "blk", pairs)

    def across_cores(shard):
        return lax.ppermute(shard, "blk", [(i, i ^ 1) for i in range(chips * CORES)])

    packed = pl.pallas_call(
        functools.partial(pack_kernel, chips),
        out_shape=[bf16((3, tokens, HD))] * chips,
        in_specs=[SMEM] + [ANY] * 3,
        out_specs=[ANY] * chips,
        scratch_shapes=[pltpu.SemaphoreType.DMA((3 * chips,))],
    )(chip, query_act, key_act, value_act)
    packed = [packed[0]] + [by_chips(packed[step], step) for step in range(1, chips)]
    grads = pl.pallas_call(
        functools.partial(grad_kernel, chips),
        out_shape=[bf16((tokens, HD))] * chips,
        in_specs=[SMEM, VMEM, VMEM],
        out_specs=[VMEM] * chips,
        compiler_params=LIMIT,
    )(chip, out_grad, out_weight)
    grads = [grads[0]] + [by_chips(grads[step], step) for step in range(1, chips)]
    queries, pairs = pl.pallas_call(
        functools.partial(assemble_kernel, chips, tokens),
        out_shape=[bf16((chips * tokens, HD)), bf16((2, chips * tokens, HD))],
        in_specs=[SMEM] + [ANY] * chips,
        out_specs=[ANY] * 2,
        scratch_shapes=[pltpu.SemaphoreType.DMA((3 * chips,))],
    )(chip, *packed)
    other_pairs = across_cores(pairs)

    own = neighbours.reshape(chips, CORES, per_device, NBR)
    own = lax.dynamic_index_in_dim(own, core, 1, keepdims=False)
    counts = block_counts.reshape(chips, CORES, per_device)
    counts = lax.dynamic_index_in_dim(counts, core, 1, keepdims=False).reshape(-1)
    holder = own // per_device
    table = (
        jnp.where(holder % CORES == core, 0, blocks)
        + (holder // CORES) * per_device
        + own % per_device
    ).reshape(-1)

    half = chips * tokens
    dq, own_part, other_part = pl.pallas_call(
        functools.partial(attention_kernel, chips, tokens, scale),
        out_shape=[
            bf16((half, HD)),
            jax.ShapeDtypeStruct((2, half, HD), jnp.float32),
            bf16((2, half, HD)),
        ],
        in_specs=[SMEM] * 3 + [VMEM] + [ANY] * 2 + [ANY] * chips,
        out_specs=[VMEM] * 3,
        scratch_shapes=[
            pltpu.VMEM((half, HD), jnp.bfloat16),
            pltpu.VMEM((2 * half, HD), jnp.bfloat16),
            pltpu.VMEM((2 * half, HD), jnp.bfloat16),
            pltpu.VMEM((2 * half, HD), jnp.float32),
            pltpu.VMEM((2 * half, HD), jnp.float32),
            pltpu.SemaphoreType.DMA((chips + 4,)),
        ],
        compiler_params=LIMIT,
    )(chip, table, counts, queries, pairs, other_pairs, *grads)
    arrived = across_cores(other_part)
    back = pl.pallas_call(
        functools.partial(combine_kernel, chips, tokens),
        out_shape=[bf16((3, tokens, HD))] * chips,
        in_specs=[SMEM] + [VMEM] * 3,
        out_specs=[VMEM] * chips,
        compiler_params=LIMIT,
    )(chip, dq, own_part, arrived)
    back = [back[0]] + [by_chips(back[step], chips - step) for step in range(1, chips)]
    width = 256
    whole = lambda i: (0, 0)
    return pl.pallas_call(
        functools.partial(project_kernel, chips),
        out_shape=bf16((tokens, features)),
        grid=(features // width,),
        in_specs=[SMEM] + [ANY] * chips + [pl.BlockSpec((width, features), lambda i: (i, 0))] * 3,
        out_specs=pl.BlockSpec((tokens, width), lambda i: (0, i)),
        scratch_shapes=[
            pltpu.VMEM((3, tokens, features), jnp.bfloat16),
            pltpu.SemaphoreType.DMA((3 * chips,)),
        ],
        compiler_params=LIMIT,
    )(chip, *back, *weights)


def by_window(
    out_grad, query_act, key_act, value_act, out_weight, weights, neighbours, block_counts
):
    cycle_size = lax.axis_size("blk")
    my_index = lax.axis_index("blk")
    tokens, features = query_act.shape
    head_count = features // HD
    query_blocks = tokens // BLOCK
    reach_dev = (WIN + query_blocks - 1) // query_blocks
    total_blocks = query_blocks * cycle_size
    window_blocks = (2 * reach_dev + 1) * query_blocks
    scale = 1.0 / math.sqrt(HD)
    attn_grad = lax.dot_general(
        lax.all_gather(out_grad, "sp", axis=0, tiled=True),
        out_weight,
        CONTRACT,
        preferred_element_type=jnp.float32,
    ).astype(jnp.bfloat16)
    key_value = jnp.stack((key_act, value_act))
    gathered = jnp.concatenate(
        [
            key_value if offset == 0 else passed_along(key_value, "blk", -offset)
            for offset in range(-reach_dev, reach_dev + 1)
        ],
        axis=1,
    ).reshape(2, window_blocks, BLOCK, features)
    anchor = (my_index - reach_dev) * query_blocks
    own_lists = lax.dynamic_slice_in_dim(neighbours, my_index * query_blocks, query_blocks, 0)
    own_counts = lax.dynamic_slice_in_dim(block_counts, my_index * query_blocks, query_blocks, 0)
    window_index = ((own_lists - anchor) % total_blocks).reshape(-1)
    picked = jnp.concatenate(
        [
            lax.dynamic_slice_in_dim(gathered, window_index[n], 1, 1)
            for n in range(query_blocks * NBR)
        ],
        axis=1,
    ).reshape(2, query_blocks, NBR, BLOCK, head_count, HD)
    query_heads = query_act.reshape(query_blocks, BLOCK, head_count, HD)
    grad_heads = attn_grad.reshape(query_blocks, BLOCK, head_count, HD)
    einsum = functools.partial(jnp.einsum, preferred_element_type=jnp.float32)
    scores = scale * einsum("bihd,bsjhd->bhisj", query_heads, picked[0])
    live_slots = jnp.arange(NBR)[None, :] < own_counts[:, None]
    scores = jnp.where(live_slots[:, None, None, :, None], scores, -jnp.inf)
    row_peak = jnp.max(scores, axis=(3, 4), keepdims=True)
    log_total = row_peak + jnp.log(jnp.sum(jnp.exp(scores - row_peak), axis=(3, 4), keepdims=True))
    soft_probs = jnp.exp(scores - log_total)
    probs_half = soft_probs.astype(jnp.bfloat16)
    outputs = einsum("bhisj,bsjhd->bihd", probs_half, picked[1])
    row_delta = jnp.transpose(jnp.sum(grad_heads.astype(jnp.float32) * outputs, axis=3), (0, 2, 1))
    prob_grad = einsum("bihd,bsjhd->bhisj", grad_heads, picked[1])
    dscore_half = (soft_probs * (prob_grad - row_delta[:, :, :, None, None])).astype(jnp.bfloat16)
    query_grad = scale * einsum("bhisj,bsjhd->bihd", dscore_half, picked[0])
    query_grad = query_grad.astype(jnp.bfloat16).reshape(tokens, features)
    key_slots = scale * einsum("bhisj,bihd->bsjhd", dscore_half, query_heads)
    value_slots = einsum("bhisj,bihd->bsjhd", probs_half, grad_heads)
    slot_grads = jnp.stack((key_slots, value_slots)).reshape(
        2, query_blocks * NBR, BLOCK * features
    )
    selector = (jnp.arange(window_blocks)[:, None] == window_index.reshape(1, -1)).astype(
        jnp.float32
    )
    window_grads = jnp.einsum("wn,gnc->gwc", selector, slot_grads, precision=lax.Precision.HIGHEST)
    summed = 0.0
    for offset in range(-reach_dev, reach_dev + 1):
        first = (offset + reach_dev) * query_blocks
        portion = window_grads[:, first : first + query_blocks]
        summed = summed + (portion if offset == 0 else passed_along(portion, "blk", offset))
    own_grads = summed.reshape(2, tokens, features).astype(jnp.bfloat16)
    summed_rows = 0.0
    for grad, weight in zip((query_grad, own_grads[0], own_grads[1]), weights, strict=True):
        summed_rows = summed_rows + lax.dot_general(
            grad, weight, CONTRACT, preferred_element_type=jnp.float32
        )
    input_grad = lax.psum_scatter(summed_rows, "sp", scatter_dimension=0, tiled=True)
    return input_grad.astype(jnp.bfloat16)


def body(
    out_grad,
    query_act,
    key_act,
    value_act,
    out_weight,
    query_weight,
    key_weight,
    value_weight,
    neighbours,
    block_counts,
):
    heads = query_act.shape[1] // HD
    one_head = lax.axis_size("sp") == 1 and lax.axis_size("blk") == heads * CORES
    return (head_per_chip if one_head else by_window)(
        out_grad,
        query_act,
        key_act,
        value_act,
        out_weight,
        (query_weight, key_weight, value_weight),
        neighbours,
        block_counts,
    )


def solution(mesh):
    return jax.shard_map(
        body,
        mesh=mesh,
        in_specs=(
            P(("groups", "blk", "sp"), None),
            P(("groups", "blk"), "sp"),
            P(("groups", "blk"), "sp"),
            P(("groups", "blk"), "sp"),
            P("sp", None),
            P(None, "sp"),
            P(None, "sp"),
            P(None, "sp"),
            P("groups", None),
            P("groups"),
        ),
        out_specs=P(("groups", "blk", "sp"), None),
        check_vma=False,
    )
```

time: 583 us -> 224 us (0.38)
  waiting for transfers between devices: 366 us -> 53.3 us
  Pallas kernels: 0 us -> 121 us
  local copies, waits for them, and re-layouts: 116 us -> 4.79 us
  matrix products: 52.2 us -> 0 us
  other arithmetic: 23 us -> 0.02 us
  starting transfers between devices: 22 us -> 44.2 us
    ppermute x17 -> x23, waiting for transfers between devices: 366 us -> 53.3 us  [the longest x21 50.6 us: by_chips(): return lax.ppermute(shard, 'blk', pairs)]
    pallas_call x0 -> x6, Pallas kernels: none -> 121 us  [the longest x1 49 us: head_per_chip(): pl.pallas_call(functools.partial(pack_kernel, chips), out_shape=[bf16((3,...]
    dot_general x11 -> x0, matrix products: 52.2 us -> none  [the longest x1 19.1 us: body(): jnp.einsum('wn,gnc->gwc', selector, slot_grads, precision=lax.Precision.H...]
    slice x3 -> x0, local copies, waits for them, and re-layouts: 34.5 us -> none  [the longest x1 29 us: body(): window_grads[:, (offset + reach_dev) * query_blocks:(offset + reach_dev +...]
    ppermute x17 -> x23, starting transfers between devices: 22 us -> 44.2 us  [the longest x21 44 us: by_chips(): return lax.ppermute(shard, 'blk', pairs)]
    gather x2 -> x0, local copies, waits for them, and re-layouts: 20.5 us -> none  [body(): jnp.take(gathered, window_index, axis=1)]
    unnamed x39 -> x33, local copies, waits for them, and re-layouts: 20 us -> 4.5 us
    another operation x2 -> x0, local copies, waits for them, and re-layouts: 12.6 us -> none  [body(): jnp.stack((key_slots, value_slots))]
  transfers between devices with their start and end apart: 17 -> 23, of which waited for: 15 -> 14; matrix products, arithmetic and copies ran while one was open for 3% -> 0% of each run, Pallas kernels for 0% -> 1%
where the time goes in v1:
time: 224 us; the launch traced here: 223 us
  Pallas kernels  121 us (54%)
  waiting for transfers between devices  53.3 us (24%)
  starting transfers between devices  44.2 us (20%)
  local copies, waits for them, and re-layouts  4.79 us (2%)
    ppermute x21, waiting for transfers between devices, by_chips(): return lax.ppermute(shard, 'blk', pairs)  50.6 us
    pallas_call x1, Pallas kernels, head_per_chip(): pl.pallas_call(functools.partial(pack_kernel, chips), out_shape=[bf16((3,...  49 us
    pallas_call x1, Pallas kernels, head_per_chip(): pl.pallas_call(functools.partial(assemble_kernel, chips, tokens), out_sha...  49 us
    ppermute x21, starting transfers between devices, by_chips(): return lax.ppermute(shard, 'blk', pairs)  44 us
    pallas_call x1, Pallas kernels, head_per_chip(): pl.pallas_call(functools.partial(attention_kernel, chips, tokens, scale),...  15.6 us
    pallas_call x1, Pallas kernels, head_per_chip(): pl.pallas_call(functools.partial(project_kernel, chips), out_shape=bf16((...  5.44 us
    unnamed x33, local copies, waits for them, and re-layouts  4.5 us
  transfers between devices with their start and end apart: 23, of which 14 were waited for; matrix products, arithmetic and copies ran while one was open for 0% of the time, Pallas kernels for 1%

profile of v1, /device:TPU:0, one launch (start us, length us, event | category | flops | bytes accessed | tf_op | source)
XLA Modules:
  0.0 223.3 jit_solution(11235594006053858206)
XLA Ops:
  0.0 49.0 %shard_map.100 = (bf16[3,256,128]{2,1,0:T(8,128)(2,1)}, bf16[3,256,128]{2,1,0:T(8,128)(2,1)}, bf16[3,256,128]{2,1,0:T(8,128)(2,1)}, bf16[3,256,128]{2,1,0:T(8,12...) custom-call(s32[1]{0:T(128)} %bitcast.chip_ref, ...), custom_call_target="tpu_custom_call" | custom-call | tf_op jit(solution)/shard_map/pallas_call | solution.py:234
  49.0 3.0 %collective-permute-start = (bf16[3,256,128]{2,1,0:T(8,128)(2,1)}, bf16[3,256,128]{2,1,0:T(8,128)(2,1)S(1)}, u32[]{:S(2)}, u32[]{:S(2)}) collective-permute-start(bf16[3,256,128]{2,1,0:T(8,128)(2,1)} %get-tuple-element.35), channel_id=1, source_target_pairs={{0,2},{1,3},{2,4},{3,5},{4,6},{5,7},{6,8},{7,9},{8,10},{9,11},{10,... | collective-permute-start | bytes 589832 | tf_op jit(solution)/shard_map/ppermute | solution.py:229
  52.0 1.6 collective-permute-start.1
  53.5 2.6 %collective-permute-start.2 = (bf16[3,256,128]{2,1,0:T(8,128)(2,1)}, bf16[3,256,128]{2,1,0:T(8,128)(2,1)S(1)}, u32[]{:S(2)}, u32[]{:S(2)}) collective-permute-start(bf16[3,256,128]{2,1,0:T(8,128)(2,1)} %get-tuple-element.37), channel_id=1, source_target_pairs={{0,6},{1,7},{2,8},{3,9},{4,10},{5,11},{6,12},{7,13},{8,14},{9,15},... | collective-permute-start | bytes 589832 | tf_op jit(solution)/shard_map/ppermute | solution.py:229
  56.1 1.2 collective-permute-start.3
  57.3 2.6 %collective-permute-start.4 = (bf16[3,256,128]{2,1,0:T(8,128)(2,1)}, bf16[3,256,128]{2,1,0:T(8,128)(2,1)S(1)}, u32[]{:S(2)}, u32[]{:S(2)}) collective-permute-start(bf16[3,256,128]{2,1,0:T(8,128)(2,1)} %get-tuple-element.39), channel_id=1, source_target_pairs={{0,10},{1,11},{2,12},{3,13},{4,14},{5,15},{6,0},{7,1},{8,2},{9,3},... | collective-permute-start | bytes 589832 | tf_op jit(solution)/shard_map/ppermute | solution.py:229
  60.0 1.2 collective-permute-done.refs_1_
  61.1 1.8 collective-permute-start.5
  63.0 3.4 %collective-permute-start.6 = (bf16[3,256,128]{2,1,0:T(8,128)(2,1)}, bf16[3,256,128]{2,1,0:T(8,128)(2,1)S(1)}, u32[]{:S(2)}, u32[]{:S(2)}) collective-permute-start(bf16[3,256,128]{2,1,0:T(8,128)(2,1)} %get-tuple-element.41), channel_id=1, source_target_pairs={{0,14},{1,15},{2,0},{3,1},{4,2},{5,3},{6,4},{7,5},{8,6},{9,7},{10,... | collective-permute-start | bytes 589832 | tf_op jit(solution)/shard_map/ppermute | solution.py:229
  66.4 10.7 %collective-permute-done.2.refs_3_ = bf16[3,256,128]{2,1,0:T(8,128)(2,1)S(1)} collective-permute-done((bf16[3,256,128]{2,1,0:T(8,128)(2,1)}, bf16[3,256,128]{2,1,0:T(8,128)(2,1)S(1)}, u32[]{:S(2)}, u32[]{:S(2)}) %collective-permute-start.2) | collective-permute-done | bytes 196640 | tf_op jit(solution)/shard_map/ppermute | solution.py:229
  77.1 0.2 collective-permute-done.3.refs_4_
  77.4 1.5 collective-permute-done.6.refs_7_
  78.9 0.6 copy-done.13
  79.5 49.0 %shard_map.101 = (bf16[2048,128]{1,0:T(8,128)(2,1)}, bf16[2,2048,128]{2,1,0:T(8,128)(2,1)}) custom-call(s32[1]{0:T(128)} %bitcast.chip_ref, bf16[3,256,128]{2,1,0:T(8,128)(2,1)} %get-tuple-element.34.refs_0_, bf16[3,256,128]{2,1,0:T(8,128)(2,1)} %copy-done.7, bf16[3,256,128]{2,1,0:T(8,128)(2,1)} %copy-done.8, bf16[3,256,128]{2,1,0:T(8,128)(2,1)} %copy-done.9, ...), custom_call_target="tpu_custom_call" | custom-call | tf_op jit(solution)/shard_map/pallas_call | solution.py:250
  128.5 0.1 collective-permute-start.7
  128.6 1.1 copy-done.6
  129.7 1.7 shard_map.102
  131.4 4.3 %collective-permute-start.8 = (bf16[256,128]{1,0:T(8,128)(2,1)}, bf16[256,128]{1,0:T(8,128)(2,1)S(1)}, u32[]{:S(2)}, u32[]{:S(2)}) collective-permute-start(bf16[256,128]{1,0:T(8,128)(2,1)} %get-tuple-element.45), channel_id=1, source_target_pairs={{0,2},{1,3},{2,4},{3,5},{4,6},{5,7},{6,8},{7,9},{8,10},{9,11},{10,... | collective-permute-start | bytes 196616 | tf_op jit(solution)/shard_map/ppermute | solution.py:229
  135.7 8.8 %collective-permute-start.9 = (bf16[256,128]{1,0:T(8,128)(2,1)}, bf16[256,128]{1,0:T(8,128)(2,1)S(1)}, u32[]{:S(2)}, u32[]{:S(2)}) collective-permute-start(bf16[256,128]{1,0:T(8,128)(2,1)} %get-tuple-element.46), channel_id=1, source_target_pairs={{0,4},{1,5},{2,6},{3,7},{4,8},{5,9},{6,10},{7,11},{8,12},{9,13},{1... | collective-permute-start | bytes 196616 | tf_op jit(solution)/shard_map/ppermute | solution.py:229
  144.5 2.3 %collective-permute-start.11 = (bf16[256,128]{1,0:T(8,128)(2,1)S(1)}, bf16[256,128]{1,0:T(8,128)(2,1)S(1)}, u32[]{:S(2)}, u32[]{:S(2)}) collective-permute-start(bf16[256,128]{1,0:T(8,128)(2,1)S(1)} %get-tuple-element.48), channel_id=1, source_target_pairs={{0,8},{1,9},{2,10},{3,11},{4,12},{5,13},{6,14},{7,15},{8,0},{9,1},... | collective-permute-start | bytes 196616 | tf_op jit(solution)/shard_map/ppermute | solution.py:229
  146.8 0.1 copy.12
  146.9 0.1 squeeze.6
  147.0 1.3 collective-permute-done.8.refs_1_
  148.3 2.0 collective-permute-start.12
  150.3 0.6 collective-permute-start.13
  150.9 2.9 %collective-permute-done.10.refs_3_ = bf16[256,128]{1,0:T(8,128)(2,1)S(1)} collective-permute-done((bf16[256,128]{1,0:T(8,128)(2,1)S(1)}, bf16[256,128]{1,0:T(8,128)(2,1)S(1)}, u32[]{:S(2)}, u32[]{:S(2)}) %collective-permute-start.10) | collective-permute-done | bytes 65568 | tf_op jit(solution)/shard_map/ppermute | solution.py:229
  153.8 0.1 reshape.17
  154.0 0.1 reshape.18.count_ref
  154.1 0.0 collective-permute-done.11.refs_4_
  154.1 2.1 collective-permute-done.12.refs_5_
  156.2 0.5 collective-permute-done.13.refs_6_
  156.7 1.4 collective-permute-done.14.refs_7_
  158.1 1.0 copy-done.5
  159.1 15.6 %shard_map.103 = (bf16[2048,128]{1,0:T(8,128)(2,1)S(1)}, f32[2,2048,128]{2,1,0:T(8,128)}, bf16[2,2048,128]{2,1,0:T(8,128)(2,1)S(1)}) custom-call(s32[1]{0:T(128)} %bitcast.chip_ref, s32[128]{0:T(128)S(1)} %fusion.table_ref, s32[16]{0:T(128)S(1)} %reshape.18.count_ref, bf16[2048,128]{1,0:T(8,128)(2,1)S(1)} %copy-done.5, bf16[2,2048,128]{2,1,0:T(8,128)(2,1)S(1)} %copy-done.4, ...), custom_call_target="tpu_custom_call" | custom-call | tf_op jit(solution)/shard_map/pallas_call | solution.py:271
  174.7 0.1 collective-permute-start.15
  174.8 2.6 %collective-permute-done.15.other_ref = bf16[2,2048,128]{2,1,0:T(8,128)(2,1)S(1)} collective-permute-done((bf16[2,2048,128]{2,1,0:T(8,128)(2,1)S(1)}, bf16[2,2048,128]{2,1,0:T(8,128)(2,1)S(1)}, u32[]{:S(2)}, u32[]{:S(2)}) %collective-permute-start.15) | collective-permute-done | bytes 1048608 | tf_op jit(solution)/shard_map/ppermute | solution.py:232
  177.5 1.6 copy-done.1
  179.0 0.2 shard_map.104
  179.2 3.5 %collective-permute-start.16 = (bf16[3,256,128]{2,1,0:T(8,128)(2,1)S(1)}, bf16[3,256,128]{2,1,0:T(8,128)(2,1)S(1)}, u32[]{:S(2)}, u32[]{:S(2)}) collective-permute-start(bf16[3,256,128]{2,1,0:T(8,128)(2,1)S(1)} %get-tuple-element.56), channel_id=1, source_target_pairs={{0,14},{1,15},{2,0},{3,1},{4,2},{5,3},{6,4},{7,5},{8,6},{9,7},{10,... | collective-permute-start | bytes 589832 | tf_op jit(solution)/shard_map/ppermute | solution.py:229
  182.7 1.8 collective-permute-start.17
  184.5 3.5 %collective-permute-start.19 = (bf16[3,256,128]{2,1,0:T(8,128)(2,1)S(1)}, bf16[3,256,128]{2,1,0:T(8,128)(2,1)S(1)}, u32[]{:S(2)}, u32[]{:S(2)}) collective-permute-start(bf16[3,256,128]{2,1,0:T(8,128)(2,1)S(1)} %get-tuple-element.59), channel_id=1, source_target_pairs={{0,8},{1,9},{2,10},{3,11},{4,12},{5,13},{6,14},{7,15},{8,0},{9,1},... | collective-permute-start | bytes 589832 | tf_op jit(solution)/shard_map/ppermute | solution.py:229
  188.0 0.0 collective-permute-done.16.refs_1_
  188.0 1.0 collective-permute-start.21
  189.0 3.3 %collective-permute-done.17.refs_2_ = bf16[3,256,128]{2,1,0:T(8,128)(2,1)S(1)} collective-permute-done((bf16[3,256,128]{2,1,0:T(8,128)(2,1)S(1)}, bf16[3,256,128]{2,1,0:T(8,128)(2,1)S(1)}, u32[]{:S(2)}, u32[]{:S(2)}) %collective-permute-start.17) | collective-permute-done | bytes 196640 | tf_op jit(solution)/shard_map/ppermute | solution.py:229
  192.3 4.3 %collective-permute-done.18.refs_3_ = bf16[3,256,128]{2,1,0:T(8,128)(2,1)S(1)} collective-permute-done((bf16[3,256,128]{2,1,0:T(8,128)(2,1)S(1)}, bf16[3,256,128]{2,1,0:T(8,128)(2,1)S(1)}, u32[]{:S(2)}, u32[]{:S(2)}) %collective-permute-start.18) | collective-permute-done | bytes 196640 | tf_op jit(solution)/shard_map/ppermute | solution.py:229
  196.5 21.0 %collective-permute-done.19.refs_4_ = bf16[3,256,128]{2,1,0:T(8,128)(2,1)S(1)} collective-permute-done((bf16[3,256,128]{2,1,0:T(8,128)(2,1)S(1)}, bf16[3,256,128]{2,1,0:T(8,128)(2,1)S(1)}, u32[]{:S(2)}, u32[]{:S(2)}) %collective-permute-start.19) | collective-permute-done | bytes 196640 | tf_op jit(solution)/shard_map/ppermute | solution.py:229
  217.6 0.2 collective-permute-done.20.refs_5_
  217.8 5.4 %shard_map.105 = bf16[256,1024]{1,0:T(8,128)(2,1)} custom-call(s32[1]{0:T(128)} %bitcast.chip_ref, bf16[3,256,128]{2,1,0:T(8,128)(2,1)S(1)} %get-tuple-element.55.refs_0_, bf16[3,256,128]{2,1,0:T(8,128)(2,1)S(1)} %collective-permute-done.16.refs_1_, bf16[3,256,128]{2,1,0:T(8,128)(2,1)S(1)} %collective-permute-done.17.refs_2_, ...), custom_call_target="tpu_custom_call" | custom-call | tf_op jit(solution)/shard_map/pallas_call | solution.py:301
  (43 shorter events, 0.1 us)
Async XLA Ops:
  0.0 128.6 %copy-start = (bf16[1024,1024]{1,0:T(8,128)(2,1)S(1)}, bf16[1024,1024]{1,0:T(8,128)(2,1)}, u32[]{:S(2)}) copy-start(bf16[1024,1024]{1,0:T(8,128)(2,1)} %weight_ref.1) | copy-start | bytes 6291460
  49.0 12.2 %collective-permute-start = (bf16[3,256,128]{2,1,0:T(8,128)(2,1)}, bf16[3,256,128]{2,1,0:T(8,128)(2,1)S(1)}, u32[]{:S(2)}, u32[]{:S(2)}) collective-permute-start(bf16[3,256,128]{2,1,0:T(8,128)(2,1)} %get-tuple-element.35), channel_id=1, source_target_pairs={{0,2},{1,3},{2,4},{3,5},{4,6},{5,7},{6,8},{7,9},{8,10},{9,11},{10,... | collective-permute-start | bytes 589832 | tf_op jit(solution)/shard_map/ppermute | solution.py:229
  52.0 11.0 %collective-permute-start.1 = (bf16[3,256,128]{2,1,0:T(8,128)(2,1)}, bf16[3,256,128]{2,1,0:T(8,128)(2,1)S(1)}, u32[]{:S(2)}, u32[]{:S(2)}) collective-permute-start(bf16[3,256,128]{2,1,0:T(8,128)(2,1)} %get-tuple-element.36), channel_id=1, source_target_pairs={{0,4},{1,5},{2,6},{3,7},{4,8},{5,9},{6,10},{7,11},{8,12},{9,13},{1... | collective-permute-start | bytes 589832 | tf_op jit(solution)/shard_map/ppermute | solution.py:229
  53.5 23.6 %collective-permute-start.2 = (bf16[3,256,128]{2,1,0:T(8,128)(2,1)}, bf16[3,256,128]{2,1,0:T(8,128)(2,1)S(1)}, u32[]{:S(2)}, u32[]{:S(2)}) collective-permute-start(bf16[3,256,128]{2,1,0:T(8,128)(2,1)} %get-tuple-element.37), channel_id=1, source_target_pairs={{0,6},{1,7},{2,8},{3,9},{4,10},{5,11},{6,12},{7,13},{8,14},{9,15},... | collective-permute-start | bytes 589832 | tf_op jit(solution)/shard_map/ppermute | solution.py:229
  56.1 21.2 %collective-permute-start.3 = (bf16[3,256,128]{2,1,0:T(8,128)(2,1)}, bf16[3,256,128]{2,1,0:T(8,128)(2,1)S(1)}, u32[]{:S(2)}, u32[]{:S(2)}) collective-permute-start(bf16[3,256,128]{2,1,0:T(8,128)(2,1)} %get-tuple-element.38), channel_id=1, source_target_pairs={{0,8},{1,9},{2,10},{3,11},{4,12},{5,13},{6,14},{7,15},{8,0},{9,1},... | collective-permute-start | bytes 589832 | tf_op jit(solution)/shard_map/ppermute | solution.py:229
  57.3 20.0 %collective-permute-start.4 = (bf16[3,256,128]{2,1,0:T(8,128)(2,1)}, bf16[3,256,128]{2,1,0:T(8,128)(2,1)S(1)}, u32[]{:S(2)}, u32[]{:S(2)}) collective-permute-start(bf16[3,256,128]{2,1,0:T(8,128)(2,1)} %get-tuple-element.39), channel_id=1, source_target_pairs={{0,10},{1,11},{2,12},{3,13},{4,14},{5,15},{6,0},{7,1},{8,2},{9,3},... | collective-permute-start | bytes 589832 | tf_op jit(solution)/shard_map/ppermute | solution.py:229
  61.1 17.7 %copy-start.7 = (bf16[3,256,128]{2,1,0:T(8,128)(2,1)}, bf16[3,256,128]{2,1,0:T(8,128)(2,1)S(1)}, u32[]{:S(2)}) copy-start(bf16[3,256,128]{2,1,0:T(8,128)(2,1)S(1)} %collective-permute-done.refs_1_) | copy-start | bytes 589828
  61.1 16.2 %collective-permute-start.5 = (bf16[3,256,128]{2,1,0:T(8,128)(2,1)}, bf16[3,256,128]{2,1,0:T(8,128)(2,1)S(1)}, u32[]{:S(2)}, u32[]{:S(2)}) collective-permute-start(bf16[3,256,128]{2,1,0:T(8,128)(2,1)} %get-tuple-element.40), channel_id=1, source_target_pairs={{0,12},{1,13},{2,14},{3,15},{4,0},{5,1},{6,2},{7,3},{8,4},{9,5},{1... | collective-permute-start | bytes 589832 | tf_op jit(solution)/shard_map/ppermute | solution.py:229
  63.0 15.9 %copy-start.8 = (bf16[3,256,128]{2,1,0:T(8,128)(2,1)}, bf16[3,256,128]{2,1,0:T(8,128)(2,1)S(1)}, u32[]{:S(2)}) copy-start(bf16[3,256,128]{2,1,0:T(8,128)(2,1)S(1)} %collective-permute-done.1.refs_2_) | copy-start | bytes 589828
  63.0 15.9 %collective-permute-start.6 = (bf16[3,256,128]{2,1,0:T(8,128)(2,1)}, bf16[3,256,128]{2,1,0:T(8,128)(2,1)S(1)}, u32[]{:S(2)}, u32[]{:S(2)}) collective-permute-start(bf16[3,256,128]{2,1,0:T(8,128)(2,1)} %get-tuple-element.41), channel_id=1, source_target_pairs={{0,14},{1,15},{2,0},{3,1},{4,2},{5,3},{6,4},{7,5},{8,6},{9,7},{10,... | collective-permute-start | bytes 589832 | tf_op jit(solution)/shard_map/ppermute | solution.py:229
  77.1 1.8 copy-start.9
  77.3 1.5 copy-start.10
  77.3 1.5 copy-start.11
  77.4 1.5 copy-start.12
  78.8 0.7 copy-start.13
  79.5 67.3 %copy-start.14 = (s32[32,8]{0,1:T(8,128)S(1)}, s32[32,8]{0,1:T(8,128)}, u32[]{:S(2)}) copy-start(s32[32,8]{0,1:T(8,128)} %param.18) | copy-start | bytes 3076
  79.5 74.3 %copy-start.15 = (s32[32]{0:T(128)S(1)}, s32[32]{0:T(128)}, u32[]{:S(2)}) copy-start(s32[32]{0:T(128)} %param.19) | copy-start | bytes 388
  128.5 29.6 %copy-start.4 = (bf16[2,2048,128]{2,1,0:T(8,128)(2,1)S(1)}, bf16[2,2048,128]{2,1,0:T(8,128)(2,1)}, u32[]{:S(2)}) copy-start(bf16[2,2048,128]{2,1,0:T(8,128)(2,1)} %get-tuple-element.43.own_ref) | copy-start | bytes 3145732
  128.5 29.6 %collective-permute-start.7 = (bf16[2,2048,128]{2,1,0:T(8,128)(2,1)}, bf16[2,2048,128]{2,1,0:T(8,128)(2,1)}, u32[]{:S(2)}, u32[]{:S(2)}) collective-permute-start(bf16[2,2048,128]{2,1,0:T(8,128)(2,1)} %get-tuple-element.43.own_ref), channel_id=1, source_target_pairs={{0,1},{1,0},{2,3},{3,2},{4,5},{5,4},{6,7},{7,6},{8,9},{9,8},{10,11... | collective-permute-start | bytes 3145736 | tf_op jit(solution)/shard_map/ppermute | solution.py:232
  128.6 1.1 copy-start.6
  131.4 16.9 %collective-permute-start.8 = (bf16[256,128]{1,0:T(8,128)(2,1)}, bf16[256,128]{1,0:T(8,128)(2,1)S(1)}, u32[]{:S(2)}, u32[]{:S(2)}) collective-permute-start(bf16[256,128]{1,0:T(8,128)(2,1)} %get-tuple-element.45), channel_id=1, source_target_pairs={{0,2},{1,3},{2,4},{3,5},{4,6},{5,7},{6,8},{7,9},{8,10},{9,11},{10,... | collective-permute-start | bytes 196616 | tf_op jit(solution)/shard_map/ppermute | solution.py:229
  135.7 14.6 %collective-permute-start.9 = (bf16[256,128]{1,0:T(8,128)(2,1)}, bf16[256,128]{1,0:T(8,128)(2,1)S(1)}, u32[]{:S(2)}, u32[]{:S(2)}) collective-permute-start(bf16[256,128]{1,0:T(8,128)(2,1)} %get-tuple-element.46), channel_id=1, source_target_pairs={{0,4},{1,5},{2,6},{3,7},{4,8},{5,9},{6,10},{7,11},{8,12},{9,13},{1... | collective-permute-start | bytes 196616 | tf_op jit(solution)/shard_map/ppermute | solution.py:229
  144.5 9.3 %collective-permute-start.10 = (bf16[256,128]{1,0:T(8,128)(2,1)S(1)}, bf16[256,128]{1,0:T(8,128)(2,1)S(1)}, u32[]{:S(2)}, u32[]{:S(2)}) collective-permute-start(bf16[256,128]{1,0:T(8,128)(2,1)S(1)} %get-tuple-element.47), channel_id=1, source_target_pairs={{0,6},{1,7},{2,8},{3,9},{4,10},{5,11},{6,12},{7,13},{8,14},{9,15},... | collective-permute-start | bytes 196616 | tf_op jit(solution)/shard_map/ppermute | solution.py:229
  144.5 9.6 %collective-permute-start.11 = (bf16[256,128]{1,0:T(8,128)(2,1)S(1)}, bf16[256,128]{1,0:T(8,128)(2,1)S(1)}, u32[]{:S(2)}, u32[]{:S(2)}) collective-permute-start(bf16[256,128]{1,0:T(8,128)(2,1)S(1)} %get-tuple-element.48), channel_id=1, source_target_pairs={{0,8},{1,9},{2,10},{3,11},{4,12},{5,13},{6,14},{7,15},{8,0},{9,1},... | collective-permute-start | bytes 196616 | tf_op jit(solution)/shard_map/ppermute | solution.py:229
  148.3 7.9 %collective-permute-start.12 = (bf16[256,128]{1,0:T(8,128)(2,1)S(1)}, bf16[256,128]{1,0:T(8,128)(2,1)S(1)}, u32[]{:S(2)}, u32[]{:S(2)}) collective-permute-start(bf16[256,128]{1,0:T(8,128)(2,1)S(1)} %get-tuple-element.49), channel_id=1, source_target_pairs={{0,10},{1,11},{2,12},{3,13},{4,14},{5,15},{6,0},{7,1},{8,2},{9,3},... | collective-permute-start | bytes 196616 | tf_op jit(solution)/shard_map/ppermute | solution.py:229
  150.3 6.4 %collective-permute-start.13 = (bf16[256,128]{1,0:T(8,128)(2,1)S(1)}, bf16[256,128]{1,0:T(8,128)(2,1)S(1)}, u32[]{:S(2)}, u32[]{:S(2)}) collective-permute-start(bf16[256,128]{1,0:T(8,128)(2,1)S(1)} %get-tuple-element.50), channel_id=1, source_target_pairs={{0,12},{1,13},{2,14},{3,15},{4,0},{5,1},{6,2},{7,3},{8,4},{9,5},{1... | collective-permute-start | bytes 196616 | tf_op jit(solution)/shard_map/ppermute | solution.py:229
  153.8 4.3 %collective-permute-start.14 = (bf16[256,128]{1,0:T(8,128)(2,1)S(1)}, bf16[256,128]{1,0:T(8,128)(2,1)S(1)}, u32[]{:S(2)}, u32[]{:S(2)}) collective-permute-start(bf16[256,128]{1,0:T(8,128)(2,1)S(1)} %get-tuple-element.51), channel_id=1, source_target_pairs={{0,14},{1,15},{2,0},{3,1},{4,2},{5,3},{6,4},{7,5},{8,6},{9,7},{10,... | collective-permute-start | bytes 196616 | tf_op jit(solution)/shard_map/ppermute | solution.py:229
  158.1 1.0 copy-start.5
  159.1 58.7 %copy-start.2 = (bf16[1024,1024]{1,0:T(8,128)(2,1)S(1)}, bf16[1024,1024]{1,0:T(8,128)(2,1)}, u32[]{:S(2)}) copy-start(bf16[1024,1024]{1,0:T(8,128)(2,1)} %refs_8_.1) | copy-start | bytes 6291460
  174.7 2.7 %collective-permute-start.15 = (bf16[2,2048,128]{2,1,0:T(8,128)(2,1)S(1)}, bf16[2,2048,128]{2,1,0:T(8,128)(2,1)S(1)}, u32[]{:S(2)}, u32[]{:S(2)}) collective-permute-start(bf16[2,2048,128]{2,1,0:T(8,128)(2,1)S(1)} %get-tuple-element.54), channel_id=1, source_target_pairs={{0,1},{1,0},{2,3},{3,2},{4,5},{5,4},{6,7},{7,6},{8,9},{9,8},{10,11... | collective-permute-start | bytes 3145736 | tf_op jit(solution)/shard_map/ppermute | solution.py:232
  177.4 1.6 copy-start.1
  179.0 38.8 %copy-start.3 = (bf16[1024,1024]{1,0:T(8,128)(2,1)S(1)}, bf16[1024,1024]{1,0:T(8,128)(2,1)}, u32[]{:S(2)}) copy-start(bf16[1024,1024]{1,0:T(8,128)(2,1)} %refs_9_.1) | copy-start | bytes 6291460
  179.2 8.8 %collective-permute-start.16 = (bf16[3,256,128]{2,1,0:T(8,128)(2,1)S(1)}, bf16[3,256,128]{2,1,0:T(8,128)(2,1)S(1)}, u32[]{:S(2)}, u32[]{:S(2)}) collective-permute-start(bf16[3,256,128]{2,1,0:T(8,128)(2,1)S(1)} %get-tuple-element.56), channel_id=1, source_target_pairs={{0,14},{1,15},{2,0},{3,1},{4,2},{5,3},{6,4},{7,5},{8,6},{9,7},{10,... | collective-permute-start | bytes 589832 | tf_op jit(solution)/shard_map/ppermute | solution.py:229
  182.7 9.6 %collective-permute-start.17 = (bf16[3,256,128]{2,1,0:T(8,128)(2,1)S(1)}, bf16[3,256,128]{2,1,0:T(8,128)(2,1)S(1)}, u32[]{:S(2)}, u32[]{:S(2)}) collective-permute-start(bf16[3,256,128]{2,1,0:T(8,128)(2,1)S(1)} %get-tuple-element.57), channel_id=1, source_target_pairs={{0,12},{1,13},{2,14},{3,15},{4,0},{5,1},{6,2},{7,3},{8,4},{9,5},{1... | collective-permute-start | bytes 589832 | tf_op jit(solution)/shard_map/ppermute | solution.py:229
  184.5 12.0 %collective-permute-start.18 = (bf16[3,256,128]{2,1,0:T(8,128)(2,1)S(1)}, bf16[3,256,128]{2,1,0:T(8,128)(2,1)S(1)}, u32[]{:S(2)}, u32[]{:S(2)}) collective-permute-start(bf16[3,256,128]{2,1,0:T(8,128)(2,1)S(1)} %get-tuple-element.58), channel_id=1, source_target_pairs={{0,10},{1,11},{2,12},{3,13},{4,14},{5,15},{6,0},{7,1},{8,2},{9,3},... | collective-permute-start | bytes 589832 | tf_op jit(solution)/shard_map/ppermute | solution.py:229
  184.5 33.0 %collective-permute-start.19 = (bf16[3,256,128]{2,1,0:T(8,128)(2,1)S(1)}, bf16[3,256,128]{2,1,0:T(8,128)(2,1)S(1)}, u32[]{:S(2)}, u32[]{:S(2)}) collective-permute-start(bf16[3,256,128]{2,1,0:T(8,128)(2,1)S(1)} %get-tuple-element.59), channel_id=1, source_target_pairs={{0,8},{1,9},{2,10},{3,11},{4,12},{5,13},{6,14},{7,15},{8,0},{9,1},... | collective-permute-start | bytes 589832 | tf_op jit(solution)/shard_map/ppermute | solution.py:229
  188.0 29.8 %collective-permute-start.20 = (bf16[3,256,128]{2,1,0:T(8,128)(2,1)S(1)}, bf16[3,256,128]{2,1,0:T(8,128)(2,1)S(1)}, u32[]{:S(2)}, u32[]{:S(2)}) collective-permute-start(bf16[3,256,128]{2,1,0:T(8,128)(2,1)S(1)} %get-tuple-element.60), channel_id=1, source_target_pairs={{0,6},{1,7},{2,8},{3,9},{4,10},{5,11},{6,12},{7,13},{8,14},{9,15},... | collective-permute-start | bytes 589832 | tf_op jit(solution)/shard_map/ppermute | solution.py:229
  188.0 29.8 %collective-permute-start.21 = (bf16[3,256,128]{2,1,0:T(8,128)(2,1)S(1)}, bf16[3,256,128]{2,1,0:T(8,128)(2,1)S(1)}, u32[]{:S(2)}, u32[]{:S(2)}) collective-permute-start(bf16[3,256,128]{2,1,0:T(8,128)(2,1)S(1)} %get-tuple-element.61), channel_id=1, source_target_pairs={{0,4},{1,5},{2,6},{3,7},{4,8},{5,9},{6,10},{7,11},{8,12},{9,13},{1... | collective-permute-start | bytes 589832 | tf_op jit(solution)/shard_map/ppermute | solution.py:229
  192.3 25.5 %collective-permute-start.22 = (bf16[3,256,128]{2,1,0:T(8,128)(2,1)S(1)}, bf16[3,256,128]{2,1,0:T(8,128)(2,1)S(1)}, u32[]{:S(2)}, u32[]{:S(2)}) collective-permute-start(bf16[3,256,128]{2,1,0:T(8,128)(2,1)S(1)} %get-tuple-element.62), channel_id=1, source_target_pairs={{0,2},{1,3},{2,4},{3,5},{4,6},{5,7},{6,8},{7,9},{8,10},{9,11},{10,... | collective-permute-start | bytes 589832 | tf_op jit(solution)/shard_map/ppermute | solution.py:229

commit v2 on v1

--- a/solution.py
+++ b/solution.py
@@ -39,22 +39,11 @@
 
 
 def pack_kernel(chips, chip_ref, *refs):
-    sources, outs, sem = refs[:3], refs[3 : 3 + chips], refs[-1]
-    copies = []
+    sources, outs = refs[:3], refs[3:]
     for step in range(chips):
         head = rotated(chip_ref[0], step, chips)
         for place, source in enumerate(sources):
-            copies.append(
-                pltpu.make_async_copy(
-                    source.at[:, columns(head)],
-                    outs[step].at[place],
-                    sem.at[step * 3 + place],
-                )
-            )
-    for copy in copies:
-        copy.start()
-    for copy in copies:
-        copy.wait()
+            outs[step][place] = source[:, columns(head)]
 
 
 def grad_kernel(chips, chip_ref, grad_ref, weight_ref, *outs):
@@ -69,23 +58,12 @@
 
 
 def assemble_kernel(chips, tokens, chip_ref, *refs):
-    pieces, (query_ref, pair_ref), sem = refs[:chips], refs[chips:-1], refs[-1]
-    copies = []
+    pieces, (query_ref, pair_ref) = refs[:chips], refs[chips:]
     for step in range(chips):
-        source = rotated(chip_ref[0], chips - step, chips)
-        for place in range(3):
-            target = query_ref if place == 0 else pair_ref.at[place - 1]
-            copies.append(
-                pltpu.make_async_copy(
-                    pieces[step].at[place],
-                    target.at[rows_of(source, tokens)],
-                    sem.at[step * 3 + place],
-                )
-            )
-    for copy in copies:
-        copy.start()
-    for copy in copies:
-        copy.wait()
+        rows = rows_of(rotated(chip_ref[0], chips - step, chips), tokens)
+        query_ref[rows, :] = pieces[step][0]
+        for place in range(2):
+            pair_ref[place, rows, :] = pieces[step][place + 1]
 
 
 def attention_kernel(
@@ -234,9 +212,9 @@
     packed = pl.pallas_call(
         functools.partial(pack_kernel, chips),
         out_shape=[bf16((3, tokens, HD))] * chips,
-        in_specs=[SMEM] + [ANY] * 3,
-        out_specs=[ANY] * chips,
-        scratch_shapes=[pltpu.SemaphoreType.DMA((3 * chips,))],
+        in_specs=[SMEM] + [VMEM] * 3,
+        out_specs=[VMEM] * chips,
+        compiler_params=LIMIT,
     )(chip, query_act, key_act, value_act)
     packed = [packed[0]] + [by_chips(packed[step], step) for step in range(1, chips)]
     grads = pl.pallas_call(
@@ -246,13 +224,14 @@
         out_specs=[VMEM] * chips,
         compiler_params=LIMIT,
     )(chip, out_grad, out_weight)
+    packed, _ = lax.optimization_barrier((packed, grads))
     grads = [grads[0]] + [by_chips(grads[step], step) for step in range(1, chips)]
     queries, pairs = pl.pallas_call(
         functools.partial(assemble_kernel, chips, tokens),
         out_shape=[bf16((chips * tokens, HD)), bf16((2, chips * tokens, HD))],
-        in_specs=[SMEM] + [ANY] * chips,
-        out_specs=[ANY] * 2,
-        scratch_shapes=[pltpu.SemaphoreType.DMA((3 * chips,))],
+        in_specs=[SMEM] + [VMEM] * chips,
+        out_specs=[VMEM] * 2,
+        compiler_params=LIMIT,
     )(chip, *packed)
     other_pairs = across_cores(pairs)
 

time: 224 us -> 125 us (0.56)
  Pallas kernels: 121 us -> 22.1 us
  waiting for transfers between devices: 53.3 us -> 48.8 us
  local copies, waits for them, and re-layouts: 4.79 us -> 7.73 us
    pallas_call x1, Pallas kernels: 49 us -> 0.11 us  [head_per_chip(): pl.pallas_call(functools.partial(assemble_kernel, chips, tokens), out_sha...]
    pallas_call x1, Pallas kernels: 49 us -> 0.41 us  [head_per_chip(): pl.pallas_call(functools.partial(pack_kernel, chips), out_shape=[bf16((3,...]
    ppermute x21, waiting for transfers between devices: 50.6 us -> 46.1 us  [by_chips(): return lax.ppermute(shard, 'blk', pairs)]
    unnamed x33 -> x21, local copies, waits for them, and re-layouts: 4.5 us -> 7.44 us
  transfers between devices with their start and end apart: 23 -> 23, of which waited for: 14 -> 15; matrix products, arithmetic and copies ran while one was open for 0% -> 0% of each run, Pallas kernels for 1% -> 1%
where the time goes in v2:
time: 125 us; the launch traced here: 123 us
  waiting for transfers between devices  48.8 us (39%)
  starting transfers between devices  44.5 us (36%)
  Pallas kernels  22.1 us (18%)
  local copies, waits for them, and re-layouts  7.73 us (6%)
    ppermute x21, waiting for transfers between devices, by_chips(): return lax.ppermute(shard, 'blk', pairs)  46.1 us
    ppermute x21, starting transfers between devices, by_chips(): return lax.ppermute(shard, 'blk', pairs)  44.4 us
    pallas_call x1, Pallas kernels, head_per_chip(): pl.pallas_call(functools.partial(attention_kernel, chips, tokens, scale),...  14.7 us
    unnamed x21, local copies, waits for them, and re-layouts  7.44 us
    pallas_call x1, Pallas kernels, head_per_chip(): pl.pallas_call(functools.partial(project_kernel, chips), out_shape=bf16((...  5.44 us
    ppermute x2, waiting for transfers between devices, across_cores(): lax.ppermute(shard, 'blk', [(i, i ^ 1) for i in range(chips * CORES)])  2.65 us
  transfers between devices with their start and end apart: 23, of which 15 were waited for; matrix products, arithmetic and copies ran while one was open for 0% of the time, Pallas kernels for 1%

profile of v2, /device:TPU:0, one launch (start us, length us, event | category | flops | bytes accessed | tf_op | source)
XLA Modules:
  0.0 123.3 jit_solution(2973841838870874011)
XLA Ops:
  0.0 1.0 copy-done.4
  1.0 1.0 copy-done.5
  2.1 1.0 copy-done.6
  3.1 0.4 shard_map.100
  3.5 3.0 %collective-permute-start = (bf16[3,256,128]{2,1,0:T(8,128)(2,1)S(1)}, bf16[3,256,128]{2,1,0:T(8,128)(2,1)S(1)}, u32[]{:S(2)}, u32[]{:S(2)}) collective-permute-start(bf16[3,256,128]{2,1,0:T(8,128)(2,1)S(1)} %get-tuple-element.43), channel_id=1, source_target_pairs={{0,2},{1,3},{2,4},{3,5},{4,6},{5,7},{6,8},{7,9},{8,10},{9,11},{10,... | collective-permute-start | bytes 589832 | tf_op jit(solution)/shard_map/ppermute | solution.py:207
  6.5 1.6 %collective-permute-start.1 = (bf16[3,256,128]{2,1,0:T(8,128)(2,1)S(1)}, bf16[3,256,128]{2,1,0:T(8,128)(2,1)S(1)}, u32[]{:S(2)}, u32[]{:S(2)}) collective-permute-start(bf16[3,256,128]{2,1,0:T(8,128)(2,1)S(1)} %get-tuple-element.44), channel_id=1, source_target_pairs={{0,4},{1,5},{2,6},{3,7},{4,8},{5,9},{6,10},{7,11},{8,12},{9,13},{1... | collective-permute-start | bytes 589832 | tf_op jit(solution)/shard_map/ppermute | solution.py:207
  8.1 2.6 %collective-permute-start.2 = (bf16[3,256,128]{2,1,0:T(8,128)(2,1)S(1)}, bf16[3,256,128]{2,1,0:T(8,128)(2,1)S(1)}, u32[]{:S(2)}, u32[]{:S(2)}) collective-permute-start(bf16[3,256,128]{2,1,0:T(8,128)(2,1)S(1)} %get-tuple-element.45), channel_id=1, source_target_pairs={{0,6},{1,7},{2,8},{3,9},{4,10},{5,11},{6,12},{7,13},{8,14},{9,15},... | collective-permute-start | bytes 589832 | tf_op jit(solution)/shard_map/ppermute | solution.py:207
  10.7 1.2 %collective-permute-start.3 = (bf16[3,256,128]{2,1,0:T(8,128)(2,1)S(1)}, bf16[3,256,128]{2,1,0:T(8,128)(2,1)S(1)}, u32[]{:S(2)}, u32[]{:S(2)}) collective-permute-start(bf16[3,256,128]{2,1,0:T(8,128)(2,1)S(1)} %get-tuple-element.46), channel_id=1, source_target_pairs={{0,8},{1,9},{2,10},{3,11},{4,12},{5,13},{6,14},{7,15},{8,0},{9,1},... | collective-permute-start | bytes 589832 | tf_op jit(solution)/shard_map/ppermute | solution.py:207
  11.9 2.6 %collective-permute-start.4 = (bf16[3,256,128]{2,1,0:T(8,128)(2,1)S(1)}, bf16[3,256,128]{2,1,0:T(8,128)(2,1)S(1)}, u32[]{:S(2)}, u32[]{:S(2)}) collective-permute-start(bf16[3,256,128]{2,1,0:T(8,128)(2,1)S(1)} %get-tuple-element.47), channel_id=1, source_target_pairs={{0,10},{1,11},{2,12},{3,13},{4,14},{5,15},{6,0},{7,1},{8,2},{9,3},... | collective-permute-start | bytes 589832 | tf_op jit(solution)/shard_map/ppermute | solution.py:207
  14.5 1.0 collective-permute-done.refs_1_
  15.5 1.8 %collective-permute-start.5 = (bf16[3,256,128]{2,1,0:T(8,128)(2,1)S(1)}, bf16[3,256,128]{2,1,0:T(8,128)(2,1)S(1)}, u32[]{:S(2)}, u32[]{:S(2)}) collective-permute-start(bf16[3,256,128]{2,1,0:T(8,128)(2,1)S(1)} %get-tuple-element.48), channel_id=1, source_target_pairs={{0,12},{1,13},{2,14},{3,15},{4,0},{5,1},{6,2},{7,3},{8,4},{9,5},{1... | collective-permute-start | bytes 589832 | tf_op jit(solution)/shard_map/ppermute | solution.py:207
  17.3 3.4 %collective-permute-start.6 = (bf16[3,256,128]{2,1,0:T(8,128)(2,1)S(1)}, bf16[3,256,128]{2,1,0:T(8,128)(2,1)S(1)}, u32[]{:S(2)}, u32[]{:S(2)}) collective-permute-start(bf16[3,256,128]{2,1,0:T(8,128)(2,1)S(1)} %get-tuple-element.49), channel_id=1, source_target_pairs={{0,14},{1,15},{2,0},{3,1},{4,2},{5,3},{6,4},{7,5},{8,6},{9,7},{10,... | collective-permute-start | bytes 589832 | tf_op jit(solution)/shard_map/ppermute | solution.py:207
  20.8 1.6 %copy-done = bf16[1024,1024]{1,0:T(8,128)(2,1)S(1)} copy-done((bf16[1024,1024]{1,0:T(8,128)(2,1)S(1)}, bf16[1024,1024]{1,0:T(8,128)(2,1)}, u32[]{:S(2)}) %copy-start) | copy-done | bytes 2097176
  22.4 1.0 copy-done.7
  23.4 1.2 %shard_map.101 = (bf16[256,128]{1,0:T(8,128)(2,1)S(1)}, bf16[256,128]{1,0:T(8,128)(2,1)S(1)}, bf16[256,128]{1,0:T(8,128)(2,1)S(1)}, bf16[256,128]{1,0:T(8,128)(2...) custom-call(s32[1]{0:T(128)} %bitcast.chip_ref, ...), custom_call_target="tpu_custom_call" | custom-call | tf_op jit(solution)/shard_map/pallas_call | solution.py:220
  24.7 6.8 %collective-permute-done.2.refs_3_ = bf16[3,256,128]{2,1,0:T(8,128)(2,1)S(1)} collective-permute-done((bf16[3,256,128]{2,1,0:T(8,128)(2,1)S(1)}, bf16[3,256,128]{2,1,0:T(8,128)(2,1)S(1)}, u32[]{:S(2)}, u32[]{:S(2)}) %collective-permute-start.2) | collective-permute-done | bytes 196640 | tf_op jit(solution)/shard_map/ppermute | solution.py:207
  31.5 0.2 collective-permute-done.3.refs_4_
  31.7 1.4 %collective-permute-done.6.refs_7_ = bf16[3,256,128]{2,1,0:T(8,128)(2,1)S(1)} collective-permute-done((bf16[3,256,128]{2,1,0:T(8,128)(2,1)S(1)}, bf16[3,256,128]{2,1,0:T(8,128)(2,1)S(1)}, u32[]{:S(2)}, u32[]{:S(2)}) %collective-permute-start.6) | collective-permute-done | bytes 196640 | tf_op jit(solution)/shard_map/ppermute | solution.py:207
  33.1 0.1 shard_map.102
  33.2 0.1 collective-permute-start.7
  33.3 4.3 %collective-permute-start.8 = (bf16[256,128]{1,0:T(8,128)(2,1)S(1)}, bf16[256,128]{1,0:T(8,128)(2,1)S(1)}, u32[]{:S(2)}, u32[]{:S(2)}) collective-permute-start(bf16[256,128]{1,0:T(8,128)(2,1)S(1)} %get-tuple-element.51), channel_id=1, source_target_pairs={{0,2},{1,3},{2,4},{3,5},{4,6},{5,7},{6,8},{7,9},{8,10},{9,11},{10,... | collective-permute-start | bytes 196616 | tf_op jit(solution)/shard_map/ppermute | solution.py:207
  37.6 8.9 %collective-permute-start.9 = (bf16[256,128]{1,0:T(8,128)(2,1)S(1)}, bf16[256,128]{1,0:T(8,128)(2,1)S(1)}, u32[]{:S(2)}, u32[]{:S(2)}) collective-permute-start(bf16[256,128]{1,0:T(8,128)(2,1)S(1)} %get-tuple-element.52), channel_id=1, source_target_pairs={{0,4},{1,5},{2,6},{3,7},{4,8},{5,9},{6,10},{7,11},{8,12},{9,13},{1... | collective-permute-start | bytes 196616 | tf_op jit(solution)/shard_map/ppermute | solution.py:207
  46.5 2.1 %collective-permute-start.11 = (bf16[256,128]{1,0:T(8,128)(2,1)S(1)}, bf16[256,128]{1,0:T(8,128)(2,1)S(1)}, u32[]{:S(2)}, u32[]{:S(2)}) collective-permute-start(bf16[256,128]{1,0:T(8,128)(2,1)S(1)} %get-tuple-element.54), channel_id=1, source_target_pairs={{0,8},{1,9},{2,10},{3,11},{4,12},{5,13},{6,14},{7,15},{8,0},{9,1},... | collective-permute-start | bytes 196616 | tf_op jit(solution)/shard_map/ppermute | solution.py:207
  48.6 0.1 copy.12
  48.7 0.1 squeeze.6
  48.8 1.2 collective-permute-done.8.refs_1_
  50.0 2.2 %collective-permute-start.12 = (bf16[256,128]{1,0:T(8,128)(2,1)S(1)}, bf16[256,128]{1,0:T(8,128)(2,1)S(1)}, u32[]{:S(2)}, u32[]{:S(2)}) collective-permute-start(bf16[256,128]{1,0:T(8,128)(2,1)S(1)} %get-tuple-element.55), channel_id=1, source_target_pairs={{0,10},{1,11},{2,12},{3,13},{4,14},{5,15},{6,0},{7,1},{8,2},{9,3},... | collective-permute-start | bytes 196616 | tf_op jit(solution)/shard_map/ppermute | solution.py:207
  52.2 0.7 collective-permute-start.13
  53.0 2.6 %collective-permute-done.10.refs_3_ = bf16[256,128]{1,0:T(8,128)(2,1)S(1)} collective-permute-done((bf16[256,128]{1,0:T(8,128)(2,1)S(1)}, bf16[256,128]{1,0:T(8,128)(2,1)S(1)}, u32[]{:S(2)}, u32[]{:S(2)}) %collective-permute-start.10) | collective-permute-done | bytes 65568 | tf_op jit(solution)/shard_map/ppermute | solution.py:207
  55.6 0.1 reshape.17
  55.7 0.1 reshape.18.count_ref
  55.8 0.5 collective-permute-done.11.refs_4_
  56.2 1.7 %collective-permute-done.12.refs_5_ = bf16[256,128]{1,0:T(8,128)(2,1)S(1)} collective-permute-done((bf16[256,128]{1,0:T(8,128)(2,1)S(1)}, bf16[256,128]{1,0:T(8,128)(2,1)S(1)}, u32[]{:S(2)}, u32[]{:S(2)}) %collective-permute-start.12) | collective-permute-done | bytes 65568 | tf_op jit(solution)/shard_map/ppermute | solution.py:207
  57.9 0.3 collective-permute-done.13.refs_6_
  58.2 1.6 %collective-permute-done.14.refs_7_ = bf16[256,128]{1,0:T(8,128)(2,1)S(1)} collective-permute-done((bf16[256,128]{1,0:T(8,128)(2,1)S(1)}, bf16[256,128]{1,0:T(8,128)(2,1)S(1)}, u32[]{:S(2)}, u32[]{:S(2)}) %collective-permute-start.14) | collective-permute-done | bytes 65568 | tf_op jit(solution)/shard_map/ppermute | solution.py:207
  59.8 14.7 %shard_map.103 = (bf16[2048,128]{1,0:T(8,128)(2,1)S(1)}, f32[2,2048,128]{2,1,0:T(8,128)}, bf16[2,2048,128]{2,1,0:T(8,128)(2,1)S(1)}) custom-call(s32[1]{0:T(128)} %bitcast.chip_ref, s32[128]{0:T(128)S(1)} %fusion.table_ref, s32[16]{0:T(128)S(1)} %reshape.18.count_ref, bf16[2048,128]{1,0:T(8,128)(2,1)S(1)} %get-tuple-element.66.query_ref, ...), custom_call_target="tpu_custom_call" | custom-call | tf_op jit(solution)/shard_map/pallas_call | solution.py:250
  74.6 2.6 %collective-permute-done.15.other_ref = bf16[2,2048,128]{2,1,0:T(8,128)(2,1)S(1)} collective-permute-done((bf16[2,2048,128]{2,1,0:T(8,128)(2,1)S(1)}, bf16[2,2048,128]{2,1,0:T(8,128)(2,1)S(1)}, u32[]{:S(2)}, u32[]{:S(2)}) %collective-permute-start.15) | collective-permute-done | bytes 1048608 | tf_op jit(solution)/shard_map/ppermute | solution.py:210
  77.3 1.6 %copy-done.1 = f32[2,2048,128]{2,1,0:T(8,128)S(1)} copy-done((f32[2,2048,128]{2,1,0:T(8,128)S(1)}, f32[2,2048,128]{2,1,0:T(8,128)}, u32[]{:S(2)}) %copy-start.1) | copy-done | bytes 2097176
  78.9 0.2 shard_map.104
  79.0 3.7 %collective-permute-start.16 = (bf16[3,256,128]{2,1,0:T(8,128)(2,1)S(1)}, bf16[3,256,128]{2,1,0:T(8,128)(2,1)S(1)}, u32[]{:S(2)}, u32[]{:S(2)}) collective-permute-start(bf16[3,256,128]{2,1,0:T(8,128)(2,1)S(1)} %get-tuple-element.72), channel_id=1, source_target_pairs={{0,14},{1,15},{2,0},{3,1},{4,2},{5,3},{6,4},{7,5},{8,6},{9,7},{10,... | collective-permute-start | bytes 589832 | tf_op jit(solution)/shard_map/ppermute | solution.py:207
  82.7 1.8 %collective-permute-start.17 = (bf16[3,256,128]{2,1,0:T(8,128)(2,1)S(1)}, bf16[3,256,128]{2,1,0:T(8,128)(2,1)S(1)}, u32[]{:S(2)}, u32[]{:S(2)}) collective-permute-start(bf16[3,256,128]{2,1,0:T(8,128)(2,1)S(1)} %get-tuple-element.73), channel_id=1, source_target_pairs={{0,12},{1,13},{2,14},{3,15},{4,0},{5,1},{6,2},{7,3},{8,4},{9,5},{1... | collective-permute-start | bytes 589832 | tf_op jit(solution)/shard_map/ppermute | solution.py:207
  84.5 3.5 %collective-permute-start.19 = (bf16[3,256,128]{2,1,0:T(8,128)(2,1)S(1)}, bf16[3,256,128]{2,1,0:T(8,128)(2,1)S(1)}, u32[]{:S(2)}, u32[]{:S(2)}) collective-permute-start(bf16[3,256,128]{2,1,0:T(8,128)(2,1)S(1)} %get-tuple-element.75), channel_id=1, source_target_pairs={{0,8},{1,9},{2,10},{3,11},{4,12},{5,13},{6,14},{7,15},{8,0},{9,1},... | collective-permute-start | bytes 589832 | tf_op jit(solution)/shard_map/ppermute | solution.py:207
  88.0 0.9 collective-permute-start.21
  88.9 3.4 %collective-permute-done.17.refs_2_ = bf16[3,256,128]{2,1,0:T(8,128)(2,1)S(1)} collective-permute-done((bf16[3,256,128]{2,1,0:T(8,128)(2,1)S(1)}, bf16[3,256,128]{2,1,0:T(8,128)(2,1)S(1)}, u32[]{:S(2)}, u32[]{:S(2)}) %collective-permute-start.17) | collective-permute-done | bytes 196640 | tf_op jit(solution)/shard_map/ppermute | solution.py:207
  92.3 4.3 %collective-permute-done.18.refs_3_ = bf16[3,256,128]{2,1,0:T(8,128)(2,1)S(1)} collective-permute-done((bf16[3,256,128]{2,1,0:T(8,128)(2,1)S(1)}, bf16[3,256,128]{2,1,0:T(8,128)(2,1)S(1)}, u32[]{:S(2)}, u32[]{:S(2)}) %collective-permute-start.18) | collective-permute-done | bytes 196640 | tf_op jit(solution)/shard_map/ppermute | solution.py:207
  96.5 20.9 %collective-permute-done.19.refs_4_ = bf16[3,256,128]{2,1,0:T(8,128)(2,1)S(1)} collective-permute-done((bf16[3,256,128]{2,1,0:T(8,128)(2,1)S(1)}, bf16[3,256,128]{2,1,0:T(8,128)(2,1)S(1)}, u32[]{:S(2)}, u32[]{:S(2)}) %collective-permute-start.19) | collective-permute-done | bytes 196640 | tf_op jit(solution)/shard_map/ppermute | solution.py:207
  117.4 0.4 collective-permute-done.20.refs_5_
  117.8 5.4 %shard_map.105 = bf16[256,1024]{1,0:T(8,128)(2,1)} custom-call(s32[1]{0:T(128)} %bitcast.chip_ref, bf16[3,256,128]{2,1,0:T(8,128)(2,1)S(1)} %get-tuple-element.71.refs_0_, bf16[3,256,128]{2,1,0:T(8,128)(2,1)S(1)} %collective-permute-done.16.refs_1_, bf16[3,256,128]{2,1,0:T(8,128)(2,1)S(1)} %collective-permute-done.17.refs_2_, ...), custom_call_target="tpu_custom_call" | custom-call | tf_op jit(solution)/shard_map/pallas_call | solution.py:280
  (31 shorter events, 0.2 us)
Async XLA Ops:
  0.0 1.0 copy-start.4
  1.0 1.0 copy-start.5
  2.1 1.0 copy-start.6
  3.5 12.0 %collective-permute-start = (bf16[3,256,128]{2,1,0:T(8,128)(2,1)S(1)}, bf16[3,256,128]{2,1,0:T(8,128)(2,1)S(1)}, u32[]{:S(2)}, u32[]{:S(2)}) collective-permute-start(bf16[3,256,128]{2,1,0:T(8,128)(2,1)S(1)} %get-tuple-element.43), channel_id=1, source_target_pairs={{0,2},{1,3},{2,4},{3,5},{4,6},{5,7},{6,8},{7,9},{8,10},{9,11},{10,... | collective-permute-start | bytes 589832 | tf_op jit(solution)/shard_map/ppermute | solution.py:207
  6.5 10.8 %collective-permute-start.1 = (bf16[3,256,128]{2,1,0:T(8,128)(2,1)S(1)}, bf16[3,256,128]{2,1,0:T(8,128)(2,1)S(1)}, u32[]{:S(2)}, u32[]{:S(2)}) collective-permute-start(bf16[3,256,128]{2,1,0:T(8,128)(2,1)S(1)} %get-tuple-element.44), channel_id=1, source_target_pairs={{0,4},{1,5},{2,6},{3,7},{4,8},{5,9},{6,10},{7,11},{8,12},{9,13},{1... | collective-permute-start | bytes 589832 | tf_op jit(solution)/shard_map/ppermute | solution.py:207
  8.1 23.4 %collective-permute-start.2 = (bf16[3,256,128]{2,1,0:T(8,128)(2,1)S(1)}, bf16[3,256,128]{2,1,0:T(8,128)(2,1)S(1)}, u32[]{:S(2)}, u32[]{:S(2)}) collective-permute-start(bf16[3,256,128]{2,1,0:T(8,128)(2,1)S(1)} %get-tuple-element.45), channel_id=1, source_target_pairs={{0,6},{1,7},{2,8},{3,9},{4,10},{5,11},{6,12},{7,13},{8,14},{9,15},... | collective-permute-start | bytes 589832 | tf_op jit(solution)/shard_map/ppermute | solution.py:207
  10.7 21.0 %collective-permute-start.3 = (bf16[3,256,128]{2,1,0:T(8,128)(2,1)S(1)}, bf16[3,256,128]{2,1,0:T(8,128)(2,1)S(1)}, u32[]{:S(2)}, u32[]{:S(2)}) collective-permute-start(bf16[3,256,128]{2,1,0:T(8,128)(2,1)S(1)} %get-tuple-element.46), channel_id=1, source_target_pairs={{0,8},{1,9},{2,10},{3,11},{4,12},{5,13},{6,14},{7,15},{8,0},{9,1},... | collective-permute-start | bytes 589832 | tf_op jit(solution)/shard_map/ppermute | solution.py:207
  11.9 19.8 %collective-permute-start.4 = (bf16[3,256,128]{2,1,0:T(8,128)(2,1)S(1)}, bf16[3,256,128]{2,1,0:T(8,128)(2,1)S(1)}, u32[]{:S(2)}, u32[]{:S(2)}) collective-permute-start(bf16[3,256,128]{2,1,0:T(8,128)(2,1)S(1)} %get-tuple-element.47), channel_id=1, source_target_pairs={{0,10},{1,11},{2,12},{3,13},{4,14},{5,15},{6,0},{7,1},{8,2},{9,3},... | collective-permute-start | bytes 589832 | tf_op jit(solution)/shard_map/ppermute | solution.py:207
  15.5 16.2 %collective-permute-start.5 = (bf16[3,256,128]{2,1,0:T(8,128)(2,1)S(1)}, bf16[3,256,128]{2,1,0:T(8,128)(2,1)S(1)}, u32[]{:S(2)}, u32[]{:S(2)}) collective-permute-start(bf16[3,256,128]{2,1,0:T(8,128)(2,1)S(1)} %get-tuple-element.48), channel_id=1, source_target_pairs={{0,12},{1,13},{2,14},{3,15},{4,0},{5,1},{6,2},{7,3},{8,4},{9,5},{1... | collective-permute-start | bytes 589832 | tf_op jit(solution)/shard_map/ppermute | solution.py:207
  17.3 15.8 %collective-permute-start.6 = (bf16[3,256,128]{2,1,0:T(8,128)(2,1)S(1)}, bf16[3,256,128]{2,1,0:T(8,128)(2,1)S(1)}, u32[]{:S(2)}, u32[]{:S(2)}) collective-permute-start(bf16[3,256,128]{2,1,0:T(8,128)(2,1)S(1)} %get-tuple-element.49), channel_id=1, source_target_pairs={{0,14},{1,15},{2,0},{3,1},{4,2},{5,3},{6,4},{7,5},{8,6},{9,7},{10,... | collective-permute-start | bytes 589832 | tf_op jit(solution)/shard_map/ppermute | solution.py:207
  20.8 1.6 %copy-start = (bf16[1024,1024]{1,0:T(8,128)(2,1)S(1)}, bf16[1024,1024]{1,0:T(8,128)(2,1)}, u32[]{:S(2)}) copy-start(bf16[1024,1024]{1,0:T(8,128)(2,1)} %weight_ref.1) | copy-start | bytes 6291460
  22.4 1.0 copy-start.7
  23.4 25.2 %copy-start.8 = (s32[32,8]{0,1:T(8,128)S(1)}, s32[32,8]{0,1:T(8,128)}, u32[]{:S(2)}) copy-start(s32[32,8]{0,1:T(8,128)} %param.18) | copy-start | bytes 3076
  23.4 32.2 %copy-start.9 = (s32[32]{0:T(128)S(1)}, s32[32]{0:T(128)}, u32[]{:S(2)}) copy-start(s32[32]{0:T(128)} %param.19) | copy-start | bytes 388
  33.2 26.6 %collective-permute-start.7 = (bf16[2,2048,128]{2,1,0:T(8,128)(2,1)S(1)}, bf16[2,2048,128]{2,1,0:T(8,128)(2,1)S(1)}, u32[]{:S(2)}, u32[]{:S(2)}) collective-permute-start(bf16[2,2048,128]{2,1,0:T(8,128)(2,1)S(1)} %get-tuple-element.67.own_ref), channel_id=1, source_target_pairs={{0,1},{1,0},{2,3},{3,2},{4,5},{5,4},{6,7},{7,6},{8,9},{9,8},{10,11... | collective-permute-start | bytes 3145736 | tf_op jit(solution)/shard_map/ppermute | solution.py:210
  33.3 16.7 %collective-permute-start.8 = (bf16[256,128]{1,0:T(8,128)(2,1)S(1)}, bf16[256,128]{1,0:T(8,128)(2,1)S(1)}, u32[]{:S(2)}, u32[]{:S(2)}) collective-permute-start(bf16[256,128]{1,0:T(8,128)(2,1)S(1)} %get-tuple-element.51), channel_id=1, source_target_pairs={{0,2},{1,3},{2,4},{3,5},{4,6},{5,7},{6,8},{7,9},{8,10},{9,11},{10,... | collective-permute-start | bytes 196616 | tf_op jit(solution)/shard_map/ppermute | solution.py:207
  37.6 14.6 %collective-permute-start.9 = (bf16[256,128]{1,0:T(8,128)(2,1)S(1)}, bf16[256,128]{1,0:T(8,128)(2,1)S(1)}, u32[]{:S(2)}, u32[]{:S(2)}) collective-permute-start(bf16[256,128]{1,0:T(8,128)(2,1)S(1)} %get-tuple-element.52), channel_id=1, source_target_pairs={{0,4},{1,5},{2,6},{3,7},{4,8},{5,9},{6,10},{7,11},{8,12},{9,13},{1... | collective-permute-start | bytes 196616 | tf_op jit(solution)/shard_map/ppermute | solution.py:207
  46.5 9.0 %collective-permute-start.10 = (bf16[256,128]{1,0:T(8,128)(2,1)S(1)}, bf16[256,128]{1,0:T(8,128)(2,1)S(1)}, u32[]{:S(2)}, u32[]{:S(2)}) collective-permute-start(bf16[256,128]{1,0:T(8,128)(2,1)S(1)} %get-tuple-element.53), channel_id=1, source_target_pairs={{0,6},{1,7},{2,8},{3,9},{4,10},{5,11},{6,12},{7,13},{8,14},{9,15},... | collective-permute-start | bytes 196616 | tf_op jit(solution)/shard_map/ppermute | solution.py:207
  46.5 9.7 %collective-permute-start.11 = (bf16[256,128]{1,0:T(8,128)(2,1)S(1)}, bf16[256,128]{1,0:T(8,128)(2,1)S(1)}, u32[]{:S(2)}, u32[]{:S(2)}) collective-permute-start(bf16[256,128]{1,0:T(8,128)(2,1)S(1)} %get-tuple-element.54), channel_id=1, source_target_pairs={{0,8},{1,9},{2,10},{3,11},{4,12},{5,13},{6,14},{7,15},{8,0},{9,1},... | collective-permute-start | bytes 196616 | tf_op jit(solution)/shard_map/ppermute | solution.py:207
  50.0 7.9 %collective-permute-start.12 = (bf16[256,128]{1,0:T(8,128)(2,1)S(1)}, bf16[256,128]{1,0:T(8,128)(2,1)S(1)}, u32[]{:S(2)}, u32[]{:S(2)}) collective-permute-start(bf16[256,128]{1,0:T(8,128)(2,1)S(1)} %get-tuple-element.55), channel_id=1, source_target_pairs={{0,10},{1,11},{2,12},{3,13},{4,14},{5,15},{6,0},{7,1},{8,2},{9,3},... | collective-permute-start | bytes 196616 | tf_op jit(solution)/shard_map/ppermute | solution.py:207
  52.2 6.0 %collective-permute-start.13 = (bf16[256,128]{1,0:T(8,128)(2,1)S(1)}, bf16[256,128]{1,0:T(8,128)(2,1)S(1)}, u32[]{:S(2)}, u32[]{:S(2)}) collective-permute-start(bf16[256,128]{1,0:T(8,128)(2,1)S(1)} %get-tuple-element.56), channel_id=1, source_target_pairs={{0,12},{1,13},{2,14},{3,15},{4,0},{5,1},{6,2},{7,3},{8,4},{9,5},{1... | collective-permute-start | bytes 196616 | tf_op jit(solution)/shard_map/ppermute | solution.py:207
  55.5 4.3 %collective-permute-start.14 = (bf16[256,128]{1,0:T(8,128)(2,1)S(1)}, bf16[256,128]{1,0:T(8,128)(2,1)S(1)}, u32[]{:S(2)}, u32[]{:S(2)}) collective-permute-start(bf16[256,128]{1,0:T(8,128)(2,1)S(1)} %get-tuple-element.57), channel_id=1, source_target_pairs={{0,14},{1,15},{2,0},{3,1},{4,2},{5,3},{6,4},{7,5},{8,6},{9,7},{10,... | collective-permute-start | bytes 196616 | tf_op jit(solution)/shard_map/ppermute | solution.py:207
  59.8 58.0 %copy-start.2 = (bf16[1024,1024]{1,0:T(8,128)(2,1)S(1)}, bf16[1024,1024]{1,0:T(8,128)(2,1)}, u32[]{:S(2)}) copy-start(bf16[1024,1024]{1,0:T(8,128)(2,1)} %refs_8_.1) | copy-start | bytes 6291460
  74.5 2.7 %collective-permute-start.15 = (bf16[2,2048,128]{2,1,0:T(8,128)(2,1)S(1)}, bf16[2,2048,128]{2,1,0:T(8,128)(2,1)S(1)}, u32[]{:S(2)}, u32[]{:S(2)}) collective-permute-start(bf16[2,2048,128]{2,1,0:T(8,128)(2,1)S(1)} %get-tuple-element.70), channel_id=1, source_target_pairs={{0,1},{1,0},{2,3},{3,2},{4,5},{5,4},{6,7},{7,6},{8,9},{9,8},{10,11... | collective-permute-start | bytes 3145736 | tf_op jit(solution)/shard_map/ppermute | solution.py:210
  77.3 1.6 %copy-start.1 = (f32[2,2048,128]{2,1,0:T(8,128)S(1)}, f32[2,2048,128]{2,1,0:T(8,128)}, u32[]{:S(2)}) copy-start(f32[2,2048,128]{2,1,0:T(8,128)} %get-tuple-element.69.own_ref) | copy-start | bytes 6291460
  78.9 39.0 %copy-start.3 = (bf16[1024,1024]{1,0:T(8,128)(2,1)S(1)}, bf16[1024,1024]{1,0:T(8,128)(2,1)}, u32[]{:S(2)}) copy-start(bf16[1024,1024]{1,0:T(8,128)(2,1)} %refs_9_.1) | copy-start | bytes 6291460
  79.0 9.0 %collective-permute-start.16 = (bf16[3,256,128]{2,1,0:T(8,128)(2,1)S(1)}, bf16[3,256,128]{2,1,0:T(8,128)(2,1)S(1)}, u32[]{:S(2)}, u32[]{:S(2)}) collective-permute-start(bf16[3,256,128]{2,1,0:T(8,128)(2,1)S(1)} %get-tuple-element.72), channel_id=1, source_target_pairs={{0,14},{1,15},{2,0},{3,1},{4,2},{5,3},{6,4},{7,5},{8,6},{9,7},{10,... | collective-permute-start | bytes 589832 | tf_op jit(solution)/shard_map/ppermute | solution.py:207
  82.7 9.6 %collective-permute-start.17 = (bf16[3,256,128]{2,1,0:T(8,128)(2,1)S(1)}, bf16[3,256,128]{2,1,0:T(8,128)(2,1)S(1)}, u32[]{:S(2)}, u32[]{:S(2)}) collective-permute-start(bf16[3,256,128]{2,1,0:T(8,128)(2,1)S(1)} %get-tuple-element.73), channel_id=1, source_target_pairs={{0,12},{1,13},{2,14},{3,15},{4,0},{5,1},{6,2},{7,3},{8,4},{9,5},{1... | collective-permute-start | bytes 589832 | tf_op jit(solution)/shard_map/ppermute | solution.py:207
  84.5 12.0 %collective-permute-start.18 = (bf16[3,256,128]{2,1,0:T(8,128)(2,1)S(1)}, bf16[3,256,128]{2,1,0:T(8,128)(2,1)S(1)}, u32[]{:S(2)}, u32[]{:S(2)}) collective-permute-start(bf16[3,256,128]{2,1,0:T(8,128)(2,1)S(1)} %get-tuple-element.74), channel_id=1, source_target_pairs={{0,10},{1,11},{2,12},{3,13},{4,14},{5,15},{6,0},{7,1},{8,2},{9,3},... | collective-permute-start | bytes 589832 | tf_op jit(solution)/shard_map/ppermute | solution.py:207
  84.5 32.9 %collective-permute-start.19 = (bf16[3,256,128]{2,1,0:T(8,128)(2,1)S(1)}, bf16[3,256,128]{2,1,0:T(8,128)(2,1)S(1)}, u32[]{:S(2)}, u32[]{:S(2)}) collective-permute-start(bf16[3,256,128]{2,1,0:T(8,128)(2,1)S(1)} %get-tuple-element.75), channel_id=1, source_target_pairs={{0,8},{1,9},{2,10},{3,11},{4,12},{5,13},{6,14},{7,15},{8,0},{9,1},... | collective-permute-start | bytes 589832 | tf_op jit(solution)/shard_map/ppermute | solution.py:207
  88.0 29.8 %collective-permute-start.20 = (bf16[3,256,128]{2,1,0:T(8,128)(2,1)S(1)}, bf16[3,256,128]{2,1,0:T(8,128)(2,1)S(1)}, u32[]{:S(2)}, u32[]{:S(2)}) collective-permute-start(bf16[3,256,128]{2,1,0:T(8,128)(2,1)S(1)} %get-tuple-element.76), channel_id=1, source_target_pairs={{0,6},{1,7},{2,8},{3,9},{4,10},{5,11},{6,12},{7,13},{8,14},{9,15},... | collective-permute-start | bytes 589832 | tf_op jit(solution)/shard_map/ppermute | solution.py:207
  88.0 29.8 %collective-permute-start.21 = (bf16[3,256,128]{2,1,0:T(8,128)(2,1)S(1)}, bf16[3,256,128]{2,1,0:T(8,128)(2,1)S(1)}, u32[]{:S(2)}, u32[]{:S(2)}) collective-permute-start(bf16[3,256,128]{2,1,0:T(8,128)(2,1)S(1)} %get-tuple-element.77), channel_id=1, source_target_pairs={{0,4},{1,5},{2,6},{3,7},{4,8},{5,9},{6,10},{7,11},{8,12},{9,13},{1... | collective-permute-start | bytes 589832 | tf_op jit(solution)/shard_map/ppermute | solution.py:207
  92.3 25.5 %collective-permute-start.22 = (bf16[3,256,128]{2,1,0:T(8,128)(2,1)S(1)}, bf16[3,256,128]{2,1,0:T(8,128)(2,1)S(1)}, u32[]{:S(2)}, u32[]{:S(2)}) collective-permute-start(bf16[3,256,128]{2,1,0:T(8,128)(2,1)S(1)} %get-tuple-element.78), channel_id=1, source_target_pairs={{0,2},{1,3},{2,4},{3,5},{4,6},{5,7},{6,8},{7,9},{8,10},{9,11},{10,... | collective-permute-start | bytes 589832 | tf_op jit(solution)/shard_map/ppermute | solution.py:207

commit v3 on v2

v3 whole, which is shorter than its diff:
```python
import functools
import math

import jax
import jax.numpy as jnp
from jax import lax
from jax.experimental import pallas as pl
from jax.experimental.pallas import tpu as pltpu
from jax.sharding import PartitionSpec as P

HD = 128
BLOCK = 128
NBR = 8
WIN = 8
CORES = 2
WIDTHS = (2, 4, 6, 8)
CONTRACT = (((1,), (1,)), ((), ()))
ANY = pl.BlockSpec(memory_space=pltpu.HBM)
VMEM = pl.BlockSpec(memory_space=pltpu.VMEM)
SMEM = pl.BlockSpec(memory_space=pltpu.SMEM)
LIMIT = pltpu.CompilerParams(vmem_limit_bytes=48 << 20)


def passed_along(shard, axis, by):
    size = lax.axis_size(axis)
    return lax.ppermute(shard, axis, [(i, (i + by) % size) for i in range(size)])


def rotated(chip, step, chips):
    return lax.rem(chip + step, chips)


def columns(head):
    return pl.ds(pl.multiple_of(head * HD, HD), HD)


def rows_of(block, size):
    return pl.ds(pl.multiple_of(block * size, size), size)


def pack_kernel(chips, chip_ref, *refs):
    sources, outs, sem = refs[:2], refs[2:-1], refs[-1]
    copies = [
        pltpu.make_async_copy(
            source.at[:, columns(rotated(chip_ref[0], step, chips))],
            outs[step].at[place],
            sem.at[step * 2 + place],
        )
        for step in range(chips)
        for place, source in enumerate(sources)
    ]
    for copy in copies:
        copy.start()
    for copy in copies:
        copy.wait()


def grad_kernel(chips, chip_ref, grad_ref, weight_ref, value_ref, *outs):
    for step in range(chips):
        head = rotated(chip_ref[0], step, chips)
        outs[step][0] = value_ref[:, columns(head)]
        outs[step][1] = lax.dot_general(
            grad_ref[...],
            weight_ref[rows_of(head, HD), :],
            CONTRACT,
            preferred_element_type=jnp.float32,
        ).astype(jnp.bfloat16)


def in_order(chips, tokens, chip_ref, pieces, place, target, first=0):
    for step in range(chips):
        source = rotated(chip_ref[0], chips - step, chips)
        rows = pl.ds(pl.multiple_of(first + source * tokens, tokens), tokens)
        target[rows, :] = pieces[step][place]


def assemble_kernel(chips, tokens, place, chip_ref, *refs):
    in_order(chips, tokens, chip_ref, refs[:chips], place, refs[chips])


def by_width(count_ref, blocks, work):
    def one_block(block, carry):
        count = count_ref[block]
        below = 0
        for width in WIDTHS:
            pl.when((count > below) & (count <= width))(
                functools.partial(work, block, count, width)
            )
            below = width
        return carry

    lax.fori_loop(0, blocks, one_block, 0)


def slots_of(table_ref, block, width):
    return [rows_of(table_ref[block * NBR + slot], BLOCK) for slot in range(width)]


def prob_rows(block, width):
    return pl.ds(pl.multiple_of(block * NBR * BLOCK, NBR * BLOCK), width * BLOCK)


def prob_kernel(chips, tokens, scale, chip_ref, table_ref, count_ref, *refs):
    pieces, (other_ref, prob_ref, query_buf, key_buf) = refs[:chips], refs[chips:]
    half = chips * tokens
    in_order(chips, tokens, chip_ref, pieces, 0, query_buf)
    in_order(chips, tokens, chip_ref, pieces, 1, key_buf)
    key_buf[half:] = other_ref[...]

    def work(block, count, width):
        query = query_buf[rows_of(block, BLOCK), :]
        keys = jnp.concatenate(
            [key_buf[slot, :] for slot in slots_of(table_ref, block, width)], axis=0
        )
        scores = lax.dot_general(keys, query, CONTRACT, preferred_element_type=jnp.float32)
        live = lax.broadcasted_iota(jnp.int32, scores.shape, 0) < count * BLOCK
        scores = jnp.where(live, scores, -jnp.inf)
        peak = jnp.max(scores, axis=0, keepdims=True)
        weights = jnp.exp((scores - peak) * scale)
        probs = weights * (1.0 / jnp.sum(weights, axis=0, keepdims=True))
        prob_ref[prob_rows(block, width), :] = probs.astype(jnp.bfloat16)

    by_width(count_ref, half // BLOCK, work)


def value_kernel(chips, tokens, chip_ref, table_ref, count_ref, prob_ref, *refs):
    pieces, (own_out, other_out, grad_buf, total) = refs[:chips], refs[chips:]
    half = chips * tokens
    in_order(chips, tokens, chip_ref, pieces, 1, grad_buf)
    total[...] = jnp.zeros_like(total)

    def work(block, count, width):
        grad = grad_buf[rows_of(block, BLOCK), :]
        part = jnp.dot(
            prob_ref[prob_rows(block, width), :], grad, preferred_element_type=jnp.float32
        )
        for place, slot in enumerate(slots_of(table_ref, block, width)):
            total[slot, :] += part[place * BLOCK : (place + 1) * BLOCK]

    by_width(count_ref, half // BLOCK, work)
    own_out[...] = total[:half]
    other_out[...] = total[half:].astype(jnp.bfloat16)


def score_kernel(chips, tokens, scale, chip_ref, table_ref, count_ref, prob_ref, *refs):
    firsts, seconds = refs[:chips], refs[chips : 2 * chips]
    other_key, other_value, dq_ref, own_out, other_out = refs[2 * chips : 2 * chips + 5]
    query_buf, grad_buf, key_buf, value_buf, total = refs[2 * chips + 5 :]
    half = chips * tokens
    in_order(chips, tokens, chip_ref, firsts, 0, query_buf)
    in_order(chips, tokens, chip_ref, firsts, 1, key_buf)
    in_order(chips, tokens, chip_ref, seconds, 0, value_buf)
    in_order(chips, tokens, chip_ref, seconds, 1, grad_buf)
    key_buf[half:] = other_key[...]
    value_buf[half:] = other_value[...]
    total[...] = jnp.zeros_like(total)

    def work(block, count, width):
        slots = slots_of(table_ref, block, width)
        rows = rows_of(block, BLOCK)
        keys = jnp.concatenate([key_buf[slot, :] for slot in slots], axis=0)
        values = jnp.concatenate([value_buf[slot, :] for slot in slots], axis=0)
        probs = prob_ref[prob_rows(block, width), :].astype(jnp.float32)
        prob_grad = lax.dot_general(
            values, grad_buf[rows, :], CONTRACT, preferred_element_type=jnp.float32
        )
        delta = jnp.sum(probs * prob_grad, axis=0, keepdims=True)
        dscore = (probs * (prob_grad - delta)).astype(jnp.bfloat16)
        dk = jnp.dot(dscore, query_buf[rows, :], preferred_element_type=jnp.float32)
        dq = lax.dot_general(
            dscore, keys, (((0,), (0,)), ((), ())), preferred_element_type=jnp.float32
        )
        dq_ref[rows, :] = (dq * scale).astype(jnp.bfloat16)
        for place, slot in enumerate(slots):
            total[slot, :] += dk[place * BLOCK : (place + 1) * BLOCK]

    by_width(count_ref, half // BLOCK, work)
    own_out[...] = total[:half] * scale
    other_out[...] = (total[half:] * scale).astype(jnp.bfloat16)


def combine_kernel(chips, tokens, chip_ref, own_ref, other_ref, *refs):
    done, outs = refs[: len(refs) - chips], refs[len(refs) - chips :]
    for step in range(chips):
        rows = rows_of(rotated(chip_ref[0], chips - step, chips), tokens)
        outs[step][0] = (own_ref[rows, :] + other_ref[rows, :].astype(jnp.float32)).astype(
            jnp.bfloat16
        )
        for place, source in enumerate(done):
            outs[step][place + 1] = source[rows, :]


def project_kernel(chips, places, chip_ref, *refs):
    pieces, weights = refs[:chips], refs[chips : chips + places]
    before, (out_ref, *rows_bufs) = refs[chips + places : -places - 1], refs[-places - 1 :]
    total = before[0][...] if before else None
    for place in range(places):
        for step in range(chips):
            head = rotated(chip_ref[0], step, chips)
            rows_bufs[place][:, columns(head)] = pieces[step][place]
        part = lax.dot_general(
            rows_bufs[place][...], weights[place][...], CONTRACT, preferred_element_type=jnp.float32
        )
        total = part if total is None else total + part
    out_ref[...] = total.astype(out_ref.dtype)


def head_per_chip(
    out_grad, query_act, key_act, value_act, out_weight, weights, neighbours, block_counts
):
    my_index = lax.axis_index("blk")
    chips = lax.axis_size("blk") // CORES
    tokens, features = query_act.shape
    scale = 1.0 / math.sqrt(HD)
    chip = (my_index // CORES).astype(jnp.int32).reshape(1)
    core = my_index % CORES
    per_device = tokens // BLOCK
    blocks = chips * per_device
    half = chips * tokens
    bf16 = functools.partial(jax.ShapeDtypeStruct, dtype=jnp.bfloat16)
    f32 = functools.partial(jax.ShapeDtypeStruct, dtype=jnp.float32)
    buf16 = functools.partial(pltpu.VMEM, dtype=jnp.bfloat16)
    buf32 = functools.partial(pltpu.VMEM, dtype=jnp.float32)

    def call(kernel, outs, scratch, scalars, *arrays, spec=VMEM):
        return pl.pallas_call(
            kernel,
            out_shape=outs,
            in_specs=[SMEM] * len(scalars) + [spec] * len(arrays),
            out_specs=jax.tree.map(lambda _: VMEM, outs),
            scratch_shapes=scratch,
            compiler_params=LIMIT,
        )(*scalars, *arrays)

    def by_chips(shard, step):
        pairs = [
            (CORES * c + k, CORES * ((c + step) % chips) + k)
            for c in range(chips)
            for k in range(CORES)
        ]
        return lax.ppermute(shard, "blk", pairs)

    def out_to(shards):
        return [shards[0]] + [by_chips(shards[step], step) for step in range(1, chips)]

    def back_to(shards):
        return [shards[0]] + [by_chips(shards[step], chips - step) for step in range(1, chips)]

    def across_cores(shard):
        return lax.ppermute(shard, "blk", [(i, i ^ 1) for i in range(chips * CORES)])

    own = neighbours.reshape(chips, CORES, per_device, NBR)
    own = lax.dynamic_index_in_dim(own, core, 1, keepdims=False)
    counts = block_counts.reshape(chips, CORES, per_device)
    counts = lax.dynamic_index_in_dim(counts, core, 1, keepdims=False).reshape(-1)
    holder = own // per_device
    table = (
        jnp.where(holder % CORES == core, 0, blocks)
        + (holder // CORES) * per_device
        + own % per_device
    ).reshape(-1)
    lists = (chip, table, counts)
    piece = [bf16((2, tokens, HD))] * chips
    partial_outs = [f32((half, HD)), bf16((half, HD))]
    args = functools.partial

    packed = call(
        args(pack_kernel, chips), piece, [pltpu.SemaphoreType.DMA((2 * chips,))],
        (chip,), query_act, key_act, spec=ANY,
    )
    firsts = out_to(packed)
    packed = call(
        args(grad_kernel, chips), piece, [], (chip,), out_grad, out_weight, value_act
    )
    firsts, _ = lax.optimization_barrier((firsts, packed))
    seconds = out_to(packed)
    keys = call(args(assemble_kernel, chips, tokens, 1), bf16((half, HD)), [], (chip,), *firsts)
    other_keys = across_cores(keys)
    probs = call(
        args(prob_kernel, chips, tokens, scale),
        bf16((blocks * NBR * BLOCK, HD)),
        [buf16((half, HD)), buf16((2 * half, HD))],
        lists, *firsts, other_keys,
    )
    seconds, probs = lax.optimization_barrier((seconds, probs))
    values = call(args(assemble_kernel, chips, tokens, 0), bf16((half, HD)), [], (chip,), *seconds)
    other_values = across_cores(values)
    own_dv, sent_dv = call(
        args(value_kernel, chips, tokens), partial_outs,
        [buf16((half, HD)), buf32((2 * half, HD))],
        lists, probs, *seconds,
    )
    came_dv = across_cores(sent_dv)
    dq, own_dk, sent_dk = call(
        args(score_kernel, chips, tokens, scale), [bf16((half, HD))] + partial_outs,
        [buf16((half, HD))] * 2 + [buf16((2 * half, HD))] * 2 + [buf32((2 * half, HD))],
        lists, probs, *firsts, *seconds, other_keys, other_values,
    )
    came_dk = across_cores(sent_dk)
    first_back = back_to(
        call(args(combine_kernel, chips, tokens), piece, [], (chip,), own_dv, came_dv, dq)
    )
    last_back = back_to(
        call(
            args(combine_kernel, chips, tokens), [bf16((1, tokens, HD))] * chips, [],
            (chip,), own_dk, came_dk,
        )
    )
    query_weight, key_weight, value_weight = weights
    rows_buf = buf16((tokens, features))
    most = call(
        args(project_kernel, chips, 2), f32((tokens, features)), [rows_buf] * 2,
        (chip,), *first_back, value_weight, query_weight,
    )
    last_back, most = lax.optimization_barrier((last_back, most))
    return call(
        args(project_kernel, chips, 1), bf16((tokens, features)), [rows_buf],
        (chip,), *last_back, key_weight, most,
    )


def by_window(
    out_grad, query_act, key_act, value_act, out_weight, weights, neighbours, block_counts
):
    cycle_size = lax.axis_size("blk")
    my_index = lax.axis_index("blk")
    tokens, features = query_act.shape
    head_count = features // HD
    query_blocks = tokens // BLOCK
    reach_dev = (WIN + query_blocks - 1) // query_blocks
    total_blocks = query_blocks * cycle_size
    window_blocks = (2 * reach_dev + 1) * query_blocks
    scale = 1.0 / math.sqrt(HD)
    attn_grad = lax.dot_general(
        lax.all_gather(out_grad, "sp", axis=0, tiled=True),
        out_weight,
        CONTRACT,
        preferred_element_type=jnp.float32,
    ).astype(jnp.bfloat16)
    key_value = jnp.stack((key_act, value_act))
    gathered = jnp.concatenate(
        [
            key_value if offset == 0 else passed_along(key_value, "blk", -offset)
            for offset in range(-reach_dev, reach_dev + 1)
        ],
        axis=1,
    ).reshape(2, window_blocks, BLOCK, features)
    anchor = (my_index - reach_dev) * query_blocks
    own_lists = lax.dynamic_slice_in_dim(neighbours, my_index * query_blocks, query_blocks, 0)
    own_counts = lax.dynamic_slice_in_dim(block_counts, my_index * query_blocks, query_blocks, 0)
    window_index = ((own_lists - anchor) % total_blocks).reshape(-1)
    picked = jnp.concatenate(
        [
            lax.dynamic_slice_in_dim(gathered, window_index[n], 1, 1)
            for n in range(query_blocks * NBR)
        ],
        axis=1,
    ).reshape(2, query_blocks, NBR, BLOCK, head_count, HD)
    query_heads = query_act.reshape(query_blocks, BLOCK, head_count, HD)
    grad_heads = attn_grad.reshape(query_blocks, BLOCK, head_count, HD)
    einsum = functools.partial(jnp.einsum, preferred_element_type=jnp.float32)
    scores = scale * einsum("bihd,bsjhd->bhisj", query_heads, picked[0])
    live_slots = jnp.arange(NBR)[None, :] < own_counts[:, None]
    scores = jnp.where(live_slots[:, None, None, :, None], scores, -jnp.inf)
    row_peak = jnp.max(scores, axis=(3, 4), keepdims=True)
    log_total = row_peak + jnp.log(jnp.sum(jnp.exp(scores - row_peak), axis=(3, 4), keepdims=True))
    soft_probs = jnp.exp(scores - log_total)
    probs_half = soft_probs.astype(jnp.bfloat16)
    outputs = einsum("bhisj,bsjhd->bihd", probs_half, picked[1])
    row_delta = jnp.transpose(jnp.sum(grad_heads.astype(jnp.float32) * outputs, axis=3), (0, 2, 1))
    prob_grad = einsum("bihd,bsjhd->bhisj", grad_heads, picked[1])
    dscore_half = (soft_probs * (prob_grad - row_delta[:, :, :, None, None])).astype(jnp.bfloat16)
    query_grad = scale * einsum("bhisj,bsjhd->bihd", dscore_half, picked[0])
    query_grad = query_grad.astype(jnp.bfloat16).reshape(tokens, features)
    key_slots = scale * einsum("bhisj,bihd->bsjhd", dscore_half, query_heads)
    value_slots = einsum("bhisj,bihd->bsjhd", probs_half, grad_heads)
    slot_grads = jnp.stack((key_slots, value_slots)).reshape(
        2, query_blocks * NBR, BLOCK * features
    )
    selector = (jnp.arange(window_blocks)[:, None] == window_index.reshape(1, -1)).astype(
        jnp.float32
    )
    window_grads = jnp.einsum("wn,gnc->gwc", selector, slot_grads, precision=lax.Precision.HIGHEST)
    summed = 0.0
    for offset in range(-reach_dev, reach_dev + 1):
        first = (offset + reach_dev) * query_blocks
        portion = window_grads[:, first : first + query_blocks]
        summed = summed + (portion if offset == 0 else passed_along(portion, "blk", offset))
    own_grads = summed.reshape(2, tokens, features).astype(jnp.bfloat16)
    summed_rows = 0.0
    for grad, weight in zip((query_grad, own_grads[0], own_grads[1]), weights, strict=True):
        summed_rows = summed_rows + lax.dot_general(
            grad, weight, CONTRACT, preferred_element_type=jnp.float32
        )
    input_grad = lax.psum_scatter(summed_rows, "sp", scatter_dimension=0, tiled=True)
    return input_grad.astype(jnp.bfloat16)


def body(
    out_grad,
    query_act,
    key_act,
    value_act,
    out_weight,
    query_weight,
    key_weight,
    value_weight,
    neighbours,
    block_counts,
):
    heads = query_act.shape[1] // HD
    one_head = lax.axis_size("sp") == 1 and lax.axis_size("blk") == heads * CORES
    return (head_per_chip if one_head else by_window)(
        out_grad,
        query_act,
        key_act,
        value_act,
        out_weight,
        (query_weight, key_weight, value_weight),
        neighbours,
        block_counts,
    )


def solution(mesh):
    return jax.shard_map(
        body,
        mesh=mesh,
        in_specs=(
            P(("groups", "blk", "sp"), None),
            P(("groups", "blk"), "sp"),
            P(("groups", "blk"), "sp"),
            P(("groups", "blk"), "sp"),
            P("sp", None),
            P(None, "sp"),
            P(None, "sp"),
            P(None, "sp"),
            P("groups", None),
            P("groups"),
        ),
        out_specs=P(("groups", "blk", "sp"), None),
        check_vma=False,
    )
```

time: 125 us -> 124 us (level); the launches traced: 123 us -> 124 us
  waiting for transfers between devices: 48.8 us -> 15.7 us
  starting transfers between devices: 44.5 us -> 67.8 us
  Pallas kernels: 22.1 us -> 30.6 us
  local copies, waits for them, and re-layouts: 7.73 us -> 9.39 us
    ppermute x21 -> x28, waiting for transfers between devices: 46.1 us -> 15.7 us  [by_chips(): return lax.ppermute(shard, 'blk', pairs)]
    ppermute x21 -> x28, starting transfers between devices: 44.4 us -> 67.2 us  [by_chips(): return lax.ppermute(shard, 'blk', pairs)]
    pallas_call x6 -> x11, Pallas kernels: 22.1 us -> 30.6 us  [call(): pl.pallas_call(kernel, out_shape=outs, in_specs=[SMEM] * len(scalars) + [...]
    ppermute x2 -> x4, waiting for transfers between devices: 2.65 us -> 0.01 us  [across_cores(): lax.ppermute(shard, 'blk', [(i, i ^ 1) for i in range(chips * CORES)])]
  transfers between devices with their start and end apart: 23 -> 32, of which waited for: 15 -> 9; matrix products, arithmetic and copies ran while one was open for 0% -> 1% of each run, Pallas kernels for 1% -> 23%
where the time goes in v3:
time: 124 us
  starting transfers between devices  67.8 us (55%)
  Pallas kernels  30.6 us (25%)
  waiting for transfers between devices  15.7 us (13%)
  local copies, waits for them, and re-layouts  9.39 us (8%)
    ppermute x28, starting transfers between devices, by_chips(): return lax.ppermute(shard, 'blk', pairs)  67.2 us
    pallas_call x11, Pallas kernels, call(): pl.pallas_call(kernel, out_shape=outs, in_specs=[SMEM] * len(scalars) + [...  30.6 us
    ppermute x28, waiting for transfers between devices, by_chips(): return lax.ppermute(shard, 'blk', pairs)  15.7 us
    unnamed x21, local copies, waits for them, and re-layouts  8.41 us
  transfers between devices with their start and end apart: 32, of which 9 were waited for; matrix products, arithmetic and copies ran while one was open for 1% of the time, Pallas kernels for 23%

profile of v3, /device:TPU:0, one launch (start us, length us, event | category | flops | bytes accessed | tf_op | source)
XLA Modules:
  0.0 123.8 jit_solution(2503427225085870849)
XLA Ops:
  0.0 1.0 copy-done.4
  1.0 1.0 copy-done.5
  2.1 0.5 shard_map.101
  2.6 3.0 %collective-permute-start.7 = (bf16[2,256,128]{2,1,0:T(8,128)(2,1)S(1)}, bf16[2,256,128]{2,1,0:T(8,128)(2,1)S(1)}, u32[]{:S(2)}, u32[]{:S(2)}) collective-permute-start(bf16[2,256,128]{2,1,0:T(8,128)(2,1)S(1)} %get-tuple-element.77), channel_id=1, source_target_pairs={{0,2},{1,3},{2,4},{3,5},{4,6},{5,7},{6,8},{7,9},{8,10},{9,11},{10,... | collective-permute-start | bytes 393224 | tf_op jit(solution)/shard_map/ppermute | solution.py:241
  5.5 1.6 %collective-permute-start.8 = (bf16[2,256,128]{2,1,0:T(8,128)(2,1)S(1)}, bf16[2,256,128]{2,1,0:T(8,128)(2,1)S(1)}, u32[]{:S(2)}, u32[]{:S(2)}) collective-permute-start(bf16[2,256,128]{2,1,0:T(8,128)(2,1)S(1)} %get-tuple-element.78), channel_id=1, source_target_pairs={{0,4},{1,5},{2,6},{3,7},{4,8},{5,9},{6,10},{7,11},{8,12},{9,13},{1... | collective-permute-start | bytes 393224 | tf_op jit(solution)/shard_map/ppermute | solution.py:241
  7.1 2.6 %collective-permute-start.9 = (bf16[2,256,128]{2,1,0:T(8,128)(2,1)S(1)}, bf16[2,256,128]{2,1,0:T(8,128)(2,1)S(1)}, u32[]{:S(2)}, u32[]{:S(2)}) collective-permute-start(bf16[2,256,128]{2,1,0:T(8,128)(2,1)S(1)} %get-tuple-element.79), channel_id=1, source_target_pairs={{0,6},{1,7},{2,8},{3,9},{4,10},{5,11},{6,12},{7,13},{8,14},{9,15},... | collective-permute-start | bytes 393224 | tf_op jit(solution)/shard_map/ppermute | solution.py:241
  9.7 1.2 collective-permute-start.10
  10.9 2.6 %collective-permute-start.11 = (bf16[2,256,128]{2,1,0:T(8,128)(2,1)S(1)}, bf16[2,256,128]{2,1,0:T(8,128)(2,1)S(1)}, u32[]{:S(2)}, u32[]{:S(2)}) collective-permute-start(bf16[2,256,128]{2,1,0:T(8,128)(2,1)S(1)} %get-tuple-element.81), channel_id=1, source_target_pairs={{0,10},{1,11},{2,12},{3,13},{4,14},{5,15},{6,0},{7,1},{8,2},{9,3},... | collective-permute-start | bytes 393224 | tf_op jit(solution)/shard_map/ppermute | solution.py:241
  13.5 1.4 %collective-permute-start.12 = (bf16[2,256,128]{2,1,0:T(8,128)(2,1)S(1)}, bf16[2,256,128]{2,1,0:T(8,128)(2,1)S(1)}, u32[]{:S(2)}, u32[]{:S(2)}) collective-permute-start(bf16[2,256,128]{2,1,0:T(8,128)(2,1)S(1)} %get-tuple-element.82), channel_id=1, source_target_pairs={{0,12},{1,13},{2,14},{3,15},{4,0},{5,1},{6,2},{7,3},{8,4},{9,5},{1... | collective-permute-start | bytes 393224 | tf_op jit(solution)/shard_map/ppermute | solution.py:241
  14.9 2.0 %collective-permute-start.13 = (bf16[2,256,128]{2,1,0:T(8,128)(2,1)S(1)}, bf16[2,256,128]{2,1,0:T(8,128)(2,1)S(1)}, u32[]{:S(2)}, u32[]{:S(2)}) collective-permute-start(bf16[2,256,128]{2,1,0:T(8,128)(2,1)S(1)} %get-tuple-element.83), channel_id=1, source_target_pairs={{0,14},{1,15},{2,0},{3,1},{4,2},{5,3},{6,4},{7,5},{8,6},{9,7},{10,... | collective-permute-start | bytes 393224 | tf_op jit(solution)/shard_map/ppermute | solution.py:241
  17.0 1.6 %copy-done.2 = bf16[1024,1024]{1,0:T(8,128)(2,1)S(1)} copy-done((bf16[1024,1024]{1,0:T(8,128)(2,1)S(1)}, bf16[1024,1024]{1,0:T(8,128)(2,1)}, u32[]{:S(2)}) %copy-start.2) | copy-done | bytes 2097176
  18.6 1.0 copy-done.6
  19.6 1.0 copy-done.7
  20.7 1.8 %shard_map.100 = (bf16[2,256,128]{2,1,0:T(8,128)(2,1)S(1)}, bf16[2,256,128]{2,1,0:T(8,128)(2,1)}, bf16[2,256,128]{2,1,0:T(8,128)(2,1)S(1)}, bf16[2,256,128]{2,1,...) custom-call(s32[1]{0:T(128)} %bitcast.chip_ref, ...), custom_call_target="tpu_custom_call" | custom-call | tf_op jit(solution)/shard_map/pallas_call | solution.py:226
  22.5 1.0 collective-permute-done.9.refs_3_
  23.5 0.3 collective-permute-done.10.refs_4_
  23.9 4.3 %collective-permute-start = (bf16[2,256,128]{2,1,0:T(8,128)(2,1)}, bf16[2,256,128]{2,1,0:T(8,128)(2,1)S(1)}, u32[]{:S(2)}, u32[]{:S(2)}) collective-permute-start(bf16[2,256,128]{2,1,0:T(8,128)(2,1)} %get-tuple-element.69), channel_id=1, source_target_pairs={{0,2},{1,3},{2,4},{3,5},{4,6},{5,7},{6,8},{7,9},{8,10},{9,11},{10,... | collective-permute-start | bytes 393224 | tf_op jit(solution)/shard_map/ppermute | solution.py:241
  28.3 6.0 %collective-permute-start.1 = (bf16[2,256,128]{2,1,0:T(8,128)(2,1)S(1)}, bf16[2,256,128]{2,1,0:T(8,128)(2,1)S(1)}, u32[]{:S(2)}, u32[]{:S(2)}) collective-permute-start(bf16[2,256,128]{2,1,0:T(8,128)(2,1)S(1)} %get-tuple-element.70), channel_id=1, source_target_pairs={{0,4},{1,5},{2,6},{3,7},{4,8},{5,9},{6,10},{7,11},{8,12},{9,13},{1... | collective-permute-start | bytes 393224 | tf_op jit(solution)/shard_map/ppermute | solution.py:241
  34.3 2.9 %collective-permute-start.2 = (bf16[2,256,128]{2,1,0:T(8,128)(2,1)S(1)}, bf16[2,256,128]{2,1,0:T(8,128)(2,1)S(1)}, u32[]{:S(2)}, u32[]{:S(2)}) collective-permute-start(bf16[2,256,128]{2,1,0:T(8,128)(2,1)S(1)} %get-tuple-element.71), channel_id=1, source_target_pairs={{0,6},{1,7},{2,8},{3,9},{4,10},{5,11},{6,12},{7,13},{8,14},{9,15},... | collective-permute-start | bytes 393224 | tf_op jit(solution)/shard_map/ppermute | solution.py:241
  37.2 0.1 reshape.17
  37.3 0.1 reshape.18.count_ref
  37.4 0.7 copy.12
  38.0 0.7 constant_dynamic-slice_fusion
  38.7 0.1 squeeze.6
  38.8 0.5 collective-permute-done.refs_1_.refs_9_
  39.4 2.1 %collective-permute-start.4 = (bf16[2,256,128]{2,1,0:T(8,128)(2,1)S(1)}, bf16[2,256,128]{2,1,0:T(8,128)(2,1)S(1)}, u32[]{:S(2)}, u32[]{:S(2)}) collective-permute-start(bf16[2,256,128]{2,1,0:T(8,128)(2,1)S(1)} %get-tuple-element.73), channel_id=1, source_target_pairs={{0,10},{1,11},{2,12},{3,13},{4,14},{5,15},{6,0},{7,1},{8,2},{9,3},... | collective-permute-start | bytes 393224 | tf_op jit(solution)/shard_map/ppermute | solution.py:241
  41.4 1.6 %collective-permute-start.5 = (bf16[2,256,128]{2,1,0:T(8,128)(2,1)S(1)}, bf16[2,256,128]{2,1,0:T(8,128)(2,1)S(1)}, u32[]{:S(2)}, u32[]{:S(2)}) collective-permute-start(bf16[2,256,128]{2,1,0:T(8,128)(2,1)S(1)} %get-tuple-element.74), channel_id=1, source_target_pairs={{0,12},{1,13},{2,14},{3,15},{4,0},{5,1},{6,2},{7,3},{8,4},{9,5},{1... | collective-permute-start | bytes 393224 | tf_op jit(solution)/shard_map/ppermute | solution.py:241
  43.1 13.0 %collective-permute-start.6 = (bf16[2,256,128]{2,1,0:T(8,128)(2,1)S(1)}, bf16[2,256,128]{2,1,0:T(8,128)(2,1)S(1)}, u32[]{:S(2)}, u32[]{:S(2)}) collective-permute-start(bf16[2,256,128]{2,1,0:T(8,128)(2,1)S(1)} %get-tuple-element.75), channel_id=1, source_target_pairs={{0,14},{1,15},{2,0},{3,1},{4,2},{5,3},{6,4},{7,5},{8,6},{9,7},{10,... | collective-permute-start | bytes 393224 | tf_op jit(solution)/shard_map/ppermute | solution.py:241
  56.1 6.2 %shard_map.103.prob_ref = bf16[16384,128]{1,0:T(8,128)(2,1)S(1)} custom-call(s32[1]{0:T(128)} %bitcast.chip_ref, s32[128]{0:T(128)S(1)} %fusion.table_ref, s32[16]{0:T(128)S(1)} %reshape.18.count_ref, bf16[2,256,128]{2,1,0:T(8,128)(2,1)S(1)} %get-tuple-element.84.refs_0_, bf16[2,256,128]{2,1,0:T(8,128)(2,1)S(1)} %collective-permute-done.7.refs_1_, ...), custom_call_target="tpu_custom_call" | custom-call | tf_op jit(solution)/shard_map/pallas_call | solution.py:226
  62.4 2.0 %copy-done = bf16[16384,128]{1,0:T(8,128)(2,1)} copy-done((bf16[16384,128]{1,0:T(8,128)(2,1)}, bf16[16384,128]{1,0:T(8,128)(2,1)S(1)}, u32[]{:S(2)}) %copy-start) | copy-done | bytes 4194328
  64.5 5.8 %shard_map.107 = (f32[2048,128]{1,0:T(8,128)S(1)}, bf16[2048,128]{1,0:T(8,128)(2,1)S(1)}) custom-call(s32[1]{0:T(128)} %bitcast.chip_ref, s32[128]{0:T(128)S(1)} %fusion.table_ref, s32[16]{0:T(128)S(1)} %reshape.18.count_ref, bf16[16384,128]{1,0:T(8,128)(2,1)} %copy-done, bf16[2,256,128]{2,1,0:T(8,128)(2,1)S(1)} %get-tuple-element.93.refs_0_.refs_8_, ...), custom_call_target="tpu_custom_call" | custom-call | tf_op jit(solution)/shard_map/pallas_call | solution.py:226
  70.4 0.4 collective-permute-start.24
  70.8 11.1 %shard_map.105 = (bf16[2048,128]{1,0:T(8,128)(2,1)S(1)}, f32[2048,128]{1,0:T(8,128)S(1)}, bf16[2048,128]{1,0:T(8,128)(2,1)S(1)}) custom-call(s32[1]{0:T(128)} %bitcast.chip_ref, s32[128]{0:T(128)S(1)} %fusion.table_ref, s32[16]{0:T(128)S(1)} %reshape.18.count_ref, bf16[16384,128]{1,0:T(8,128)(2,1)} %copy-done, ...), custom_call_target="tpu_custom_call" | custom-call | tf_op jit(solution)/shard_map/pallas_call | solution.py:226
  82.0 0.1 shard_map.108
  82.4 4.3 %collective-permute-start.28 = (bf16[2,256,128]{2,1,0:T(8,128)(2,1)S(1)}, bf16[2,256,128]{2,1,0:T(8,128)(2,1)S(1)}, u32[]{:S(2)}, u32[]{:S(2)}) collective-permute-start(bf16[2,256,128]{2,1,0:T(8,128)(2,1)S(1)} %get-tuple-element.118), channel_id=1, source_target_pairs={{0,8},{1,9},{2,10},{3,11},{4,12},{5,13},{6,14},{7,15},{8,0},{9,1},... | collective-permute-start | bytes 393224 | tf_op jit(solution)/shard_map/ppermute | solution.py:241
  86.6 1.5 %collective-permute-done.25.refs_1_ = bf16[2,256,128]{2,1,0:T(8,128)(2,1)S(1)} collective-permute-done((bf16[2,256,128]{2,1,0:T(8,128)(2,1)S(1)}, bf16[2,256,128]{2,1,0:T(8,128)(2,1)S(1)}, u32[]{:S(2)}, u32[]{:S(2)}) %collective-permute-start.25) | collective-permute-done | bytes 131104 | tf_op jit(solution)/shard_map/ppermute | solution.py:241
  88.1 1.9 %collective-permute-done.26.refs_2_ = bf16[2,256,128]{2,1,0:T(8,128)(2,1)S(1)} collective-permute-done((bf16[2,256,128]{2,1,0:T(8,128)(2,1)S(1)}, bf16[2,256,128]{2,1,0:T(8,128)(2,1)S(1)}, u32[]{:S(2)}, u32[]{:S(2)}) %collective-permute-start.26) | collective-permute-done | bytes 131104 | tf_op jit(solution)/shard_map/ppermute | solution.py:241
  90.0 0.9 collective-permute-start.31
  90.9 0.1 shard_map.106
  91.0 1.6 %collective-permute-done.27.refs_3_ = bf16[2,256,128]{2,1,0:T(8,128)(2,1)S(1)} collective-permute-done((bf16[2,256,128]{2,1,0:T(8,128)(2,1)S(1)}, bf16[2,256,128]{2,1,0:T(8,128)(2,1)S(1)}, u32[]{:S(2)}, u32[]{:S(2)}) %collective-permute-start.27) | collective-permute-done | bytes 131104 | tf_op jit(solution)/shard_map/ppermute | solution.py:241
  92.6 9.9 %collective-permute-start.17 = (bf16[1,256,128]{2,1,0:T(8,128)(2,1)S(1)}, bf16[1,256,128]{2,1,0:T(8,128)(2,1)S(1)}, u32[]{:S(2)}, u32[]{:S(2)}) collective-permute-start(bf16[1,256,128]{2,1,0:T(8,128)(2,1)S(1)} %get-tuple-element.104), channel_id=1, source_target_pairs={{0,14},{1,15},{2,0},{3,1},{4,2},{5,3},{6,4},{7,5},{8,6},{9,7},{10,... | collective-permute-start | bytes 196616 | tf_op jit(solution)/shard_map/ppermute | solution.py:241
  102.5 2.6 %collective-permute-done.28.refs_4_ = bf16[2,256,128]{2,1,0:T(8,128)(2,1)S(1)} collective-permute-done((bf16[2,256,128]{2,1,0:T(8,128)(2,1)S(1)}, bf16[2,256,128]{2,1,0:T(8,128)(2,1)S(1)}, u32[]{:S(2)}, u32[]{:S(2)}) %collective-permute-start.28) | collective-permute-done | bytes 131104 | tf_op jit(solution)/shard_map/ppermute | solution.py:241
  105.1 2.7 %collective-permute-done.29.refs_5_ = bf16[2,256,128]{2,1,0:T(8,128)(2,1)S(1)} collective-permute-done((bf16[2,256,128]{2,1,0:T(8,128)(2,1)S(1)}, bf16[2,256,128]{2,1,0:T(8,128)(2,1)S(1)}, u32[]{:S(2)}, u32[]{:S(2)}) %collective-permute-start.29) | collective-permute-done | bytes 131104 | tf_op jit(solution)/shard_map/ppermute | solution.py:241
  107.8 5.4 %collective-permute-start.20 = (bf16[1,256,128]{2,1,0:T(8,128)(2,1)S(1)}, bf16[1,256,128]{2,1,0:T(8,128)(2,1)S(1)}, u32[]{:S(2)}, u32[]{:S(2)}) collective-permute-start(bf16[1,256,128]{2,1,0:T(8,128)(2,1)S(1)} %get-tuple-element.107), channel_id=1, source_target_pairs={{0,8},{1,9},{2,10},{3,11},{4,12},{5,13},{6,14},{7,15},{8,0},{9,1},... | collective-permute-start | bytes 196616 | tf_op jit(solution)/shard_map/ppermute | solution.py:241
  113.3 2.0 %collective-permute-start.23 = (bf16[1,256,128]{2,1,0:T(8,128)(2,1)S(1)}, bf16[1,256,128]{2,1,0:T(8,128)(2,1)S(1)}, u32[]{:S(2)}, u32[]{:S(2)}) collective-permute-start(bf16[1,256,128]{2,1,0:T(8,128)(2,1)S(1)} %get-tuple-element.110), channel_id=1, source_target_pairs={{0,2},{1,3},{2,4},{3,5},{4,6},{5,7},{6,8},{7,9},{8,10},{9,11},{10,... | collective-permute-start | bytes 196616 | tf_op jit(solution)/shard_map/ppermute | solution.py:241
  115.4 3.2 %shard_map.109.refs_9_ = f32[256,1024]{1,0:T(8,128)S(1)} custom-call(s32[1]{0:T(128)} %bitcast.chip_ref, bf16[2,256,128]{2,1,0:T(8,128)(2,1)S(1)} %get-tuple-element.114.refs_0_, bf16[2,256,128]{2,1,0:T(8,128)(2,1)S(1)} %collective-permute-done.25.refs_1_, bf16[2,256,128]{2,1,0:T(8,128)(2,1)S(1)} %collective-permute-done.26.refs_2_, ...), custom_call_target="tpu_custom_call" | custom-call | tf_op jit(solution)/shard_map/pallas_call | solution.py:226
  118.6 3.5 %collective-permute-done.21.refs_5_ = bf16[1,256,128]{2,1,0:T(8,128)(2,1)S(1)} collective-permute-done((bf16[1,256,128]{2,1,0:T(8,128)(2,1)S(1)}, bf16[1,256,128]{2,1,0:T(8,128)(2,1)S(1)}, u32[]{:S(2)}, u32[]{:S(2)}) %collective-permute-start.21) | collective-permute-done | bytes 65568 | tf_op jit(solution)/shard_map/ppermute | solution.py:241
  122.1 1.6 %shard_map.110 = bf16[256,1024]{1,0:T(8,128)(2,1)} custom-call(s32[1]{0:T(128)} %bitcast.chip_ref, bf16[1,256,128]{2,1,0:T(8,128)(2,1)S(1)} %get-tuple-element.122.refs_0_, bf16[1,256,128]{2,1,0:T(8,128)(2,1)S(1)} %collective-permute-done.17.refs_1_, bf16[1,256,128]{2,1,0:T(8,128)(2,1)S(1)} %collective-permute-done.18.refs_2_, ...), custom_call_target="tpu_custom_call" | custom-call | tf_op jit(solution)/shard_map/pallas_call | solution.py:226
  (54 shorter events, 0.7 us)
Async XLA Ops:
  0.0 1.0 copy-start.4
  1.0 1.0 copy-start.5
  2.6 11.0 %collective-permute-start.7 = (bf16[2,256,128]{2,1,0:T(8,128)(2,1)S(1)}, bf16[2,256,128]{2,1,0:T(8,128)(2,1)S(1)}, u32[]{:S(2)}, u32[]{:S(2)}) collective-permute-start(bf16[2,256,128]{2,1,0:T(8,128)(2,1)S(1)} %get-tuple-element.77), channel_id=1, source_target_pairs={{0,2},{1,3},{2,4},{3,5},{4,6},{5,7},{6,8},{7,9},{8,10},{9,11},{10,... | collective-permute-start | bytes 393224 | tf_op jit(solution)/shard_map/ppermute | solution.py:241
  5.5 9.4 %collective-permute-start.8 = (bf16[2,256,128]{2,1,0:T(8,128)(2,1)S(1)}, bf16[2,256,128]{2,1,0:T(8,128)(2,1)S(1)}, u32[]{:S(2)}, u32[]{:S(2)}) collective-permute-start(bf16[2,256,128]{2,1,0:T(8,128)(2,1)S(1)} %get-tuple-element.78), channel_id=1, source_target_pairs={{0,4},{1,5},{2,6},{3,7},{4,8},{5,9},{6,10},{7,11},{8,12},{9,13},{1... | collective-permute-start | bytes 393224 | tf_op jit(solution)/shard_map/ppermute | solution.py:241
  7.1 16.3 %collective-permute-start.9 = (bf16[2,256,128]{2,1,0:T(8,128)(2,1)S(1)}, bf16[2,256,128]{2,1,0:T(8,128)(2,1)S(1)}, u32[]{:S(2)}, u32[]{:S(2)}) collective-permute-start(bf16[2,256,128]{2,1,0:T(8,128)(2,1)S(1)} %get-tuple-element.79), channel_id=1, source_target_pairs={{0,6},{1,7},{2,8},{3,9},{4,10},{5,11},{6,12},{7,13},{8,14},{9,15},... | collective-permute-start | bytes 393224 | tf_op jit(solution)/shard_map/ppermute | solution.py:241
  9.7 14.1 %collective-permute-start.10 = (bf16[2,256,128]{2,1,0:T(8,128)(2,1)S(1)}, bf16[2,256,128]{2,1,0:T(8,128)(2,1)S(1)}, u32[]{:S(2)}, u32[]{:S(2)}) collective-permute-start(bf16[2,256,128]{2,1,0:T(8,128)(2,1)S(1)} %get-tuple-element.80), channel_id=1, source_target_pairs={{0,8},{1,9},{2,10},{3,11},{4,12},{5,13},{6,14},{7,15},{8,0},{9,1},... | collective-permute-start | bytes 393224 | tf_op jit(solution)/shard_map/ppermute | solution.py:241
  10.9 12.9 %collective-permute-start.11 = (bf16[2,256,128]{2,1,0:T(8,128)(2,1)S(1)}, bf16[2,256,128]{2,1,0:T(8,128)(2,1)S(1)}, u32[]{:S(2)}, u32[]{:S(2)}) collective-permute-start(bf16[2,256,128]{2,1,0:T(8,128)(2,1)S(1)} %get-tuple-element.81), channel_id=1, source_target_pairs={{0,10},{1,11},{2,12},{3,13},{4,14},{5,15},{6,0},{7,1},{8,2},{9,3},... | collective-permute-start | bytes 393224 | tf_op jit(solution)/shard_map/ppermute | solution.py:241
  13.5 10.3 %collective-permute-start.12 = (bf16[2,256,128]{2,1,0:T(8,128)(2,1)S(1)}, bf16[2,256,128]{2,1,0:T(8,128)(2,1)S(1)}, u32[]{:S(2)}, u32[]{:S(2)}) collective-permute-start(bf16[2,256,128]{2,1,0:T(8,128)(2,1)S(1)} %get-tuple-element.82), channel_id=1, source_target_pairs={{0,12},{1,13},{2,14},{3,15},{4,0},{5,1},{6,2},{7,3},{8,4},{9,5},{1... | collective-permute-start | bytes 393224 | tf_op jit(solution)/shard_map/ppermute | solution.py:241
  14.9 8.9 %collective-permute-start.13 = (bf16[2,256,128]{2,1,0:T(8,128)(2,1)S(1)}, bf16[2,256,128]{2,1,0:T(8,128)(2,1)S(1)}, u32[]{:S(2)}, u32[]{:S(2)}) collective-permute-start(bf16[2,256,128]{2,1,0:T(8,128)(2,1)S(1)} %get-tuple-element.83), channel_id=1, source_target_pairs={{0,14},{1,15},{2,0},{3,1},{4,2},{5,3},{6,4},{7,5},{8,6},{9,7},{10,... | collective-permute-start | bytes 393224 | tf_op jit(solution)/shard_map/ppermute | solution.py:241
  17.0 1.6 %copy-start.2 = (bf16[1024,1024]{1,0:T(8,128)(2,1)S(1)}, bf16[1024,1024]{1,0:T(8,128)(2,1)}, u32[]{:S(2)}) copy-start(bf16[1024,1024]{1,0:T(8,128)(2,1)} %weight_ref.1) | copy-start | bytes 6291460
  18.6 1.0 copy-start.6
  19.6 1.0 copy-start.7
  20.7 16.5 %copy-start.9 = (s32[32]{0:T(128)S(1)}, s32[32]{0:T(128)}, u32[]{:S(2)}) copy-start(s32[32]{0:T(128)} %param.19) | copy-start | bytes 388
  20.7 16.7 %copy-start.8 = (s32[32,8]{0,1:T(8,128)S(1)}, s32[32,8]{0,1:T(8,128)}, u32[]{:S(2)}) copy-start(s32[32,8]{0,1:T(8,128)} %param.18) | copy-start | bytes 3076
  23.9 19.2 %collective-permute-start.14 = (bf16[2048,128]{1,0:T(8,128)(2,1)S(1)}, bf16[2048,128]{1,0:T(8,128)(2,1)S(1)}, u32[]{:S(2)}, u32[]{:S(2)}) collective-permute-start(bf16[2048,128]{1,0:T(8,128)(2,1)S(1)} %shard_map.102), channel_id=1, source_target_pairs={{0,1},{1,0},{2,3},{3,2},{4,5},{5,4},{6,7},{7,6},{8,9},{9,8},{10,11... | collective-permute-start | bytes 1572872 | tf_op jit(solution)/shard_map/ppermute | solution.py:250
  23.9 15.4 %collective-permute-start = (bf16[2,256,128]{2,1,0:T(8,128)(2,1)}, bf16[2,256,128]{2,1,0:T(8,128)(2,1)S(1)}, u32[]{:S(2)}, u32[]{:S(2)}) collective-permute-start(bf16[2,256,128]{2,1,0:T(8,128)(2,1)} %get-tuple-element.69), channel_id=1, source_target_pairs={{0,2},{1,3},{2,4},{3,5},{4,6},{5,7},{6,8},{7,9},{8,10},{9,11},{10,... | collective-permute-start | bytes 393224 | tf_op jit(solution)/shard_map/ppermute | solution.py:241
  28.3 13.2 %collective-permute-start.1 = (bf16[2,256,128]{2,1,0:T(8,128)(2,1)S(1)}, bf16[2,256,128]{2,1,0:T(8,128)(2,1)S(1)}, u32[]{:S(2)}, u32[]{:S(2)}) collective-permute-start(bf16[2,256,128]{2,1,0:T(8,128)(2,1)S(1)} %get-tuple-element.70), channel_id=1, source_target_pairs={{0,4},{1,5},{2,6},{3,7},{4,8},{5,9},{6,10},{7,11},{8,12},{9,13},{1... | collective-permute-start | bytes 393224 | tf_op jit(solution)/shard_map/ppermute | solution.py:241
  34.3 30.1 %collective-permute-start.2 = (bf16[2,256,128]{2,1,0:T(8,128)(2,1)S(1)}, bf16[2,256,128]{2,1,0:T(8,128)(2,1)S(1)}, u32[]{:S(2)}, u32[]{:S(2)}) collective-permute-start(bf16[2,256,128]{2,1,0:T(8,128)(2,1)S(1)} %get-tuple-element.71), channel_id=1, source_target_pairs={{0,6},{1,7},{2,8},{3,9},{4,10},{5,11},{6,12},{7,13},{8,14},{9,15},... | collective-permute-start | bytes 393224 | tf_op jit(solution)/shard_map/ppermute | solution.py:241
  37.2 27.2 %collective-permute-start.3 = (bf16[2,256,128]{2,1,0:T(8,128)(2,1)S(1)}, bf16[2,256,128]{2,1,0:T(8,128)(2,1)S(1)}, u32[]{:S(2)}, u32[]{:S(2)}) collective-permute-start(bf16[2,256,128]{2,1,0:T(8,128)(2,1)S(1)} %get-tuple-element.72), channel_id=1, source_target_pairs={{0,8},{1,9},{2,10},{3,11},{4,12},{5,13},{6,14},{7,15},{8,0},{9,1},... | collective-permute-start | bytes 393224 | tf_op jit(solution)/shard_map/ppermute | solution.py:241
  39.4 25.0 %collective-permute-start.4 = (bf16[2,256,128]{2,1,0:T(8,128)(2,1)S(1)}, bf16[2,256,128]{2,1,0:T(8,128)(2,1)S(1)}, u32[]{:S(2)}, u32[]{:S(2)}) collective-permute-start(bf16[2,256,128]{2,1,0:T(8,128)(2,1)S(1)} %get-tuple-element.73), channel_id=1, source_target_pairs={{0,10},{1,11},{2,12},{3,13},{4,14},{5,15},{6,0},{7,1},{8,2},{9,3},... | collective-permute-start | bytes 393224 | tf_op jit(solution)/shard_map/ppermute | solution.py:241
  41.4 22.9 %collective-permute-start.5 = (bf16[2,256,128]{2,1,0:T(8,128)(2,1)S(1)}, bf16[2,256,128]{2,1,0:T(8,128)(2,1)S(1)}, u32[]{:S(2)}, u32[]{:S(2)}) collective-permute-start(bf16[2,256,128]{2,1,0:T(8,128)(2,1)S(1)} %get-tuple-element.74), channel_id=1, source_target_pairs={{0,12},{1,13},{2,14},{3,15},{4,0},{5,1},{6,2},{7,3},{8,4},{9,5},{1... | collective-permute-start | bytes 393224 | tf_op jit(solution)/shard_map/ppermute | solution.py:241
  43.1 21.3 %collective-permute-start.6 = (bf16[2,256,128]{2,1,0:T(8,128)(2,1)S(1)}, bf16[2,256,128]{2,1,0:T(8,128)(2,1)S(1)}, u32[]{:S(2)}, u32[]{:S(2)}) collective-permute-start(bf16[2,256,128]{2,1,0:T(8,128)(2,1)S(1)} %get-tuple-element.75), channel_id=1, source_target_pairs={{0,14},{1,15},{2,0},{3,1},{4,2},{5,3},{6,4},{7,5},{8,6},{9,7},{10,... | collective-permute-start | bytes 393224 | tf_op jit(solution)/shard_map/ppermute | solution.py:241
  62.4 2.0 %copy-start = (bf16[16384,128]{1,0:T(8,128)(2,1)}, bf16[16384,128]{1,0:T(8,128)(2,1)S(1)}, u32[]{:S(2)}) copy-start(bf16[16384,128]{1,0:T(8,128)(2,1)S(1)} %shard_map.103.prob_ref) | copy-start | bytes 12582916
  64.4 6.4 %collective-permute-start.15 = (bf16[2048,128]{1,0:T(8,128)(2,1)S(1)}, bf16[2048,128]{1,0:T(8,128)(2,1)S(1)}, u32[]{:S(2)}, u32[]{:S(2)}) collective-permute-start(bf16[2048,128]{1,0:T(8,128)(2,1)S(1)} %shard_map.104), channel_id=1, source_target_pairs={{0,1},{1,0},{2,3},{3,2},{4,5},{5,4},{6,7},{7,6},{8,9},{9,8},{10,11... | collective-permute-start | bytes 1572872 | tf_op jit(solution)/shard_map/ppermute | solution.py:250
  70.4 11.7 %collective-permute-start.24 = (bf16[2048,128]{1,0:T(8,128)(2,1)S(1)}, bf16[2048,128]{1,0:T(8,128)(2,1)S(1)}, u32[]{:S(2)}, u32[]{:S(2)}) collective-permute-start(bf16[2048,128]{1,0:T(8,128)(2,1)S(1)} %get-tuple-element.112), channel_id=1, source_target_pairs={{0,1},{1,0},{2,3},{3,2},{4,5},{5,4},{6,7},{7,6},{8,9},{9,8},{10,11... | collective-permute-start | bytes 1572872 | tf_op jit(solution)/shard_map/ppermute | solution.py:250
  81.9 33.4 %copy-start.1 = (bf16[1024,1024]{1,0:T(8,128)(2,1)S(1)}, bf16[1024,1024]{1,0:T(8,128)(2,1)}, u32[]{:S(2)}) copy-start(bf16[1024,1024]{1,0:T(8,128)(2,1)} %refs_8_.2) | copy-start | bytes 6291460
  81.9 8.1 %collective-permute-start.16 = (bf16[2048,128]{1,0:T(8,128)(2,1)S(1)}, bf16[2048,128]{1,0:T(8,128)(2,1)S(1)}, u32[]{:S(2)}, u32[]{:S(2)}) collective-permute-start(bf16[2048,128]{1,0:T(8,128)(2,1)S(1)} %get-tuple-element.102), channel_id=1, source_target_pairs={{0,1},{1,0},{2,3},{3,2},{4,5},{5,4},{6,7},{7,6},{8,9},{9,8},{10,11... | collective-permute-start | bytes 1572872 | tf_op jit(solution)/shard_map/ppermute | solution.py:250
  82.2 5.9 %collective-permute-start.25 = (bf16[2,256,128]{2,1,0:T(8,128)(2,1)S(1)}, bf16[2,256,128]{2,1,0:T(8,128)(2,1)S(1)}, u32[]{:S(2)}, u32[]{:S(2)}) collective-permute-start(bf16[2,256,128]{2,1,0:T(8,128)(2,1)S(1)} %get-tuple-element.115), channel_id=1, source_target_pairs={{0,14},{1,15},{2,0},{3,1},{4,2},{5,3},{6,4},{7,5},{8,6},{9,7},{10,... | collective-permute-start | bytes 393224 | tf_op jit(solution)/shard_map/ppermute | solution.py:241
  82.2 7.8 %collective-permute-start.26 = (bf16[2,256,128]{2,1,0:T(8,128)(2,1)S(1)}, bf16[2,256,128]{2,1,0:T(8,128)(2,1)S(1)}, u32[]{:S(2)}, u32[]{:S(2)}) collective-permute-start(bf16[2,256,128]{2,1,0:T(8,128)(2,1)S(1)} %get-tuple-element.116), channel_id=1, source_target_pairs={{0,12},{1,13},{2,14},{3,15},{4,0},{5,1},{6,2},{7,3},{8,4},{9,5},{1... | collective-permute-start | bytes 393224 | tf_op jit(solution)/shard_map/ppermute | solution.py:241
  82.3 10.3 %collective-permute-start.27 = (bf16[2,256,128]{2,1,0:T(8,128)(2,1)S(1)}, bf16[2,256,128]{2,1,0:T(8,128)(2,1)S(1)}, u32[]{:S(2)}, u32[]{:S(2)}) collective-permute-start(bf16[2,256,128]{2,1,0:T(8,128)(2,1)S(1)} %get-tuple-element.117), channel_id=1, source_target_pairs={{0,10},{1,11},{2,12},{3,13},{4,14},{5,15},{6,0},{7,1},{8,2},{9,3},... | collective-permute-start | bytes 393224 | tf_op jit(solution)/shard_map/ppermute | solution.py:241
  82.4 22.7 %collective-permute-start.28 = (bf16[2,256,128]{2,1,0:T(8,128)(2,1)S(1)}, bf16[2,256,128]{2,1,0:T(8,128)(2,1)S(1)}, u32[]{:S(2)}, u32[]{:S(2)}) collective-permute-start(bf16[2,256,128]{2,1,0:T(8,128)(2,1)S(1)} %get-tuple-element.118), channel_id=1, source_target_pairs={{0,8},{1,9},{2,10},{3,11},{4,12},{5,13},{6,14},{7,15},{8,0},{9,1},... | collective-permute-start | bytes 393224 | tf_op jit(solution)/shard_map/ppermute | solution.py:241
  88.1 19.7 %collective-permute-start.29 = (bf16[2,256,128]{2,1,0:T(8,128)(2,1)S(1)}, bf16[2,256,128]{2,1,0:T(8,128)(2,1)S(1)}, u32[]{:S(2)}, u32[]{:S(2)}) collective-permute-start(bf16[2,256,128]{2,1,0:T(8,128)(2,1)S(1)} %get-tuple-element.119), channel_id=1, source_target_pairs={{0,6},{1,7},{2,8},{3,9},{4,10},{5,11},{6,12},{7,13},{8,14},{9,15},... | collective-permute-start | bytes 393224 | tf_op jit(solution)/shard_map/ppermute | solution.py:241
  90.0 17.8 %collective-permute-start.30 = (bf16[2,256,128]{2,1,0:T(8,128)(2,1)S(1)}, bf16[2,256,128]{2,1,0:T(8,128)(2,1)S(1)}, u32[]{:S(2)}, u32[]{:S(2)}) collective-permute-start(bf16[2,256,128]{2,1,0:T(8,128)(2,1)S(1)} %get-tuple-element.120), channel_id=1, source_target_pairs={{0,4},{1,5},{2,6},{3,7},{4,8},{5,9},{6,10},{7,11},{8,12},{9,13},{1... | collective-permute-start | bytes 393224 | tf_op jit(solution)/shard_map/ppermute | solution.py:241
  90.0 23.2 %collective-permute-start.31 = (bf16[2,256,128]{2,1,0:T(8,128)(2,1)S(1)}, bf16[2,256,128]{2,1,0:T(8,128)(2,1)S(1)}, u32[]{:S(2)}, u32[]{:S(2)}) collective-permute-start(bf16[2,256,128]{2,1,0:T(8,128)(2,1)S(1)} %get-tuple-element.121), channel_id=1, source_target_pairs={{0,2},{1,3},{2,4},{3,5},{4,6},{5,7},{6,8},{7,9},{8,10},{9,11},{10,... | collective-permute-start | bytes 393224 | tf_op jit(solution)/shard_map/ppermute | solution.py:241
  92.6 20.7 %collective-permute-start.17 = (bf16[1,256,128]{2,1,0:T(8,128)(2,1)S(1)}, bf16[1,256,128]{2,1,0:T(8,128)(2,1)S(1)}, u32[]{:S(2)}, u32[]{:S(2)}) collective-permute-start(bf16[1,256,128]{2,1,0:T(8,128)(2,1)S(1)} %get-tuple-element.104), channel_id=1, source_target_pairs={{0,14},{1,15},{2,0},{3,1},{4,2},{5,3},{6,4},{7,5},{8,6},{9,7},{10,... | collective-permute-start | bytes 196616 | tf_op jit(solution)/shard_map/ppermute | solution.py:241
  105.1 8.2 %collective-permute-start.18 = (bf16[1,256,128]{2,1,0:T(8,128)(2,1)S(1)}, bf16[1,256,128]{2,1,0:T(8,128)(2,1)S(1)}, u32[]{:S(2)}, u32[]{:S(2)}) collective-permute-start(bf16[1,256,128]{2,1,0:T(8,128)(2,1)S(1)} %get-tuple-element.105), channel_id=1, source_target_pairs={{0,12},{1,13},{2,14},{3,15},{4,0},{5,1},{6,2},{7,3},{8,4},{9,5},{1... | collective-permute-start | bytes 196616 | tf_op jit(solution)/shard_map/ppermute | solution.py:241
  107.8 10.8 %collective-permute-start.19 = (bf16[1,256,128]{2,1,0:T(8,128)(2,1)S(1)}, bf16[1,256,128]{2,1,0:T(8,128)(2,1)S(1)}, u32[]{:S(2)}, u32[]{:S(2)}) collective-permute-start(bf16[1,256,128]{2,1,0:T(8,128)(2,1)S(1)} %get-tuple-element.106), channel_id=1, source_target_pairs={{0,10},{1,11},{2,12},{3,13},{4,14},{5,15},{6,0},{7,1},{8,2},{9,3},... | collective-permute-start | bytes 196616 | tf_op jit(solution)/shard_map/ppermute | solution.py:241
  107.8 10.8 %collective-permute-start.20 = (bf16[1,256,128]{2,1,0:T(8,128)(2,1)S(1)}, bf16[1,256,128]{2,1,0:T(8,128)(2,1)S(1)}, u32[]{:S(2)}, u32[]{:S(2)}) collective-permute-start(bf16[1,256,128]{2,1,0:T(8,128)(2,1)S(1)} %get-tuple-element.107), channel_id=1, source_target_pairs={{0,8},{1,9},{2,10},{3,11},{4,12},{5,13},{6,14},{7,15},{8,0},{9,1},... | collective-permute-start | bytes 196616 | tf_op jit(solution)/shard_map/ppermute | solution.py:241
  113.2 8.9 %collective-permute-start.21 = (bf16[1,256,128]{2,1,0:T(8,128)(2,1)S(1)}, bf16[1,256,128]{2,1,0:T(8,128)(2,1)S(1)}, u32[]{:S(2)}, u32[]{:S(2)}) collective-permute-start(bf16[1,256,128]{2,1,0:T(8,128)(2,1)S(1)} %get-tuple-element.108), channel_id=1, source_target_pairs={{0,6},{1,7},{2,8},{3,9},{4,10},{5,11},{6,12},{7,13},{8,14},{9,15},... | collective-permute-start | bytes 196616 | tf_op jit(solution)/shard_map/ppermute | solution.py:241
  113.2 8.9 %collective-permute-start.22 = (bf16[1,256,128]{2,1,0:T(8,128)(2,1)S(1)}, bf16[1,256,128]{2,1,0:T(8,128)(2,1)S(1)}, u32[]{:S(2)}, u32[]{:S(2)}) collective-permute-start(bf16[1,256,128]{2,1,0:T(8,128)(2,1)S(1)} %get-tuple-element.109), channel_id=1, source_target_pairs={{0,4},{1,5},{2,6},{3,7},{4,8},{5,9},{6,10},{7,11},{8,12},{9,13},{1... | collective-permute-start | bytes 196616 | tf_op jit(solution)/shard_map/ppermute | solution.py:241
  113.3 8.8 %collective-permute-start.23 = (bf16[1,256,128]{2,1,0:T(8,128)(2,1)S(1)}, bf16[1,256,128]{2,1,0:T(8,128)(2,1)S(1)}, u32[]{:S(2)}, u32[]{:S(2)}) collective-permute-start(bf16[1,256,128]{2,1,0:T(8,128)(2,1)S(1)} %get-tuple-element.110), channel_id=1, source_target_pairs={{0,2},{1,3},{2,4},{3,5},{4,6},{5,7},{6,8},{7,9},{8,10},{9,11},{10,... | collective-permute-start | bytes 196616 | tf_op jit(solution)/shard_map/ppermute | solution.py:241
  115.4 6.8 %copy-start.3 = (bf16[1024,1024]{1,0:T(8,128)(2,1)S(1)}, bf16[1024,1024]{1,0:T(8,128)(2,1)}, u32[]{:S(2)}) copy-start(bf16[1024,1024]{1,0:T(8,128)(2,1)} %refs_8_.3) | copy-start | bytes 6291460

commit v4 on v3

v4 whole, which is shorter than its diff:
```python
import functools
import math

import jax
import jax.numpy as jnp
from jax import lax
from jax.experimental import pallas as pl
from jax.experimental.pallas import tpu as pltpu
from jax.sharding import PartitionSpec as P

HD = 128
BLOCK = 128
NBR = 8
WIN = 8
CORES = 2
WIDTHS = (2, 4, 6, 8)
CONTRACT = (((1,), (1,)), ((), ()))
ANY = pl.BlockSpec(memory_space=pl.ANY)
VMEM = pl.BlockSpec(memory_space=pltpu.VMEM)
SMEM = pl.BlockSpec(memory_space=pltpu.SMEM)
LIMIT = pltpu.CompilerParams(vmem_limit_bytes=48 << 20)


def passed_along(shard, axis, by):
    size = lax.axis_size(axis)
    return lax.ppermute(shard, axis, [(i, (i + by) % size) for i in range(size)])


def rotated(chip, step, chips):
    return lax.rem(chip + step, chips)


def columns(head):
    return pl.ds(pl.multiple_of(head * HD, HD), HD)


def rows_of(block, size):
    return pl.ds(pl.multiple_of(block * size, size), size)


def pack_kernel(chips, chip_ref, *refs):
    sources, outs, sem = refs[:2], refs[2:-1], refs[-1]
    copies = [
        pltpu.make_async_copy(
            source.at[:, columns(rotated(chip_ref[0], step, chips))],
            outs[step].at[:, place * HD : (place + 1) * HD],
            sem.at[step * 2 + place],
        )
        for step in range(chips)
        for place, source in enumerate(sources)
    ]
    for copy in copies:
        copy.start()
    for copy in copies:
        copy.wait()


def grad_kernel(chips, chip_ref, grad_ref, weight_ref, query_ref, *outs):
    for step in range(chips):
        head = rotated(chip_ref[0], step, chips)
        outs[step][:, :HD] = query_ref[:, columns(head)]
        outs[step][:, HD:] = lax.dot_general(
            grad_ref[...],
            weight_ref[rows_of(head, HD), :],
            CONTRACT,
            preferred_element_type=jnp.float32,
        ).astype(jnp.bfloat16)


def assemble_kernel(chips, tokens, chip_ref, *refs):
    pieces, out_ref = refs[:chips], refs[chips]
    for step in range(chips):
        source = rotated(chip_ref[0], chips - step, chips)
        out_ref[rows_of(source, tokens), :] = pieces[step][...]


def turn_kernel(blocks, own_ref, other_ref, pair_ref, turned_ref):
    for side, source in enumerate((own_ref, other_ref)):
        pair_ref[side * blocks * BLOCK : (side + 1) * blocks * BLOCK] = source[...]
        for block in range(blocks):
            turned_ref[side * blocks + block] = jnp.transpose(
                source[block * BLOCK : (block + 1) * BLOCK, :HD]
            )


def attention_kernel(chips, tokens, scale, chip_ref, table_ref, count_ref, order_ref, *refs):
    pair_ref, turned_ref, pieces = refs[0], refs[1], refs[2 : 2 + chips]
    dq_ref, own_out, other_out, ask_buf, give_buf, total = refs[2 + chips :]
    blocks = chips * tokens // BLOCK
    half = blocks * BLOCK
    per_device = tokens // BLOCK
    zero = jnp.zeros((BLOCK, HD), jnp.bfloat16)
    for step in range(chips):
        source = rotated(chip_ref[0], chips - step, chips)
        for place in range(per_device):
            piece = pieces[step][place * BLOCK : (place + 1) * BLOCK, :]
            query, grad = piece[:, :HD], piece[:, HD:]
            block = source * per_device + place
            ask_buf[block, :BLOCK, :HD] = query
            ask_buf[block, :BLOCK, HD:] = zero
            ask_buf[block, BLOCK:, :HD] = zero
            ask_buf[block, BLOCK:, HD:] = grad
            give_buf[block, :BLOCK, :HD] = grad
            give_buf[block, :BLOCK, HD:] = zero
            give_buf[block, BLOCK:, :HD] = zero
            give_buf[block, BLOCK:, HD:] = query
    total[...] = jnp.zeros_like(total)

    def attend(block, count, width):
        index = [table_ref[block * NBR + slot] for slot in range(width)]
        slots = [rows_of(which, BLOCK) for which in index]
        pairs = jnp.concatenate([pair_ref[slot, :] for slot in slots], axis=0)
        both = lax.dot_general(pairs, ask_buf[block], CONTRACT, preferred_element_type=jnp.float32)
        scores, prob_grad = both[:, :BLOCK], both[:, BLOCK:]
        rest = (width - 1) * BLOCK
        last = jnp.where(count == width, scores[rest:], -jnp.inf)
        scores = jnp.concatenate([scores[:rest], last], axis=0) if rest else last
        peak = jnp.max(scores, axis=0, keepdims=True)
        weights = jnp.exp2((scores - peak) * (scale * math.log2(math.e)))
        probs = weights * (1.0 / jnp.sum(weights, axis=0, keepdims=True))
        half_probs = probs.astype(jnp.bfloat16)
        delta = jnp.sum(half_probs.astype(jnp.float32) * prob_grad, axis=0, keepdims=True)
        dscore = (probs * (prob_grad - delta)).astype(jnp.bfloat16)
        turned = jnp.concatenate([turned_ref[which] for which in index], axis=1)
        dq = jnp.dot(turned, dscore, preferred_element_type=jnp.float32)
        given = jnp.dot(
            jnp.concatenate([half_probs, dscore], axis=1),
            give_buf[block],
            preferred_element_type=jnp.float32,
        )
        dq_ref[rows_of(block, BLOCK), :] = jnp.transpose(dq * scale).astype(jnp.bfloat16)
        return slots, given

    def add(slots, given):
        for place, slot in enumerate(slots):
            total[slot, :] += given[place * BLOCK : (place + 1) * BLOCK]

    def two_blocks(pair, carry):
        block, mate = order_ref[2 * pair], order_ref[2 * pair + 1]
        count, other = count_ref[block], count_ref[mate]

        def work(width):
            first = attend(block, count, width)
            second = attend(mate, other, width)
            add(*first)
            add(*second)

        same = (count + 1) // 2 == (other + 1) // 2

        def alone(which, many):
            for width in WIDTHS:
                @pl.when((many > width - 2) & (many <= width))
                def _():
                    add(*attend(which, many, width))

        for width in WIDTHS:
            pl.when(same & (count > width - 2) & (count <= width))(functools.partial(work, width))

        @pl.when(jnp.logical_not(same))
        def _():
            alone(block, count)
            alone(mate, other)

        return carry

    lax.fori_loop(0, blocks // 2, two_blocks, 0)
    for part, out in ((slice(0, half), own_out), (slice(half, None), other_out)):
        out[:, :HD] = (total[part, HD:] * scale).astype(out.dtype)
        out[:, HD:] = total[part, :HD].astype(out.dtype)


def combine_kernel(chips, tokens, chip_ref, dq_ref, own_ref, other_ref, *outs):
    for step in range(chips):
        rows = rows_of(rotated(chip_ref[0], chips - step, chips), tokens)
        outs[step][:, :HD] = dq_ref[rows, :]
        outs[step][:, HD:] = (own_ref[rows, :] + other_ref[rows, :].astype(jnp.float32)).astype(
            jnp.bfloat16
        )


def project_kernel(chips, steps, chip_ref, *refs):
    pieces, weights = refs[: len(steps)], refs[len(steps) : len(steps) + 3]
    before, (out_ref, rows_buf, weight_buf) = refs[len(steps) + 3 : -3], refs[-3:]
    total = before[0][...] if before else None
    for place in range(3):
        for at, step in enumerate(steps):
            head = rotated(chip_ref[0], step, chips)
            rows_buf[place, :, at * HD : (at + 1) * HD] = pieces[at][
                :, place * HD : (place + 1) * HD
            ]
            weight_buf[place, :, at * HD : (at + 1) * HD] = weights[place][:, columns(head)]
        part = lax.dot_general(
            rows_buf[place], weight_buf[place], CONTRACT, preferred_element_type=jnp.float32
        )
        total = part if total is None else total + part
    out_ref[...] = total.astype(out_ref.dtype)


def head_per_chip(
    out_grad, query_act, key_act, value_act, out_weight, weights, neighbours, block_counts
):
    my_index = lax.axis_index("blk")
    chips = lax.axis_size("blk") // CORES
    tokens, features = query_act.shape
    scale = 1.0 / math.sqrt(HD)
    chip = (my_index // CORES).astype(jnp.int32).reshape(1)
    core = my_index % CORES
    per_device = tokens // BLOCK
    blocks = chips * per_device
    half = chips * tokens
    bf16 = functools.partial(jax.ShapeDtypeStruct, dtype=jnp.bfloat16)
    f32 = functools.partial(jax.ShapeDtypeStruct, dtype=jnp.float32)
    buf16 = functools.partial(pltpu.VMEM, dtype=jnp.bfloat16)
    buf32 = functools.partial(pltpu.VMEM, dtype=jnp.float32)

    def call(kernel, outs, scratch, scalars, *arrays, spec=VMEM):
        return pl.pallas_call(
            kernel,
            out_shape=outs,
            in_specs=[SMEM] * len(scalars) + [spec] * len(arrays),
            out_specs=jax.tree.map(lambda _: VMEM, outs),
            scratch_shapes=scratch,
            compiler_params=LIMIT,
        )(*scalars, *arrays)

    def by_chips(shard, step):
        pairs = [
            (CORES * c + k, CORES * ((c + step) % chips) + k)
            for c in range(chips)
            for k in range(CORES)
        ]
        return lax.ppermute(shard, "blk", pairs)

    def out_to(shards):
        return [shards[0]] + [by_chips(shards[step], step) for step in range(1, chips)]

    def across_cores(shard):
        return lax.ppermute(shard, "blk", [(i, i ^ 1) for i in range(chips * CORES)])

    own = neighbours.reshape(chips, CORES, per_device, NBR)
    own = lax.dynamic_index_in_dim(own, core, 1, keepdims=False)
    counts = block_counts.reshape(chips, CORES, per_device)
    counts = lax.dynamic_index_in_dim(counts, core, 1, keepdims=False).reshape(-1)
    holder = own // per_device
    table = (
        jnp.where(holder % CORES == core, 0, blocks)
        + (holder // CORES) * per_device
        + own % per_device
    ).reshape(-1)
    ids = jnp.arange(blocks, dtype=jnp.int32)
    rank_key = counts * blocks + ids
    rank = jnp.sum((rank_key[None, :] > rank_key[:, None]).astype(jnp.int32), axis=1)
    order = jnp.sum(jnp.where(rank[:, None] == ids[None, :], ids[:, None], 0), axis=0)

    args = functools.partial
    piece = [bf16((tokens, 2 * HD))] * chips
    pairs = call(
        args(pack_kernel, chips), piece, [pltpu.SemaphoreType.DMA((2 * chips,))],
        (chip,), key_act, value_act, spec=ANY,
    )
    pairs = out_to(pairs)
    asks = call(args(grad_kernel, chips), piece, [], (chip,), out_grad, out_weight, query_act)
    pairs, _ = lax.optimization_barrier((pairs, asks))
    asks = out_to(asks)
    own_pairs = call(
        args(assemble_kernel, chips, tokens), bf16((half, 2 * HD)), [], (chip,), *pairs
    )
    other_pairs = across_cores(own_pairs)
    both_pairs, turned = call(
        args(turn_kernel, blocks), [bf16((2 * half, 2 * HD)), bf16((2 * blocks, HD, BLOCK))], [],
        (), own_pairs, other_pairs,
    )
    dq, own_part, sent_part = call(
        args(attention_kernel, chips, tokens, scale),
        [bf16((half, HD)), f32((half, 2 * HD)), bf16((half, 2 * HD))],
        [
            buf16((blocks, 2 * BLOCK, 2 * HD)),
            buf16((blocks, 2 * BLOCK, 2 * HD)),
            buf32((2 * half, 2 * HD)),
        ],
        (chip, table, counts, order), both_pairs, turned, *asks,
    )
    came_part = across_cores(sent_part)
    back = call(
        args(combine_kernel, chips, tokens), [bf16((tokens, 3 * HD))] * chips, [],
        (chip,), dq, own_part, came_part,
    )
    back = [back[0]] + [by_chips(back[step], chips - step) for step in range(1, chips)]
    near = [min(step, chips - step) * 4 <= chips for step in range(chips)]
    early = [step for step in range(chips) if near[step]]
    late = [step for step in range(chips) if not near[step]]

    def project(steps, outs, *before):
        return call(
            args(project_kernel, chips, steps), outs,
            [buf16((3, tokens, len(steps) * HD)), buf16((3, features, len(steps) * HD))],
            (chip,), *(back[step] for step in steps), *weights, *before,
        )

    return project(late, bf16((tokens, features)), project(early, f32((tokens, features))))


def by_window(
    out_grad, query_act, key_act, value_act, out_weight, weights, neighbours, block_counts
):
    cycle_size = lax.axis_size("blk")
    my_index = lax.axis_index("blk")
    tokens, features = query_act.shape
    head_count = features // HD
    query_blocks = tokens // BLOCK
    reach_dev = (WIN + query_blocks - 1) // query_blocks
    total_blocks = query_blocks * cycle_size
    window_blocks = (2 * reach_dev + 1) * query_blocks
    scale = 1.0 / math.sqrt(HD)
    attn_grad = lax.dot_general(
        lax.all_gather(out_grad, "sp", axis=0, tiled=True),
        out_weight,
        CONTRACT,
        preferred_element_type=jnp.float32,
    ).astype(jnp.bfloat16)
    key_value = jnp.stack((key_act, value_act))
    gathered = jnp.concatenate(
        [
            key_value if offset == 0 else passed_along(key_value, "blk", -offset)
            for offset in range(-reach_dev, reach_dev + 1)
        ],
        axis=1,
    ).reshape(2, window_blocks, BLOCK, features)
    anchor = (my_index - reach_dev) * query_blocks
    own_lists = lax.dynamic_slice_in_dim(neighbours, my_index * query_blocks, query_blocks, 0)
    own_counts = lax.dynamic_slice_in_dim(block_counts, my_index * query_blocks, query_blocks, 0)
    window_index = ((own_lists - anchor) % total_blocks).reshape(-1)
    picked = jnp.concatenate(
        [
            lax.dynamic_slice_in_dim(gathered, window_index[n], 1, 1)
            for n in range(query_blocks * NBR)
        ],
        axis=1,
    ).reshape(2, query_blocks, NBR, BLOCK, head_count, HD)
    query_heads = query_act.reshape(query_blocks, BLOCK, head_count, HD)
    grad_heads = attn_grad.reshape(query_blocks, BLOCK, head_count, HD)
    einsum = functools.partial(jnp.einsum, preferred_element_type=jnp.float32)
    scores = scale * einsum("bihd,bsjhd->bhisj", query_heads, picked[0])
    live_slots = jnp.arange(NBR)[None, :] < own_counts[:, None]
    scores = jnp.where(live_slots[:, None, None, :, None], scores, -jnp.inf)
    row_peak = jnp.max(scores, axis=(3, 4), keepdims=True)
    log_total = row_peak + jnp.log(jnp.sum(jnp.exp(scores - row_peak), axis=(3, 4), keepdims=True))
    soft_probs = jnp.exp(scores - log_total)
    probs_half = soft_probs.astype(jnp.bfloat16)
    outputs = einsum("bhisj,bsjhd->bihd", probs_half, picked[1])
    row_delta = jnp.transpose(jnp.sum(grad_heads.astype(jnp.float32) * outputs, axis=3), (0, 2, 1))
    prob_grad = einsum("bihd,bsjhd->bhisj", grad_heads, picked[1])
    dscore_half = (soft_probs * (prob_grad - row_delta[:, :, :, None, None])).astype(jnp.bfloat16)
    query_grad = scale * einsum("bhisj,bsjhd->bihd", dscore_half, picked[0])
    query_grad = query_grad.astype(jnp.bfloat16).reshape(tokens, features)
    key_slots = scale * einsum("bhisj,bihd->bsjhd", dscore_half, query_heads)
    value_slots = einsum("bhisj,bihd->bsjhd", probs_half, grad_heads)
    slot_grads = jnp.stack((key_slots, value_slots)).reshape(
        2, query_blocks * NBR, BLOCK * features
    )
    selector = (jnp.arange(window_blocks)[:, None] == window_index.reshape(1, -1)).astype(
        jnp.float32
    )
    window_grads = jnp.einsum("wn,gnc->gwc", selector, slot_grads, precision=lax.Precision.HIGHEST)
    summed = 0.0
    for offset in range(-reach_dev, reach_dev + 1):
        first = (offset + reach_dev) * query_blocks
        portion = window_grads[:, first : first + query_blocks]
        summed = summed + (portion if offset == 0 else passed_along(portion, "blk", offset))
    own_grads = summed.reshape(2, tokens, features).astype(jnp.bfloat16)
    summed_rows = 0.0
    for grad, weight in zip((query_grad, own_grads[0], own_grads[1]), weights, strict=True):
        summed_rows = summed_rows + lax.dot_general(
            grad, weight, CONTRACT, preferred_element_type=jnp.float32
        )
    input_grad = lax.psum_scatter(summed_rows, "sp", scatter_dimension=0, tiled=True)
    return input_grad.astype(jnp.bfloat16)


def body(
    out_grad,
    query_act,
    key_act,
    value_act,
    out_weight,
    query_weight,
    key_weight,
    value_weight,
    neighbours,
    block_counts,
):
    heads = query_act.shape[1] // HD
    one_head = lax.axis_size("sp") == 1 and lax.axis_size("blk") == heads * CORES
    return (head_per_chip if one_head else by_window)(
        out_grad,
        query_act,
        key_act,
        value_act,
        out_weight,
        (query_weight, key_weight, value_weight),
        neighbours,
        block_counts,
    )


def solution(mesh):
    return jax.shard_map(
        body,
        mesh=mesh,
        in_specs=(
            P(("groups", "blk", "sp"), None),
            P(("groups", "blk"), "sp"),
            P(("groups", "blk"), "sp"),
            P(("groups", "blk"), "sp"),
            P("sp", None),
            P(None, "sp"),
            P(None, "sp"),
            P(None, "sp"),
            P("groups", None),
            P("groups"),
        ),
        out_specs=P(("groups", "blk", "sp"), None),
        check_vma=False,
    )
```

time: 124 us -> 121 us (0.976)
  waiting for transfers between devices: 15.7 us -> 29 us
  starting transfers between devices: 67.8 us -> 57.2 us
  Pallas kernels: 30.6 us -> 24.5 us
    ppermute x28 -> x21, waiting for transfers between devices: 15.7 us -> 26.4 us  [by_chips(): return lax.ppermute(shard, 'blk', pairs)]
    ppermute x28 -> x21, starting transfers between devices: 67.2 us -> 57.1 us  [by_chips(): return lax.ppermute(shard, 'blk', pairs)]
    pallas_call x11 -> x8, Pallas kernels: 30.6 us -> 24.5 us  [call(): pl.pallas_call(kernel, out_shape=outs, in_specs=[SMEM] * len(scalars) + [...]
    ppermute x4 -> x2, waiting for transfers between devices: 0.01 us -> 2.65 us  [across_cores(): lax.ppermute(shard, 'blk', [(i, i ^ 1) for i in range(chips * CORES)])]
  transfers between devices with their start and end apart: 32 -> 23, of which waited for: 9 -> 10; matrix products, arithmetic and copies ran while one was open for 1% -> 2% of each run, Pallas kernels for 23% -> 5%
where the time goes in v4:
time: 121 us; the launch traced here: 120 us
  starting transfers between devices  57.2 us (47%)
  waiting for transfers between devices  29 us (24%)
  Pallas kernels  24.5 us (20%)
  local copies, waits for them, and re-layouts  8.75 us (7%)
    ppermute x21, starting transfers between devices, by_chips(): return lax.ppermute(shard, 'blk', pairs)  57.1 us
    ppermute x21, waiting for transfers between devices, by_chips(): return lax.ppermute(shard, 'blk', pairs)  26.4 us
    pallas_call x8, Pallas kernels, call(): pl.pallas_call(kernel, out_shape=outs, in_specs=[SMEM] * len(scalars) + [...  24.5 us
    unnamed x21, local copies, waits for them, and re-layouts  7.78 us
    ppermute x2, waiting for transfers between devices, across_cores(): lax.ppermute(shard, 'blk', [(i, i ^ 1) for i in range(chips * CORES)])  2.65 us
  transfers between devices with their start and end apart: 23, of which 10 were waited for; matrix products, arithmetic and copies ran while one was open for 2% of the time, Pallas kernels for 5%

profile of v4, /device:TPU:0, one launch (start us, length us, event | category | flops | bytes accessed | tf_op | source)
XLA Modules:
  0.0 119.9 jit_solution(4635588875130038055)
XLA Ops:
  0.0 1.0 copy-done.4
  1.0 1.0 copy-done.5
  2.1 0.5 shard_map.100
  2.6 3.0 %collective-permute-start = (bf16[256,256]{1,0:T(8,128)(2,1)S(1)}, bf16[256,256]{1,0:T(8,128)(2,1)S(1)}, u32[]{:S(2)}, u32[]{:S(2)}) collective-permute-start(bf16[256,256]{1,0:T(8,128)(2,1)S(1)} %get-tuple-element.43), channel_id=1, source_target_pairs={{0,2},{1,3},{2,4},{3,5},{4,6},{5,7},{6,8},{7,9},{8,10},{9,11},{10,... | collective-permute-start | bytes 393224 | tf_op jit(solution)/shard_map/ppermute | solution.py:232
  5.5 1.6 %collective-permute-start.1 = (bf16[256,256]{1,0:T(8,128)(2,1)S(1)}, bf16[256,256]{1,0:T(8,128)(2,1)S(1)}, u32[]{:S(2)}, u32[]{:S(2)}) collective-permute-start(bf16[256,256]{1,0:T(8,128)(2,1)S(1)} %get-tuple-element.44), channel_id=1, source_target_pairs={{0,4},{1,5},{2,6},{3,7},{4,8},{5,9},{6,10},{7,11},{8,12},{9,13},{1... | collective-permute-start | bytes 393224 | tf_op jit(solution)/shard_map/ppermute | solution.py:232
  7.1 2.6 %collective-permute-start.2 = (bf16[256,256]{1,0:T(8,128)(2,1)S(1)}, bf16[256,256]{1,0:T(8,128)(2,1)S(1)}, u32[]{:S(2)}, u32[]{:S(2)}) collective-permute-start(bf16[256,256]{1,0:T(8,128)(2,1)S(1)} %get-tuple-element.45), channel_id=1, source_target_pairs={{0,6},{1,7},{2,8},{3,9},{4,10},{5,11},{6,12},{7,13},{8,14},{9,15},... | collective-permute-start | bytes 393224 | tf_op jit(solution)/shard_map/ppermute | solution.py:232
  9.7 1.2 %collective-permute-start.3 = (bf16[256,256]{1,0:T(8,128)(2,1)S(1)}, bf16[256,256]{1,0:T(8,128)(2,1)S(1)}, u32[]{:S(2)}, u32[]{:S(2)}) collective-permute-start(bf16[256,256]{1,0:T(8,128)(2,1)S(1)} %get-tuple-element.46), channel_id=1, source_target_pairs={{0,8},{1,9},{2,10},{3,11},{4,12},{5,13},{6,14},{7,15},{8,0},{9,1},... | collective-permute-start | bytes 393224 | tf_op jit(solution)/shard_map/ppermute | solution.py:232
  10.9 2.6 %collective-permute-start.4 = (bf16[256,256]{1,0:T(8,128)(2,1)S(1)}, bf16[256,256]{1,0:T(8,128)(2,1)S(1)}, u32[]{:S(2)}, u32[]{:S(2)}) collective-permute-start(bf16[256,256]{1,0:T(8,128)(2,1)S(1)} %get-tuple-element.47), channel_id=1, source_target_pairs={{0,10},{1,11},{2,12},{3,13},{4,14},{5,15},{6,0},{7,1},{8,2},{9,3},... | collective-permute-start | bytes 393224 | tf_op jit(solution)/shard_map/ppermute | solution.py:232
  13.5 1.4 %collective-permute-start.5 = (bf16[256,256]{1,0:T(8,128)(2,1)S(1)}, bf16[256,256]{1,0:T(8,128)(2,1)S(1)}, u32[]{:S(2)}, u32[]{:S(2)}) collective-permute-start(bf16[256,256]{1,0:T(8,128)(2,1)S(1)} %get-tuple-element.48), channel_id=1, source_target_pairs={{0,12},{1,13},{2,14},{3,15},{4,0},{5,1},{6,2},{7,3},{8,4},{9,5},{1... | collective-permute-start | bytes 393224 | tf_op jit(solution)/shard_map/ppermute | solution.py:232
  14.9 2.0 %collective-permute-start.6 = (bf16[256,256]{1,0:T(8,128)(2,1)S(1)}, bf16[256,256]{1,0:T(8,128)(2,1)S(1)}, u32[]{:S(2)}, u32[]{:S(2)}) collective-permute-start(bf16[256,256]{1,0:T(8,128)(2,1)S(1)} %get-tuple-element.49), channel_id=1, source_target_pairs={{0,14},{1,15},{2,0},{3,1},{4,2},{5,3},{6,4},{7,5},{8,6},{9,7},{10,... | collective-permute-start | bytes 393224 | tf_op jit(solution)/shard_map/ppermute | solution.py:232
  17.0 1.6 %copy-done.2 = bf16[1024,1024]{1,0:T(8,128)(2,1)S(1)} copy-done((bf16[1024,1024]{1,0:T(8,128)(2,1)S(1)}, bf16[1024,1024]{1,0:T(8,128)(2,1)}, u32[]{:S(2)}) %copy-start.2) | copy-done | bytes 2097176
  18.6 1.0 copy-done.6
  19.6 1.0 copy-done.7
  20.7 1.8 %shard_map.101 = (bf16[256,256]{1,0:T(8,128)(2,1)S(1)}, bf16[256,256]{1,0:T(8,128)(2,1)}, bf16[256,256]{1,0:T(8,128)(2,1)S(1)}, bf16[256,256]{1,0:T(8,128)(2,1)S...) custom-call(s32[1]{0:T(128)} %bitcast.chip_ref, ...), custom_call_target="tpu_custom_call" | custom-call | tf_op jit(solution)/shard_map/pallas_call | solution.py:217
  22.5 1.0 collective-permute-done.2.refs_3_
  23.5 0.3 collective-permute-done.3.refs_4_
  24.0 4.3 %collective-permute-start.8 = (bf16[256,256]{1,0:T(8,128)(2,1)}, bf16[256,256]{1,0:T(8,128)(2,1)S(1)}, u32[]{:S(2)}, u32[]{:S(2)}) collective-permute-start(bf16[256,256]{1,0:T(8,128)(2,1)} %get-tuple-element.51), channel_id=1, source_target_pairs={{0,2},{1,3},{2,4},{3,5},{4,6},{5,7},{6,8},{7,9},{8,10},{9,11},{10,... | collective-permute-start | bytes 393224 | tf_op jit(solution)/shard_map/ppermute | solution.py:232
  28.3 6.0 %collective-permute-start.9 = (bf16[256,256]{1,0:T(8,128)(2,1)S(1)}, bf16[256,256]{1,0:T(8,128)(2,1)S(1)}, u32[]{:S(2)}, u32[]{:S(2)}) collective-permute-start(bf16[256,256]{1,0:T(8,128)(2,1)S(1)} %get-tuple-element.52), channel_id=1, source_target_pairs={{0,4},{1,5},{2,6},{3,7},{4,8},{5,9},{6,10},{7,11},{8,12},{9,13},{1... | collective-permute-start | bytes 393224 | tf_op jit(solution)/shard_map/ppermute | solution.py:232
  34.3 2.9 %collective-permute-start.10 = (bf16[256,256]{1,0:T(8,128)(2,1)S(1)}, bf16[256,256]{1,0:T(8,128)(2,1)S(1)}, u32[]{:S(2)}, u32[]{:S(2)}) collective-permute-start(bf16[256,256]{1,0:T(8,128)(2,1)S(1)} %get-tuple-element.53), channel_id=1, source_target_pairs={{0,6},{1,7},{2,8},{3,9},{4,10},{5,11},{6,12},{7,13},{8,14},{9,15},... | collective-permute-start | bytes 393224 | tf_op jit(solution)/shard_map/ppermute | solution.py:232
  37.2 0.1 reshape.36
  37.3 0.1 reshape.37.count_ref
  37.4 0.7 copy.13
  38.1 0.7 constant_dynamic-slice_fusion
  38.8 0.1 squeeze.6
  38.9 0.5 collective-permute-done.8.refs_3_
  39.4 2.1 %collective-permute-start.12 = (bf16[256,256]{1,0:T(8,128)(2,1)S(1)}, bf16[256,256]{1,0:T(8,128)(2,1)S(1)}, u32[]{:S(2)}, u32[]{:S(2)}) collective-permute-start(bf16[256,256]{1,0:T(8,128)(2,1)S(1)} %get-tuple-element.55), channel_id=1, source_target_pairs={{0,10},{1,11},{2,12},{3,13},{4,14},{5,15},{6,0},{7,1},{8,2},{9,3},... | collective-permute-start | bytes 393224 | tf_op jit(solution)/shard_map/ppermute | solution.py:232
  41.5 1.6 %collective-permute-start.13 = (bf16[256,256]{1,0:T(8,128)(2,1)S(1)}, bf16[256,256]{1,0:T(8,128)(2,1)S(1)}, u32[]{:S(2)}, u32[]{:S(2)}) collective-permute-start(bf16[256,256]{1,0:T(8,128)(2,1)S(1)} %get-tuple-element.56), channel_id=1, source_target_pairs={{0,12},{1,13},{2,14},{3,15},{4,0},{5,1},{6,2},{7,3},{8,4},{9,5},{1... | collective-permute-start | bytes 393224 | tf_op jit(solution)/shard_map/ppermute | solution.py:232
  43.1 13.0 %collective-permute-start.14 = (bf16[256,256]{1,0:T(8,128)(2,1)S(1)}, bf16[256,256]{1,0:T(8,128)(2,1)S(1)}, u32[]{:S(2)}, u32[]{:S(2)}) collective-permute-start(bf16[256,256]{1,0:T(8,128)(2,1)S(1)} %get-tuple-element.57), channel_id=1, source_target_pairs={{0,14},{1,15},{2,0},{3,1},{4,2},{5,3},{6,4},{7,5},{8,6},{9,7},{10,... | collective-permute-start | bytes 393224 | tf_op jit(solution)/shard_map/ppermute | solution.py:232
  56.2 0.2 convert_reduce_fusion
  56.3 0.1 select_reduce_fusion.order_ref
  56.4 0.4 shard_map.103
  56.9 1.3 %copy-done.3 = bf16[4096,256]{1,0:T(8,128)(2,1)} copy-done((bf16[4096,256]{1,0:T(8,128)(2,1)}, bf16[4096,256]{1,0:T(8,128)(2,1)S(1)}, u32[]{:S(2)}) %copy-start.3) | copy-done | bytes 2097176
  58.2 0.5 collective-permute-done.14.refs_9_
  58.7 13.8 %shard_map.104 = (bf16[2048,128]{1,0:T(8,128)(2,1)S(1)}, f32[2048,256]{1,0:T(8,128)S(1)}, bf16[2048,256]{1,0:T(8,128)(2,1)S(1)}) custom-call(s32[1]{0:T(128)} %bitcast.chip_ref, s32[128]{0:T(128)S(1)} %fusion.table_ref, s32[16]{0:T(128)S(1)} %reshape.37.count_ref, s32[16]{0:T(128)S(1)} %select_reduce_fusion.order_ref, bf16[4096,256]{1,0:T(8,128)(2,1)} %copy-done.3, ...), custom_call_target="tpu_custom_call" | custom-call | tf_op jit(solution)/shard_map/pallas_call | solution.py:217
  72.6 2.6 %collective-permute-done.15.other_ref = bf16[2048,256]{1,0:T(8,128)(2,1)S(1)} collective-permute-done((bf16[2048,256]{1,0:T(8,128)(2,1)S(1)}, bf16[2048,256]{1,0:T(8,128)(2,1)S(1)}, u32[]{:S(2)}, u32[]{:S(2)}) %collective-permute-start.15) | collective-permute-done | bytes 1048608 | tf_op jit(solution)/shard_map/ppermute | solution.py:238
  75.3 0.2 shard_map.105
  75.5 5.2 %collective-permute-start.19 = (bf16[256,384]{1,0:T(8,128)(2,1)S(1)}, bf16[256,384]{1,0:T(8,128)(2,1)S(1)}, u32[]{:S(2)}, u32[]{:S(2)}) collective-permute-start(bf16[256,384]{1,0:T(8,128)(2,1)S(1)} %get-tuple-element.75), channel_id=1, source_target_pairs={{0,14},{1,15},{2,0},{3,1},{4,2},{5,3},{6,4},{7,5},{8,6},{9,7},{10,... | collective-permute-start | bytes 589832 | tf_op jit(solution)/shard_map/ppermute | solution.py:232
  80.7 2.0 %collective-permute-start.21 = (bf16[256,384]{1,0:T(8,128)(2,1)S(1)}, bf16[256,384]{1,0:T(8,128)(2,1)S(1)}, u32[]{:S(2)}, u32[]{:S(2)}) collective-permute-start(bf16[256,384]{1,0:T(8,128)(2,1)S(1)} %get-tuple-element.77), channel_id=1, source_target_pairs={{0,4},{1,5},{2,6},{3,7},{4,8},{5,9},{6,10},{7,11},{8,12},{9,13},{1... | collective-permute-start | bytes 589832 | tf_op jit(solution)/shard_map/ppermute | solution.py:232
  82.7 3.3 %collective-permute-start.16 = (bf16[256,384]{1,0:T(8,128)(2,1)S(1)}, bf16[256,384]{1,0:T(8,128)(2,1)S(1)}, u32[]{:S(2)}, u32[]{:S(2)}) collective-permute-start(bf16[256,384]{1,0:T(8,128)(2,1)S(1)} %get-tuple-element.71), channel_id=1, source_target_pairs={{0,10},{1,11},{2,12},{3,13},{4,14},{5,15},{6,0},{7,1},{8,2},{9,3},... | collective-permute-start | bytes 589832 | tf_op jit(solution)/shard_map/ppermute | solution.py:232
  86.0 0.6 collective-permute-start.17
  86.5 3.7 %collective-permute-done.20.refs_2_ = bf16[256,384]{1,0:T(8,128)(2,1)S(1)} collective-permute-done((bf16[256,384]{1,0:T(8,128)(2,1)S(1)}, bf16[256,384]{1,0:T(8,128)(2,1)S(1)}, u32[]{:S(2)}, u32[]{:S(2)}) %collective-permute-start.20) | collective-permute-done | bytes 196640 | tf_op jit(solution)/shard_map/ppermute | solution.py:232
  90.2 1.6 %collective-permute-start.18 = (bf16[256,384]{1,0:T(8,128)(2,1)S(1)}, bf16[256,384]{1,0:T(8,128)(2,1)S(1)}, u32[]{:S(2)}, u32[]{:S(2)}) collective-permute-start(bf16[256,384]{1,0:T(8,128)(2,1)S(1)} %get-tuple-element.73), channel_id=1, source_target_pairs={{0,6},{1,7},{2,8},{3,9},{4,10},{5,11},{6,12},{7,13},{8,14},{9,15},... | collective-permute-start | bytes 589832 | tf_op jit(solution)/shard_map/ppermute | solution.py:232
  91.8 2.6 %collective-permute-done.21.refs_3_ = bf16[256,384]{1,0:T(8,128)(2,1)S(1)} collective-permute-done((bf16[256,384]{1,0:T(8,128)(2,1)S(1)}, bf16[256,384]{1,0:T(8,128)(2,1)S(1)}, u32[]{:S(2)}, u32[]{:S(2)}) %collective-permute-start.21) | collective-permute-done | bytes 196640 | tf_op jit(solution)/shard_map/ppermute | solution.py:232
  94.4 0.5 collective-permute-done.22.refs_4_
  94.9 4.1 %shard_map.106.refs_6_ = f32[256,1024]{1,0:T(8,128)S(1)} custom-call(s32[1]{0:T(128)} %bitcast.chip_ref, bf16[256,384]{1,0:T(8,128)(2,1)S(1)} %get-tuple-element.74.refs_0_, bf16[256,384]{1,0:T(8,128)(2,1)S(1)} %collective-permute-done.19.refs_1_, bf16[256,384]{1,0:T(8,128)(2,1)S(1)} %collective-permute-done.20.refs_2_, ...), custom_call_target="tpu_custom_call" | custom-call | tf_op jit(solution)/shard_map/pallas_call | solution.py:217
  99.0 14.4 %collective-permute-done.17.refs_1_ = bf16[256,384]{1,0:T(8,128)(2,1)S(1)} collective-permute-done((bf16[256,384]{1,0:T(8,128)(2,1)S(1)}, bf16[256,384]{1,0:T(8,128)(2,1)S(1)}, u32[]{:S(2)}, u32[]{:S(2)}) %collective-permute-start.17) | collective-permute-done | bytes 196640 | tf_op jit(solution)/shard_map/ppermute | solution.py:232
  113.4 2.9 %collective-permute-done.18.refs_2_ = bf16[256,384]{1,0:T(8,128)(2,1)S(1)} collective-permute-done((bf16[256,384]{1,0:T(8,128)(2,1)S(1)}, bf16[256,384]{1,0:T(8,128)(2,1)S(1)}, u32[]{:S(2)}, u32[]{:S(2)}) %collective-permute-start.18) | collective-permute-done | bytes 196640 | tf_op jit(solution)/shard_map/ppermute | solution.py:232
  116.4 3.6 %shard_map.107 = bf16[256,1024]{1,0:T(8,128)(2,1)} custom-call(s32[1]{0:T(128)} %bitcast.chip_ref, bf16[256,384]{1,0:T(8,128)(2,1)S(1)} %collective-permute-done.16.refs_0_, bf16[256,384]{1,0:T(8,128)(2,1)S(1)} %collective-permute-done.17.refs_1_, bf16[256,384]{1,0:T(8,128)(2,1)S(1)} %collective-permute-done.18.refs_2_, bf16[1024,1024]{1,0:T(8,128)(2,1)S(1)} %copy-done, ...), custom_call_target="tpu_custom_call" | custom-call | tf_op jit(solution)/shard_map/pallas_call | solution.py:217
  (36 shorter events, 0.3 us)
Async XLA Ops:
  0.0 1.0 copy-start.4
  1.0 1.0 copy-start.5
  2.6 11.0 %collective-permute-start = (bf16[256,256]{1,0:T(8,128)(2,1)S(1)}, bf16[256,256]{1,0:T(8,128)(2,1)S(1)}, u32[]{:S(2)}, u32[]{:S(2)}) collective-permute-start(bf16[256,256]{1,0:T(8,128)(2,1)S(1)} %get-tuple-element.43), channel_id=1, source_target_pairs={{0,2},{1,3},{2,4},{3,5},{4,6},{5,7},{6,8},{7,9},{8,10},{9,11},{10,... | collective-permute-start | bytes 393224 | tf_op jit(solution)/shard_map/ppermute | solution.py:232
  5.5 9.4 %collective-permute-start.1 = (bf16[256,256]{1,0:T(8,128)(2,1)S(1)}, bf16[256,256]{1,0:T(8,128)(2,1)S(1)}, u32[]{:S(2)}, u32[]{:S(2)}) collective-permute-start(bf16[256,256]{1,0:T(8,128)(2,1)S(1)} %get-tuple-element.44), channel_id=1, source_target_pairs={{0,4},{1,5},{2,6},{3,7},{4,8},{5,9},{6,10},{7,11},{8,12},{9,13},{1... | collective-permute-start | bytes 393224 | tf_op jit(solution)/shard_map/ppermute | solution.py:232
  7.1 16.3 %collective-permute-start.2 = (bf16[256,256]{1,0:T(8,128)(2,1)S(1)}, bf16[256,256]{1,0:T(8,128)(2,1)S(1)}, u32[]{:S(2)}, u32[]{:S(2)}) collective-permute-start(bf16[256,256]{1,0:T(8,128)(2,1)S(1)} %get-tuple-element.45), channel_id=1, source_target_pairs={{0,6},{1,7},{2,8},{3,9},{4,10},{5,11},{6,12},{7,13},{8,14},{9,15},... | collective-permute-start | bytes 393224 | tf_op jit(solution)/shard_map/ppermute | solution.py:232
  9.7 14.1 %collective-permute-start.3 = (bf16[256,256]{1,0:T(8,128)(2,1)S(1)}, bf16[256,256]{1,0:T(8,128)(2,1)S(1)}, u32[]{:S(2)}, u32[]{:S(2)}) collective-permute-start(bf16[256,256]{1,0:T(8,128)(2,1)S(1)} %get-tuple-element.46), channel_id=1, source_target_pairs={{0,8},{1,9},{2,10},{3,11},{4,12},{5,13},{6,14},{7,15},{8,0},{9,1},... | collective-permute-start | bytes 393224 | tf_op jit(solution)/shard_map/ppermute | solution.py:232
  10.9 12.9 %collective-permute-start.4 = (bf16[256,256]{1,0:T(8,128)(2,1)S(1)}, bf16[256,256]{1,0:T(8,128)(2,1)S(1)}, u32[]{:S(2)}, u32[]{:S(2)}) collective-permute-start(bf16[256,256]{1,0:T(8,128)(2,1)S(1)} %get-tuple-element.47), channel_id=1, source_target_pairs={{0,10},{1,11},{2,12},{3,13},{4,14},{5,15},{6,0},{7,1},{8,2},{9,3},... | collective-permute-start | bytes 393224 | tf_op jit(solution)/shard_map/ppermute | solution.py:232
  13.5 10.3 %collective-permute-start.5 = (bf16[256,256]{1,0:T(8,128)(2,1)S(1)}, bf16[256,256]{1,0:T(8,128)(2,1)S(1)}, u32[]{:S(2)}, u32[]{:S(2)}) collective-permute-start(bf16[256,256]{1,0:T(8,128)(2,1)S(1)} %get-tuple-element.48), channel_id=1, source_target_pairs={{0,12},{1,13},{2,14},{3,15},{4,0},{5,1},{6,2},{7,3},{8,4},{9,5},{1... | collective-permute-start | bytes 393224 | tf_op jit(solution)/shard_map/ppermute | solution.py:232
  14.9 8.9 %collective-permute-start.6 = (bf16[256,256]{1,0:T(8,128)(2,1)S(1)}, bf16[256,256]{1,0:T(8,128)(2,1)S(1)}, u32[]{:S(2)}, u32[]{:S(2)}) collective-permute-start(bf16[256,256]{1,0:T(8,128)(2,1)S(1)} %get-tuple-element.49), channel_id=1, source_target_pairs={{0,14},{1,15},{2,0},{3,1},{4,2},{5,3},{6,4},{7,5},{8,6},{9,7},{10,... | collective-permute-start | bytes 393224 | tf_op jit(solution)/shard_map/ppermute | solution.py:232
  17.0 1.6 %copy-start.2 = (bf16[1024,1024]{1,0:T(8,128)(2,1)S(1)}, bf16[1024,1024]{1,0:T(8,128)(2,1)}, u32[]{:S(2)}) copy-start(bf16[1024,1024]{1,0:T(8,128)(2,1)} %weight_ref.1) | copy-start | bytes 6291460
  18.6 1.0 copy-start.6
  19.6 1.0 copy-start.7
  20.7 16.5 %copy-start.9 = (s32[32]{0:T(128)S(1)}, s32[32]{0:T(128)}, u32[]{:S(2)}) copy-start(s32[32]{0:T(128)} %param.19) | copy-start | bytes 388
  20.7 16.7 %copy-start.8 = (s32[32,8]{0,1:T(8,128)S(1)}, s32[32,8]{0,1:T(8,128)}, u32[]{:S(2)}) copy-start(s32[32,8]{0,1:T(8,128)} %param.18) | copy-start | bytes 3076
  23.9 19.3 %collective-permute-start.7 = (bf16[2048,256]{1,0:T(8,128)(2,1)S(1)}, bf16[2048,256]{1,0:T(8,128)(2,1)S(1)}, u32[]{:S(2)}, u32[]{:S(2)}) collective-permute-start(bf16[2048,256]{1,0:T(8,128)(2,1)S(1)} %shard_map.102.own_ref), channel_id=1, source_target_pairs={{0,1},{1,0},{2,3},{3,2},{4,5},{5,4},{6,7},{7,6},{8,9},{9,8},{10,11... | collective-permute-start | bytes 3145736 | tf_op jit(solution)/shard_map/ppermute | solution.py:238
  24.0 15.4 %collective-permute-start.8 = (bf16[256,256]{1,0:T(8,128)(2,1)}, bf16[256,256]{1,0:T(8,128)(2,1)S(1)}, u32[]{:S(2)}, u32[]{:S(2)}) collective-permute-start(bf16[256,256]{1,0:T(8,128)(2,1)} %get-tuple-element.51), channel_id=1, source_target_pairs={{0,2},{1,3},{2,4},{3,5},{4,6},{5,7},{6,8},{7,9},{8,10},{9,11},{10,... | collective-permute-start | bytes 393224 | tf_op jit(solution)/shard_map/ppermute | solution.py:232
  28.3 13.2 %collective-permute-start.9 = (bf16[256,256]{1,0:T(8,128)(2,1)S(1)}, bf16[256,256]{1,0:T(8,128)(2,1)S(1)}, u32[]{:S(2)}, u32[]{:S(2)}) collective-permute-start(bf16[256,256]{1,0:T(8,128)(2,1)S(1)} %get-tuple-element.52), channel_id=1, source_target_pairs={{0,4},{1,5},{2,6},{3,7},{4,8},{5,9},{6,10},{7,11},{8,12},{9,13},{1... | collective-permute-start | bytes 393224 | tf_op jit(solution)/shard_map/ppermute | solution.py:232
  34.3 23.9 %collective-permute-start.10 = (bf16[256,256]{1,0:T(8,128)(2,1)S(1)}, bf16[256,256]{1,0:T(8,128)(2,1)S(1)}, u32[]{:S(2)}, u32[]{:S(2)}) collective-permute-start(bf16[256,256]{1,0:T(8,128)(2,1)S(1)} %get-tuple-element.53), channel_id=1, source_target_pairs={{0,6},{1,7},{2,8},{3,9},{4,10},{5,11},{6,12},{7,13},{8,14},{9,15},... | collective-permute-start | bytes 393224 | tf_op jit(solution)/shard_map/ppermute | solution.py:232
  37.2 21.0 %collective-permute-start.11 = (bf16[256,256]{1,0:T(8,128)(2,1)S(1)}, bf16[256,256]{1,0:T(8,128)(2,1)S(1)}, u32[]{:S(2)}, u32[]{:S(2)}) collective-permute-start(bf16[256,256]{1,0:T(8,128)(2,1)S(1)} %get-tuple-element.54), channel_id=1, source_target_pairs={{0,8},{1,9},{2,10},{3,11},{4,12},{5,13},{6,14},{7,15},{8,0},{9,1},... | collective-permute-start | bytes 393224 | tf_op jit(solution)/shard_map/ppermute | solution.py:232
  39.4 18.8 %collective-permute-start.12 = (bf16[256,256]{1,0:T(8,128)(2,1)S(1)}, bf16[256,256]{1,0:T(8,128)(2,1)S(1)}, u32[]{:S(2)}, u32[]{:S(2)}) collective-permute-start(bf16[256,256]{1,0:T(8,128)(2,1)S(1)} %get-tuple-element.55), channel_id=1, source_target_pairs={{0,10},{1,11},{2,12},{3,13},{4,14},{5,15},{6,0},{7,1},{8,2},{9,3},... | collective-permute-start | bytes 393224 | tf_op jit(solution)/shard_map/ppermute | solution.py:232
  41.5 16.7 %collective-permute-start.13 = (bf16[256,256]{1,0:T(8,128)(2,1)S(1)}, bf16[256,256]{1,0:T(8,128)(2,1)S(1)}, u32[]{:S(2)}, u32[]{:S(2)}) collective-permute-start(bf16[256,256]{1,0:T(8,128)(2,1)S(1)} %get-tuple-element.56), channel_id=1, source_target_pairs={{0,12},{1,13},{2,14},{3,15},{4,0},{5,1},{6,2},{7,3},{8,4},{9,5},{1... | collective-permute-start | bytes 393224 | tf_op jit(solution)/shard_map/ppermute | solution.py:232
  43.1 15.5 %collective-permute-start.14 = (bf16[256,256]{1,0:T(8,128)(2,1)S(1)}, bf16[256,256]{1,0:T(8,128)(2,1)S(1)}, u32[]{:S(2)}, u32[]{:S(2)}) collective-permute-start(bf16[256,256]{1,0:T(8,128)(2,1)S(1)} %get-tuple-element.57), channel_id=1, source_target_pairs={{0,14},{1,15},{2,0},{3,1},{4,2},{5,3},{6,4},{7,5},{8,6},{9,7},{10,... | collective-permute-start | bytes 393224 | tf_op jit(solution)/shard_map/ppermute | solution.py:232
  56.9 1.3 %copy-start.3 = (bf16[4096,256]{1,0:T(8,128)(2,1)}, bf16[4096,256]{1,0:T(8,128)(2,1)S(1)}, u32[]{:S(2)}) copy-start(bf16[4096,256]{1,0:T(8,128)(2,1)S(1)} %get-tuple-element.66.refs_0_) | copy-start | bytes 6291460
  72.5 22.4 %copy-start = (bf16[1024,1024]{1,0:T(8,128)(2,1)S(1)}, bf16[1024,1024]{1,0:T(8,128)(2,1)}, u32[]{:S(2)}) copy-start(bf16[1024,1024]{1,0:T(8,128)(2,1)} %refs_3_.1) | copy-start | bytes 6291460
  72.5 2.7 %collective-permute-start.15 = (bf16[2048,256]{1,0:T(8,128)(2,1)S(1)}, bf16[2048,256]{1,0:T(8,128)(2,1)S(1)}, u32[]{:S(2)}, u32[]{:S(2)}) collective-permute-start(bf16[2048,256]{1,0:T(8,128)(2,1)S(1)} %get-tuple-element.70), channel_id=1, source_target_pairs={{0,1},{1,0},{2,3},{3,2},{4,5},{5,4},{6,7},{7,6},{8,9},{9,8},{10,11... | collective-permute-start | bytes 3145736 | tf_op jit(solution)/shard_map/ppermute | solution.py:238
  75.5 10.5 %collective-permute-start.19 = (bf16[256,384]{1,0:T(8,128)(2,1)S(1)}, bf16[256,384]{1,0:T(8,128)(2,1)S(1)}, u32[]{:S(2)}, u32[]{:S(2)}) collective-permute-start(bf16[256,384]{1,0:T(8,128)(2,1)S(1)} %get-tuple-element.75), channel_id=1, source_target_pairs={{0,14},{1,15},{2,0},{3,1},{4,2},{5,3},{6,4},{7,5},{8,6},{9,7},{10,... | collective-permute-start | bytes 589832 | tf_op jit(solution)/shard_map/ppermute | solution.py:232
  80.7 9.5 %collective-permute-start.20 = (bf16[256,384]{1,0:T(8,128)(2,1)S(1)}, bf16[256,384]{1,0:T(8,128)(2,1)S(1)}, u32[]{:S(2)}, u32[]{:S(2)}) collective-permute-start(bf16[256,384]{1,0:T(8,128)(2,1)S(1)} %get-tuple-element.76), channel_id=1, source_target_pairs={{0,12},{1,13},{2,14},{3,15},{4,0},{5,1},{6,2},{7,3},{8,4},{9,5},{1... | collective-permute-start | bytes 589832 | tf_op jit(solution)/shard_map/ppermute | solution.py:232
  80.7 13.7 %collective-permute-start.21 = (bf16[256,384]{1,0:T(8,128)(2,1)S(1)}, bf16[256,384]{1,0:T(8,128)(2,1)S(1)}, u32[]{:S(2)}, u32[]{:S(2)}) collective-permute-start(bf16[256,384]{1,0:T(8,128)(2,1)S(1)} %get-tuple-element.77), channel_id=1, source_target_pairs={{0,4},{1,5},{2,6},{3,7},{4,8},{5,9},{6,10},{7,11},{8,12},{9,13},{1... | collective-permute-start | bytes 589832 | tf_op jit(solution)/shard_map/ppermute | solution.py:232
  82.7 12.2 %collective-permute-start.22 = (bf16[256,384]{1,0:T(8,128)(2,1)S(1)}, bf16[256,384]{1,0:T(8,128)(2,1)S(1)}, u32[]{:S(2)}, u32[]{:S(2)}) collective-permute-start(bf16[256,384]{1,0:T(8,128)(2,1)S(1)} %get-tuple-element.78), channel_id=1, source_target_pairs={{0,2},{1,3},{2,4},{3,5},{4,6},{5,7},{6,8},{7,9},{8,10},{9,11},{10,... | collective-permute-start | bytes 589832 | tf_op jit(solution)/shard_map/ppermute | solution.py:232
  82.7 16.3 %collective-permute-start.16 = (bf16[256,384]{1,0:T(8,128)(2,1)S(1)}, bf16[256,384]{1,0:T(8,128)(2,1)S(1)}, u32[]{:S(2)}, u32[]{:S(2)}) collective-permute-start(bf16[256,384]{1,0:T(8,128)(2,1)S(1)} %get-tuple-element.71), channel_id=1, source_target_pairs={{0,10},{1,11},{2,12},{3,13},{4,14},{5,15},{6,0},{7,1},{8,2},{9,3},... | collective-permute-start | bytes 589832 | tf_op jit(solution)/shard_map/ppermute | solution.py:232
  86.0 27.4 %collective-permute-start.17 = (bf16[256,384]{1,0:T(8,128)(2,1)S(1)}, bf16[256,384]{1,0:T(8,128)(2,1)S(1)}, u32[]{:S(2)}, u32[]{:S(2)}) collective-permute-start(bf16[256,384]{1,0:T(8,128)(2,1)S(1)} %get-tuple-element.72), channel_id=1, source_target_pairs={{0,8},{1,9},{2,10},{3,11},{4,12},{5,13},{6,14},{7,15},{8,0},{9,1},... | collective-permute-start | bytes 589832 | tf_op jit(solution)/shard_map/ppermute | solution.py:232
  90.2 26.1 %collective-permute-start.18 = (bf16[256,384]{1,0:T(8,128)(2,1)S(1)}, bf16[256,384]{1,0:T(8,128)(2,1)S(1)}, u32[]{:S(2)}, u32[]{:S(2)}) collective-permute-start(bf16[256,384]{1,0:T(8,128)(2,1)S(1)} %get-tuple-element.73), channel_id=1, source_target_pairs={{0,6},{1,7},{2,8},{3,9},{4,10},{5,11},{6,12},{7,13},{8,14},{9,15},... | collective-permute-start | bytes 589832 | tf_op jit(solution)/shard_map/ppermute | solution.py:232
  94.9 21.4 %copy-start.1 = (bf16[1024,1024]{1,0:T(8,128)(2,1)S(1)}, bf16[1024,1024]{1,0:T(8,128)(2,1)}, u32[]{:S(2)}) copy-start(bf16[1024,1024]{1,0:T(8,128)(2,1)} %refs_4_.1) | copy-start | bytes 6291460

commit v5 on v4

--- a/solution.py
+++ b/solution.py
@@ -14,6 +14,7 @@
 WIN = 8
 CORES = 2
 WIDTHS = (2, 4, 6, 8)
+GROUP = 4
 CONTRACT = (((1,), (1,)), ((), ()))
 ANY = pl.BlockSpec(memory_space=pl.ANY)
 VMEM = pl.BlockSpec(memory_space=pltpu.VMEM)
@@ -85,36 +86,38 @@
 
 def attention_kernel(chips, tokens, scale, chip_ref, table_ref, count_ref, order_ref, *refs):
     pair_ref, turned_ref, pieces = refs[0], refs[1], refs[2 : 2 + chips]
-    dq_ref, own_out, other_out, ask_buf, give_buf, total = refs[2 + chips :]
+    dq_ref, total, sent_out, ask_buf, give_buf = refs[2 + chips :]
     blocks = chips * tokens // BLOCK
     half = blocks * BLOCK
     per_device = tokens // BLOCK
-    zero = jnp.zeros((BLOCK, HD), jnp.bfloat16)
+    ask_buf[...] = jnp.zeros_like(ask_buf)
+    give_buf[...] = jnp.zeros_like(give_buf)
     for step in range(chips):
         source = rotated(chip_ref[0], chips - step, chips)
         for place in range(per_device):
             piece = pieces[step][place * BLOCK : (place + 1) * BLOCK, :]
             query, grad = piece[:, :HD], piece[:, HD:]
             block = source * per_device + place
-            ask_buf[block, :BLOCK, :HD] = query
-            ask_buf[block, :BLOCK, HD:] = zero
-            ask_buf[block, BLOCK:, :HD] = zero
-            ask_buf[block, BLOCK:, HD:] = grad
+            ask_buf[block, :HD, :BLOCK] = jnp.transpose(query)
+            ask_buf[block, HD:, BLOCK:] = jnp.transpose(grad)
             give_buf[block, :BLOCK, :HD] = grad
-            give_buf[block, :BLOCK, HD:] = zero
-            give_buf[block, BLOCK:, :HD] = zero
             give_buf[block, BLOCK:, HD:] = query
     total[...] = jnp.zeros_like(total)
 
-    def attend(block, count, width):
+    def attend(block, width):
+        count = count_ref[block]
         index = [table_ref[block * NBR + slot] for slot in range(width)]
         slots = [rows_of(which, BLOCK) for which in index]
         pairs = jnp.concatenate([pair_ref[slot, :] for slot in slots], axis=0)
-        both = lax.dot_general(pairs, ask_buf[block], CONTRACT, preferred_element_type=jnp.float32)
+        both = jnp.dot(pairs, ask_buf[block], preferred_element_type=jnp.float32)
         scores, prob_grad = both[:, :BLOCK], both[:, BLOCK:]
-        rest = (width - 1) * BLOCK
-        last = jnp.where(count == width, scores[rest:], -jnp.inf)
-        scores = jnp.concatenate([scores[:rest], last], axis=0) if rest else last
+        scores = jnp.concatenate(
+            [
+                jnp.where(slot < count, scores[slot * BLOCK : (slot + 1) * BLOCK], -jnp.inf)
+                for slot in range(width)
+            ],
+            axis=0,
+        )
         peak = jnp.max(scores, axis=0, keepdims=True)
         weights = jnp.exp2((scores - peak) * (scale * math.log2(math.e)))
         probs = weights * (1.0 / jnp.sum(weights, axis=0, keepdims=True))
@@ -131,51 +134,32 @@
         dq_ref[rows_of(block, BLOCK), :] = jnp.transpose(dq * scale).astype(jnp.bfloat16)
         return slots, given
 
-    def add(slots, given):
-        for place, slot in enumerate(slots):
-            total[slot, :] += given[place * BLOCK : (place + 1) * BLOCK]
-
-    def two_blocks(pair, carry):
-        block, mate = order_ref[2 * pair], order_ref[2 * pair + 1]
-        count, other = count_ref[block], count_ref[mate]
+    def one_group(group, carry):
+        members = [order_ref[group * GROUP + member] for member in range(GROUP)]
+        most = count_ref[members[0]]
 
         def work(width):
-            first = attend(block, count, width)
-            second = attend(mate, other, width)
-            add(*first)
-            add(*second)
-
-        same = (count + 1) // 2 == (other + 1) // 2
-
-        def alone(which, many):
-            for width in WIDTHS:
-                @pl.when((many > width - 2) & (many <= width))
-                def _():
-                    add(*attend(which, many, width))
-
+            for slots, given in [attend(member, width) for member in members]:
+                for place, slot in enumerate(slots):
+                    total[slot, :] += given[place * BLOCK : (place + 1) * BLOCK]
+
+        below = 0
         for width in WIDTHS:
-            pl.when(same & (count > width - 2) & (count <= width))(functools.partial(work, width))
-
-        @pl.when(jnp.logical_not(same))
-        def _():
-            alone(block, count)
-            alone(mate, other)
-
+            pl.when((most > below) & (most <= width))(functools.partial(work, width))
+            below = width
         return carry
 
-    lax.fori_loop(0, blocks // 2, two_blocks, 0)
-    for part, out in ((slice(0, half), own_out), (slice(half, None), other_out)):
-        out[:, :HD] = (total[part, HD:] * scale).astype(out.dtype)
-        out[:, HD:] = total[part, :HD].astype(out.dtype)
-
-
-def combine_kernel(chips, tokens, chip_ref, dq_ref, own_ref, other_ref, *outs):
+    lax.fori_loop(0, blocks // GROUP, one_group, 0)
+    sent_out[...] = total[half:].astype(jnp.bfloat16)
+
+
+def combine_kernel(chips, tokens, scale, chip_ref, dq_ref, own_ref, other_ref, *outs):
     for step in range(chips):
         rows = rows_of(rotated(chip_ref[0], chips - step, chips), tokens)
         outs[step][:, :HD] = dq_ref[rows, :]
-        outs[step][:, HD:] = (own_ref[rows, :] + other_ref[rows, :].astype(jnp.float32)).astype(
-            jnp.bfloat16
-        )
+        summed = own_ref[rows, :] + other_ref[rows, :].astype(jnp.float32)
+        outs[step][:, HD : 2 * HD] = (summed[:, HD:] * scale).astype(jnp.bfloat16)
+        outs[step][:, 2 * HD :] = summed[:, :HD].astype(jnp.bfloat16)
 
 
 def project_kernel(chips, steps, chip_ref, *refs):
@@ -211,7 +195,6 @@
     bf16 = functools.partial(jax.ShapeDtypeStruct, dtype=jnp.bfloat16)
     f32 = functools.partial(jax.ShapeDtypeStruct, dtype=jnp.float32)
     buf16 = functools.partial(pltpu.VMEM, dtype=jnp.bfloat16)
-    buf32 = functools.partial(pltpu.VMEM, dtype=jnp.float32)
 
     def call(kernel, outs, scratch, scalars, *arrays, spec=VMEM):
         return pl.pallas_call(
@@ -272,17 +255,16 @@
     )
     dq, own_part, sent_part = call(
         args(attention_kernel, chips, tokens, scale),
-        [bf16((half, HD)), f32((half, 2 * HD)), bf16((half, 2 * HD))],
+        [bf16((half, HD)), f32((2 * half, 2 * HD)), bf16((half, 2 * HD))],
         [
+            buf16((blocks, 2 * HD, 2 * BLOCK)),
             buf16((blocks, 2 * BLOCK, 2 * HD)),
-            buf16((blocks, 2 * BLOCK, 2 * HD)),
-            buf32((2 * half, 2 * HD)),
         ],
         (chip, table, counts, order), both_pairs, turned, *asks,
     )
     came_part = across_cores(sent_part)
     back = call(
-        args(combine_kernel, chips, tokens), [bf16((tokens, 3 * HD))] * chips, [],
+        args(combine_kernel, chips, tokens, scale), [bf16((tokens, 3 * HD))] * chips, [],
         (chip,), dq, own_part, came_part,
     )
     back = [back[0]] + [by_chips(back[step], chips - step) for step in range(1, chips)]

time: 121 us -> 121 us (level)
  local copies, waits for them, and re-layouts: 8.75 us -> 7.42 us
  waiting for transfers between devices: 29 us -> 30.3 us
    unnamed x21 -> x19, local copies, waits for them, and re-layouts: 7.78 us -> 6.44 us
    ppermute x21, waiting for transfers between devices: 26.4 us -> 27.7 us  [by_chips(): return lax.ppermute(shard, 'blk', pairs)]
where the time goes in v5:
time: 121 us; the launch traced here: 120 us
  starting transfers between devices  57.1 us (47%)
  waiting for transfers between devices  30.3 us (25%)
  Pallas kernels  24.3 us (20%)
  local copies, waits for them, and re-layouts  7.42 us (6%)
    ppermute x21, starting transfers between devices, by_chips(): return lax.ppermute(shard, 'blk', pairs)  57.1 us
    ppermute x21, waiting for transfers between devices, by_chips(): return lax.ppermute(shard, 'blk', pairs)  27.7 us
    pallas_call x8, Pallas kernels, call(): pl.pallas_call(kernel, out_shape=outs, in_specs=[SMEM] * len(scalars) + [...  24.3 us
    unnamed x19, local copies, waits for them, and re-layouts  6.44 us
    ppermute x2, waiting for transfers between devices, across_cores(): lax.ppermute(shard, 'blk', [(i, i ^ 1) for i in range(chips * CORES)])  2.66 us
  transfers between devices with their start and end apart: 23, of which 10 were waited for; matrix products, arithmetic and copies ran while one was open for 2% of the time, Pallas kernels for 5%

profile of v5, /device:TPU:0, one launch (start us, length us, event | category | flops | bytes accessed | tf_op | source)
XLA Modules:
  0.0 119.7 jit_solution(4105282706847412175)
XLA Ops:
  0.0 1.0 copy-done.3
  1.0 1.0 copy-done.4
  2.1 0.5 shard_map.100
  2.6 3.0 %collective-permute-start = (bf16[256,256]{1,0:T(8,128)(2,1)S(1)}, bf16[256,256]{1,0:T(8,128)(2,1)S(1)}, u32[]{:S(2)}, u32[]{:S(2)}) collective-permute-start(bf16[256,256]{1,0:T(8,128)(2,1)S(1)} %get-tuple-element.43), channel_id=1, source_target_pairs={{0,2},{1,3},{2,4},{3,5},{4,6},{5,7},{6,8},{7,9},{8,10},{9,11},{10,... | collective-permute-start | bytes 393224 | tf_op jit(solution)/shard_map/ppermute | solution.py:215
  5.5 1.6 %collective-permute-start.1 = (bf16[256,256]{1,0:T(8,128)(2,1)S(1)}, bf16[256,256]{1,0:T(8,128)(2,1)S(1)}, u32[]{:S(2)}, u32[]{:S(2)}) collective-permute-start(bf16[256,256]{1,0:T(8,128)(2,1)S(1)} %get-tuple-element.44), channel_id=1, source_target_pairs={{0,4},{1,5},{2,6},{3,7},{4,8},{5,9},{6,10},{7,11},{8,12},{9,13},{1... | collective-permute-start | bytes 393224 | tf_op jit(solution)/shard_map/ppermute | solution.py:215
  7.1 2.6 %collective-permute-start.2 = (bf16[256,256]{1,0:T(8,128)(2,1)S(1)}, bf16[256,256]{1,0:T(8,128)(2,1)S(1)}, u32[]{:S(2)}, u32[]{:S(2)}) collective-permute-start(bf16[256,256]{1,0:T(8,128)(2,1)S(1)} %get-tuple-element.45), channel_id=1, source_target_pairs={{0,6},{1,7},{2,8},{3,9},{4,10},{5,11},{6,12},{7,13},{8,14},{9,15},... | collective-permute-start | bytes 393224 | tf_op jit(solution)/shard_map/ppermute | solution.py:215
  9.7 1.2 %collective-permute-start.3 = (bf16[256,256]{1,0:T(8,128)(2,1)S(1)}, bf16[256,256]{1,0:T(8,128)(2,1)S(1)}, u32[]{:S(2)}, u32[]{:S(2)}) collective-permute-start(bf16[256,256]{1,0:T(8,128)(2,1)S(1)} %get-tuple-element.46), channel_id=1, source_target_pairs={{0,8},{1,9},{2,10},{3,11},{4,12},{5,13},{6,14},{7,15},{8,0},{9,1},... | collective-permute-start | bytes 393224 | tf_op jit(solution)/shard_map/ppermute | solution.py:215
  10.9 2.6 %collective-permute-start.4 = (bf16[256,256]{1,0:T(8,128)(2,1)S(1)}, bf16[256,256]{1,0:T(8,128)(2,1)S(1)}, u32[]{:S(2)}, u32[]{:S(2)}) collective-permute-start(bf16[256,256]{1,0:T(8,128)(2,1)S(1)} %get-tuple-element.47), channel_id=1, source_target_pairs={{0,10},{1,11},{2,12},{3,13},{4,14},{5,15},{6,0},{7,1},{8,2},{9,3},... | collective-permute-start | bytes 393224 | tf_op jit(solution)/shard_map/ppermute | solution.py:215
  13.5 1.4 %collective-permute-start.5 = (bf16[256,256]{1,0:T(8,128)(2,1)S(1)}, bf16[256,256]{1,0:T(8,128)(2,1)S(1)}, u32[]{:S(2)}, u32[]{:S(2)}) collective-permute-start(bf16[256,256]{1,0:T(8,128)(2,1)S(1)} %get-tuple-element.48), channel_id=1, source_target_pairs={{0,12},{1,13},{2,14},{3,15},{4,0},{5,1},{6,2},{7,3},{8,4},{9,5},{1... | collective-permute-start | bytes 393224 | tf_op jit(solution)/shard_map/ppermute | solution.py:215
  14.9 2.0 %collective-permute-start.6 = (bf16[256,256]{1,0:T(8,128)(2,1)S(1)}, bf16[256,256]{1,0:T(8,128)(2,1)S(1)}, u32[]{:S(2)}, u32[]{:S(2)}) collective-permute-start(bf16[256,256]{1,0:T(8,128)(2,1)S(1)} %get-tuple-element.49), channel_id=1, source_target_pairs={{0,14},{1,15},{2,0},{3,1},{4,2},{5,3},{6,4},{7,5},{8,6},{9,7},{10,... | collective-permute-start | bytes 393224 | tf_op jit(solution)/shard_map/ppermute | solution.py:215
  17.0 1.6 %copy-done.2 = bf16[1024,1024]{1,0:T(8,128)(2,1)S(1)} copy-done((bf16[1024,1024]{1,0:T(8,128)(2,1)S(1)}, bf16[1024,1024]{1,0:T(8,128)(2,1)}, u32[]{:S(2)}) %copy-start.2) | copy-done | bytes 2097176
  18.6 1.0 copy-done.5
  19.6 1.0 copy-done.6
  20.7 1.8 %shard_map.101 = (bf16[256,256]{1,0:T(8,128)(2,1)S(1)}, bf16[256,256]{1,0:T(8,128)(2,1)}, bf16[256,256]{1,0:T(8,128)(2,1)S(1)}, bf16[256,256]{1,0:T(8,128)(2,1)S...) custom-call(s32[1]{0:T(128)} %bitcast.chip_ref, ...), custom_call_target="tpu_custom_call" | custom-call | tf_op jit(solution)/shard_map/pallas_call | solution.py:200
  22.5 1.0 collective-permute-done.2.refs_3_
  23.5 0.3 collective-permute-done.3.refs_4_
  23.8 0.1 shard_map.102.own_ref
  24.0 4.3 %collective-permute-start.8 = (bf16[256,256]{1,0:T(8,128)(2,1)}, bf16[256,256]{1,0:T(8,128)(2,1)S(1)}, u32[]{:S(2)}, u32[]{:S(2)}) collective-permute-start(bf16[256,256]{1,0:T(8,128)(2,1)} %get-tuple-element.51), channel_id=1, source_target_pairs={{0,2},{1,3},{2,4},{3,5},{4,6},{5,7},{6,8},{7,9},{8,10},{9,11},{10,... | collective-permute-start | bytes 393224 | tf_op jit(solution)/shard_map/ppermute | solution.py:215
  28.3 6.0 %collective-permute-start.9 = (bf16[256,256]{1,0:T(8,128)(2,1)S(1)}, bf16[256,256]{1,0:T(8,128)(2,1)S(1)}, u32[]{:S(2)}, u32[]{:S(2)}) collective-permute-start(bf16[256,256]{1,0:T(8,128)(2,1)S(1)} %get-tuple-element.52), channel_id=1, source_target_pairs={{0,4},{1,5},{2,6},{3,7},{4,8},{5,9},{6,10},{7,11},{8,12},{9,13},{1... | collective-permute-start | bytes 393224 | tf_op jit(solution)/shard_map/ppermute | solution.py:215
  34.3 2.9 %collective-permute-start.10 = (bf16[256,256]{1,0:T(8,128)(2,1)S(1)}, bf16[256,256]{1,0:T(8,128)(2,1)S(1)}, u32[]{:S(2)}, u32[]{:S(2)}) collective-permute-start(bf16[256,256]{1,0:T(8,128)(2,1)S(1)} %get-tuple-element.53), channel_id=1, source_target_pairs={{0,6},{1,7},{2,8},{3,9},{4,10},{5,11},{6,12},{7,13},{8,14},{9,15},... | collective-permute-start | bytes 393224 | tf_op jit(solution)/shard_map/ppermute | solution.py:215
  37.2 0.1 reshape.36
  37.3 0.1 reshape.37.count_ref
  37.4 0.7 copy.13
  38.1 0.7 constant_dynamic-slice_fusion
  38.8 0.1 squeeze.6
  38.9 0.5 collective-permute-done.8.refs_3_
  39.4 2.1 %collective-permute-start.12 = (bf16[256,256]{1,0:T(8,128)(2,1)S(1)}, bf16[256,256]{1,0:T(8,128)(2,1)S(1)}, u32[]{:S(2)}, u32[]{:S(2)}) collective-permute-start(bf16[256,256]{1,0:T(8,128)(2,1)S(1)} %get-tuple-element.55), channel_id=1, source_target_pairs={{0,10},{1,11},{2,12},{3,13},{4,14},{5,15},{6,0},{7,1},{8,2},{9,3},... | collective-permute-start | bytes 393224 | tf_op jit(solution)/shard_map/ppermute | solution.py:215
  41.5 1.6 %collective-permute-start.13 = (bf16[256,256]{1,0:T(8,128)(2,1)S(1)}, bf16[256,256]{1,0:T(8,128)(2,1)S(1)}, u32[]{:S(2)}, u32[]{:S(2)}) collective-permute-start(bf16[256,256]{1,0:T(8,128)(2,1)S(1)} %get-tuple-element.56), channel_id=1, source_target_pairs={{0,12},{1,13},{2,14},{3,15},{4,0},{5,1},{6,2},{7,3},{8,4},{9,5},{1... | collective-permute-start | bytes 393224 | tf_op jit(solution)/shard_map/ppermute | solution.py:215
  43.1 13.0 %collective-permute-start.14 = (bf16[256,256]{1,0:T(8,128)(2,1)S(1)}, bf16[256,256]{1,0:T(8,128)(2,1)S(1)}, u32[]{:S(2)}, u32[]{:S(2)}) collective-permute-start(bf16[256,256]{1,0:T(8,128)(2,1)S(1)} %get-tuple-element.57), channel_id=1, source_target_pairs={{0,14},{1,15},{2,0},{3,1},{4,2},{5,3},{6,4},{7,5},{8,6},{9,7},{10,... | collective-permute-start | bytes 393224 | tf_op jit(solution)/shard_map/ppermute | solution.py:215
  56.2 0.2 convert_reduce_fusion
  56.3 0.1 select_reduce_fusion.order_ref
  56.4 0.4 shard_map.103
  56.9 1.8 %collective-permute-done.14.refs_9_ = bf16[256,256]{1,0:T(8,128)(2,1)S(1)} collective-permute-done((bf16[256,256]{1,0:T(8,128)(2,1)S(1)}, bf16[256,256]{1,0:T(8,128)(2,1)S(1)}, u32[]{:S(2)}, u32[]{:S(2)}) %collective-permute-start.14) | collective-permute-done | bytes 131104 | tf_op jit(solution)/shard_map/ppermute | solution.py:215
  58.7 11.3 %shard_map.104 = (bf16[2048,128]{1,0:T(8,128)(2,1)S(1)}, f32[4096,256]{1,0:T(8,128)}, bf16[2048,256]{1,0:T(8,128)(2,1)S(1)}) custom-call(s32[1]{0:T(128)} %bitcast.chip_ref, s32[128]{0:T(128)S(1)} %fusion.table_ref, s32[16]{0:T(128)S(1)} %reshape.37.count_ref, s32[16]{0:T(128)S(1)} %select_reduce_fusion.order_ref, ...), custom_call_target="tpu_custom_call" | custom-call | tf_op jit(solution)/shard_map/pallas_call | solution.py:200
  70.0 2.7 %collective-permute-done.15.other_ref = bf16[2048,256]{1,0:T(8,128)(2,1)S(1)} collective-permute-done((bf16[2048,256]{1,0:T(8,128)(2,1)S(1)}, bf16[2048,256]{1,0:T(8,128)(2,1)S(1)}, u32[]{:S(2)}, u32[]{:S(2)}) %collective-permute-start.15) | collective-permute-done | bytes 1048608 | tf_op jit(solution)/shard_map/ppermute | solution.py:221
  72.6 2.7 %shard_map.105 = (bf16[256,384]{1,0:T(8,128)(2,1)S(1)}, bf16[256,384]{1,0:T(8,128)(2,1)S(1)}, bf16[256,384]{1,0:T(8,128)(2,1)S(1)}, bf16[256,384]{1,0:T(8,128)(2...) custom-call(s32[1]{0:T(128)} %bitcast.chip_ref, ...), custom_call_target="tpu_custom_call" | custom-call | tf_op jit(solution)/shard_map/pallas_call | solution.py:200
  75.3 5.2 %collective-permute-start.19 = (bf16[256,384]{1,0:T(8,128)(2,1)S(1)}, bf16[256,384]{1,0:T(8,128)(2,1)S(1)}, u32[]{:S(2)}, u32[]{:S(2)}) collective-permute-start(bf16[256,384]{1,0:T(8,128)(2,1)S(1)} %get-tuple-element.75), channel_id=1, source_target_pairs={{0,14},{1,15},{2,0},{3,1},{4,2},{5,3},{6,4},{7,5},{8,6},{9,7},{10,... | collective-permute-start | bytes 589832 | tf_op jit(solution)/shard_map/ppermute | solution.py:215
  80.5 2.0 %collective-permute-start.21 = (bf16[256,384]{1,0:T(8,128)(2,1)S(1)}, bf16[256,384]{1,0:T(8,128)(2,1)S(1)}, u32[]{:S(2)}, u32[]{:S(2)}) collective-permute-start(bf16[256,384]{1,0:T(8,128)(2,1)S(1)} %get-tuple-element.77), channel_id=1, source_target_pairs={{0,4},{1,5},{2,6},{3,7},{4,8},{5,9},{6,10},{7,11},{8,12},{9,13},{1... | collective-permute-start | bytes 589832 | tf_op jit(solution)/shard_map/ppermute | solution.py:215
  82.5 3.3 %collective-permute-start.16 = (bf16[256,384]{1,0:T(8,128)(2,1)S(1)}, bf16[256,384]{1,0:T(8,128)(2,1)S(1)}, u32[]{:S(2)}, u32[]{:S(2)}) collective-permute-start(bf16[256,384]{1,0:T(8,128)(2,1)S(1)} %get-tuple-element.71), channel_id=1, source_target_pairs={{0,10},{1,11},{2,12},{3,13},{4,14},{5,15},{6,0},{7,1},{8,2},{9,3},... | collective-permute-start | bytes 589832 | tf_op jit(solution)/shard_map/ppermute | solution.py:215
  85.8 0.6 collective-permute-start.17
  86.3 3.7 %collective-permute-done.20.refs_2_ = bf16[256,384]{1,0:T(8,128)(2,1)S(1)} collective-permute-done((bf16[256,384]{1,0:T(8,128)(2,1)S(1)}, bf16[256,384]{1,0:T(8,128)(2,1)S(1)}, u32[]{:S(2)}, u32[]{:S(2)}) %collective-permute-start.20) | collective-permute-done | bytes 196640 | tf_op jit(solution)/shard_map/ppermute | solution.py:215
  90.0 1.6 %collective-permute-start.18 = (bf16[256,384]{1,0:T(8,128)(2,1)S(1)}, bf16[256,384]{1,0:T(8,128)(2,1)S(1)}, u32[]{:S(2)}, u32[]{:S(2)}) collective-permute-start(bf16[256,384]{1,0:T(8,128)(2,1)S(1)} %get-tuple-element.73), channel_id=1, source_target_pairs={{0,6},{1,7},{2,8},{3,9},{4,10},{5,11},{6,12},{7,13},{8,14},{9,15},... | collective-permute-start | bytes 589832 | tf_op jit(solution)/shard_map/ppermute | solution.py:215
  91.6 2.6 %collective-permute-done.21.refs_3_ = bf16[256,384]{1,0:T(8,128)(2,1)S(1)} collective-permute-done((bf16[256,384]{1,0:T(8,128)(2,1)S(1)}, bf16[256,384]{1,0:T(8,128)(2,1)S(1)}, u32[]{:S(2)}, u32[]{:S(2)}) %collective-permute-start.21) | collective-permute-done | bytes 196640 | tf_op jit(solution)/shard_map/ppermute | solution.py:215
  94.2 0.5 collective-permute-done.22.refs_4_
  94.7 4.1 %shard_map.106.refs_6_ = f32[256,1024]{1,0:T(8,128)S(1)} custom-call(s32[1]{0:T(128)} %bitcast.chip_ref, bf16[256,384]{1,0:T(8,128)(2,1)S(1)} %get-tuple-element.74.refs_0_, bf16[256,384]{1,0:T(8,128)(2,1)S(1)} %collective-permute-done.19.refs_1_, bf16[256,384]{1,0:T(8,128)(2,1)S(1)} %collective-permute-done.20.refs_2_, ...), custom_call_target="tpu_custom_call" | custom-call | tf_op jit(solution)/shard_map/pallas_call | solution.py:200
  98.8 14.8 %collective-permute-done.17.refs_1_ = bf16[256,384]{1,0:T(8,128)(2,1)S(1)} collective-permute-done((bf16[256,384]{1,0:T(8,128)(2,1)S(1)}, bf16[256,384]{1,0:T(8,128)(2,1)S(1)}, u32[]{:S(2)}, u32[]{:S(2)}) %collective-permute-start.17) | collective-permute-done | bytes 196640 | tf_op jit(solution)/shard_map/ppermute | solution.py:215
  113.6 2.6 %collective-permute-done.18.refs_2_ = bf16[256,384]{1,0:T(8,128)(2,1)S(1)} collective-permute-done((bf16[256,384]{1,0:T(8,128)(2,1)S(1)}, bf16[256,384]{1,0:T(8,128)(2,1)S(1)}, u32[]{:S(2)}, u32[]{:S(2)}) %collective-permute-start.18) | collective-permute-done | bytes 196640 | tf_op jit(solution)/shard_map/ppermute | solution.py:215
  116.1 3.6 %shard_map.107 = bf16[256,1024]{1,0:T(8,128)(2,1)} custom-call(s32[1]{0:T(128)} %bitcast.chip_ref, bf16[256,384]{1,0:T(8,128)(2,1)S(1)} %collective-permute-done.16.refs_0_, bf16[256,384]{1,0:T(8,128)(2,1)S(1)} %collective-permute-done.17.refs_1_, bf16[256,384]{1,0:T(8,128)(2,1)S(1)} %collective-permute-done.18.refs_2_, bf16[1024,1024]{1,0:T(8,128)(2,1)S(1)} %copy-done, ...), custom_call_target="tpu_custom_call" | custom-call | tf_op jit(solution)/shard_map/pallas_call | solution.py:200
  (34 shorter events, 0.2 us)
Async XLA Ops:
  0.0 1.0 copy-start.3
  1.0 1.0 copy-start.4
  2.6 11.0 %collective-permute-start = (bf16[256,256]{1,0:T(8,128)(2,1)S(1)}, bf16[256,256]{1,0:T(8,128)(2,1)S(1)}, u32[]{:S(2)}, u32[]{:S(2)}) collective-permute-start(bf16[256,256]{1,0:T(8,128)(2,1)S(1)} %get-tuple-element.43), channel_id=1, source_target_pairs={{0,2},{1,3},{2,4},{3,5},{4,6},{5,7},{6,8},{7,9},{8,10},{9,11},{10,... | collective-permute-start | bytes 393224 | tf_op jit(solution)/shard_map/ppermute | solution.py:215
  5.5 9.4 %collective-permute-start.1 = (bf16[256,256]{1,0:T(8,128)(2,1)S(1)}, bf16[256,256]{1,0:T(8,128)(2,1)S(1)}, u32[]{:S(2)}, u32[]{:S(2)}) collective-permute-start(bf16[256,256]{1,0:T(8,128)(2,1)S(1)} %get-tuple-element.44), channel_id=1, source_target_pairs={{0,4},{1,5},{2,6},{3,7},{4,8},{5,9},{6,10},{7,11},{8,12},{9,13},{1... | collective-permute-start | bytes 393224 | tf_op jit(solution)/shard_map/ppermute | solution.py:215
  7.1 16.3 %collective-permute-start.2 = (bf16[256,256]{1,0:T(8,128)(2,1)S(1)}, bf16[256,256]{1,0:T(8,128)(2,1)S(1)}, u32[]{:S(2)}, u32[]{:S(2)}) collective-permute-start(bf16[256,256]{1,0:T(8,128)(2,1)S(1)} %get-tuple-element.45), channel_id=1, source_target_pairs={{0,6},{1,7},{2,8},{3,9},{4,10},{5,11},{6,12},{7,13},{8,14},{9,15},... | collective-permute-start | bytes 393224 | tf_op jit(solution)/shard_map/ppermute | solution.py:215
  9.7 14.1 %collective-permute-start.3 = (bf16[256,256]{1,0:T(8,128)(2,1)S(1)}, bf16[256,256]{1,0:T(8,128)(2,1)S(1)}, u32[]{:S(2)}, u32[]{:S(2)}) collective-permute-start(bf16[256,256]{1,0:T(8,128)(2,1)S(1)} %get-tuple-element.46), channel_id=1, source_target_pairs={{0,8},{1,9},{2,10},{3,11},{4,12},{5,13},{6,14},{7,15},{8,0},{9,1},... | collective-permute-start | bytes 393224 | tf_op jit(solution)/shard_map/ppermute | solution.py:215
  10.9 12.9 %collective-permute-start.4 = (bf16[256,256]{1,0:T(8,128)(2,1)S(1)}, bf16[256,256]{1,0:T(8,128)(2,1)S(1)}, u32[]{:S(2)}, u32[]{:S(2)}) collective-permute-start(bf16[256,256]{1,0:T(8,128)(2,1)S(1)} %get-tuple-element.47), channel_id=1, source_target_pairs={{0,10},{1,11},{2,12},{3,13},{4,14},{5,15},{6,0},{7,1},{8,2},{9,3},... | collective-permute-start | bytes 393224 | tf_op jit(solution)/shard_map/ppermute | solution.py:215
  13.5 10.3 %collective-permute-start.5 = (bf16[256,256]{1,0:T(8,128)(2,1)S(1)}, bf16[256,256]{1,0:T(8,128)(2,1)S(1)}, u32[]{:S(2)}, u32[]{:S(2)}) collective-permute-start(bf16[256,256]{1,0:T(8,128)(2,1)S(1)} %get-tuple-element.48), channel_id=1, source_target_pairs={{0,12},{1,13},{2,14},{3,15},{4,0},{5,1},{6,2},{7,3},{8,4},{9,5},{1... | collective-permute-start | bytes 393224 | tf_op jit(solution)/shard_map/ppermute | solution.py:215
  14.9 8.9 %collective-permute-start.6 = (bf16[256,256]{1,0:T(8,128)(2,1)S(1)}, bf16[256,256]{1,0:T(8,128)(2,1)S(1)}, u32[]{:S(2)}, u32[]{:S(2)}) collective-permute-start(bf16[256,256]{1,0:T(8,128)(2,1)S(1)} %get-tuple-element.49), channel_id=1, source_target_pairs={{0,14},{1,15},{2,0},{3,1},{4,2},{5,3},{6,4},{7,5},{8,6},{9,7},{10,... | collective-permute-start | bytes 393224 | tf_op jit(solution)/shard_map/ppermute | solution.py:215
  17.0 1.6 %copy-start.2 = (bf16[1024,1024]{1,0:T(8,128)(2,1)S(1)}, bf16[1024,1024]{1,0:T(8,128)(2,1)}, u32[]{:S(2)}) copy-start(bf16[1024,1024]{1,0:T(8,128)(2,1)} %weight_ref.1) | copy-start | bytes 6291460
  18.6 1.0 copy-start.5
  19.6 1.0 copy-start.6
  20.7 16.5 %copy-start.8 = (s32[32]{0:T(128)S(1)}, s32[32]{0:T(128)}, u32[]{:S(2)}) copy-start(s32[32]{0:T(128)} %param.19) | copy-start | bytes 388
  20.7 16.7 %copy-start.7 = (s32[32,8]{0,1:T(8,128)S(1)}, s32[32,8]{0,1:T(8,128)}, u32[]{:S(2)}) copy-start(s32[32,8]{0,1:T(8,128)} %param.18) | copy-start | bytes 3076
  23.9 19.3 %collective-permute-start.7 = (bf16[2048,256]{1,0:T(8,128)(2,1)S(1)}, bf16[2048,256]{1,0:T(8,128)(2,1)S(1)}, u32[]{:S(2)}, u32[]{:S(2)}) collective-permute-start(bf16[2048,256]{1,0:T(8,128)(2,1)S(1)} %shard_map.102.own_ref), channel_id=1, source_target_pairs={{0,1},{1,0},{2,3},{3,2},{4,5},{5,4},{6,7},{7,6},{8,9},{9,8},{10,11... | collective-permute-start | bytes 3145736 | tf_op jit(solution)/shard_map/ppermute | solution.py:221
  24.0 15.4 %collective-permute-start.8 = (bf16[256,256]{1,0:T(8,128)(2,1)}, bf16[256,256]{1,0:T(8,128)(2,1)S(1)}, u32[]{:S(2)}, u32[]{:S(2)}) collective-permute-start(bf16[256,256]{1,0:T(8,128)(2,1)} %get-tuple-element.51), channel_id=1, source_target_pairs={{0,2},{1,3},{2,4},{3,5},{4,6},{5,7},{6,8},{7,9},{8,10},{9,11},{10,... | collective-permute-start | bytes 393224 | tf_op jit(solution)/shard_map/ppermute | solution.py:215
  28.3 13.2 %collective-permute-start.9 = (bf16[256,256]{1,0:T(8,128)(2,1)S(1)}, bf16[256,256]{1,0:T(8,128)(2,1)S(1)}, u32[]{:S(2)}, u32[]{:S(2)}) collective-permute-start(bf16[256,256]{1,0:T(8,128)(2,1)S(1)} %get-tuple-element.52), channel_id=1, source_target_pairs={{0,4},{1,5},{2,6},{3,7},{4,8},{5,9},{6,10},{7,11},{8,12},{9,13},{1... | collective-permute-start | bytes 393224 | tf_op jit(solution)/shard_map/ppermute | solution.py:215
  34.3 22.6 %collective-permute-start.10 = (bf16[256,256]{1,0:T(8,128)(2,1)S(1)}, bf16[256,256]{1,0:T(8,128)(2,1)S(1)}, u32[]{:S(2)}, u32[]{:S(2)}) collective-permute-start(bf16[256,256]{1,0:T(8,128)(2,1)S(1)} %get-tuple-element.53), channel_id=1, source_target_pairs={{0,6},{1,7},{2,8},{3,9},{4,10},{5,11},{6,12},{7,13},{8,14},{9,15},... | collective-permute-start | bytes 393224 | tf_op jit(solution)/shard_map/ppermute | solution.py:215
  37.2 19.7 %collective-permute-start.11 = (bf16[256,256]{1,0:T(8,128)(2,1)S(1)}, bf16[256,256]{1,0:T(8,128)(2,1)S(1)}, u32[]{:S(2)}, u32[]{:S(2)}) collective-permute-start(bf16[256,256]{1,0:T(8,128)(2,1)S(1)} %get-tuple-element.54), channel_id=1, source_target_pairs={{0,8},{1,9},{2,10},{3,11},{4,12},{5,13},{6,14},{7,15},{8,0},{9,1},... | collective-permute-start | bytes 393224 | tf_op jit(solution)/shard_map/ppermute | solution.py:215
  39.4 17.5 %collective-permute-start.12 = (bf16[256,256]{1,0:T(8,128)(2,1)S(1)}, bf16[256,256]{1,0:T(8,128)(2,1)S(1)}, u32[]{:S(2)}, u32[]{:S(2)}) collective-permute-start(bf16[256,256]{1,0:T(8,128)(2,1)S(1)} %get-tuple-element.55), channel_id=1, source_target_pairs={{0,10},{1,11},{2,12},{3,13},{4,14},{5,15},{6,0},{7,1},{8,2},{9,3},... | collective-permute-start | bytes 393224 | tf_op jit(solution)/shard_map/ppermute | solution.py:215
  41.5 15.4 %collective-permute-start.13 = (bf16[256,256]{1,0:T(8,128)(2,1)S(1)}, bf16[256,256]{1,0:T(8,128)(2,1)S(1)}, u32[]{:S(2)}, u32[]{:S(2)}) collective-permute-start(bf16[256,256]{1,0:T(8,128)(2,1)S(1)} %get-tuple-element.56), channel_id=1, source_target_pairs={{0,12},{1,13},{2,14},{3,15},{4,0},{5,1},{6,2},{7,3},{8,4},{9,5},{1... | collective-permute-start | bytes 393224 | tf_op jit(solution)/shard_map/ppermute | solution.py:215
  43.1 15.5 %collective-permute-start.14 = (bf16[256,256]{1,0:T(8,128)(2,1)S(1)}, bf16[256,256]{1,0:T(8,128)(2,1)S(1)}, u32[]{:S(2)}, u32[]{:S(2)}) collective-permute-start(bf16[256,256]{1,0:T(8,128)(2,1)S(1)} %get-tuple-element.57), channel_id=1, source_target_pairs={{0,14},{1,15},{2,0},{3,1},{4,2},{5,3},{6,4},{7,5},{8,6},{9,7},{10,... | collective-permute-start | bytes 393224 | tf_op jit(solution)/shard_map/ppermute | solution.py:215
  69.9 2.7 %collective-permute-start.15 = (bf16[2048,256]{1,0:T(8,128)(2,1)S(1)}, bf16[2048,256]{1,0:T(8,128)(2,1)S(1)}, u32[]{:S(2)}, u32[]{:S(2)}) collective-permute-start(bf16[2048,256]{1,0:T(8,128)(2,1)S(1)} %get-tuple-element.70), channel_id=1, source_target_pairs={{0,1},{1,0},{2,3},{3,2},{4,5},{5,4},{6,7},{7,6},{8,9},{9,8},{10,11... | collective-permute-start | bytes 3145736 | tf_op jit(solution)/shard_map/ppermute | solution.py:221
  72.6 22.1 %copy-start = (bf16[1024,1024]{1,0:T(8,128)(2,1)S(1)}, bf16[1024,1024]{1,0:T(8,128)(2,1)}, u32[]{:S(2)}) copy-start(bf16[1024,1024]{1,0:T(8,128)(2,1)} %refs_3_.1) | copy-start | bytes 6291460
  75.3 10.5 %collective-permute-start.19 = (bf16[256,384]{1,0:T(8,128)(2,1)S(1)}, bf16[256,384]{1,0:T(8,128)(2,1)S(1)}, u32[]{:S(2)}, u32[]{:S(2)}) collective-permute-start(bf16[256,384]{1,0:T(8,128)(2,1)S(1)} %get-tuple-element.75), channel_id=1, source_target_pairs={{0,14},{1,15},{2,0},{3,1},{4,2},{5,3},{6,4},{7,5},{8,6},{9,7},{10,... | collective-permute-start | bytes 589832 | tf_op jit(solution)/shard_map/ppermute | solution.py:215
  80.5 9.5 %collective-permute-start.20 = (bf16[256,384]{1,0:T(8,128)(2,1)S(1)}, bf16[256,384]{1,0:T(8,128)(2,1)S(1)}, u32[]{:S(2)}, u32[]{:S(2)}) collective-permute-start(bf16[256,384]{1,0:T(8,128)(2,1)S(1)} %get-tuple-element.76), channel_id=1, source_target_pairs={{0,12},{1,13},{2,14},{3,15},{4,0},{5,1},{6,2},{7,3},{8,4},{9,5},{1... | collective-permute-start | bytes 589832 | tf_op jit(solution)/shard_map/ppermute | solution.py:215
  80.5 13.7 %collective-permute-start.21 = (bf16[256,384]{1,0:T(8,128)(2,1)S(1)}, bf16[256,384]{1,0:T(8,128)(2,1)S(1)}, u32[]{:S(2)}, u32[]{:S(2)}) collective-permute-start(bf16[256,384]{1,0:T(8,128)(2,1)S(1)} %get-tuple-element.77), channel_id=1, source_target_pairs={{0,4},{1,5},{2,6},{3,7},{4,8},{5,9},{6,10},{7,11},{8,12},{9,13},{1... | collective-permute-start | bytes 589832 | tf_op jit(solution)/shard_map/ppermute | solution.py:215
  82.5 12.2 %collective-permute-start.22 = (bf16[256,384]{1,0:T(8,128)(2,1)S(1)}, bf16[256,384]{1,0:T(8,128)(2,1)S(1)}, u32[]{:S(2)}, u32[]{:S(2)}) collective-permute-start(bf16[256,384]{1,0:T(8,128)(2,1)S(1)} %get-tuple-element.78), channel_id=1, source_target_pairs={{0,2},{1,3},{2,4},{3,5},{4,6},{5,7},{6,8},{7,9},{8,10},{9,11},{10,... | collective-permute-start | bytes 589832 | tf_op jit(solution)/shard_map/ppermute | solution.py:215
  82.5 16.3 %collective-permute-start.16 = (bf16[256,384]{1,0:T(8,128)(2,1)S(1)}, bf16[256,384]{1,0:T(8,128)(2,1)S(1)}, u32[]{:S(2)}, u32[]{:S(2)}) collective-permute-start(bf16[256,384]{1,0:T(8,128)(2,1)S(1)} %get-tuple-element.71), channel_id=1, source_target_pairs={{0,10},{1,11},{2,12},{3,13},{4,14},{5,15},{6,0},{7,1},{8,2},{9,3},... | collective-permute-start | bytes 589832 | tf_op jit(solution)/shard_map/ppermute | solution.py:215
  85.8 27.8 %collective-permute-start.17 = (bf16[256,384]{1,0:T(8,128)(2,1)S(1)}, bf16[256,384]{1,0:T(8,128)(2,1)S(1)}, u32[]{:S(2)}, u32[]{:S(2)}) collective-permute-start(bf16[256,384]{1,0:T(8,128)(2,1)S(1)} %get-tuple-element.72), channel_id=1, source_target_pairs={{0,8},{1,9},{2,10},{3,11},{4,12},{5,13},{6,14},{7,15},{8,0},{9,1},... | collective-permute-start | bytes 589832 | tf_op jit(solution)/shard_map/ppermute | solution.py:215
  90.0 26.1 %collective-permute-start.18 = (bf16[256,384]{1,0:T(8,128)(2,1)S(1)}, bf16[256,384]{1,0:T(8,128)(2,1)S(1)}, u32[]{:S(2)}, u32[]{:S(2)}) collective-permute-start(bf16[256,384]{1,0:T(8,128)(2,1)S(1)} %get-tuple-element.73), channel_id=1, source_target_pairs={{0,6},{1,7},{2,8},{3,9},{4,10},{5,11},{6,12},{7,13},{8,14},{9,15},... | collective-permute-start | bytes 589832 | tf_op jit(solution)/shard_map/ppermute | solution.py:215
  94.7 21.4 %copy-start.1 = (bf16[1024,1024]{1,0:T(8,128)(2,1)S(1)}, bf16[1024,1024]{1,0:T(8,128)(2,1)}, u32[]{:S(2)}) copy-start(bf16[1024,1024]{1,0:T(8,128)(2,1)} %refs_4_.1) | copy-start | bytes 6291460

commit v6 on v5

--- a/solution.py
+++ b/solution.py
@@ -19,7 +19,7 @@
 ANY = pl.BlockSpec(memory_space=pl.ANY)
 VMEM = pl.BlockSpec(memory_space=pltpu.VMEM)
 SMEM = pl.BlockSpec(memory_space=pltpu.SMEM)
-LIMIT = pltpu.CompilerParams(vmem_limit_bytes=48 << 20)
+LIMIT = pltpu.CompilerParams(vmem_limit_bytes=30 << 20)
 
 
 def passed_along(shard, axis, by):

time: 121 us -> 115 us (0.950); the launches traced: 120 us -> 116 us
  Pallas kernels: 24.3 us -> 17.8 us
  waiting for transfers between devices: 30.3 us -> 32.7 us
    pallas_call x8, Pallas kernels: 24.3 us -> 17.8 us  [call(): pl.pallas_call(kernel, out_shape=outs, in_specs=[SMEM] * len(scalars) + [...]
    ppermute x21, waiting for transfers between devices: 27.7 us -> 30.1 us  [by_chips(): return lax.ppermute(shard, 'blk', pairs)]
    unnamed x19 -> x21, local copies, waits for them, and re-layouts: 6.44 us -> 6.45 us
  transfers between devices with their start and end apart: 23 -> 23, of which waited for: 10 -> 11; matrix products, arithmetic and copies ran while one was open for 2% -> 2% of each run, Pallas kernels for 5% -> 3%
where the time goes in v6:
time: 115 us; the launch traced here: 116 us
  starting transfers between devices  57.2 us (50%)
  waiting for transfers between devices  32.7 us (28%)
  Pallas kernels  17.8 us (15%)
  local copies, waits for them, and re-layouts  7.42 us (6%)
    ppermute x21, starting transfers between devices, by_chips(): return lax.ppermute(shard, 'blk', pairs)  57.1 us
    ppermute x21, waiting for transfers between devices, by_chips(): return lax.ppermute(shard, 'blk', pairs)  30.1 us
    pallas_call x8, Pallas kernels, call(): pl.pallas_call(kernel, out_shape=outs, in_specs=[SMEM] * len(scalars) + [...  17.8 us
    unnamed x21, local copies, waits for them, and re-layouts  6.45 us
    ppermute x2, waiting for transfers between devices, across_cores(): lax.ppermute(shard, 'blk', [(i, i ^ 1) for i in range(chips * CORES)])  2.65 us
  transfers between devices with their start and end apart: 23, of which 11 were waited for; matrix products, arithmetic and copies ran while one was open for 2% of the time, Pallas kernels for 3%

profile of v6, /device:TPU:0, one launch (start us, length us, event | category | flops | bytes accessed | tf_op | source)
XLA Modules:
  0.0 115.6 jit_solution(1858729272349926683)
XLA Ops:
  0.0 1.0 copy-done.4
  1.0 1.0 copy-done.5
  2.1 0.5 shard_map.100
  2.6 3.0 %collective-permute-start = (bf16[256,256]{1,0:T(8,128)(2,1)S(1)}, bf16[256,256]{1,0:T(8,128)(2,1)S(1)}, u32[]{:S(2)}, u32[]{:S(2)}) collective-permute-start(bf16[256,256]{1,0:T(8,128)(2,1)S(1)} %get-tuple-element.43), channel_id=1, source_target_pairs={{0,2},{1,3},{2,4},{3,5},{4,6},{5,7},{6,8},{7,9},{8,10},{9,11},{10,... | collective-permute-start | bytes 393224 | tf_op jit(solution)/shard_map/ppermute | solution.py:215
  5.5 1.6 %collective-permute-start.1 = (bf16[256,256]{1,0:T(8,128)(2,1)S(1)}, bf16[256,256]{1,0:T(8,128)(2,1)S(1)}, u32[]{:S(2)}, u32[]{:S(2)}) collective-permute-start(bf16[256,256]{1,0:T(8,128)(2,1)S(1)} %get-tuple-element.44), channel_id=1, source_target_pairs={{0,4},{1,5},{2,6},{3,7},{4,8},{5,9},{6,10},{7,11},{8,12},{9,13},{1... | collective-permute-start | bytes 393224 | tf_op jit(solution)/shard_map/ppermute | solution.py:215
  7.1 2.6 %collective-permute-start.2 = (bf16[256,256]{1,0:T(8,128)(2,1)S(1)}, bf16[256,256]{1,0:T(8,128)(2,1)S(1)}, u32[]{:S(2)}, u32[]{:S(2)}) collective-permute-start(bf16[256,256]{1,0:T(8,128)(2,1)S(1)} %get-tuple-element.45), channel_id=1, source_target_pairs={{0,6},{1,7},{2,8},{3,9},{4,10},{5,11},{6,12},{7,13},{8,14},{9,15},... | collective-permute-start | bytes 393224 | tf_op jit(solution)/shard_map/ppermute | solution.py:215
  9.7 1.2 %collective-permute-start.3 = (bf16[256,256]{1,0:T(8,128)(2,1)S(1)}, bf16[256,256]{1,0:T(8,128)(2,1)S(1)}, u32[]{:S(2)}, u32[]{:S(2)}) collective-permute-start(bf16[256,256]{1,0:T(8,128)(2,1)S(1)} %get-tuple-element.46), channel_id=1, source_target_pairs={{0,8},{1,9},{2,10},{3,11},{4,12},{5,13},{6,14},{7,15},{8,0},{9,1},... | collective-permute-start | bytes 393224 | tf_op jit(solution)/shard_map/ppermute | solution.py:215
  10.9 2.6 %collective-permute-start.4 = (bf16[256,256]{1,0:T(8,128)(2,1)S(1)}, bf16[256,256]{1,0:T(8,128)(2,1)S(1)}, u32[]{:S(2)}, u32[]{:S(2)}) collective-permute-start(bf16[256,256]{1,0:T(8,128)(2,1)S(1)} %get-tuple-element.47), channel_id=1, source_target_pairs={{0,10},{1,11},{2,12},{3,13},{4,14},{5,15},{6,0},{7,1},{8,2},{9,3},... | collective-permute-start | bytes 393224 | tf_op jit(solution)/shard_map/ppermute | solution.py:215
  13.5 1.4 %collective-permute-start.5 = (bf16[256,256]{1,0:T(8,128)(2,1)S(1)}, bf16[256,256]{1,0:T(8,128)(2,1)S(1)}, u32[]{:S(2)}, u32[]{:S(2)}) collective-permute-start(bf16[256,256]{1,0:T(8,128)(2,1)S(1)} %get-tuple-element.48), channel_id=1, source_target_pairs={{0,12},{1,13},{2,14},{3,15},{4,0},{5,1},{6,2},{7,3},{8,4},{9,5},{1... | collective-permute-start | bytes 393224 | tf_op jit(solution)/shard_map/ppermute | solution.py:215
  14.9 2.0 %collective-permute-start.6 = (bf16[256,256]{1,0:T(8,128)(2,1)S(1)}, bf16[256,256]{1,0:T(8,128)(2,1)S(1)}, u32[]{:S(2)}, u32[]{:S(2)}) collective-permute-start(bf16[256,256]{1,0:T(8,128)(2,1)S(1)} %get-tuple-element.49), channel_id=1, source_target_pairs={{0,14},{1,15},{2,0},{3,1},{4,2},{5,3},{6,4},{7,5},{8,6},{9,7},{10,... | collective-permute-start | bytes 393224 | tf_op jit(solution)/shard_map/ppermute | solution.py:215
  17.0 1.6 %copy-done.3 = bf16[1024,1024]{1,0:T(8,128)(2,1)S(1)} copy-done((bf16[1024,1024]{1,0:T(8,128)(2,1)S(1)}, bf16[1024,1024]{1,0:T(8,128)(2,1)}, u32[]{:S(2)}) %copy-start.3) | copy-done | bytes 2097176
  18.6 1.0 copy-done.6
  19.6 1.0 copy-done.7
  20.7 1.8 %shard_map.101 = (bf16[256,256]{1,0:T(8,128)(2,1)S(1)}, bf16[256,256]{1,0:T(8,128)(2,1)}, bf16[256,256]{1,0:T(8,128)(2,1)S(1)}, bf16[256,256]{1,0:T(8,128)(2,1)S...) custom-call(s32[1]{0:T(128)} %bitcast.chip_ref, ...), custom_call_target="tpu_custom_call" | custom-call | tf_op jit(solution)/shard_map/pallas_call | solution.py:200
  22.5 1.0 collective-permute-done.2.refs_3_
  23.5 0.3 collective-permute-done.3.refs_4_
  24.0 4.3 %collective-permute-start.8 = (bf16[256,256]{1,0:T(8,128)(2,1)}, bf16[256,256]{1,0:T(8,128)(2,1)S(1)}, u32[]{:S(2)}, u32[]{:S(2)}) collective-permute-start(bf16[256,256]{1,0:T(8,128)(2,1)} %get-tuple-element.51), channel_id=1, source_target_pairs={{0,2},{1,3},{2,4},{3,5},{4,6},{5,7},{6,8},{7,9},{8,10},{9,11},{10,... | collective-permute-start | bytes 393224 | tf_op jit(solution)/shard_map/ppermute | solution.py:215
  28.3 6.0 %collective-permute-start.9 = (bf16[256,256]{1,0:T(8,128)(2,1)S(1)}, bf16[256,256]{1,0:T(8,128)(2,1)S(1)}, u32[]{:S(2)}, u32[]{:S(2)}) collective-permute-start(bf16[256,256]{1,0:T(8,128)(2,1)S(1)} %get-tuple-element.52), channel_id=1, source_target_pairs={{0,4},{1,5},{2,6},{3,7},{4,8},{5,9},{6,10},{7,11},{8,12},{9,13},{1... | collective-permute-start | bytes 393224 | tf_op jit(solution)/shard_map/ppermute | solution.py:215
  34.3 2.9 %collective-permute-start.10 = (bf16[256,256]{1,0:T(8,128)(2,1)S(1)}, bf16[256,256]{1,0:T(8,128)(2,1)S(1)}, u32[]{:S(2)}, u32[]{:S(2)}) collective-permute-start(bf16[256,256]{1,0:T(8,128)(2,1)S(1)} %get-tuple-element.53), channel_id=1, source_target_pairs={{0,6},{1,7},{2,8},{3,9},{4,10},{5,11},{6,12},{7,13},{8,14},{9,15},... | collective-permute-start | bytes 393224 | tf_op jit(solution)/shard_map/ppermute | solution.py:215
  37.2 0.1 reshape.36
  37.3 0.1 reshape.37.count_ref
  37.4 0.7 copy.13
  38.1 0.7 constant_dynamic-slice_fusion
  38.8 0.1 squeeze.6
  38.9 0.5 collective-permute-done.8.refs_3_
  39.4 2.1 %collective-permute-start.12 = (bf16[256,256]{1,0:T(8,128)(2,1)S(1)}, bf16[256,256]{1,0:T(8,128)(2,1)S(1)}, u32[]{:S(2)}, u32[]{:S(2)}) collective-permute-start(bf16[256,256]{1,0:T(8,128)(2,1)S(1)} %get-tuple-element.55), channel_id=1, source_target_pairs={{0,10},{1,11},{2,12},{3,13},{4,14},{5,15},{6,0},{7,1},{8,2},{9,3},... | collective-permute-start | bytes 393224 | tf_op jit(solution)/shard_map/ppermute | solution.py:215
  41.5 1.6 %collective-permute-start.13 = (bf16[256,256]{1,0:T(8,128)(2,1)S(1)}, bf16[256,256]{1,0:T(8,128)(2,1)S(1)}, u32[]{:S(2)}, u32[]{:S(2)}) collective-permute-start(bf16[256,256]{1,0:T(8,128)(2,1)S(1)} %get-tuple-element.56), channel_id=1, source_target_pairs={{0,12},{1,13},{2,14},{3,15},{4,0},{5,1},{6,2},{7,3},{8,4},{9,5},{1... | collective-permute-start | bytes 393224 | tf_op jit(solution)/shard_map/ppermute | solution.py:215
  43.1 13.0 %collective-permute-start.14 = (bf16[256,256]{1,0:T(8,128)(2,1)S(1)}, bf16[256,256]{1,0:T(8,128)(2,1)S(1)}, u32[]{:S(2)}, u32[]{:S(2)}) collective-permute-start(bf16[256,256]{1,0:T(8,128)(2,1)S(1)} %get-tuple-element.57), channel_id=1, source_target_pairs={{0,14},{1,15},{2,0},{3,1},{4,2},{5,3},{6,4},{7,5},{8,6},{9,7},{10,... | collective-permute-start | bytes 393224 | tf_op jit(solution)/shard_map/ppermute | solution.py:215
  56.2 0.2 convert_reduce_fusion
  56.3 0.1 select_reduce_fusion.order_ref
  56.4 0.4 shard_map.103
  56.9 1.8 %collective-permute-done.14.refs_9_ = bf16[256,256]{1,0:T(8,128)(2,1)S(1)} collective-permute-done((bf16[256,256]{1,0:T(8,128)(2,1)S(1)}, bf16[256,256]{1,0:T(8,128)(2,1)S(1)}, u32[]{:S(2)}, u32[]{:S(2)}) %collective-permute-start.14) | collective-permute-done | bytes 131104 | tf_op jit(solution)/shard_map/ppermute | solution.py:215
  58.7 11.0 %shard_map.104 = (bf16[2048,128]{1,0:T(8,128)(2,1)S(1)}, f32[4096,256]{1,0:T(8,128)S(1)}, bf16[2048,256]{1,0:T(8,128)(2,1)S(1)}) custom-call(s32[1]{0:T(128)} %bitcast.chip_ref, s32[128]{0:T(128)S(1)} %fusion.table_ref, s32[16]{0:T(128)S(1)} %reshape.37.count_ref, s32[16]{0:T(128)S(1)} %select_reduce_fusion.order_ref, ...), custom_call_target="tpu_custom_call" | custom-call | tf_op jit(solution)/shard_map/pallas_call | solution.py:200
  69.8 2.6 %collective-permute-done.15.other_ref = bf16[2048,256]{1,0:T(8,128)(2,1)S(1)} collective-permute-done((bf16[2048,256]{1,0:T(8,128)(2,1)S(1)}, bf16[2048,256]{1,0:T(8,128)(2,1)S(1)}, u32[]{:S(2)}, u32[]{:S(2)}) %collective-permute-start.15) | collective-permute-done | bytes 1048608 | tf_op jit(solution)/shard_map/ppermute | solution.py:221
  72.4 0.3 shard_map.105
  72.8 5.2 %collective-permute-start.19 = (bf16[256,384]{1,0:T(8,128)(2,1)S(1)}, bf16[256,384]{1,0:T(8,128)(2,1)S(1)}, u32[]{:S(2)}, u32[]{:S(2)}) collective-permute-start(bf16[256,384]{1,0:T(8,128)(2,1)S(1)} %get-tuple-element.75), channel_id=1, source_target_pairs={{0,14},{1,15},{2,0},{3,1},{4,2},{5,3},{6,4},{7,5},{8,6},{9,7},{10,... | collective-permute-start | bytes 589832 | tf_op jit(solution)/shard_map/ppermute | solution.py:215
  78.0 2.0 %collective-permute-start.21 = (bf16[256,384]{1,0:T(8,128)(2,1)S(1)}, bf16[256,384]{1,0:T(8,128)(2,1)S(1)}, u32[]{:S(2)}, u32[]{:S(2)}) collective-permute-start(bf16[256,384]{1,0:T(8,128)(2,1)S(1)} %get-tuple-element.77), channel_id=1, source_target_pairs={{0,4},{1,5},{2,6},{3,7},{4,8},{5,9},{6,10},{7,11},{8,12},{9,13},{1... | collective-permute-start | bytes 589832 | tf_op jit(solution)/shard_map/ppermute | solution.py:215
  80.0 3.3 %collective-permute-start.16 = (bf16[256,384]{1,0:T(8,128)(2,1)S(1)}, bf16[256,384]{1,0:T(8,128)(2,1)S(1)}, u32[]{:S(2)}, u32[]{:S(2)}) collective-permute-start(bf16[256,384]{1,0:T(8,128)(2,1)S(1)} %get-tuple-element.71), channel_id=1, source_target_pairs={{0,10},{1,11},{2,12},{3,13},{4,14},{5,15},{6,0},{7,1},{8,2},{9,3},... | collective-permute-start | bytes 589832 | tf_op jit(solution)/shard_map/ppermute | solution.py:215
  83.3 0.6 collective-permute-start.17
  83.8 3.7 %collective-permute-done.20.refs_2_ = bf16[256,384]{1,0:T(8,128)(2,1)S(1)} collective-permute-done((bf16[256,384]{1,0:T(8,128)(2,1)S(1)}, bf16[256,384]{1,0:T(8,128)(2,1)S(1)}, u32[]{:S(2)}, u32[]{:S(2)}) %collective-permute-start.20) | collective-permute-done | bytes 196640 | tf_op jit(solution)/shard_map/ppermute | solution.py:215
  87.5 1.6 %collective-permute-start.18 = (bf16[256,384]{1,0:T(8,128)(2,1)S(1)}, bf16[256,384]{1,0:T(8,128)(2,1)S(1)}, u32[]{:S(2)}, u32[]{:S(2)}) collective-permute-start(bf16[256,384]{1,0:T(8,128)(2,1)S(1)} %get-tuple-element.73), channel_id=1, source_target_pairs={{0,6},{1,7},{2,8},{3,9},{4,10},{5,11},{6,12},{7,13},{8,14},{9,15},... | collective-permute-start | bytes 589832 | tf_op jit(solution)/shard_map/ppermute | solution.py:215
  89.1 2.6 %collective-permute-done.21.refs_3_ = bf16[256,384]{1,0:T(8,128)(2,1)S(1)} collective-permute-done((bf16[256,384]{1,0:T(8,128)(2,1)S(1)}, bf16[256,384]{1,0:T(8,128)(2,1)S(1)}, u32[]{:S(2)}, u32[]{:S(2)}) %collective-permute-start.21) | collective-permute-done | bytes 196640 | tf_op jit(solution)/shard_map/ppermute | solution.py:215
  91.7 0.5 collective-permute-done.22.refs_4_
  92.2 1.7 %shard_map.106.refs_6_ = f32[256,1024]{1,0:T(8,128)S(1)} custom-call(s32[1]{0:T(128)} %bitcast.chip_ref, bf16[256,384]{1,0:T(8,128)(2,1)S(1)} %get-tuple-element.74.refs_0_, bf16[256,384]{1,0:T(8,128)(2,1)S(1)} %collective-permute-done.19.refs_1_, bf16[256,384]{1,0:T(8,128)(2,1)S(1)} %collective-permute-done.20.refs_2_, ...), custom_call_target="tpu_custom_call" | custom-call | tf_op jit(solution)/shard_map/pallas_call | solution.py:200
  93.9 2.0 %collective-permute-done.16.refs_0_ = bf16[256,384]{1,0:T(8,128)(2,1)S(1)} collective-permute-done((bf16[256,384]{1,0:T(8,128)(2,1)S(1)}, bf16[256,384]{1,0:T(8,128)(2,1)S(1)}, u32[]{:S(2)}, u32[]{:S(2)}) %collective-permute-start.16) | collective-permute-done | bytes 196640 | tf_op jit(solution)/shard_map/ppermute | solution.py:215
  95.9 14.5 %collective-permute-done.17.refs_1_ = bf16[256,384]{1,0:T(8,128)(2,1)S(1)} collective-permute-done((bf16[256,384]{1,0:T(8,128)(2,1)S(1)}, bf16[256,384]{1,0:T(8,128)(2,1)S(1)}, u32[]{:S(2)}, u32[]{:S(2)}) %collective-permute-start.17) | collective-permute-done | bytes 196640 | tf_op jit(solution)/shard_map/ppermute | solution.py:215
  110.5 3.2 %collective-permute-done.18.refs_2_ = bf16[256,384]{1,0:T(8,128)(2,1)S(1)} collective-permute-done((bf16[256,384]{1,0:T(8,128)(2,1)S(1)}, bf16[256,384]{1,0:T(8,128)(2,1)S(1)}, u32[]{:S(2)}, u32[]{:S(2)}) %collective-permute-start.18) | collective-permute-done | bytes 196640 | tf_op jit(solution)/shard_map/ppermute | solution.py:215
  113.6 2.0 %shard_map.107 = bf16[256,1024]{1,0:T(8,128)(2,1)} custom-call(s32[1]{0:T(128)} %bitcast.chip_ref, bf16[256,384]{1,0:T(8,128)(2,1)S(1)} %collective-permute-done.16.refs_0_, bf16[256,384]{1,0:T(8,128)(2,1)S(1)} %collective-permute-done.17.refs_1_, bf16[256,384]{1,0:T(8,128)(2,1)S(1)} %collective-permute-done.18.refs_2_, bf16[1024,1024]{1,0:T(8,128)(2,1)S(1)} %copy-done, ...), custom_call_target="tpu_custom_call" | custom-call | tf_op jit(solution)/shard_map/pallas_call | solution.py:200
  (36 shorter events, 0.3 us)
Async XLA Ops:
  0.0 1.0 copy-start.4
  1.0 1.0 copy-start.5
  2.6 11.0 %collective-permute-start = (bf16[256,256]{1,0:T(8,128)(2,1)S(1)}, bf16[256,256]{1,0:T(8,128)(2,1)S(1)}, u32[]{:S(2)}, u32[]{:S(2)}) collective-permute-start(bf16[256,256]{1,0:T(8,128)(2,1)S(1)} %get-tuple-element.43), channel_id=1, source_target_pairs={{0,2},{1,3},{2,4},{3,5},{4,6},{5,7},{6,8},{7,9},{8,10},{9,11},{10,... | collective-permute-start | bytes 393224 | tf_op jit(solution)/shard_map/ppermute | solution.py:215
  5.5 9.4 %collective-permute-start.1 = (bf16[256,256]{1,0:T(8,128)(2,1)S(1)}, bf16[256,256]{1,0:T(8,128)(2,1)S(1)}, u32[]{:S(2)}, u32[]{:S(2)}) collective-permute-start(bf16[256,256]{1,0:T(8,128)(2,1)S(1)} %get-tuple-element.44), channel_id=1, source_target_pairs={{0,4},{1,5},{2,6},{3,7},{4,8},{5,9},{6,10},{7,11},{8,12},{9,13},{1... | collective-permute-start | bytes 393224 | tf_op jit(solution)/shard_map/ppermute | solution.py:215
  7.1 16.3 %collective-permute-start.2 = (bf16[256,256]{1,0:T(8,128)(2,1)S(1)}, bf16[256,256]{1,0:T(8,128)(2,1)S(1)}, u32[]{:S(2)}, u32[]{:S(2)}) collective-permute-start(bf16[256,256]{1,0:T(8,128)(2,1)S(1)} %get-tuple-element.45), channel_id=1, source_target_pairs={{0,6},{1,7},{2,8},{3,9},{4,10},{5,11},{6,12},{7,13},{8,14},{9,15},... | collective-permute-start | bytes 393224 | tf_op jit(solution)/shard_map/ppermute | solution.py:215
  9.7 14.1 %collective-permute-start.3 = (bf16[256,256]{1,0:T(8,128)(2,1)S(1)}, bf16[256,256]{1,0:T(8,128)(2,1)S(1)}, u32[]{:S(2)}, u32[]{:S(2)}) collective-permute-start(bf16[256,256]{1,0:T(8,128)(2,1)S(1)} %get-tuple-element.46), channel_id=1, source_target_pairs={{0,8},{1,9},{2,10},{3,11},{4,12},{5,13},{6,14},{7,15},{8,0},{9,1},... | collective-permute-start | bytes 393224 | tf_op jit(solution)/shard_map/ppermute | solution.py:215
  10.9 12.9 %collective-permute-start.4 = (bf16[256,256]{1,0:T(8,128)(2,1)S(1)}, bf16[256,256]{1,0:T(8,128)(2,1)S(1)}, u32[]{:S(2)}, u32[]{:S(2)}) collective-permute-start(bf16[256,256]{1,0:T(8,128)(2,1)S(1)} %get-tuple-element.47), channel_id=1, source_target_pairs={{0,10},{1,11},{2,12},{3,13},{4,14},{5,15},{6,0},{7,1},{8,2},{9,3},... | collective-permute-start | bytes 393224 | tf_op jit(solution)/shard_map/ppermute | solution.py:215
  13.5 10.3 %collective-permute-start.5 = (bf16[256,256]{1,0:T(8,128)(2,1)S(1)}, bf16[256,256]{1,0:T(8,128)(2,1)S(1)}, u32[]{:S(2)}, u32[]{:S(2)}) collective-permute-start(bf16[256,256]{1,0:T(8,128)(2,1)S(1)} %get-tuple-element.48), channel_id=1, source_target_pairs={{0,12},{1,13},{2,14},{3,15},{4,0},{5,1},{6,2},{7,3},{8,4},{9,5},{1... | collective-permute-start | bytes 393224 | tf_op jit(solution)/shard_map/ppermute | solution.py:215
  14.9 8.9 %collective-permute-start.6 = (bf16[256,256]{1,0:T(8,128)(2,1)S(1)}, bf16[256,256]{1,0:T(8,128)(2,1)S(1)}, u32[]{:S(2)}, u32[]{:S(2)}) collective-permute-start(bf16[256,256]{1,0:T(8,128)(2,1)S(1)} %get-tuple-element.49), channel_id=1, source_target_pairs={{0,14},{1,15},{2,0},{3,1},{4,2},{5,3},{6,4},{7,5},{8,6},{9,7},{10,... | collective-permute-start | bytes 393224 | tf_op jit(solution)/shard_map/ppermute | solution.py:215
  17.0 1.6 %copy-start.3 = (bf16[1024,1024]{1,0:T(8,128)(2,1)S(1)}, bf16[1024,1024]{1,0:T(8,128)(2,1)}, u32[]{:S(2)}) copy-start(bf16[1024,1024]{1,0:T(8,128)(2,1)} %weight_ref.1) | copy-start | bytes 6291460
  18.6 1.0 copy-start.6
  19.6 1.0 copy-start.7
  20.7 16.5 %copy-start.9 = (s32[32]{0:T(128)S(1)}, s32[32]{0:T(128)}, u32[]{:S(2)}) copy-start(s32[32]{0:T(128)} %param.19) | copy-start | bytes 388
  20.7 16.7 %copy-start.8 = (s32[32,8]{0,1:T(8,128)S(1)}, s32[32,8]{0,1:T(8,128)}, u32[]{:S(2)}) copy-start(s32[32,8]{0,1:T(8,128)} %param.18) | copy-start | bytes 3076
  23.9 19.3 %collective-permute-start.7 = (bf16[2048,256]{1,0:T(8,128)(2,1)S(1)}, bf16[2048,256]{1,0:T(8,128)(2,1)S(1)}, u32[]{:S(2)}, u32[]{:S(2)}) collective-permute-start(bf16[2048,256]{1,0:T(8,128)(2,1)S(1)} %shard_map.102.own_ref), channel_id=1, source_target_pairs={{0,1},{1,0},{2,3},{3,2},{4,5},{5,4},{6,7},{7,6},{8,9},{9,8},{10,11... | collective-permute-start | bytes 3145736 | tf_op jit(solution)/shard_map/ppermute | solution.py:221
  24.0 15.4 %collective-permute-start.8 = (bf16[256,256]{1,0:T(8,128)(2,1)}, bf16[256,256]{1,0:T(8,128)(2,1)S(1)}, u32[]{:S(2)}, u32[]{:S(2)}) collective-permute-start(bf16[256,256]{1,0:T(8,128)(2,1)} %get-tuple-element.51), channel_id=1, source_target_pairs={{0,2},{1,3},{2,4},{3,5},{4,6},{5,7},{6,8},{7,9},{8,10},{9,11},{10,... | collective-permute-start | bytes 393224 | tf_op jit(solution)/shard_map/ppermute | solution.py:215
  28.3 13.2 %collective-permute-start.9 = (bf16[256,256]{1,0:T(8,128)(2,1)S(1)}, bf16[256,256]{1,0:T(8,128)(2,1)S(1)}, u32[]{:S(2)}, u32[]{:S(2)}) collective-permute-start(bf16[256,256]{1,0:T(8,128)(2,1)S(1)} %get-tuple-element.52), channel_id=1, source_target_pairs={{0,4},{1,5},{2,6},{3,7},{4,8},{5,9},{6,10},{7,11},{8,12},{9,13},{1... | collective-permute-start | bytes 393224 | tf_op jit(solution)/shard_map/ppermute | solution.py:215
  34.3 22.6 %collective-permute-start.10 = (bf16[256,256]{1,0:T(8,128)(2,1)S(1)}, bf16[256,256]{1,0:T(8,128)(2,1)S(1)}, u32[]{:S(2)}, u32[]{:S(2)}) collective-permute-start(bf16[256,256]{1,0:T(8,128)(2,1)S(1)} %get-tuple-element.53), channel_id=1, source_target_pairs={{0,6},{1,7},{2,8},{3,9},{4,10},{5,11},{6,12},{7,13},{8,14},{9,15},... | collective-permute-start | bytes 393224 | tf_op jit(solution)/shard_map/ppermute | solution.py:215
  37.2 19.7 %collective-permute-start.11 = (bf16[256,256]{1,0:T(8,128)(2,1)S(1)}, bf16[256,256]{1,0:T(8,128)(2,1)S(1)}, u32[]{:S(2)}, u32[]{:S(2)}) collective-permute-start(bf16[256,256]{1,0:T(8,128)(2,1)S(1)} %get-tuple-element.54), channel_id=1, source_target_pairs={{0,8},{1,9},{2,10},{3,11},{4,12},{5,13},{6,14},{7,15},{8,0},{9,1},... | collective-permute-start | bytes 393224 | tf_op jit(solution)/shard_map/ppermute | solution.py:215
  39.4 17.5 %collective-permute-start.12 = (bf16[256,256]{1,0:T(8,128)(2,1)S(1)}, bf16[256,256]{1,0:T(8,128)(2,1)S(1)}, u32[]{:S(2)}, u32[]{:S(2)}) collective-permute-start(bf16[256,256]{1,0:T(8,128)(2,1)S(1)} %get-tuple-element.55), channel_id=1, source_target_pairs={{0,10},{1,11},{2,12},{3,13},{4,14},{5,15},{6,0},{7,1},{8,2},{9,3},... | collective-permute-start | bytes 393224 | tf_op jit(solution)/shard_map/ppermute | solution.py:215
  41.5 15.4 %collective-permute-start.13 = (bf16[256,256]{1,0:T(8,128)(2,1)S(1)}, bf16[256,256]{1,0:T(8,128)(2,1)S(1)}, u32[]{:S(2)}, u32[]{:S(2)}) collective-permute-start(bf16[256,256]{1,0:T(8,128)(2,1)S(1)} %get-tuple-element.56), channel_id=1, source_target_pairs={{0,12},{1,13},{2,14},{3,15},{4,0},{5,1},{6,2},{7,3},{8,4},{9,5},{1... | collective-permute-start | bytes 393224 | tf_op jit(solution)/shard_map/ppermute | solution.py:215
  43.1 15.5 %collective-permute-start.14 = (bf16[256,256]{1,0:T(8,128)(2,1)S(1)}, bf16[256,256]{1,0:T(8,128)(2,1)S(1)}, u32[]{:S(2)}, u32[]{:S(2)}) collective-permute-start(bf16[256,256]{1,0:T(8,128)(2,1)S(1)} %get-tuple-element.57), channel_id=1, source_target_pairs={{0,14},{1,15},{2,0},{3,1},{4,2},{5,3},{6,4},{7,5},{8,6},{9,7},{10,... | collective-permute-start | bytes 393224 | tf_op jit(solution)/shard_map/ppermute | solution.py:215
  58.7 33.5 %copy-start.2 = (bf16[1024,1024]{1,0:T(8,128)(2,1)S(1)}, bf16[1024,1024]{1,0:T(8,128)(2,1)}, u32[]{:S(2)}) copy-start(bf16[1024,1024]{1,0:T(8,128)(2,1)} %refs_5_.3) | copy-start | bytes 6291460
  69.7 2.7 %collective-permute-start.15 = (bf16[2048,256]{1,0:T(8,128)(2,1)S(1)}, bf16[2048,256]{1,0:T(8,128)(2,1)S(1)}, u32[]{:S(2)}, u32[]{:S(2)}) collective-permute-start(bf16[2048,256]{1,0:T(8,128)(2,1)S(1)} %get-tuple-element.70), channel_id=1, source_target_pairs={{0,1},{1,0},{2,3},{3,2},{4,5},{5,4},{6,7},{7,6},{8,9},{9,8},{10,11... | collective-permute-start | bytes 3145736 | tf_op jit(solution)/shard_map/ppermute | solution.py:221
  72.4 19.8 %copy-start = (bf16[1024,1024]{1,0:T(8,128)(2,1)S(1)}, bf16[1024,1024]{1,0:T(8,128)(2,1)}, u32[]{:S(2)}) copy-start(bf16[1024,1024]{1,0:T(8,128)(2,1)} %refs_3_.1) | copy-start | bytes 6291460
  72.4 19.8 %copy-start.1 = (bf16[1024,1024]{1,0:T(8,128)(2,1)S(1)}, bf16[1024,1024]{1,0:T(8,128)(2,1)}, u32[]{:S(2)}) copy-start(bf16[1024,1024]{1,0:T(8,128)(2,1)} %refs_4_.1) | copy-start | bytes 6291460
  72.8 10.5 %collective-permute-start.19 = (bf16[256,384]{1,0:T(8,128)(2,1)S(1)}, bf16[256,384]{1,0:T(8,128)(2,1)S(1)}, u32[]{:S(2)}, u32[]{:S(2)}) collective-permute-start(bf16[256,384]{1,0:T(8,128)(2,1)S(1)} %get-tuple-element.75), channel_id=1, source_target_pairs={{0,14},{1,15},{2,0},{3,1},{4,2},{5,3},{6,4},{7,5},{8,6},{9,7},{10,... | collective-permute-start | bytes 589832 | tf_op jit(solution)/shard_map/ppermute | solution.py:215
  78.0 9.5 %collective-permute-start.20 = (bf16[256,384]{1,0:T(8,128)(2,1)S(1)}, bf16[256,384]{1,0:T(8,128)(2,1)S(1)}, u32[]{:S(2)}, u32[]{:S(2)}) collective-permute-start(bf16[256,384]{1,0:T(8,128)(2,1)S(1)} %get-tuple-element.76), channel_id=1, source_target_pairs={{0,12},{1,13},{2,14},{3,15},{4,0},{5,1},{6,2},{7,3},{8,4},{9,5},{1... | collective-permute-start | bytes 589832 | tf_op jit(solution)/shard_map/ppermute | solution.py:215
  78.0 13.7 %collective-permute-start.21 = (bf16[256,384]{1,0:T(8,128)(2,1)S(1)}, bf16[256,384]{1,0:T(8,128)(2,1)S(1)}, u32[]{:S(2)}, u32[]{:S(2)}) collective-permute-start(bf16[256,384]{1,0:T(8,128)(2,1)S(1)} %get-tuple-element.77), channel_id=1, source_target_pairs={{0,4},{1,5},{2,6},{3,7},{4,8},{5,9},{6,10},{7,11},{8,12},{9,13},{1... | collective-permute-start | bytes 589832 | tf_op jit(solution)/shard_map/ppermute | solution.py:215
  80.0 12.2 %collective-permute-start.22 = (bf16[256,384]{1,0:T(8,128)(2,1)S(1)}, bf16[256,384]{1,0:T(8,128)(2,1)S(1)}, u32[]{:S(2)}, u32[]{:S(2)}) collective-permute-start(bf16[256,384]{1,0:T(8,128)(2,1)S(1)} %get-tuple-element.78), channel_id=1, source_target_pairs={{0,2},{1,3},{2,4},{3,5},{4,6},{5,7},{6,8},{7,9},{8,10},{9,11},{10,... | collective-permute-start | bytes 589832 | tf_op jit(solution)/shard_map/ppermute | solution.py:215
  80.0 16.0 %collective-permute-start.16 = (bf16[256,384]{1,0:T(8,128)(2,1)S(1)}, bf16[256,384]{1,0:T(8,128)(2,1)S(1)}, u32[]{:S(2)}, u32[]{:S(2)}) collective-permute-start(bf16[256,384]{1,0:T(8,128)(2,1)S(1)} %get-tuple-element.71), channel_id=1, source_target_pairs={{0,10},{1,11},{2,12},{3,13},{4,14},{5,15},{6,0},{7,1},{8,2},{9,3},... | collective-permute-start | bytes 589832 | tf_op jit(solution)/shard_map/ppermute | solution.py:215
  83.3 27.2 %collective-permute-start.17 = (bf16[256,384]{1,0:T(8,128)(2,1)S(1)}, bf16[256,384]{1,0:T(8,128)(2,1)S(1)}, u32[]{:S(2)}, u32[]{:S(2)}) collective-permute-start(bf16[256,384]{1,0:T(8,128)(2,1)S(1)} %get-tuple-element.72), channel_id=1, source_target_pairs={{0,8},{1,9},{2,10},{3,11},{4,12},{5,13},{6,14},{7,15},{8,0},{9,1},... | collective-permute-start | bytes 589832 | tf_op jit(solution)/shard_map/ppermute | solution.py:215
  87.5 26.2 %collective-permute-start.18 = (bf16[256,384]{1,0:T(8,128)(2,1)S(1)}, bf16[256,384]{1,0:T(8,128)(2,1)S(1)}, u32[]{:S(2)}, u32[]{:S(2)}) collective-permute-start(bf16[256,384]{1,0:T(8,128)(2,1)S(1)} %get-tuple-element.73), channel_id=1, source_target_pairs={{0,6},{1,7},{2,8},{3,9},{4,10},{5,11},{6,12},{7,13},{8,14},{9,15},... | collective-permute-start | bytes 589832 | tf_op jit(solution)/shard_map/ppermute | solution.py:215

commit v7 on v6

--- a/solution.py
+++ b/solution.py
@@ -15,11 +15,12 @@
 CORES = 2
 WIDTHS = (2, 4, 6, 8)
 GROUP = 4
+AHEAD = (0, 4)
 CONTRACT = (((1,), (1,)), ((), ()))
 ANY = pl.BlockSpec(memory_space=pl.ANY)
 VMEM = pl.BlockSpec(memory_space=pltpu.VMEM)
 SMEM = pl.BlockSpec(memory_space=pltpu.SMEM)
-LIMIT = pltpu.CompilerParams(vmem_limit_bytes=30 << 20)
+LIMIT = pltpu.CompilerParams(vmem_limit_bytes=22 << 20)
 
 
 def passed_along(shard, axis, by):
@@ -75,7 +76,9 @@
         out_ref[rows_of(source, tokens), :] = pieces[step][...]
 
 
-def turn_kernel(blocks, own_ref, other_ref, pair_ref, turned_ref):
+def turn_kernel(blocks, own_ref, other_ref, pair_ref, turned_ref, *cleared):
+    for buf in cleared:
+        buf[...] = jnp.zeros_like(buf)
     for side, source in enumerate((own_ref, other_ref)):
         pair_ref[side * blocks * BLOCK : (side + 1) * blocks * BLOCK] = source[...]
         for block in range(blocks):
@@ -85,13 +88,11 @@
 
 
 def attention_kernel(chips, tokens, scale, chip_ref, table_ref, count_ref, order_ref, *refs):
-    pair_ref, turned_ref, pieces = refs[0], refs[1], refs[2 : 2 + chips]
-    dq_ref, total, sent_out, ask_buf, give_buf = refs[2 + chips :]
+    pair_ref, turned_ref, pieces = refs[0], refs[1], refs[5 : 5 + chips]
+    total, ask_buf, give_buf, sent_out, *dq_outs, dq_ref = refs[5 + chips :]
     blocks = chips * tokens // BLOCK
     half = blocks * BLOCK
     per_device = tokens // BLOCK
-    ask_buf[...] = jnp.zeros_like(ask_buf)
-    give_buf[...] = jnp.zeros_like(give_buf)
     for step in range(chips):
         source = rotated(chip_ref[0], chips - step, chips)
         for place in range(per_device):
@@ -102,7 +103,6 @@
             ask_buf[block, HD:, BLOCK:] = jnp.transpose(grad)
             give_buf[block, :BLOCK, :HD] = grad
             give_buf[block, BLOCK:, HD:] = query
-    total[...] = jnp.zeros_like(total)
 
     def attend(block, width):
         count = count_ref[block]
@@ -151,13 +151,17 @@
 
     lax.fori_loop(0, blocks // GROUP, one_group, 0)
     sent_out[...] = total[half:].astype(jnp.bfloat16)
-
-
-def combine_kernel(chips, tokens, scale, chip_ref, dq_ref, own_ref, other_ref, *outs):
     for step in range(chips):
         rows = rows_of(rotated(chip_ref[0], chips - step, chips), tokens)
-        outs[step][:, :HD] = dq_ref[rows, :]
+        dq_outs[step][...] = dq_ref[rows, :]
+
+
+def combine_kernel(chips, tokens, scale, chip_ref, own_ref, other_ref, *refs):
+    dqs, outs = refs[:chips], refs[chips:]
+    for step in range(chips):
+        rows = rows_of(rotated(chip_ref[0], chips - step, chips), tokens)
         summed = own_ref[rows, :] + other_ref[rows, :].astype(jnp.float32)
+        outs[step][:, :HD] = dqs[step][...]
         outs[step][:, HD : 2 * HD] = (summed[:, HD:] * scale).astype(jnp.bfloat16)
         outs[step][:, 2 * HD :] = summed[:, :HD].astype(jnp.bfloat16)
 
@@ -196,13 +200,14 @@
     f32 = functools.partial(jax.ShapeDtypeStruct, dtype=jnp.float32)
     buf16 = functools.partial(pltpu.VMEM, dtype=jnp.bfloat16)
 
-    def call(kernel, outs, scratch, scalars, *arrays, spec=VMEM):
+    def call(kernel, outs, scratch, scalars, *arrays, spec=VMEM, aliases=()):
         return pl.pallas_call(
             kernel,
             out_shape=outs,
             in_specs=[SMEM] * len(scalars) + [spec] * len(arrays),
             out_specs=jax.tree.map(lambda _: VMEM, outs),
             scratch_shapes=scratch,
+            input_output_aliases={len(scalars) + at: to for at, to in aliases},
             compiler_params=LIMIT,
         )(*scalars, *arrays)
 
@@ -239,33 +244,35 @@
     piece = [bf16((tokens, 2 * HD))] * chips
     pairs = call(
         args(pack_kernel, chips), piece, [pltpu.SemaphoreType.DMA((2 * chips,))],
-        (chip,), key_act, value_act, spec=ANY,
-    )
+        (chip,), *(pltpu.with_memory_space_constraint(x, pltpu.HBM) for x in (key_act, value_act)), spec=ANY,
+    )
+    pairs, out_grad = lax.optimization_barrier((pairs, out_grad))
     pairs = out_to(pairs)
     asks = call(args(grad_kernel, chips), piece, [], (chip,), out_grad, out_weight, query_act)
-    pairs, _ = lax.optimization_barrier((pairs, asks))
     asks = out_to(asks)
+    pairs, _ = lax.optimization_barrier((pairs, [asks[step] for step in AHEAD]))
     own_pairs = call(
         args(assemble_kernel, chips, tokens), bf16((half, 2 * HD)), [], (chip,), *pairs
     )
     other_pairs = across_cores(own_pairs)
-    both_pairs, turned = call(
-        args(turn_kernel, blocks), [bf16((2 * half, 2 * HD)), bf16((2 * blocks, HD, BLOCK))], [],
+    cleared = [f32((2 * half, 2 * HD))] + [bf16((blocks, 2 * HD, 2 * BLOCK))] * 2
+    both_pairs, turned, *cleared = call(
+        args(turn_kernel, blocks),
+        [bf16((2 * half, 2 * HD)), bf16((2 * blocks, HD, BLOCK))] + cleared, [],
         (), own_pairs, other_pairs,
     )
-    dq, own_part, sent_part = call(
+    sums, _, _, sent_part, *dqs = call(
         args(attention_kernel, chips, tokens, scale),
-        [bf16((half, HD)), f32((2 * half, 2 * HD)), bf16((half, 2 * HD))],
-        [
-            buf16((blocks, 2 * HD, 2 * BLOCK)),
-            buf16((blocks, 2 * BLOCK, 2 * HD)),
-        ],
-        (chip, table, counts, order), both_pairs, turned, *asks,
+        [*(f32(c.shape) if c.dtype == jnp.float32 else bf16(c.shape) for c in cleared)]
+        + [bf16((half, 2 * HD))] + [bf16((tokens, HD))] * chips,
+        [buf16((half, HD))],
+        (chip, table, counts, order), both_pairs, turned, *cleared, *asks,
+        aliases=[(2, 0), (3, 1), (4, 2)],
     )
     came_part = across_cores(sent_part)
     back = call(
         args(combine_kernel, chips, tokens, scale), [bf16((tokens, 3 * HD))] * chips, [],
-        (chip,), dq, own_part, came_part,
+        (chip,), sums, came_part, *dqs,
     )
     back = [back[0]] + [by_chips(back[step], chips - step) for step in range(1, chips)]
     near = [min(step, chips - step) * 4 <= chips for step in range(chips)]

time: 115 us -> 112 us (0.974)
  starting transfers between devices: 57.2 us -> 47.3 us
  waiting for transfers between devices: 32.7 us -> 42.2 us
  local copies, waits for them, and re-layouts: 7.42 us -> 5.35 us
  Pallas kernels: 17.8 us -> 16.5 us
    ppermute x21, starting transfers between devices: 57.1 us -> 45.3 us  [by_chips(): return lax.ppermute(shard, 'blk', pairs)]
    ppermute x21, waiting for transfers between devices: 30.1 us -> 39.9 us  [by_chips(): return lax.ppermute(shard, 'blk', pairs)]
    unnamed x21 -> x17, local copies, waits for them, and re-layouts: 6.45 us -> 4.38 us
    ppermute x2, starting transfers between devices: 0.14 us -> 2.02 us  [across_cores(): lax.ppermute(shard, 'blk', [(i, i ^ 1) for i in range(chips * CORES)])]
    pallas_call x8, Pallas kernels: 17.8 us -> 16.5 us  [call(): pl.pallas_call(kernel, out_shape=outs, in_specs=[SMEM] * len(scalars) + [...]
  transfers between devices with their start and end apart: 23 -> 23, of which waited for: 11 -> 11; matrix products, arithmetic and copies ran while one was open for 2% -> 2% of each run, Pallas kernels for 3% -> 4%
where the time goes in v7:
time: 112 us
  starting transfers between devices  47.3 us (42%)
  waiting for transfers between devices  42.2 us (38%)
  Pallas kernels  16.5 us (15%)
  local copies, waits for them, and re-layouts  5.35 us (5%)
    ppermute x21, starting transfers between devices, by_chips(): return lax.ppermute(shard, 'blk', pairs)  45.3 us
    ppermute x21, waiting for transfers between devices, by_chips(): return lax.ppermute(shard, 'blk', pairs)  39.9 us
    pallas_call x8, Pallas kernels, call(): pl.pallas_call(kernel, out_shape=outs, in_specs=[SMEM] * len(scalars) + [...  16.5 us
    unnamed x17, local copies, waits for them, and re-layouts  4.38 us
    ppermute x2, waiting for transfers between devices, across_cores(): lax.ppermute(shard, 'blk', [(i, i ^ 1) for i in range(chips * CORES)])  2.29 us
  transfers between devices with their start and end apart: 23, of which 11 were waited for; matrix products, arithmetic and copies ran while one was open for 2% of the time, Pallas kernels for 4%

profile of v7, /device:TPU:0, one launch (start us, length us, event | category | flops | bytes accessed | tf_op | source)
XLA Modules:
  0.0 111.8 jit_solution(9230462356573670240)
XLA Ops:
  0.0 1.4 %shard_map.100 = (bf16[256,256]{1,0:T(8,128)(2,1)S(1)}, bf16[256,256]{1,0:T(8,128)(2,1)S(1)}, bf16[256,256]{1,0:T(8,128)(2,1)S(1)}, bf16[256,256]{1,0:T(8,128)(2...) custom-call(s32[1]{0:T(128)} %bitcast.chip_ref, ...), custom_call_target="tpu_custom_call" | custom-call | tf_op jit(solution)/shard_map/pallas_call | solution.py:204
  1.4 3.0 %collective-permute-start = (bf16[256,256]{1,0:T(8,128)(2,1)S(1)}, bf16[256,256]{1,0:T(8,128)(2,1)S(1)}, u32[]{:S(2)}, u32[]{:S(2)}) collective-permute-start(bf16[256,256]{1,0:T(8,128)(2,1)S(1)} %get-tuple-element.70), channel_id=1, source_target_pairs={{0,2},{1,3},{2,4},{3,5},{4,6},{5,7},{6,8},{7,9},{8,10},{9,11},{10,... | collective-permute-start | bytes 393224 | tf_op jit(solution)/shard_map/ppermute | solution.py:220
  4.4 1.6 %collective-permute-start.1 = (bf16[256,256]{1,0:T(8,128)(2,1)S(1)}, bf16[256,256]{1,0:T(8,128)(2,1)S(1)}, u32[]{:S(2)}, u32[]{:S(2)}) collective-permute-start(bf16[256,256]{1,0:T(8,128)(2,1)S(1)} %get-tuple-element.71), channel_id=1, source_target_pairs={{0,4},{1,5},{2,6},{3,7},{4,8},{5,9},{6,10},{7,11},{8,12},{9,13},{1... | collective-permute-start | bytes 393224 | tf_op jit(solution)/shard_map/ppermute | solution.py:220
  6.0 2.6 %collective-permute-start.2 = (bf16[256,256]{1,0:T(8,128)(2,1)S(1)}, bf16[256,256]{1,0:T(8,128)(2,1)S(1)}, u32[]{:S(2)}, u32[]{:S(2)}) collective-permute-start(bf16[256,256]{1,0:T(8,128)(2,1)S(1)} %get-tuple-element.72), channel_id=1, source_target_pairs={{0,6},{1,7},{2,8},{3,9},{4,10},{5,11},{6,12},{7,13},{8,14},{9,15},... | collective-permute-start | bytes 393224 | tf_op jit(solution)/shard_map/ppermute | solution.py:220
  8.6 1.2 %collective-permute-start.3 = (bf16[256,256]{1,0:T(8,128)(2,1)S(1)}, bf16[256,256]{1,0:T(8,128)(2,1)S(1)}, u32[]{:S(2)}, u32[]{:S(2)}) collective-permute-start(bf16[256,256]{1,0:T(8,128)(2,1)S(1)} %get-tuple-element.73), channel_id=1, source_target_pairs={{0,8},{1,9},{2,10},{3,11},{4,12},{5,13},{6,14},{7,15},{8,0},{9,1},... | collective-permute-start | bytes 393224 | tf_op jit(solution)/shard_map/ppermute | solution.py:220
  9.8 2.6 %collective-permute-start.4 = (bf16[256,256]{1,0:T(8,128)(2,1)S(1)}, bf16[256,256]{1,0:T(8,128)(2,1)S(1)}, u32[]{:S(2)}, u32[]{:S(2)}) collective-permute-start(bf16[256,256]{1,0:T(8,128)(2,1)S(1)} %get-tuple-element.74), channel_id=1, source_target_pairs={{0,10},{1,11},{2,12},{3,13},{4,14},{5,15},{6,0},{7,1},{8,2},{9,3},... | collective-permute-start | bytes 393224 | tf_op jit(solution)/shard_map/ppermute | solution.py:220
  12.4 1.6 %copy-done.3 = bf16[1024,1024]{1,0:T(8,128)(2,1)S(1)} copy-done((bf16[1024,1024]{1,0:T(8,128)(2,1)S(1)}, bf16[1024,1024]{1,0:T(8,128)(2,1)}, u32[]{:S(2)}) %copy-start.3) | copy-done | bytes 2097176
  14.0 1.0 copy-done.4
  15.1 1.0 copy-done.5
  16.1 1.8 %shard_map.101 = (bf16[256,256]{1,0:T(8,128)(2,1)S(1)}, bf16[256,256]{1,0:T(8,128)(2,1)}, bf16[256,256]{1,0:T(8,128)(2,1)S(1)}, bf16[256,256]{1,0:T(8,128)(2,1)S...) custom-call(s32[1]{0:T(128)} %bitcast.chip_ref, ...), custom_call_target="tpu_custom_call" | custom-call | tf_op jit(solution)/shard_map/pallas_call | solution.py:204
  17.9 1.3 %collective-permute-start.5 = (bf16[256,256]{1,0:T(8,128)(2,1)S(1)}, bf16[256,256]{1,0:T(8,128)(2,1)S(1)}, u32[]{:S(2)}, u32[]{:S(2)}) collective-permute-start(bf16[256,256]{1,0:T(8,128)(2,1)S(1)} %get-tuple-element.75), channel_id=1, source_target_pairs={{0,12},{1,13},{2,14},{3,15},{4,0},{5,1},{6,2},{7,3},{8,4},{9,5},{1... | collective-permute-start | bytes 393224 | tf_op jit(solution)/shard_map/ppermute | solution.py:220
  19.3 1.4 %collective-permute-start.6 = (bf16[256,256]{1,0:T(8,128)(2,1)S(1)}, bf16[256,256]{1,0:T(8,128)(2,1)S(1)}, u32[]{:S(2)}, u32[]{:S(2)}) collective-permute-start(bf16[256,256]{1,0:T(8,128)(2,1)S(1)} %get-tuple-element.76), channel_id=1, source_target_pairs={{0,14},{1,15},{2,0},{3,1},{4,2},{5,3},{6,4},{7,5},{8,6},{9,7},{10,... | collective-permute-start | bytes 393224 | tf_op jit(solution)/shard_map/ppermute | solution.py:220
  20.7 1.7 %collective-permute-done.2.refs_3_ = bf16[256,256]{1,0:T(8,128)(2,1)S(1)} collective-permute-done((bf16[256,256]{1,0:T(8,128)(2,1)S(1)}, bf16[256,256]{1,0:T(8,128)(2,1)S(1)}, u32[]{:S(2)}, u32[]{:S(2)}) %collective-permute-start.2) | collective-permute-done | bytes 131104 | tf_op jit(solution)/shard_map/ppermute | solution.py:220
  22.4 5.4 %collective-permute-start.7 = (bf16[256,256]{1,0:T(8,128)(2,1)S(1)}, bf16[256,256]{1,0:T(8,128)(2,1)S(1)}, u32[]{:S(2)}, u32[]{:S(2)}) collective-permute-start(bf16[256,256]{1,0:T(8,128)(2,1)S(1)} %get-tuple-element.79), channel_id=1, source_target_pairs={{0,8},{1,9},{2,10},{3,11},{4,12},{5,13},{6,14},{7,15},{8,0},{9,1},... | collective-permute-start | bytes 393224 | tf_op jit(solution)/shard_map/ppermute | solution.py:220
  27.8 0.4 collective-permute-done.5.refs_6_
  28.3 8.3 %collective-permute-done.7.refs_9_ = bf16[256,256]{1,0:T(8,128)(2,1)S(1)} collective-permute-done((bf16[256,256]{1,0:T(8,128)(2,1)S(1)}, bf16[256,256]{1,0:T(8,128)(2,1)S(1)}, u32[]{:S(2)}, u32[]{:S(2)}) %collective-permute-start.7) | collective-permute-done | bytes 131104 | tf_op jit(solution)/shard_map/ppermute | solution.py:220
  36.7 0.3 collective-permute-start.9
  37.1 0.2 collective-permute-start.10
  37.3 3.1 %collective-permute-start.11 = (bf16[256,256]{1,0:T(8,128)(2,1)S(1)}, bf16[256,256]{1,0:T(8,128)(2,1)S(1)}, u32[]{:S(2)}, u32[]{:S(2)}) collective-permute-start(bf16[256,256]{1,0:T(8,128)(2,1)S(1)} %get-tuple-element.95), channel_id=1, source_target_pairs={{0,6},{1,7},{2,8},{3,9},{4,10},{5,11},{6,12},{7,13},{8,14},{9,15},... | collective-permute-start | bytes 393224 | tf_op jit(solution)/shard_map/ppermute | solution.py:220
  40.4 1.7 %collective-permute-start.12 = (bf16[256,256]{1,0:T(8,128)(2,1)S(1)}, bf16[256,256]{1,0:T(8,128)(2,1)S(1)}, u32[]{:S(2)}, u32[]{:S(2)}) collective-permute-start(bf16[256,256]{1,0:T(8,128)(2,1)S(1)} %get-tuple-element.96), channel_id=1, source_target_pairs={{0,10},{1,11},{2,12},{3,13},{4,14},{5,15},{6,0},{7,1},{8,2},{9,3},... | collective-permute-start | bytes 393224 | tf_op jit(solution)/shard_map/ppermute | solution.py:220
  42.1 0.1 reshape.36
  42.3 0.7 copy.16
  43.0 0.7 constant_dynamic-slice_fusion
  43.7 0.1 squeeze.6
  43.8 2.4 %collective-permute-done.9.refs_6_ = bf16[256,256]{1,0:T(8,128)(2,1)S(1)} collective-permute-done((bf16[256,256]{1,0:T(8,128)(2,1)}, bf16[256,256]{1,0:T(8,128)(2,1)S(1)}, u32[]{:S(2)}, u32[]{:S(2)}) %collective-permute-start.9) | collective-permute-done | bytes 131104 | tf_op jit(solution)/shard_map/ppermute | solution.py:220
  46.2 0.3 collective-permute-start.13
  46.5 1.7 %collective-permute-start.14 = (bf16[256,256]{1,0:T(8,128)(2,1)S(1)}, bf16[256,256]{1,0:T(8,128)(2,1)S(1)}, u32[]{:S(2)}, u32[]{:S(2)}) collective-permute-start(bf16[256,256]{1,0:T(8,128)(2,1)S(1)} %get-tuple-element.98), channel_id=1, source_target_pairs={{0,14},{1,15},{2,0},{3,1},{4,2},{5,3},{6,4},{7,5},{8,6},{9,7},{10,... | collective-permute-start | bytes 393224 | tf_op jit(solution)/shard_map/ppermute | solution.py:220
  48.2 0.2 convert_reduce_fusion
  48.4 0.1 select_reduce_fusion.order_ref
  48.5 1.0 shard_map.103
  49.5 4.7 %collective-permute-done.11.refs_8_ = bf16[256,256]{1,0:T(8,128)(2,1)S(1)} collective-permute-done((bf16[256,256]{1,0:T(8,128)(2,1)S(1)}, bf16[256,256]{1,0:T(8,128)(2,1)S(1)}, u32[]{:S(2)}, u32[]{:S(2)}) %collective-permute-start.11) | collective-permute-done | bytes 131104 | tf_op jit(solution)/shard_map/ppermute | solution.py:220
  54.2 0.7 collective-permute-done.13.refs_11_
  54.9 1.5 %collective-permute-done.14.refs_12_ = bf16[256,256]{1,0:T(8,128)(2,1)S(1)} collective-permute-done((bf16[256,256]{1,0:T(8,128)(2,1)S(1)}, bf16[256,256]{1,0:T(8,128)(2,1)S(1)}, u32[]{:S(2)}, u32[]{:S(2)}) %collective-permute-start.14) | collective-permute-done | bytes 131104 | tf_op jit(solution)/shard_map/ppermute | solution.py:220
  56.4 8.3 %shard_map.104 = (f32[4096,256]{1,0:T(8,128)S(1)}, bf16[16,256,256]{2,1,0:T(8,128)(2,1)S(1)}, bf16[16,256,256]{2,1,0:T(8,128)(2,1)S(1)}, bf16[2048,256]{1,0:T(8,...) custom-call(s32[1]{0:T(128)} %bitcast.chip_ref, ...), custom_call_target="tpu_custom_call", output_to_operand_aliasing={{0}: (6, {}), {1}: (7, {}), {2}: (8, {})} | custom-call | tf_op jit(solution)/shard_map/pallas_call | solution.py:204
  64.7 2.0 %collective-permute-start.15 = (bf16[2048,256]{1,0:T(8,128)(2,1)S(1)}, bf16[2048,256]{1,0:T(8,128)(2,1)S(1)}, u32[]{:S(2)}, u32[]{:S(2)}) collective-permute-start(bf16[2048,256]{1,0:T(8,128)(2,1)S(1)} %get-tuple-element.100), channel_id=1, source_target_pairs={{0,1},{1,0},{2,3},{3,2},{4,5},{5,4},{6,7},{7,6},{8,9},{9,8},{10,11... | collective-permute-start | bytes 3145736 | tf_op jit(solution)/shard_map/ppermute | solution.py:226
  66.6 2.3 %collective-permute-done.15.other_ref = bf16[2048,256]{1,0:T(8,128)(2,1)S(1)} collective-permute-done((bf16[2048,256]{1,0:T(8,128)(2,1)S(1)}, bf16[2048,256]{1,0:T(8,128)(2,1)S(1)}, u32[]{:S(2)}, u32[]{:S(2)}) %collective-permute-start.15) | collective-permute-done | bytes 1048608 | tf_op jit(solution)/shard_map/ppermute | solution.py:226
  68.9 0.3 shard_map.105
  69.2 3.6 %collective-permute-start.19 = (bf16[256,384]{1,0:T(8,128)(2,1)S(1)}, bf16[256,384]{1,0:T(8,128)(2,1)S(1)}, u32[]{:S(2)}, u32[]{:S(2)}) collective-permute-start(bf16[256,384]{1,0:T(8,128)(2,1)S(1)} %get-tuple-element.113), channel_id=1, source_target_pairs={{0,14},{1,15},{2,0},{3,1},{4,2},{5,3},{6,4},{7,5},{8,6},{9,7},{10,... | collective-permute-start | bytes 589832 | tf_op jit(solution)/shard_map/ppermute | solution.py:220
  72.9 1.2 %collective-permute-start.20 = (bf16[256,384]{1,0:T(8,128)(2,1)S(1)}, bf16[256,384]{1,0:T(8,128)(2,1)S(1)}, u32[]{:S(2)}, u32[]{:S(2)}) collective-permute-start(bf16[256,384]{1,0:T(8,128)(2,1)S(1)} %get-tuple-element.114), channel_id=1, source_target_pairs={{0,12},{1,13},{2,14},{3,15},{4,0},{5,1},{6,2},{7,3},{8,4},{9,5},{1... | collective-permute-start | bytes 589832 | tf_op jit(solution)/shard_map/ppermute | solution.py:220
  74.1 0.8 collective-permute-start.21
  74.9 4.5 %collective-permute-start.16 = (bf16[256,384]{1,0:T(8,128)(2,1)S(1)}, bf16[256,384]{1,0:T(8,128)(2,1)S(1)}, u32[]{:S(2)}, u32[]{:S(2)}) collective-permute-start(bf16[256,384]{1,0:T(8,128)(2,1)S(1)} %get-tuple-element.109), channel_id=1, source_target_pairs={{0,10},{1,11},{2,12},{3,13},{4,14},{5,15},{6,0},{7,1},{8,2},{9,3},... | collective-permute-start | bytes 589832 | tf_op jit(solution)/shard_map/ppermute | solution.py:220
  79.4 1.0 collective-permute-start.17
  80.4 1.9 %collective-permute-done.20.refs_2_ = bf16[256,384]{1,0:T(8,128)(2,1)S(1)} collective-permute-done((bf16[256,384]{1,0:T(8,128)(2,1)S(1)}, bf16[256,384]{1,0:T(8,128)(2,1)S(1)}, u32[]{:S(2)}, u32[]{:S(2)}) %collective-permute-start.20) | collective-permute-done | bytes 196640 | tf_op jit(solution)/shard_map/ppermute | solution.py:220
  82.4 7.5 %collective-permute-start.18 = (bf16[256,384]{1,0:T(8,128)(2,1)S(1)}, bf16[256,384]{1,0:T(8,128)(2,1)S(1)}, u32[]{:S(2)}, u32[]{:S(2)}) collective-permute-start(bf16[256,384]{1,0:T(8,128)(2,1)S(1)} %get-tuple-element.111), channel_id=1, source_target_pairs={{0,6},{1,7},{2,8},{3,9},{4,10},{5,11},{6,12},{7,13},{8,14},{9,15},... | collective-permute-start | bytes 589832 | tf_op jit(solution)/shard_map/ppermute | solution.py:220
  89.9 1.7 %shard_map.106.refs_6_ = f32[256,1024]{1,0:T(8,128)S(1)} custom-call(s32[1]{0:T(128)} %bitcast.chip_ref, bf16[256,384]{1,0:T(8,128)(2,1)S(1)} %get-tuple-element.112.refs_0_, bf16[256,384]{1,0:T(8,128)(2,1)S(1)} %collective-permute-done.19.refs_1_, bf16[256,384]{1,0:T(8,128)(2,1)S(1)} %collective-permute-done.20.refs_2_, ...), custom_call_target="tpu_custom_call" | custom-call | tf_op jit(solution)/shard_map/pallas_call | solution.py:204
  91.6 0.2 collective-permute-done.16.refs_0_
  91.8 18.0 %collective-permute-done.17.refs_1_ = bf16[256,384]{1,0:T(8,128)(2,1)S(1)} collective-permute-done((bf16[256,384]{1,0:T(8,128)(2,1)S(1)}, bf16[256,384]{1,0:T(8,128)(2,1)S(1)}, u32[]{:S(2)}, u32[]{:S(2)}) %collective-permute-start.17) | collective-permute-done | bytes 196640 | tf_op jit(solution)/shard_map/ppermute | solution.py:220
  109.8 2.0 %shard_map.107 = bf16[256,1024]{1,0:T(8,128)(2,1)} custom-call(s32[1]{0:T(128)} %bitcast.chip_ref, bf16[256,384]{1,0:T(8,128)(2,1)S(1)} %collective-permute-done.16.refs_0_, bf16[256,384]{1,0:T(8,128)(2,1)S(1)} %collective-permute-done.17.refs_1_, bf16[256,384]{1,0:T(8,128)(2,1)S(1)} %collective-permute-done.18.refs_2_, bf16[1024,1024]{1,0:T(8,128)(2,1)S(1)} %copy-done, ...), custom_call_target="tpu_custom_call" | custom-call | tf_op jit(solution)/shard_map/pallas_call | solution.py:204
  (32 shorter events, 0.4 us)
Async XLA Ops:
  1.4 40.9 %copy-start.6 = (s32[32,8]{0,1:T(8,128)S(1)}, s32[32,8]{0,1:T(8,128)}, u32[]{:S(2)}) copy-start(s32[32,8]{0,1:T(8,128)} %param.18) | copy-start | bytes 3076
  1.4 40.6 %copy-start.7 = (s32[32]{0:T(128)S(1)}, s32[32]{0:T(128)}, u32[]{:S(2)}) copy-start(s32[32]{0:T(128)} %param.19) | copy-start | bytes 388
  1.4 16.5 %collective-permute-start = (bf16[256,256]{1,0:T(8,128)(2,1)S(1)}, bf16[256,256]{1,0:T(8,128)(2,1)S(1)}, u32[]{:S(2)}, u32[]{:S(2)}) collective-permute-start(bf16[256,256]{1,0:T(8,128)(2,1)S(1)} %get-tuple-element.70), channel_id=1, source_target_pairs={{0,2},{1,3},{2,4},{3,5},{4,6},{5,7},{6,8},{7,9},{8,10},{9,11},{10,... | collective-permute-start | bytes 393224 | tf_op jit(solution)/shard_map/ppermute | solution.py:220
  4.4 14.8 %collective-permute-start.1 = (bf16[256,256]{1,0:T(8,128)(2,1)S(1)}, bf16[256,256]{1,0:T(8,128)(2,1)S(1)}, u32[]{:S(2)}, u32[]{:S(2)}) collective-permute-start(bf16[256,256]{1,0:T(8,128)(2,1)S(1)} %get-tuple-element.71), channel_id=1, source_target_pairs={{0,4},{1,5},{2,6},{3,7},{4,8},{5,9},{6,10},{7,11},{8,12},{9,13},{1... | collective-permute-start | bytes 393224 | tf_op jit(solution)/shard_map/ppermute | solution.py:220
  6.0 16.4 %collective-permute-start.2 = (bf16[256,256]{1,0:T(8,128)(2,1)S(1)}, bf16[256,256]{1,0:T(8,128)(2,1)S(1)}, u32[]{:S(2)}, u32[]{:S(2)}) collective-permute-start(bf16[256,256]{1,0:T(8,128)(2,1)S(1)} %get-tuple-element.72), channel_id=1, source_target_pairs={{0,6},{1,7},{2,8},{3,9},{4,10},{5,11},{6,12},{7,13},{8,14},{9,15},... | collective-permute-start | bytes 393224 | tf_op jit(solution)/shard_map/ppermute | solution.py:220
  8.6 19.2 %collective-permute-start.3 = (bf16[256,256]{1,0:T(8,128)(2,1)S(1)}, bf16[256,256]{1,0:T(8,128)(2,1)S(1)}, u32[]{:S(2)}, u32[]{:S(2)}) collective-permute-start(bf16[256,256]{1,0:T(8,128)(2,1)S(1)} %get-tuple-element.73), channel_id=1, source_target_pairs={{0,8},{1,9},{2,10},{3,11},{4,12},{5,13},{6,14},{7,15},{8,0},{9,1},... | collective-permute-start | bytes 393224 | tf_op jit(solution)/shard_map/ppermute | solution.py:220
  9.8 18.0 %collective-permute-start.4 = (bf16[256,256]{1,0:T(8,128)(2,1)S(1)}, bf16[256,256]{1,0:T(8,128)(2,1)S(1)}, u32[]{:S(2)}, u32[]{:S(2)}) collective-permute-start(bf16[256,256]{1,0:T(8,128)(2,1)S(1)} %get-tuple-element.74), channel_id=1, source_target_pairs={{0,10},{1,11},{2,12},{3,13},{4,14},{5,15},{6,0},{7,1},{8,2},{9,3},... | collective-permute-start | bytes 393224 | tf_op jit(solution)/shard_map/ppermute | solution.py:220
  12.4 1.6 %copy-start.3 = (bf16[1024,1024]{1,0:T(8,128)(2,1)S(1)}, bf16[1024,1024]{1,0:T(8,128)(2,1)}, u32[]{:S(2)}) copy-start(bf16[1024,1024]{1,0:T(8,128)(2,1)} %weight_ref.1) | copy-start | bytes 6291460
  14.0 1.0 copy-start.4
  15.1 1.0 copy-start.5
  17.9 10.3 %collective-permute-start.5 = (bf16[256,256]{1,0:T(8,128)(2,1)S(1)}, bf16[256,256]{1,0:T(8,128)(2,1)S(1)}, u32[]{:S(2)}, u32[]{:S(2)}) collective-permute-start(bf16[256,256]{1,0:T(8,128)(2,1)S(1)} %get-tuple-element.75), channel_id=1, source_target_pairs={{0,12},{1,13},{2,14},{3,15},{4,0},{5,1},{6,2},{7,3},{8,4},{9,5},{1... | collective-permute-start | bytes 393224 | tf_op jit(solution)/shard_map/ppermute | solution.py:220
  19.3 9.0 %collective-permute-start.6 = (bf16[256,256]{1,0:T(8,128)(2,1)S(1)}, bf16[256,256]{1,0:T(8,128)(2,1)S(1)}, u32[]{:S(2)}, u32[]{:S(2)}) collective-permute-start(bf16[256,256]{1,0:T(8,128)(2,1)S(1)} %get-tuple-element.76), channel_id=1, source_target_pairs={{0,14},{1,15},{2,0},{3,1},{4,2},{5,3},{6,4},{7,5},{8,6},{9,7},{10,... | collective-permute-start | bytes 393224 | tf_op jit(solution)/shard_map/ppermute | solution.py:220
  22.4 14.2 %collective-permute-start.7 = (bf16[256,256]{1,0:T(8,128)(2,1)S(1)}, bf16[256,256]{1,0:T(8,128)(2,1)S(1)}, u32[]{:S(2)}, u32[]{:S(2)}) collective-permute-start(bf16[256,256]{1,0:T(8,128)(2,1)S(1)} %get-tuple-element.79), channel_id=1, source_target_pairs={{0,8},{1,9},{2,10},{3,11},{4,12},{5,13},{6,14},{7,15},{8,0},{9,1},... | collective-permute-start | bytes 393224 | tf_op jit(solution)/shard_map/ppermute | solution.py:220
  36.6 9.9 %collective-permute-start.8 = (bf16[2048,256]{1,0:T(8,128)(2,1)S(1)}, bf16[2048,256]{1,0:T(8,128)(2,1)S(1)}, u32[]{:S(2)}, u32[]{:S(2)}) collective-permute-start(bf16[2048,256]{1,0:T(8,128)(2,1)S(1)} %shard_map.102.own_ref), channel_id=1, source_target_pairs={{0,1},{1,0},{2,3},{3,2},{4,5},{5,4},{6,7},{7,6},{8,9},{9,8},{10,11... | collective-permute-start | bytes 3145736 | tf_op jit(solution)/shard_map/ppermute | solution.py:226
  36.7 9.5 %collective-permute-start.9 = (bf16[256,256]{1,0:T(8,128)(2,1)}, bf16[256,256]{1,0:T(8,128)(2,1)S(1)}, u32[]{:S(2)}, u32[]{:S(2)}) collective-permute-start(bf16[256,256]{1,0:T(8,128)(2,1)} %get-tuple-element.93), channel_id=1, source_target_pairs={{0,2},{1,3},{2,4},{3,5},{4,6},{5,7},{6,8},{7,9},{8,10},{9,11},{10,... | collective-permute-start | bytes 393224 | tf_op jit(solution)/shard_map/ppermute | solution.py:220
  37.1 12.4 %collective-permute-start.10 = (bf16[256,256]{1,0:T(8,128)(2,1)S(1)}, bf16[256,256]{1,0:T(8,128)(2,1)S(1)}, u32[]{:S(2)}, u32[]{:S(2)}) collective-permute-start(bf16[256,256]{1,0:T(8,128)(2,1)S(1)} %get-tuple-element.94), channel_id=1, source_target_pairs={{0,4},{1,5},{2,6},{3,7},{4,8},{5,9},{6,10},{7,11},{8,12},{9,13},{1... | collective-permute-start | bytes 393224 | tf_op jit(solution)/shard_map/ppermute | solution.py:220
  37.3 16.9 %collective-permute-start.11 = (bf16[256,256]{1,0:T(8,128)(2,1)S(1)}, bf16[256,256]{1,0:T(8,128)(2,1)S(1)}, u32[]{:S(2)}, u32[]{:S(2)}) collective-permute-start(bf16[256,256]{1,0:T(8,128)(2,1)S(1)} %get-tuple-element.95), channel_id=1, source_target_pairs={{0,6},{1,7},{2,8},{3,9},{4,10},{5,11},{6,12},{7,13},{8,14},{9,15},... | collective-permute-start | bytes 393224 | tf_op jit(solution)/shard_map/ppermute | solution.py:220
  40.4 13.8 %collective-permute-start.12 = (bf16[256,256]{1,0:T(8,128)(2,1)S(1)}, bf16[256,256]{1,0:T(8,128)(2,1)S(1)}, u32[]{:S(2)}, u32[]{:S(2)}) collective-permute-start(bf16[256,256]{1,0:T(8,128)(2,1)S(1)} %get-tuple-element.96), channel_id=1, source_target_pairs={{0,10},{1,11},{2,12},{3,13},{4,14},{5,15},{6,0},{7,1},{8,2},{9,3},... | collective-permute-start | bytes 393224 | tf_op jit(solution)/shard_map/ppermute | solution.py:220
  46.2 8.7 %collective-permute-start.13 = (bf16[256,256]{1,0:T(8,128)(2,1)S(1)}, bf16[256,256]{1,0:T(8,128)(2,1)S(1)}, u32[]{:S(2)}, u32[]{:S(2)}) collective-permute-start(bf16[256,256]{1,0:T(8,128)(2,1)S(1)} %get-tuple-element.97), channel_id=1, source_target_pairs={{0,12},{1,13},{2,14},{3,15},{4,0},{5,1},{6,2},{7,3},{8,4},{9,5},{1... | collective-permute-start | bytes 393224 | tf_op jit(solution)/shard_map/ppermute | solution.py:220
  46.5 9.9 %collective-permute-start.14 = (bf16[256,256]{1,0:T(8,128)(2,1)S(1)}, bf16[256,256]{1,0:T(8,128)(2,1)S(1)}, u32[]{:S(2)}, u32[]{:S(2)}) collective-permute-start(bf16[256,256]{1,0:T(8,128)(2,1)S(1)} %get-tuple-element.98), channel_id=1, source_target_pairs={{0,14},{1,15},{2,0},{3,1},{4,2},{5,3},{6,4},{7,5},{8,6},{9,7},{10,... | collective-permute-start | bytes 393224 | tf_op jit(solution)/shard_map/ppermute | solution.py:220
  56.4 33.5 %copy-start.2 = (bf16[1024,1024]{1,0:T(8,128)(2,1)S(1)}, bf16[1024,1024]{1,0:T(8,128)(2,1)}, u32[]{:S(2)}) copy-start(bf16[1024,1024]{1,0:T(8,128)(2,1)} %refs_5_.3) | copy-start | bytes 6291460
  64.7 4.2 %collective-permute-start.15 = (bf16[2048,256]{1,0:T(8,128)(2,1)S(1)}, bf16[2048,256]{1,0:T(8,128)(2,1)S(1)}, u32[]{:S(2)}, u32[]{:S(2)}) collective-permute-start(bf16[2048,256]{1,0:T(8,128)(2,1)S(1)} %get-tuple-element.100), channel_id=1, source_target_pairs={{0,1},{1,0},{2,3},{3,2},{4,5},{5,4},{6,7},{7,6},{8,9},{9,8},{10,11... | collective-permute-start | bytes 3145736 | tf_op jit(solution)/shard_map/ppermute | solution.py:226
  68.9 21.0 %copy-start = (bf16[1024,1024]{1,0:T(8,128)(2,1)S(1)}, bf16[1024,1024]{1,0:T(8,128)(2,1)}, u32[]{:S(2)}) copy-start(bf16[1024,1024]{1,0:T(8,128)(2,1)} %refs_3_.1) | copy-start | bytes 6291460
  68.9 21.0 %copy-start.1 = (bf16[1024,1024]{1,0:T(8,128)(2,1)S(1)}, bf16[1024,1024]{1,0:T(8,128)(2,1)}, u32[]{:S(2)}) copy-start(bf16[1024,1024]{1,0:T(8,128)(2,1)} %refs_4_.1) | copy-start | bytes 6291460
  69.2 10.2 %collective-permute-start.19 = (bf16[256,384]{1,0:T(8,128)(2,1)S(1)}, bf16[256,384]{1,0:T(8,128)(2,1)S(1)}, u32[]{:S(2)}, u32[]{:S(2)}) collective-permute-start(bf16[256,384]{1,0:T(8,128)(2,1)S(1)} %get-tuple-element.113), channel_id=1, source_target_pairs={{0,14},{1,15},{2,0},{3,1},{4,2},{5,3},{6,4},{7,5},{8,6},{9,7},{10,... | collective-permute-start | bytes 589832 | tf_op jit(solution)/shard_map/ppermute | solution.py:220
  72.9 9.5 %collective-permute-start.20 = (bf16[256,384]{1,0:T(8,128)(2,1)S(1)}, bf16[256,384]{1,0:T(8,128)(2,1)S(1)}, u32[]{:S(2)}, u32[]{:S(2)}) collective-permute-start(bf16[256,384]{1,0:T(8,128)(2,1)S(1)} %get-tuple-element.114), channel_id=1, source_target_pairs={{0,12},{1,13},{2,14},{3,15},{4,0},{5,1},{6,2},{7,3},{8,4},{9,5},{1... | collective-permute-start | bytes 589832 | tf_op jit(solution)/shard_map/ppermute | solution.py:220
  74.1 15.8 %collective-permute-start.21 = (bf16[256,384]{1,0:T(8,128)(2,1)S(1)}, bf16[256,384]{1,0:T(8,128)(2,1)S(1)}, u32[]{:S(2)}, u32[]{:S(2)}) collective-permute-start(bf16[256,384]{1,0:T(8,128)(2,1)S(1)} %get-tuple-element.115), channel_id=1, source_target_pairs={{0,4},{1,5},{2,6},{3,7},{4,8},{5,9},{6,10},{7,11},{8,12},{9,13},{1... | collective-permute-start | bytes 589832 | tf_op jit(solution)/shard_map/ppermute | solution.py:220
  74.9 15.0 %collective-permute-start.22 = (bf16[256,384]{1,0:T(8,128)(2,1)S(1)}, bf16[256,384]{1,0:T(8,128)(2,1)S(1)}, u32[]{:S(2)}, u32[]{:S(2)}) collective-permute-start(bf16[256,384]{1,0:T(8,128)(2,1)S(1)} %get-tuple-element.116), channel_id=1, source_target_pairs={{0,2},{1,3},{2,4},{3,5},{4,6},{5,7},{6,8},{7,9},{8,10},{9,11},{10,... | collective-permute-start | bytes 589832 | tf_op jit(solution)/shard_map/ppermute | solution.py:220
  74.9 16.9 %collective-permute-start.16 = (bf16[256,384]{1,0:T(8,128)(2,1)S(1)}, bf16[256,384]{1,0:T(8,128)(2,1)S(1)}, u32[]{:S(2)}, u32[]{:S(2)}) collective-permute-start(bf16[256,384]{1,0:T(8,128)(2,1)S(1)} %get-tuple-element.109), channel_id=1, source_target_pairs={{0,10},{1,11},{2,12},{3,13},{4,14},{5,15},{6,0},{7,1},{8,2},{9,3},... | collective-permute-start | bytes 589832 | tf_op jit(solution)/shard_map/ppermute | solution.py:220
  79.4 30.4 %collective-permute-start.17 = (bf16[256,384]{1,0:T(8,128)(2,1)S(1)}, bf16[256,384]{1,0:T(8,128)(2,1)S(1)}, u32[]{:S(2)}, u32[]{:S(2)}) collective-permute-start(bf16[256,384]{1,0:T(8,128)(2,1)S(1)} %get-tuple-element.110), channel_id=1, source_target_pairs={{0,8},{1,9},{2,10},{3,11},{4,12},{5,13},{6,14},{7,15},{8,0},{9,1},... | collective-permute-start | bytes 589832 | tf_op jit(solution)/shard_map/ppermute | solution.py:220
  82.4 27.5 %collective-permute-start.18 = (bf16[256,384]{1,0:T(8,128)(2,1)S(1)}, bf16[256,384]{1,0:T(8,128)(2,1)S(1)}, u32[]{:S(2)}, u32[]{:S(2)}) collective-permute-start(bf16[256,384]{1,0:T(8,128)(2,1)S(1)} %get-tuple-element.111), channel_id=1, source_target_pairs={{0,6},{1,7},{2,8},{3,9},{4,10},{5,11},{6,12},{7,13},{8,14},{9,15},... | collective-permute-start | bytes 589832 | tf_op jit(solution)/shard_map/ppermute | solution.py:220

commit v8 on v7

--- a/solution.py
+++ b/solution.py
@@ -15,7 +15,7 @@
 CORES = 2
 WIDTHS = (2, 4, 6, 8)
 GROUP = 4
-AHEAD = (0, 4)
+AHEAD = (0, 4, 2)
 CONTRACT = (((1,), (1,)), ((), ()))
 ANY = pl.BlockSpec(memory_space=pl.ANY)
 VMEM = pl.BlockSpec(memory_space=pltpu.VMEM)
@@ -275,7 +275,7 @@
         (chip,), sums, came_part, *dqs,
     )
     back = [back[0]] + [by_chips(back[step], chips - step) for step in range(1, chips)]
-    near = [min(step, chips - step) * 4 <= chips for step in range(chips)]
+    near = [min(step, chips - step) * 8 <= 3 * chips for step in range(chips)]
     early = [step for step in range(chips) if near[step]]
     late = [step for step in range(chips) if not near[step]]
 

time: 112 us -> 111 us (level)
  waiting for transfers between devices: 42.2 us -> 30.3 us
  starting transfers between devices: 47.3 us -> 56.4 us
    ppermute x21, waiting for transfers between devices: 39.9 us -> 28 us  [by_chips(): return lax.ppermute(shard, 'blk', pairs)]
    ppermute x21, starting transfers between devices: 45.3 us -> 55.4 us  [by_chips(): return lax.ppermute(shard, 'blk', pairs)]
  transfers between devices with their start and end apart: 23 -> 23, of which waited for: 11 -> 9; matrix products, arithmetic and copies ran while one was open for 2% -> 2% of each run, Pallas kernels for 4% -> 5%
where the time goes in v8:
time: 111 us; the launch traced here: 110 us
  starting transfers between devices  56.4 us (51%)
  waiting for transfers between devices  30.3 us (27%)
  Pallas kernels  17.4 us (16%)
  local copies, waits for them, and re-layouts  5.35 us (5%)
    ppermute x21, starting transfers between devices, by_chips(): return lax.ppermute(shard, 'blk', pairs)  55.4 us
    ppermute x21, waiting for transfers between devices, by_chips(): return lax.ppermute(shard, 'blk', pairs)  28 us
    pallas_call x8, Pallas kernels, call(): pl.pallas_call(kernel, out_shape=outs, in_specs=[SMEM] * len(scalars) + [...  17.4 us
    unnamed x17, local copies, waits for them, and re-layouts  4.38 us
    ppermute x2, waiting for transfers between devices, across_cores(): lax.ppermute(shard, 'blk', [(i, i ^ 1) for i in range(chips * CORES)])  2.29 us
  transfers between devices with their start and end apart: 23, of which 9 were waited for; matrix products, arithmetic and copies ran while one was open for 2% of the time, Pallas kernels for 5%

profile of v8, /device:TPU:0, one launch (start us, length us, event | category | flops | bytes accessed | tf_op | source)
XLA Modules:
  0.0 110.0 jit_solution(17198784045801126703)
XLA Ops:
  0.0 1.4 %shard_map.100 = (bf16[256,256]{1,0:T(8,128)(2,1)S(1)}, bf16[256,256]{1,0:T(8,128)(2,1)S(1)}, bf16[256,256]{1,0:T(8,128)(2,1)S(1)}, bf16[256,256]{1,0:T(8,128)(2...) custom-call(s32[1]{0:T(128)} %bitcast.chip_ref, ...), custom_call_target="tpu_custom_call" | custom-call | tf_op jit(solution)/shard_map/pallas_call | solution.py:204
  1.4 3.0 %collective-permute-start = (bf16[256,256]{1,0:T(8,128)(2,1)S(1)}, bf16[256,256]{1,0:T(8,128)(2,1)S(1)}, u32[]{:S(2)}, u32[]{:S(2)}) collective-permute-start(bf16[256,256]{1,0:T(8,128)(2,1)S(1)} %get-tuple-element.70), channel_id=1, source_target_pairs={{0,2},{1,3},{2,4},{3,5},{4,6},{5,7},{6,8},{7,9},{8,10},{9,11},{10,... | collective-permute-start | bytes 393224 | tf_op jit(solution)/shard_map/ppermute | solution.py:220
  4.4 1.6 %collective-permute-start.1 = (bf16[256,256]{1,0:T(8,128)(2,1)S(1)}, bf16[256,256]{1,0:T(8,128)(2,1)S(1)}, u32[]{:S(2)}, u32[]{:S(2)}) collective-permute-start(bf16[256,256]{1,0:T(8,128)(2,1)S(1)} %get-tuple-element.71), channel_id=1, source_target_pairs={{0,4},{1,5},{2,6},{3,7},{4,8},{5,9},{6,10},{7,11},{8,12},{9,13},{1... | collective-permute-start | bytes 393224 | tf_op jit(solution)/shard_map/ppermute | solution.py:220
  6.0 2.6 %collective-permute-start.2 = (bf16[256,256]{1,0:T(8,128)(2,1)S(1)}, bf16[256,256]{1,0:T(8,128)(2,1)S(1)}, u32[]{:S(2)}, u32[]{:S(2)}) collective-permute-start(bf16[256,256]{1,0:T(8,128)(2,1)S(1)} %get-tuple-element.72), channel_id=1, source_target_pairs={{0,6},{1,7},{2,8},{3,9},{4,10},{5,11},{6,12},{7,13},{8,14},{9,15},... | collective-permute-start | bytes 393224 | tf_op jit(solution)/shard_map/ppermute | solution.py:220
  8.6 1.2 %collective-permute-start.3 = (bf16[256,256]{1,0:T(8,128)(2,1)S(1)}, bf16[256,256]{1,0:T(8,128)(2,1)S(1)}, u32[]{:S(2)}, u32[]{:S(2)}) collective-permute-start(bf16[256,256]{1,0:T(8,128)(2,1)S(1)} %get-tuple-element.73), channel_id=1, source_target_pairs={{0,8},{1,9},{2,10},{3,11},{4,12},{5,13},{6,14},{7,15},{8,0},{9,1},... | collective-permute-start | bytes 393224 | tf_op jit(solution)/shard_map/ppermute | solution.py:220
  9.8 2.6 %collective-permute-start.4 = (bf16[256,256]{1,0:T(8,128)(2,1)S(1)}, bf16[256,256]{1,0:T(8,128)(2,1)S(1)}, u32[]{:S(2)}, u32[]{:S(2)}) collective-permute-start(bf16[256,256]{1,0:T(8,128)(2,1)S(1)} %get-tuple-element.74), channel_id=1, source_target_pairs={{0,10},{1,11},{2,12},{3,13},{4,14},{5,15},{6,0},{7,1},{8,2},{9,3},... | collective-permute-start | bytes 393224 | tf_op jit(solution)/shard_map/ppermute | solution.py:220
  12.4 1.6 %copy-done.3 = bf16[1024,1024]{1,0:T(8,128)(2,1)S(1)} copy-done((bf16[1024,1024]{1,0:T(8,128)(2,1)S(1)}, bf16[1024,1024]{1,0:T(8,128)(2,1)}, u32[]{:S(2)}) %copy-start.3) | copy-done | bytes 2097176
  14.0 1.0 copy-done.4
  15.1 1.0 copy-done.5
  16.1 1.8 %shard_map.101 = (bf16[256,256]{1,0:T(8,128)(2,1)S(1)}, bf16[256,256]{1,0:T(8,128)(2,1)}, bf16[256,256]{1,0:T(8,128)(2,1)S(1)}, bf16[256,256]{1,0:T(8,128)(2,1)S...) custom-call(s32[1]{0:T(128)} %bitcast.chip_ref, ...), custom_call_target="tpu_custom_call" | custom-call | tf_op jit(solution)/shard_map/pallas_call | solution.py:204
  17.9 1.3 %collective-permute-start.5 = (bf16[256,256]{1,0:T(8,128)(2,1)S(1)}, bf16[256,256]{1,0:T(8,128)(2,1)S(1)}, u32[]{:S(2)}, u32[]{:S(2)}) collective-permute-start(bf16[256,256]{1,0:T(8,128)(2,1)S(1)} %get-tuple-element.75), channel_id=1, source_target_pairs={{0,12},{1,13},{2,14},{3,15},{4,0},{5,1},{6,2},{7,3},{8,4},{9,5},{1... | collective-permute-start | bytes 393224 | tf_op jit(solution)/shard_map/ppermute | solution.py:220
  19.3 1.4 %collective-permute-start.6 = (bf16[256,256]{1,0:T(8,128)(2,1)S(1)}, bf16[256,256]{1,0:T(8,128)(2,1)S(1)}, u32[]{:S(2)}, u32[]{:S(2)}) collective-permute-start(bf16[256,256]{1,0:T(8,128)(2,1)S(1)} %get-tuple-element.76), channel_id=1, source_target_pairs={{0,14},{1,15},{2,0},{3,1},{4,2},{5,3},{6,4},{7,5},{8,6},{9,7},{10,... | collective-permute-start | bytes 393224 | tf_op jit(solution)/shard_map/ppermute | solution.py:220
  20.7 1.7 %collective-permute-done.2.refs_3_ = bf16[256,256]{1,0:T(8,128)(2,1)S(1)} collective-permute-done((bf16[256,256]{1,0:T(8,128)(2,1)S(1)}, bf16[256,256]{1,0:T(8,128)(2,1)S(1)}, u32[]{:S(2)}, u32[]{:S(2)}) %collective-permute-start.2) | collective-permute-done | bytes 131104 | tf_op jit(solution)/shard_map/ppermute | solution.py:220
  22.4 5.4 %collective-permute-start.7 = (bf16[256,256]{1,0:T(8,128)(2,1)S(1)}, bf16[256,256]{1,0:T(8,128)(2,1)S(1)}, u32[]{:S(2)}, u32[]{:S(2)}) collective-permute-start(bf16[256,256]{1,0:T(8,128)(2,1)S(1)} %get-tuple-element.79), channel_id=1, source_target_pairs={{0,8},{1,9},{2,10},{3,11},{4,12},{5,13},{6,14},{7,15},{8,0},{9,1},... | collective-permute-start | bytes 393224 | tf_op jit(solution)/shard_map/ppermute | solution.py:220
  27.8 4.7 %collective-permute-start.8 = (bf16[256,256]{1,0:T(8,128)(2,1)S(1)}, bf16[256,256]{1,0:T(8,128)(2,1)S(1)}, u32[]{:S(2)}, u32[]{:S(2)}) collective-permute-start(bf16[256,256]{1,0:T(8,128)(2,1)S(1)} %get-tuple-element.80), channel_id=1, source_target_pairs={{0,4},{1,5},{2,6},{3,7},{4,8},{5,9},{6,10},{7,11},{8,12},{9,13},{1... | collective-permute-start | bytes 393224 | tf_op jit(solution)/shard_map/ppermute | solution.py:220
  32.5 6.8 %collective-permute-done.7.refs_9_ = bf16[256,256]{1,0:T(8,128)(2,1)S(1)} collective-permute-done((bf16[256,256]{1,0:T(8,128)(2,1)S(1)}, bf16[256,256]{1,0:T(8,128)(2,1)S(1)}, u32[]{:S(2)}, u32[]{:S(2)}) %collective-permute-start.7) | collective-permute-done | bytes 131104 | tf_op jit(solution)/shard_map/ppermute | solution.py:220
  39.4 0.1 shard_map.102.own_ref
  39.5 0.3 collective-permute-start.10
  39.9 1.9 %collective-permute-start.11 = (bf16[256,256]{1,0:T(8,128)(2,1)S(1)}, bf16[256,256]{1,0:T(8,128)(2,1)S(1)}, u32[]{:S(2)}, u32[]{:S(2)}) collective-permute-start(bf16[256,256]{1,0:T(8,128)(2,1)S(1)} %get-tuple-element.95), channel_id=1, source_target_pairs={{0,6},{1,7},{2,8},{3,9},{4,10},{5,11},{6,12},{7,13},{8,14},{9,15},... | collective-permute-start | bytes 393224 | tf_op jit(solution)/shard_map/ppermute | solution.py:220
  41.7 2.0 %collective-permute-start.12 = (bf16[256,256]{1,0:T(8,128)(2,1)S(1)}, bf16[256,256]{1,0:T(8,128)(2,1)S(1)}, u32[]{:S(2)}, u32[]{:S(2)}) collective-permute-start(bf16[256,256]{1,0:T(8,128)(2,1)S(1)} %get-tuple-element.96), channel_id=1, source_target_pairs={{0,10},{1,11},{2,12},{3,13},{4,14},{5,15},{6,0},{7,1},{8,2},{9,3},... | collective-permute-start | bytes 393224 | tf_op jit(solution)/shard_map/ppermute | solution.py:220
  43.7 1.0 collective-permute-start.13
  44.7 0.1 reshape.36
  44.8 0.1 reshape.37.count_ref
  44.9 0.7 copy.16
  45.6 0.7 constant_dynamic-slice_fusion
  46.3 0.1 squeeze.6
  46.4 2.8 %collective-permute-start.14 = (bf16[256,256]{1,0:T(8,128)(2,1)S(1)}, bf16[256,256]{1,0:T(8,128)(2,1)S(1)}, u32[]{:S(2)}, u32[]{:S(2)}) collective-permute-start(bf16[256,256]{1,0:T(8,128)(2,1)S(1)} %get-tuple-element.98), channel_id=1, source_target_pairs={{0,14},{1,15},{2,0},{3,1},{4,2},{5,3},{6,4},{7,5},{8,6},{9,7},{10,... | collective-permute-start | bytes 393224 | tf_op jit(solution)/shard_map/ppermute | solution.py:220
  49.2 0.2 convert_reduce_fusion
  49.4 0.1 select_reduce_fusion.order_ref
  49.5 1.0 shard_map.103
  50.5 3.2 %collective-permute-done.11.refs_8_ = bf16[256,256]{1,0:T(8,128)(2,1)S(1)} collective-permute-done((bf16[256,256]{1,0:T(8,128)(2,1)S(1)}, bf16[256,256]{1,0:T(8,128)(2,1)S(1)}, u32[]{:S(2)}, u32[]{:S(2)}) %collective-permute-start.11) | collective-permute-done | bytes 131104 | tf_op jit(solution)/shard_map/ppermute | solution.py:220
  53.7 2.0 %collective-permute-done.14.refs_12_ = bf16[256,256]{1,0:T(8,128)(2,1)S(1)} collective-permute-done((bf16[256,256]{1,0:T(8,128)(2,1)S(1)}, bf16[256,256]{1,0:T(8,128)(2,1)S(1)}, u32[]{:S(2)}, u32[]{:S(2)}) %collective-permute-start.14) | collective-permute-done | bytes 131104 | tf_op jit(solution)/shard_map/ppermute | solution.py:220
  55.7 9.0 %shard_map.104 = (f32[4096,256]{1,0:T(8,128)S(1)}, bf16[16,256,256]{2,1,0:T(8,128)(2,1)S(1)}, bf16[16,256,256]{2,1,0:T(8,128)(2,1)S(1)}, bf16[2048,256]{1,0:T(8,...) custom-call(s32[1]{0:T(128)} %bitcast.chip_ref, ...), custom_call_target="tpu_custom_call", output_to_operand_aliasing={{0}: (6, {}), {1}: (7, {}), {2}: (8, {})} | custom-call | tf_op jit(solution)/shard_map/pallas_call | solution.py:204
  64.7 1.0 collective-permute-start.15
  65.6 2.3 %collective-permute-done.15.other_ref = bf16[2048,256]{1,0:T(8,128)(2,1)S(1)} collective-permute-done((bf16[2048,256]{1,0:T(8,128)(2,1)S(1)}, bf16[2048,256]{1,0:T(8,128)(2,1)S(1)}, u32[]{:S(2)}, u32[]{:S(2)}) %collective-permute-start.15) | collective-permute-done | bytes 1048608 | tf_op jit(solution)/shard_map/ppermute | solution.py:226
  67.9 0.3 shard_map.105
  68.3 4.1 %collective-permute-start.17 = (bf16[256,384]{1,0:T(8,128)(2,1)S(1)}, bf16[256,384]{1,0:T(8,128)(2,1)S(1)}, u32[]{:S(2)}, u32[]{:S(2)}) collective-permute-start(bf16[256,384]{1,0:T(8,128)(2,1)S(1)} %get-tuple-element.111), channel_id=1, source_target_pairs={{0,14},{1,15},{2,0},{3,1},{4,2},{5,3},{6,4},{7,5},{8,6},{9,7},{10,... | collective-permute-start | bytes 589832 | tf_op jit(solution)/shard_map/ppermute | solution.py:220
  72.3 1.6 %collective-permute-start.19 = (bf16[256,384]{1,0:T(8,128)(2,1)S(1)}, bf16[256,384]{1,0:T(8,128)(2,1)S(1)}, u32[]{:S(2)}, u32[]{:S(2)}) collective-permute-start(bf16[256,384]{1,0:T(8,128)(2,1)S(1)} %get-tuple-element.113), channel_id=1, source_target_pairs={{0,10},{1,11},{2,12},{3,13},{4,14},{5,15},{6,0},{7,1},{8,2},{9,3},... | collective-permute-start | bytes 589832 | tf_op jit(solution)/shard_map/ppermute | solution.py:220
  73.9 1.4 %collective-permute-start.20 = (bf16[256,384]{1,0:T(8,128)(2,1)S(1)}, bf16[256,384]{1,0:T(8,128)(2,1)S(1)}, u32[]{:S(2)}, u32[]{:S(2)}) collective-permute-start(bf16[256,384]{1,0:T(8,128)(2,1)S(1)} %get-tuple-element.114), channel_id=1, source_target_pairs={{0,6},{1,7},{2,8},{3,9},{4,10},{5,11},{6,12},{7,13},{8,14},{9,15},... | collective-permute-start | bytes 589832 | tf_op jit(solution)/shard_map/ppermute | solution.py:220
  75.3 2.0 %collective-permute-start.21 = (bf16[256,384]{1,0:T(8,128)(2,1)S(1)}, bf16[256,384]{1,0:T(8,128)(2,1)S(1)}, u32[]{:S(2)}, u32[]{:S(2)}) collective-permute-start(bf16[256,384]{1,0:T(8,128)(2,1)S(1)} %get-tuple-element.115), channel_id=1, source_target_pairs={{0,4},{1,5},{2,6},{3,7},{4,8},{5,9},{6,10},{7,11},{8,12},{9,13},{1... | collective-permute-start | bytes 589832 | tf_op jit(solution)/shard_map/ppermute | solution.py:220
  77.3 0.4 collective-permute-done.17.refs_1_
  77.6 0.5 collective-permute-start.22
  78.1 3.7 %collective-permute-done.18.refs_2_ = bf16[256,384]{1,0:T(8,128)(2,1)S(1)} collective-permute-done((bf16[256,384]{1,0:T(8,128)(2,1)S(1)}, bf16[256,384]{1,0:T(8,128)(2,1)S(1)}, u32[]{:S(2)}, u32[]{:S(2)}) %collective-permute-start.18) | collective-permute-done | bytes 196640 | tf_op jit(solution)/shard_map/ppermute | solution.py:220
  81.9 14.1 %collective-permute-start.16 = (bf16[256,384]{1,0:T(8,128)(2,1)S(1)}, bf16[256,384]{1,0:T(8,128)(2,1)S(1)}, u32[]{:S(2)}, u32[]{:S(2)}) collective-permute-start(bf16[256,384]{1,0:T(8,128)(2,1)S(1)} %get-tuple-element.109), channel_id=1, source_target_pairs={{0,8},{1,9},{2,10},{3,11},{4,12},{5,13},{6,14},{7,15},{8,0},{9,1},... | collective-permute-start | bytes 589832 | tf_op jit(solution)/shard_map/ppermute | solution.py:220
  95.9 8.9 %collective-permute-done.20.refs_4_ = bf16[256,384]{1,0:T(8,128)(2,1)S(1)} collective-permute-done((bf16[256,384]{1,0:T(8,128)(2,1)S(1)}, bf16[256,384]{1,0:T(8,128)(2,1)S(1)}, u32[]{:S(2)}, u32[]{:S(2)}) %collective-permute-start.20) | collective-permute-done | bytes 196640 | tf_op jit(solution)/shard_map/ppermute | solution.py:220
  104.9 2.4 %shard_map.106.refs_4_ = f32[256,1024]{1,0:T(8,128)S(1)} custom-call(s32[1]{0:T(128)} %bitcast.chip_ref, bf16[256,384]{1,0:T(8,128)(2,1)S(1)} %get-tuple-element.110.refs_0_, bf16[256,384]{1,0:T(8,128)(2,1)S(1)} %collective-permute-done.17.refs_1_, bf16[256,384]{1,0:T(8,128)(2,1)S(1)} %collective-permute-done.18.refs_2_, ...), custom_call_target="tpu_custom_call" | custom-call | tf_op jit(solution)/shard_map/pallas_call | solution.py:204
  107.3 1.2 %collective-permute-done.16.refs_0_ = bf16[256,384]{1,0:T(8,128)(2,1)S(1)} collective-permute-done((bf16[256,384]{1,0:T(8,128)(2,1)S(1)}, bf16[256,384]{1,0:T(8,128)(2,1)S(1)}, u32[]{:S(2)}, u32[]{:S(2)}) %collective-permute-start.16) | collective-permute-done | bytes 196640 | tf_op jit(solution)/shard_map/ppermute | solution.py:220
  108.5 1.5 %shard_map.107 = bf16[256,1024]{1,0:T(8,128)(2,1)} custom-call(s32[1]{0:T(128)} %bitcast.chip_ref, bf16[256,384]{1,0:T(8,128)(2,1)S(1)} %collective-permute-done.16.refs_0_, bf16[1024,1024]{1,0:T(8,128)(2,1)S(1)} %copy-done, bf16[1024,1024]{1,0:T(8,128)(2,1)S(1)} %copy-done.1, bf16[1024,1024]{1,0:T(8,128)(2,1)S(1)} %copy-done.2, ...), custom_call_target="tpu_custom_call" | custom-call | tf_op jit(solution)/shard_map/pallas_call | solution.py:204
  (32 shorter events, 0.2 us)
Async XLA Ops:
  1.4 43.5 %copy-start.6 = (s32[32,8]{0,1:T(8,128)S(1)}, s32[32,8]{0,1:T(8,128)}, u32[]{:S(2)}) copy-start(s32[32,8]{0,1:T(8,128)} %param.18) | copy-start | bytes 3076
  1.4 43.2 %copy-start.7 = (s32[32]{0:T(128)S(1)}, s32[32]{0:T(128)}, u32[]{:S(2)}) copy-start(s32[32]{0:T(128)} %param.19) | copy-start | bytes 388
  1.4 16.5 %collective-permute-start = (bf16[256,256]{1,0:T(8,128)(2,1)S(1)}, bf16[256,256]{1,0:T(8,128)(2,1)S(1)}, u32[]{:S(2)}, u32[]{:S(2)}) collective-permute-start(bf16[256,256]{1,0:T(8,128)(2,1)S(1)} %get-tuple-element.70), channel_id=1, source_target_pairs={{0,2},{1,3},{2,4},{3,5},{4,6},{5,7},{6,8},{7,9},{8,10},{9,11},{10,... | collective-permute-start | bytes 393224 | tf_op jit(solution)/shard_map/ppermute | solution.py:220
  4.4 14.8 %collective-permute-start.1 = (bf16[256,256]{1,0:T(8,128)(2,1)S(1)}, bf16[256,256]{1,0:T(8,128)(2,1)S(1)}, u32[]{:S(2)}, u32[]{:S(2)}) collective-permute-start(bf16[256,256]{1,0:T(8,128)(2,1)S(1)} %get-tuple-element.71), channel_id=1, source_target_pairs={{0,4},{1,5},{2,6},{3,7},{4,8},{5,9},{6,10},{7,11},{8,12},{9,13},{1... | collective-permute-start | bytes 393224 | tf_op jit(solution)/shard_map/ppermute | solution.py:220
  6.0 16.4 %collective-permute-start.2 = (bf16[256,256]{1,0:T(8,128)(2,1)S(1)}, bf16[256,256]{1,0:T(8,128)(2,1)S(1)}, u32[]{:S(2)}, u32[]{:S(2)}) collective-permute-start(bf16[256,256]{1,0:T(8,128)(2,1)S(1)} %get-tuple-element.72), channel_id=1, source_target_pairs={{0,6},{1,7},{2,8},{3,9},{4,10},{5,11},{6,12},{7,13},{8,14},{9,15},... | collective-permute-start | bytes 393224 | tf_op jit(solution)/shard_map/ppermute | solution.py:220
  8.6 19.2 %collective-permute-start.3 = (bf16[256,256]{1,0:T(8,128)(2,1)S(1)}, bf16[256,256]{1,0:T(8,128)(2,1)S(1)}, u32[]{:S(2)}, u32[]{:S(2)}) collective-permute-start(bf16[256,256]{1,0:T(8,128)(2,1)S(1)} %get-tuple-element.73), channel_id=1, source_target_pairs={{0,8},{1,9},{2,10},{3,11},{4,12},{5,13},{6,14},{7,15},{8,0},{9,1},... | collective-permute-start | bytes 393224 | tf_op jit(solution)/shard_map/ppermute | solution.py:220
  9.8 22.7 %collective-permute-start.4 = (bf16[256,256]{1,0:T(8,128)(2,1)S(1)}, bf16[256,256]{1,0:T(8,128)(2,1)S(1)}, u32[]{:S(2)}, u32[]{:S(2)}) collective-permute-start(bf16[256,256]{1,0:T(8,128)(2,1)S(1)} %get-tuple-element.74), channel_id=1, source_target_pairs={{0,10},{1,11},{2,12},{3,13},{4,14},{5,15},{6,0},{7,1},{8,2},{9,3},... | collective-permute-start | bytes 393224 | tf_op jit(solution)/shard_map/ppermute | solution.py:220
  12.4 1.6 %copy-start.3 = (bf16[1024,1024]{1,0:T(8,128)(2,1)S(1)}, bf16[1024,1024]{1,0:T(8,128)(2,1)}, u32[]{:S(2)}) copy-start(bf16[1024,1024]{1,0:T(8,128)(2,1)} %weight_ref.1) | copy-start | bytes 6291460
  14.0 1.0 copy-start.4
  15.1 1.0 copy-start.5
  17.9 14.6 %collective-permute-start.5 = (bf16[256,256]{1,0:T(8,128)(2,1)S(1)}, bf16[256,256]{1,0:T(8,128)(2,1)S(1)}, u32[]{:S(2)}, u32[]{:S(2)}) collective-permute-start(bf16[256,256]{1,0:T(8,128)(2,1)S(1)} %get-tuple-element.75), channel_id=1, source_target_pairs={{0,12},{1,13},{2,14},{3,15},{4,0},{5,1},{6,2},{7,3},{8,4},{9,5},{1... | collective-permute-start | bytes 393224 | tf_op jit(solution)/shard_map/ppermute | solution.py:220
  19.3 13.3 %collective-permute-start.6 = (bf16[256,256]{1,0:T(8,128)(2,1)S(1)}, bf16[256,256]{1,0:T(8,128)(2,1)S(1)}, u32[]{:S(2)}, u32[]{:S(2)}) collective-permute-start(bf16[256,256]{1,0:T(8,128)(2,1)S(1)} %get-tuple-element.76), channel_id=1, source_target_pairs={{0,14},{1,15},{2,0},{3,1},{4,2},{5,3},{6,4},{7,5},{8,6},{9,7},{10,... | collective-permute-start | bytes 393224 | tf_op jit(solution)/shard_map/ppermute | solution.py:220
  22.4 17.0 %collective-permute-start.7 = (bf16[256,256]{1,0:T(8,128)(2,1)S(1)}, bf16[256,256]{1,0:T(8,128)(2,1)S(1)}, u32[]{:S(2)}, u32[]{:S(2)}) collective-permute-start(bf16[256,256]{1,0:T(8,128)(2,1)S(1)} %get-tuple-element.79), channel_id=1, source_target_pairs={{0,8},{1,9},{2,10},{3,11},{4,12},{5,13},{6,14},{7,15},{8,0},{9,1},... | collective-permute-start | bytes 393224 | tf_op jit(solution)/shard_map/ppermute | solution.py:220
  27.8 11.6 %collective-permute-start.8 = (bf16[256,256]{1,0:T(8,128)(2,1)S(1)}, bf16[256,256]{1,0:T(8,128)(2,1)S(1)}, u32[]{:S(2)}, u32[]{:S(2)}) collective-permute-start(bf16[256,256]{1,0:T(8,128)(2,1)S(1)} %get-tuple-element.80), channel_id=1, source_target_pairs={{0,4},{1,5},{2,6},{3,7},{4,8},{5,9},{6,10},{7,11},{8,12},{9,13},{1... | collective-permute-start | bytes 393224 | tf_op jit(solution)/shard_map/ppermute | solution.py:220
  39.5 6.9 %collective-permute-start.9 = (bf16[2048,256]{1,0:T(8,128)(2,1)S(1)}, bf16[2048,256]{1,0:T(8,128)(2,1)S(1)}, u32[]{:S(2)}, u32[]{:S(2)}) collective-permute-start(bf16[2048,256]{1,0:T(8,128)(2,1)S(1)} %shard_map.102.own_ref), channel_id=1, source_target_pairs={{0,1},{1,0},{2,3},{3,2},{4,5},{5,4},{6,7},{7,6},{8,9},{9,8},{10,11... | collective-permute-start | bytes 3145736 | tf_op jit(solution)/shard_map/ppermute | solution.py:226
  39.5 10.9 %collective-permute-start.10 = (bf16[256,256]{1,0:T(8,128)(2,1)}, bf16[256,256]{1,0:T(8,128)(2,1)S(1)}, u32[]{:S(2)}, u32[]{:S(2)}) collective-permute-start(bf16[256,256]{1,0:T(8,128)(2,1)} %get-tuple-element.94), channel_id=1, source_target_pairs={{0,2},{1,3},{2,4},{3,5},{4,6},{5,7},{6,8},{7,9},{8,10},{9,11},{10,... | collective-permute-start | bytes 393224 | tf_op jit(solution)/shard_map/ppermute | solution.py:220
  39.9 13.8 %collective-permute-start.11 = (bf16[256,256]{1,0:T(8,128)(2,1)S(1)}, bf16[256,256]{1,0:T(8,128)(2,1)S(1)}, u32[]{:S(2)}, u32[]{:S(2)}) collective-permute-start(bf16[256,256]{1,0:T(8,128)(2,1)S(1)} %get-tuple-element.95), channel_id=1, source_target_pairs={{0,6},{1,7},{2,8},{3,9},{4,10},{5,11},{6,12},{7,13},{8,14},{9,15},... | collective-permute-start | bytes 393224 | tf_op jit(solution)/shard_map/ppermute | solution.py:220
  41.7 11.9 %collective-permute-start.12 = (bf16[256,256]{1,0:T(8,128)(2,1)S(1)}, bf16[256,256]{1,0:T(8,128)(2,1)S(1)}, u32[]{:S(2)}, u32[]{:S(2)}) collective-permute-start(bf16[256,256]{1,0:T(8,128)(2,1)S(1)} %get-tuple-element.96), channel_id=1, source_target_pairs={{0,10},{1,11},{2,12},{3,13},{4,14},{5,15},{6,0},{7,1},{8,2},{9,3},... | collective-permute-start | bytes 393224 | tf_op jit(solution)/shard_map/ppermute | solution.py:220
  43.7 10.0 %collective-permute-start.13 = (bf16[256,256]{1,0:T(8,128)(2,1)S(1)}, bf16[256,256]{1,0:T(8,128)(2,1)S(1)}, u32[]{:S(2)}, u32[]{:S(2)}) collective-permute-start(bf16[256,256]{1,0:T(8,128)(2,1)S(1)} %get-tuple-element.97), channel_id=1, source_target_pairs={{0,12},{1,13},{2,14},{3,15},{4,0},{5,1},{6,2},{7,3},{8,4},{9,5},{1... | collective-permute-start | bytes 393224 | tf_op jit(solution)/shard_map/ppermute | solution.py:220
  46.4 9.3 %collective-permute-start.14 = (bf16[256,256]{1,0:T(8,128)(2,1)S(1)}, bf16[256,256]{1,0:T(8,128)(2,1)S(1)}, u32[]{:S(2)}, u32[]{:S(2)}) collective-permute-start(bf16[256,256]{1,0:T(8,128)(2,1)S(1)} %get-tuple-element.98), channel_id=1, source_target_pairs={{0,14},{1,15},{2,0},{3,1},{4,2},{5,3},{6,4},{7,5},{8,6},{9,7},{10,... | collective-permute-start | bytes 393224 | tf_op jit(solution)/shard_map/ppermute | solution.py:220
  55.7 49.2 %copy-start.2 = (bf16[1024,1024]{1,0:T(8,128)(2,1)S(1)}, bf16[1024,1024]{1,0:T(8,128)(2,1)}, u32[]{:S(2)}) copy-start(bf16[1024,1024]{1,0:T(8,128)(2,1)} %refs_3_.1) | copy-start | bytes 6291460
  64.7 3.3 %collective-permute-start.15 = (bf16[2048,256]{1,0:T(8,128)(2,1)S(1)}, bf16[2048,256]{1,0:T(8,128)(2,1)S(1)}, u32[]{:S(2)}, u32[]{:S(2)}) collective-permute-start(bf16[2048,256]{1,0:T(8,128)(2,1)S(1)} %get-tuple-element.100), channel_id=1, source_target_pairs={{0,1},{1,0},{2,3},{3,2},{4,5},{5,4},{6,7},{7,6},{8,9},{9,8},{10,11... | collective-permute-start | bytes 3145736 | tf_op jit(solution)/shard_map/ppermute | solution.py:226
  67.9 37.0 %copy-start = (bf16[1024,1024]{1,0:T(8,128)(2,1)S(1)}, bf16[1024,1024]{1,0:T(8,128)(2,1)}, u32[]{:S(2)}) copy-start(bf16[1024,1024]{1,0:T(8,128)(2,1)} %refs_1_.3) | copy-start | bytes 6291460
  67.9 37.0 %copy-start.1 = (bf16[1024,1024]{1,0:T(8,128)(2,1)S(1)}, bf16[1024,1024]{1,0:T(8,128)(2,1)}, u32[]{:S(2)}) copy-start(bf16[1024,1024]{1,0:T(8,128)(2,1)} %refs_2_.1) | copy-start | bytes 6291460
  68.3 9.4 %collective-permute-start.17 = (bf16[256,384]{1,0:T(8,128)(2,1)S(1)}, bf16[256,384]{1,0:T(8,128)(2,1)S(1)}, u32[]{:S(2)}, u32[]{:S(2)}) collective-permute-start(bf16[256,384]{1,0:T(8,128)(2,1)S(1)} %get-tuple-element.111), channel_id=1, source_target_pairs={{0,14},{1,15},{2,0},{3,1},{4,2},{5,3},{6,4},{7,5},{8,6},{9,7},{10,... | collective-permute-start | bytes 589832 | tf_op jit(solution)/shard_map/ppermute | solution.py:220
  72.3 9.5 %collective-permute-start.18 = (bf16[256,384]{1,0:T(8,128)(2,1)S(1)}, bf16[256,384]{1,0:T(8,128)(2,1)S(1)}, u32[]{:S(2)}, u32[]{:S(2)}) collective-permute-start(bf16[256,384]{1,0:T(8,128)(2,1)S(1)} %get-tuple-element.112), channel_id=1, source_target_pairs={{0,12},{1,13},{2,14},{3,15},{4,0},{5,1},{6,2},{7,3},{8,4},{9,5},{1... | collective-permute-start | bytes 589832 | tf_op jit(solution)/shard_map/ppermute | solution.py:220
  72.3 23.6 %collective-permute-start.19 = (bf16[256,384]{1,0:T(8,128)(2,1)S(1)}, bf16[256,384]{1,0:T(8,128)(2,1)S(1)}, u32[]{:S(2)}, u32[]{:S(2)}) collective-permute-start(bf16[256,384]{1,0:T(8,128)(2,1)S(1)} %get-tuple-element.113), channel_id=1, source_target_pairs={{0,10},{1,11},{2,12},{3,13},{4,14},{5,15},{6,0},{7,1},{8,2},{9,3},... | collective-permute-start | bytes 589832 | tf_op jit(solution)/shard_map/ppermute | solution.py:220
  73.9 31.0 %collective-permute-start.20 = (bf16[256,384]{1,0:T(8,128)(2,1)S(1)}, bf16[256,384]{1,0:T(8,128)(2,1)S(1)}, u32[]{:S(2)}, u32[]{:S(2)}) collective-permute-start(bf16[256,384]{1,0:T(8,128)(2,1)S(1)} %get-tuple-element.114), channel_id=1, source_target_pairs={{0,6},{1,7},{2,8},{3,9},{4,10},{5,11},{6,12},{7,13},{8,14},{9,15},... | collective-permute-start | bytes 589832 | tf_op jit(solution)/shard_map/ppermute | solution.py:220
  75.3 29.6 %collective-permute-start.21 = (bf16[256,384]{1,0:T(8,128)(2,1)S(1)}, bf16[256,384]{1,0:T(8,128)(2,1)S(1)}, u32[]{:S(2)}, u32[]{:S(2)}) collective-permute-start(bf16[256,384]{1,0:T(8,128)(2,1)S(1)} %get-tuple-element.115), channel_id=1, source_target_pairs={{0,4},{1,5},{2,6},{3,7},{4,8},{5,9},{6,10},{7,11},{8,12},{9,13},{1... | collective-permute-start | bytes 589832 | tf_op jit(solution)/shard_map/ppermute | solution.py:220
  77.6 27.2 %collective-permute-start.22 = (bf16[256,384]{1,0:T(8,128)(2,1)S(1)}, bf16[256,384]{1,0:T(8,128)(2,1)S(1)}, u32[]{:S(2)}, u32[]{:S(2)}) collective-permute-start(bf16[256,384]{1,0:T(8,128)(2,1)S(1)} %get-tuple-element.116), channel_id=1, source_target_pairs={{0,2},{1,3},{2,4},{3,5},{4,6},{5,7},{6,8},{7,9},{8,10},{9,11},{10,... | collective-permute-start | bytes 589832 | tf_op jit(solution)/shard_map/ppermute | solution.py:220
  81.9 26.6 %collective-permute-start.16 = (bf16[256,384]{1,0:T(8,128)(2,1)S(1)}, bf16[256,384]{1,0:T(8,128)(2,1)S(1)}, u32[]{:S(2)}, u32[]{:S(2)}) collective-permute-start(bf16[256,384]{1,0:T(8,128)(2,1)S(1)} %get-tuple-element.109), channel_id=1, source_target_pairs={{0,8},{1,9},{2,10},{3,11},{4,12},{5,13},{6,14},{7,15},{8,0},{9,1},... | collective-permute-start | bytes 589832 | tf_op jit(solution)/shard_map/ppermute | solution.py:220

commit v9 on v8

--- a/solution.py
+++ b/solution.py
@@ -13,7 +13,7 @@
 NBR = 8
 WIN = 8
 CORES = 2
-WIDTHS = (2, 4, 6, 8)
+WIDTHS = (2, 4, 8)
 GROUP = 4
 AHEAD = (0, 4, 2)
 CONTRACT = (((1,), (1,)), ((), ()))

time: 111 us -> 112 us (level)
  Pallas kernels: 17.4 us -> 19.7 us
  starting transfers between devices: 56.4 us -> 54.9 us
    pallas_call x8, Pallas kernels: 17.4 us -> 19.7 us  [call(): pl.pallas_call(kernel, out_shape=outs, in_specs=[SMEM] * len(scalars) + [...]
where the time goes in v9:
time: 112 us; the launch traced here: 111 us
  starting transfers between devices  54.9 us (49%)
  waiting for transfers between devices  31.1 us (28%)
  Pallas kernels  19.7 us (18%)
  local copies, waits for them, and re-layouts  5.35 us (5%)
    ppermute x21, starting transfers between devices, by_chips(): return lax.ppermute(shard, 'blk', pairs)  54.7 us
    ppermute x21, waiting for transfers between devices, by_chips(): return lax.ppermute(shard, 'blk', pairs)  28.4 us
    pallas_call x8, Pallas kernels, call(): pl.pallas_call(kernel, out_shape=outs, in_specs=[SMEM] * len(scalars) + [...  19.7 us
    unnamed x17, local copies, waits for them, and re-layouts  4.38 us
    ppermute x2, waiting for transfers between devices, across_cores(): lax.ppermute(shard, 'blk', [(i, i ^ 1) for i in range(chips * CORES)])  2.65 us
  transfers between devices with their start and end apart: 23, of which 9 were waited for; matrix products, arithmetic and copies ran while one was open for 2% of the time, Pallas kernels for 5%

profile of v9, /device:TPU:0, one launch (start us, length us, event | category | flops | bytes accessed | tf_op | source)
XLA Modules:
  0.0 111.5 jit_solution(5504837372010996457)
XLA Ops:
  0.0 1.4 %shard_map.100 = (bf16[256,256]{1,0:T(8,128)(2,1)S(1)}, bf16[256,256]{1,0:T(8,128)(2,1)S(1)}, bf16[256,256]{1,0:T(8,128)(2,1)S(1)}, bf16[256,256]{1,0:T(8,128)(2...) custom-call(s32[1]{0:T(128)} %bitcast.chip_ref, ...), custom_call_target="tpu_custom_call" | custom-call | tf_op jit(solution)/shard_map/pallas_call | solution.py:204
  1.4 3.0 %collective-permute-start = (bf16[256,256]{1,0:T(8,128)(2,1)S(1)}, bf16[256,256]{1,0:T(8,128)(2,1)S(1)}, u32[]{:S(2)}, u32[]{:S(2)}) collective-permute-start(bf16[256,256]{1,0:T(8,128)(2,1)S(1)} %get-tuple-element.70), channel_id=1, source_target_pairs={{0,2},{1,3},{2,4},{3,5},{4,6},{5,7},{6,8},{7,9},{8,10},{9,11},{10,... | collective-permute-start | bytes 393224 | tf_op jit(solution)/shard_map/ppermute | solution.py:220
  4.4 1.6 %collective-permute-start.1 = (bf16[256,256]{1,0:T(8,128)(2,1)S(1)}, bf16[256,256]{1,0:T(8,128)(2,1)S(1)}, u32[]{:S(2)}, u32[]{:S(2)}) collective-permute-start(bf16[256,256]{1,0:T(8,128)(2,1)S(1)} %get-tuple-element.71), channel_id=1, source_target_pairs={{0,4},{1,5},{2,6},{3,7},{4,8},{5,9},{6,10},{7,11},{8,12},{9,13},{1... | collective-permute-start | bytes 393224 | tf_op jit(solution)/shard_map/ppermute | solution.py:220
  6.0 2.6 %collective-permute-start.2 = (bf16[256,256]{1,0:T(8,128)(2,1)S(1)}, bf16[256,256]{1,0:T(8,128)(2,1)S(1)}, u32[]{:S(2)}, u32[]{:S(2)}) collective-permute-start(bf16[256,256]{1,0:T(8,128)(2,1)S(1)} %get-tuple-element.72), channel_id=1, source_target_pairs={{0,6},{1,7},{2,8},{3,9},{4,10},{5,11},{6,12},{7,13},{8,14},{9,15},... | collective-permute-start | bytes 393224 | tf_op jit(solution)/shard_map/ppermute | solution.py:220
  8.6 1.2 %collective-permute-start.3 = (bf16[256,256]{1,0:T(8,128)(2,1)S(1)}, bf16[256,256]{1,0:T(8,128)(2,1)S(1)}, u32[]{:S(2)}, u32[]{:S(2)}) collective-permute-start(bf16[256,256]{1,0:T(8,128)(2,1)S(1)} %get-tuple-element.73), channel_id=1, source_target_pairs={{0,8},{1,9},{2,10},{3,11},{4,12},{5,13},{6,14},{7,15},{8,0},{9,1},... | collective-permute-start | bytes 393224 | tf_op jit(solution)/shard_map/ppermute | solution.py:220
  9.8 2.6 %collective-permute-start.4 = (bf16[256,256]{1,0:T(8,128)(2,1)S(1)}, bf16[256,256]{1,0:T(8,128)(2,1)S(1)}, u32[]{:S(2)}, u32[]{:S(2)}) collective-permute-start(bf16[256,256]{1,0:T(8,128)(2,1)S(1)} %get-tuple-element.74), channel_id=1, source_target_pairs={{0,10},{1,11},{2,12},{3,13},{4,14},{5,15},{6,0},{7,1},{8,2},{9,3},... | collective-permute-start | bytes 393224 | tf_op jit(solution)/shard_map/ppermute | solution.py:220
  12.4 1.6 %copy-done.3 = bf16[1024,1024]{1,0:T(8,128)(2,1)S(1)} copy-done((bf16[1024,1024]{1,0:T(8,128)(2,1)S(1)}, bf16[1024,1024]{1,0:T(8,128)(2,1)}, u32[]{:S(2)}) %copy-start.3) | copy-done | bytes 2097176
  14.0 1.0 copy-done.4
  15.1 1.0 copy-done.5
  16.1 1.8 %shard_map.101 = (bf16[256,256]{1,0:T(8,128)(2,1)S(1)}, bf16[256,256]{1,0:T(8,128)(2,1)}, bf16[256,256]{1,0:T(8,128)(2,1)S(1)}, bf16[256,256]{1,0:T(8,128)(2,1)S...) custom-call(s32[1]{0:T(128)} %bitcast.chip_ref, ...), custom_call_target="tpu_custom_call" | custom-call | tf_op jit(solution)/shard_map/pallas_call | solution.py:204
  17.9 1.3 %collective-permute-start.5 = (bf16[256,256]{1,0:T(8,128)(2,1)S(1)}, bf16[256,256]{1,0:T(8,128)(2,1)S(1)}, u32[]{:S(2)}, u32[]{:S(2)}) collective-permute-start(bf16[256,256]{1,0:T(8,128)(2,1)S(1)} %get-tuple-element.75), channel_id=1, source_target_pairs={{0,12},{1,13},{2,14},{3,15},{4,0},{5,1},{6,2},{7,3},{8,4},{9,5},{1... | collective-permute-start | bytes 393224 | tf_op jit(solution)/shard_map/ppermute | solution.py:220
  19.3 1.4 %collective-permute-start.6 = (bf16[256,256]{1,0:T(8,128)(2,1)S(1)}, bf16[256,256]{1,0:T(8,128)(2,1)S(1)}, u32[]{:S(2)}, u32[]{:S(2)}) collective-permute-start(bf16[256,256]{1,0:T(8,128)(2,1)S(1)} %get-tuple-element.76), channel_id=1, source_target_pairs={{0,14},{1,15},{2,0},{3,1},{4,2},{5,3},{6,4},{7,5},{8,6},{9,7},{10,... | collective-permute-start | bytes 393224 | tf_op jit(solution)/shard_map/ppermute | solution.py:220
  20.7 1.7 %collective-permute-done.2.refs_3_ = bf16[256,256]{1,0:T(8,128)(2,1)S(1)} collective-permute-done((bf16[256,256]{1,0:T(8,128)(2,1)S(1)}, bf16[256,256]{1,0:T(8,128)(2,1)S(1)}, u32[]{:S(2)}, u32[]{:S(2)}) %collective-permute-start.2) | collective-permute-done | bytes 131104 | tf_op jit(solution)/shard_map/ppermute | solution.py:220
  22.4 5.4 %collective-permute-start.7 = (bf16[256,256]{1,0:T(8,128)(2,1)S(1)}, bf16[256,256]{1,0:T(8,128)(2,1)S(1)}, u32[]{:S(2)}, u32[]{:S(2)}) collective-permute-start(bf16[256,256]{1,0:T(8,128)(2,1)S(1)} %get-tuple-element.79), channel_id=1, source_target_pairs={{0,8},{1,9},{2,10},{3,11},{4,12},{5,13},{6,14},{7,15},{8,0},{9,1},... | collective-permute-start | bytes 393224 | tf_op jit(solution)/shard_map/ppermute | solution.py:220
  27.8 4.7 %collective-permute-start.8 = (bf16[256,256]{1,0:T(8,128)(2,1)S(1)}, bf16[256,256]{1,0:T(8,128)(2,1)S(1)}, u32[]{:S(2)}, u32[]{:S(2)}) collective-permute-start(bf16[256,256]{1,0:T(8,128)(2,1)S(1)} %get-tuple-element.80), channel_id=1, source_target_pairs={{0,4},{1,5},{2,6},{3,7},{4,8},{5,9},{6,10},{7,11},{8,12},{9,13},{1... | collective-permute-start | bytes 393224 | tf_op jit(solution)/shard_map/ppermute | solution.py:220
  32.5 6.8 %collective-permute-done.7.refs_9_ = bf16[256,256]{1,0:T(8,128)(2,1)S(1)} collective-permute-done((bf16[256,256]{1,0:T(8,128)(2,1)S(1)}, bf16[256,256]{1,0:T(8,128)(2,1)S(1)}, u32[]{:S(2)}, u32[]{:S(2)}) %collective-permute-start.7) | collective-permute-done | bytes 131104 | tf_op jit(solution)/shard_map/ppermute | solution.py:220
  39.4 0.1 shard_map.102.own_ref
  39.5 0.1 collective-permute-start.9
  39.5 0.3 collective-permute-start.10
  39.9 1.9 %collective-permute-start.11 = (bf16[256,256]{1,0:T(8,128)(2,1)S(1)}, bf16[256,256]{1,0:T(8,128)(2,1)S(1)}, u32[]{:S(2)}, u32[]{:S(2)}) collective-permute-start(bf16[256,256]{1,0:T(8,128)(2,1)S(1)} %get-tuple-element.95), channel_id=1, source_target_pairs={{0,6},{1,7},{2,8},{3,9},{4,10},{5,11},{6,12},{7,13},{8,14},{9,15},... | collective-permute-start | bytes 393224 | tf_op jit(solution)/shard_map/ppermute | solution.py:220
  41.7 2.0 %collective-permute-start.12 = (bf16[256,256]{1,0:T(8,128)(2,1)S(1)}, bf16[256,256]{1,0:T(8,128)(2,1)S(1)}, u32[]{:S(2)}, u32[]{:S(2)}) collective-permute-start(bf16[256,256]{1,0:T(8,128)(2,1)S(1)} %get-tuple-element.96), channel_id=1, source_target_pairs={{0,10},{1,11},{2,12},{3,13},{4,14},{5,15},{6,0},{7,1},{8,2},{9,3},... | collective-permute-start | bytes 393224 | tf_op jit(solution)/shard_map/ppermute | solution.py:220
  43.7 1.0 collective-permute-start.13
  44.7 0.1 reshape.36
  44.8 0.1 reshape.37.count_ref
  44.9 0.7 copy.16
  45.6 0.7 constant_dynamic-slice_fusion
  46.3 0.1 squeeze.6
  46.4 2.6 %collective-permute-start.14 = (bf16[256,256]{1,0:T(8,128)(2,1)S(1)}, bf16[256,256]{1,0:T(8,128)(2,1)S(1)}, u32[]{:S(2)}, u32[]{:S(2)}) collective-permute-start(bf16[256,256]{1,0:T(8,128)(2,1)S(1)} %get-tuple-element.98), channel_id=1, source_target_pairs={{0,14},{1,15},{2,0},{3,1},{4,2},{5,3},{6,4},{7,5},{8,6},{9,7},{10,... | collective-permute-start | bytes 393224 | tf_op jit(solution)/shard_map/ppermute | solution.py:220
  49.0 0.2 convert_reduce_fusion
  49.2 0.1 select_reduce_fusion.order_ref
  49.3 1.0 shard_map.103
  50.3 3.4 %collective-permute-done.11.refs_8_ = bf16[256,256]{1,0:T(8,128)(2,1)S(1)} collective-permute-done((bf16[256,256]{1,0:T(8,128)(2,1)S(1)}, bf16[256,256]{1,0:T(8,128)(2,1)S(1)}, u32[]{:S(2)}, u32[]{:S(2)}) %collective-permute-start.11) | collective-permute-done | bytes 131104 | tf_op jit(solution)/shard_map/ppermute | solution.py:220
  53.7 2.0 %collective-permute-done.14.refs_12_ = bf16[256,256]{1,0:T(8,128)(2,1)S(1)} collective-permute-done((bf16[256,256]{1,0:T(8,128)(2,1)S(1)}, bf16[256,256]{1,0:T(8,128)(2,1)S(1)}, u32[]{:S(2)}, u32[]{:S(2)}) %collective-permute-start.14) | collective-permute-done | bytes 131104 | tf_op jit(solution)/shard_map/ppermute | solution.py:220
  55.7 11.3 %shard_map.104 = (f32[4096,256]{1,0:T(8,128)S(1)}, bf16[16,256,256]{2,1,0:T(8,128)(2,1)S(1)}, bf16[16,256,256]{2,1,0:T(8,128)(2,1)S(1)}, bf16[2048,256]{1,0:T(8,...) custom-call(s32[1]{0:T(128)} %bitcast.chip_ref, ...), custom_call_target="tpu_custom_call", output_to_operand_aliasing={{0}: (6, {}), {1}: (7, {}), {2}: (8, {})} | custom-call | tf_op jit(solution)/shard_map/pallas_call | solution.py:204
  67.0 0.1 collective-permute-start.15
  67.0 2.6 %collective-permute-done.15.other_ref = bf16[2048,256]{1,0:T(8,128)(2,1)S(1)} collective-permute-done((bf16[2048,256]{1,0:T(8,128)(2,1)S(1)}, bf16[2048,256]{1,0:T(8,128)(2,1)S(1)}, u32[]{:S(2)}, u32[]{:S(2)}) %collective-permute-start.15) | collective-permute-done | bytes 1048608 | tf_op jit(solution)/shard_map/ppermute | solution.py:226
  69.7 0.3 shard_map.105
  70.0 4.5 %collective-permute-start.17 = (bf16[256,384]{1,0:T(8,128)(2,1)S(1)}, bf16[256,384]{1,0:T(8,128)(2,1)S(1)}, u32[]{:S(2)}, u32[]{:S(2)}) collective-permute-start(bf16[256,384]{1,0:T(8,128)(2,1)S(1)} %get-tuple-element.111), channel_id=1, source_target_pairs={{0,14},{1,15},{2,0},{3,1},{4,2},{5,3},{6,4},{7,5},{8,6},{9,7},{10,... | collective-permute-start | bytes 589832 | tf_op jit(solution)/shard_map/ppermute | solution.py:220
  74.5 1.1 collective-permute-start.19
  75.6 1.8 %collective-permute-start.20 = (bf16[256,384]{1,0:T(8,128)(2,1)S(1)}, bf16[256,384]{1,0:T(8,128)(2,1)S(1)}, u32[]{:S(2)}, u32[]{:S(2)}) collective-permute-start(bf16[256,384]{1,0:T(8,128)(2,1)S(1)} %get-tuple-element.114), channel_id=1, source_target_pairs={{0,6},{1,7},{2,8},{3,9},{4,10},{5,11},{6,12},{7,13},{8,14},{9,15},... | collective-permute-start | bytes 589832 | tf_op jit(solution)/shard_map/ppermute | solution.py:220
  77.5 2.0 %collective-permute-start.21 = (bf16[256,384]{1,0:T(8,128)(2,1)S(1)}, bf16[256,384]{1,0:T(8,128)(2,1)S(1)}, u32[]{:S(2)}, u32[]{:S(2)}) collective-permute-start(bf16[256,384]{1,0:T(8,128)(2,1)S(1)} %get-tuple-element.115), channel_id=1, source_target_pairs={{0,4},{1,5},{2,6},{3,7},{4,8},{5,9},{6,10},{7,11},{8,12},{9,13},{1... | collective-permute-start | bytes 589832 | tf_op jit(solution)/shard_map/ppermute | solution.py:220
  79.5 0.4 collective-permute-done.17.refs_1_
  79.9 4.2 %collective-permute-done.18.refs_2_ = bf16[256,384]{1,0:T(8,128)(2,1)S(1)} collective-permute-done((bf16[256,384]{1,0:T(8,128)(2,1)S(1)}, bf16[256,384]{1,0:T(8,128)(2,1)S(1)}, u32[]{:S(2)}, u32[]{:S(2)}) %collective-permute-start.18) | collective-permute-done | bytes 196640 | tf_op jit(solution)/shard_map/ppermute | solution.py:220
  84.1 13.6 %collective-permute-start.16 = (bf16[256,384]{1,0:T(8,128)(2,1)S(1)}, bf16[256,384]{1,0:T(8,128)(2,1)S(1)}, u32[]{:S(2)}, u32[]{:S(2)}) collective-permute-start(bf16[256,384]{1,0:T(8,128)(2,1)S(1)} %get-tuple-element.109), channel_id=1, source_target_pairs={{0,8},{1,9},{2,10},{3,11},{4,12},{5,13},{6,14},{7,15},{8,0},{9,1},... | collective-permute-start | bytes 589832 | tf_op jit(solution)/shard_map/ppermute | solution.py:220
  97.7 8.9 %collective-permute-done.20.refs_4_ = bf16[256,384]{1,0:T(8,128)(2,1)S(1)} collective-permute-done((bf16[256,384]{1,0:T(8,128)(2,1)S(1)}, bf16[256,384]{1,0:T(8,128)(2,1)S(1)}, u32[]{:S(2)}, u32[]{:S(2)}) %collective-permute-start.20) | collective-permute-done | bytes 196640 | tf_op jit(solution)/shard_map/ppermute | solution.py:220
  106.7 2.4 %shard_map.106.refs_4_ = f32[256,1024]{1,0:T(8,128)S(1)} custom-call(s32[1]{0:T(128)} %bitcast.chip_ref, bf16[256,384]{1,0:T(8,128)(2,1)S(1)} %get-tuple-element.110.refs_0_, bf16[256,384]{1,0:T(8,128)(2,1)S(1)} %collective-permute-done.17.refs_1_, bf16[256,384]{1,0:T(8,128)(2,1)S(1)} %collective-permute-done.18.refs_2_, ...), custom_call_target="tpu_custom_call" | custom-call | tf_op jit(solution)/shard_map/pallas_call | solution.py:204
  109.0 0.9 collective-permute-done.16.refs_0_
  110.0 1.5 %shard_map.107 = bf16[256,1024]{1,0:T(8,128)(2,1)} custom-call(s32[1]{0:T(128)} %bitcast.chip_ref, bf16[256,384]{1,0:T(8,128)(2,1)S(1)} %collective-permute-done.16.refs_0_, bf16[1024,1024]{1,0:T(8,128)(2,1)S(1)} %copy-done, bf16[1024,1024]{1,0:T(8,128)(2,1)S(1)} %copy-done.1, bf16[1024,1024]{1,0:T(8,128)(2,1)S(1)} %copy-done.2, ...), custom_call_target="tpu_custom_call" | custom-call | tf_op jit(solution)/shard_map/pallas_call | solution.py:204
  (32 shorter events, 0.1 us)
Async XLA Ops:
  1.4 43.5 %copy-start.6 = (s32[32,8]{0,1:T(8,128)S(1)}, s32[32,8]{0,1:T(8,128)}, u32[]{:S(2)}) copy-start(s32[32,8]{0,1:T(8,128)} %param.18) | copy-start | bytes 3076
  1.4 43.2 %copy-start.7 = (s32[32]{0:T(128)S(1)}, s32[32]{0:T(128)}, u32[]{:S(2)}) copy-start(s32[32]{0:T(128)} %param.19) | copy-start | bytes 388
  1.4 16.5 %collective-permute-start = (bf16[256,256]{1,0:T(8,128)(2,1)S(1)}, bf16[256,256]{1,0:T(8,128)(2,1)S(1)}, u32[]{:S(2)}, u32[]{:S(2)}) collective-permute-start(bf16[256,256]{1,0:T(8,128)(2,1)S(1)} %get-tuple-element.70), channel_id=1, source_target_pairs={{0,2},{1,3},{2,4},{3,5},{4,6},{5,7},{6,8},{7,9},{8,10},{9,11},{10,... | collective-permute-start | bytes 393224 | tf_op jit(solution)/shard_map/ppermute | solution.py:220
  4.4 14.8 %collective-permute-start.1 = (bf16[256,256]{1,0:T(8,128)(2,1)S(1)}, bf16[256,256]{1,0:T(8,128)(2,1)S(1)}, u32[]{:S(2)}, u32[]{:S(2)}) collective-permute-start(bf16[256,256]{1,0:T(8,128)(2,1)S(1)} %get-tuple-element.71), channel_id=1, source_target_pairs={{0,4},{1,5},{2,6},{3,7},{4,8},{5,9},{6,10},{7,11},{8,12},{9,13},{1... | collective-permute-start | bytes 393224 | tf_op jit(solution)/shard_map/ppermute | solution.py:220
  6.0 16.4 %collective-permute-start.2 = (bf16[256,256]{1,0:T(8,128)(2,1)S(1)}, bf16[256,256]{1,0:T(8,128)(2,1)S(1)}, u32[]{:S(2)}, u32[]{:S(2)}) collective-permute-start(bf16[256,256]{1,0:T(8,128)(2,1)S(1)} %get-tuple-element.72), channel_id=1, source_target_pairs={{0,6},{1,7},{2,8},{3,9},{4,10},{5,11},{6,12},{7,13},{8,14},{9,15},... | collective-permute-start | bytes 393224 | tf_op jit(solution)/shard_map/ppermute | solution.py:220
  8.6 19.2 %collective-permute-start.3 = (bf16[256,256]{1,0:T(8,128)(2,1)S(1)}, bf16[256,256]{1,0:T(8,128)(2,1)S(1)}, u32[]{:S(2)}, u32[]{:S(2)}) collective-permute-start(bf16[256,256]{1,0:T(8,128)(2,1)S(1)} %get-tuple-element.73), channel_id=1, source_target_pairs={{0,8},{1,9},{2,10},{3,11},{4,12},{5,13},{6,14},{7,15},{8,0},{9,1},... | collective-permute-start | bytes 393224 | tf_op jit(solution)/shard_map/ppermute | solution.py:220
  9.8 22.7 %collective-permute-start.4 = (bf16[256,256]{1,0:T(8,128)(2,1)S(1)}, bf16[256,256]{1,0:T(8,128)(2,1)S(1)}, u32[]{:S(2)}, u32[]{:S(2)}) collective-permute-start(bf16[256,256]{1,0:T(8,128)(2,1)S(1)} %get-tuple-element.74), channel_id=1, source_target_pairs={{0,10},{1,11},{2,12},{3,13},{4,14},{5,15},{6,0},{7,1},{8,2},{9,3},... | collective-permute-start | bytes 393224 | tf_op jit(solution)/shard_map/ppermute | solution.py:220
  12.4 1.6 %copy-start.3 = (bf16[1024,1024]{1,0:T(8,128)(2,1)S(1)}, bf16[1024,1024]{1,0:T(8,128)(2,1)}, u32[]{:S(2)}) copy-start(bf16[1024,1024]{1,0:T(8,128)(2,1)} %weight_ref.1) | copy-start | bytes 6291460
  14.0 1.0 copy-start.4
  15.1 1.0 copy-start.5
  17.9 14.6 %collective-permute-start.5 = (bf16[256,256]{1,0:T(8,128)(2,1)S(1)}, bf16[256,256]{1,0:T(8,128)(2,1)S(1)}, u32[]{:S(2)}, u32[]{:S(2)}) collective-permute-start(bf16[256,256]{1,0:T(8,128)(2,1)S(1)} %get-tuple-element.75), channel_id=1, source_target_pairs={{0,12},{1,13},{2,14},{3,15},{4,0},{5,1},{6,2},{7,3},{8,4},{9,5},{1... | collective-permute-start | bytes 393224 | tf_op jit(solution)/shard_map/ppermute | solution.py:220
  19.3 13.3 %collective-permute-start.6 = (bf16[256,256]{1,0:T(8,128)(2,1)S(1)}, bf16[256,256]{1,0:T(8,128)(2,1)S(1)}, u32[]{:S(2)}, u32[]{:S(2)}) collective-permute-start(bf16[256,256]{1,0:T(8,128)(2,1)S(1)} %get-tuple-element.76), channel_id=1, source_target_pairs={{0,14},{1,15},{2,0},{3,1},{4,2},{5,3},{6,4},{7,5},{8,6},{9,7},{10,... | collective-permute-start | bytes 393224 | tf_op jit(solution)/shard_map/ppermute | solution.py:220
  22.4 17.0 %collective-permute-start.7 = (bf16[256,256]{1,0:T(8,128)(2,1)S(1)}, bf16[256,256]{1,0:T(8,128)(2,1)S(1)}, u32[]{:S(2)}, u32[]{:S(2)}) collective-permute-start(bf16[256,256]{1,0:T(8,128)(2,1)S(1)} %get-tuple-element.79), channel_id=1, source_target_pairs={{0,8},{1,9},{2,10},{3,11},{4,12},{5,13},{6,14},{7,15},{8,0},{9,1},... | collective-permute-start | bytes 393224 | tf_op jit(solution)/shard_map/ppermute | solution.py:220
  27.8 11.6 %collective-permute-start.8 = (bf16[256,256]{1,0:T(8,128)(2,1)S(1)}, bf16[256,256]{1,0:T(8,128)(2,1)S(1)}, u32[]{:S(2)}, u32[]{:S(2)}) collective-permute-start(bf16[256,256]{1,0:T(8,128)(2,1)S(1)} %get-tuple-element.80), channel_id=1, source_target_pairs={{0,4},{1,5},{2,6},{3,7},{4,8},{5,9},{6,10},{7,11},{8,12},{9,13},{1... | collective-permute-start | bytes 393224 | tf_op jit(solution)/shard_map/ppermute | solution.py:220
  39.5 6.9 %collective-permute-start.9 = (bf16[2048,256]{1,0:T(8,128)(2,1)S(1)}, bf16[2048,256]{1,0:T(8,128)(2,1)S(1)}, u32[]{:S(2)}, u32[]{:S(2)}) collective-permute-start(bf16[2048,256]{1,0:T(8,128)(2,1)S(1)} %shard_map.102.own_ref), channel_id=1, source_target_pairs={{0,1},{1,0},{2,3},{3,2},{4,5},{5,4},{6,7},{7,6},{8,9},{9,8},{10,11... | collective-permute-start | bytes 3145736 | tf_op jit(solution)/shard_map/ppermute | solution.py:226
  39.5 10.7 %collective-permute-start.10 = (bf16[256,256]{1,0:T(8,128)(2,1)}, bf16[256,256]{1,0:T(8,128)(2,1)S(1)}, u32[]{:S(2)}, u32[]{:S(2)}) collective-permute-start(bf16[256,256]{1,0:T(8,128)(2,1)} %get-tuple-element.94), channel_id=1, source_target_pairs={{0,2},{1,3},{2,4},{3,5},{4,6},{5,7},{6,8},{7,9},{8,10},{9,11},{10,... | collective-permute-start | bytes 393224 | tf_op jit(solution)/shard_map/ppermute | solution.py:220
  39.9 13.8 %collective-permute-start.11 = (bf16[256,256]{1,0:T(8,128)(2,1)S(1)}, bf16[256,256]{1,0:T(8,128)(2,1)S(1)}, u32[]{:S(2)}, u32[]{:S(2)}) collective-permute-start(bf16[256,256]{1,0:T(8,128)(2,1)S(1)} %get-tuple-element.95), channel_id=1, source_target_pairs={{0,6},{1,7},{2,8},{3,9},{4,10},{5,11},{6,12},{7,13},{8,14},{9,15},... | collective-permute-start | bytes 393224 | tf_op jit(solution)/shard_map/ppermute | solution.py:220
  41.7 11.9 %collective-permute-start.12 = (bf16[256,256]{1,0:T(8,128)(2,1)S(1)}, bf16[256,256]{1,0:T(8,128)(2,1)S(1)}, u32[]{:S(2)}, u32[]{:S(2)}) collective-permute-start(bf16[256,256]{1,0:T(8,128)(2,1)S(1)} %get-tuple-element.96), channel_id=1, source_target_pairs={{0,10},{1,11},{2,12},{3,13},{4,14},{5,15},{6,0},{7,1},{8,2},{9,3},... | collective-permute-start | bytes 393224 | tf_op jit(solution)/shard_map/ppermute | solution.py:220
  43.7 10.0 %collective-permute-start.13 = (bf16[256,256]{1,0:T(8,128)(2,1)S(1)}, bf16[256,256]{1,0:T(8,128)(2,1)S(1)}, u32[]{:S(2)}, u32[]{:S(2)}) collective-permute-start(bf16[256,256]{1,0:T(8,128)(2,1)S(1)} %get-tuple-element.97), channel_id=1, source_target_pairs={{0,12},{1,13},{2,14},{3,15},{4,0},{5,1},{6,2},{7,3},{8,4},{9,5},{1... | collective-permute-start | bytes 393224 | tf_op jit(solution)/shard_map/ppermute | solution.py:220
  46.4 9.3 %collective-permute-start.14 = (bf16[256,256]{1,0:T(8,128)(2,1)S(1)}, bf16[256,256]{1,0:T(8,128)(2,1)S(1)}, u32[]{:S(2)}, u32[]{:S(2)}) collective-permute-start(bf16[256,256]{1,0:T(8,128)(2,1)S(1)} %get-tuple-element.98), channel_id=1, source_target_pairs={{0,14},{1,15},{2,0},{3,1},{4,2},{5,3},{6,4},{7,5},{8,6},{9,7},{10,... | collective-permute-start | bytes 393224 | tf_op jit(solution)/shard_map/ppermute | solution.py:220
  55.7 51.0 %copy-start.2 = (bf16[1024,1024]{1,0:T(8,128)(2,1)S(1)}, bf16[1024,1024]{1,0:T(8,128)(2,1)}, u32[]{:S(2)}) copy-start(bf16[1024,1024]{1,0:T(8,128)(2,1)} %refs_3_.1) | copy-start | bytes 6291460
  67.0 2.7 %collective-permute-start.15 = (bf16[2048,256]{1,0:T(8,128)(2,1)S(1)}, bf16[2048,256]{1,0:T(8,128)(2,1)S(1)}, u32[]{:S(2)}, u32[]{:S(2)}) collective-permute-start(bf16[2048,256]{1,0:T(8,128)(2,1)S(1)} %get-tuple-element.100), channel_id=1, source_target_pairs={{0,1},{1,0},{2,3},{3,2},{4,5},{5,4},{6,7},{7,6},{8,9},{9,8},{10,11... | collective-permute-start | bytes 3145736 | tf_op jit(solution)/shard_map/ppermute | solution.py:226
  69.7 37.0 %copy-start = (bf16[1024,1024]{1,0:T(8,128)(2,1)S(1)}, bf16[1024,1024]{1,0:T(8,128)(2,1)}, u32[]{:S(2)}) copy-start(bf16[1024,1024]{1,0:T(8,128)(2,1)} %refs_1_.3) | copy-start | bytes 6291460
  69.7 37.0 %copy-start.1 = (bf16[1024,1024]{1,0:T(8,128)(2,1)S(1)}, bf16[1024,1024]{1,0:T(8,128)(2,1)}, u32[]{:S(2)}) copy-start(bf16[1024,1024]{1,0:T(8,128)(2,1)} %refs_2_.1) | copy-start | bytes 6291460
  70.0 9.9 %collective-permute-start.17 = (bf16[256,384]{1,0:T(8,128)(2,1)S(1)}, bf16[256,384]{1,0:T(8,128)(2,1)S(1)}, u32[]{:S(2)}, u32[]{:S(2)}) collective-permute-start(bf16[256,384]{1,0:T(8,128)(2,1)S(1)} %get-tuple-element.111), channel_id=1, source_target_pairs={{0,14},{1,15},{2,0},{3,1},{4,2},{5,3},{6,4},{7,5},{8,6},{9,7},{10,... | collective-permute-start | bytes 589832 | tf_op jit(solution)/shard_map/ppermute | solution.py:220
  74.5 9.6 %collective-permute-start.18 = (bf16[256,384]{1,0:T(8,128)(2,1)S(1)}, bf16[256,384]{1,0:T(8,128)(2,1)S(1)}, u32[]{:S(2)}, u32[]{:S(2)}) collective-permute-start(bf16[256,384]{1,0:T(8,128)(2,1)S(1)} %get-tuple-element.112), channel_id=1, source_target_pairs={{0,12},{1,13},{2,14},{3,15},{4,0},{5,1},{6,2},{7,3},{8,4},{9,5},{1... | collective-permute-start | bytes 589832 | tf_op jit(solution)/shard_map/ppermute | solution.py:220
  74.5 23.1 %collective-permute-start.19 = (bf16[256,384]{1,0:T(8,128)(2,1)S(1)}, bf16[256,384]{1,0:T(8,128)(2,1)S(1)}, u32[]{:S(2)}, u32[]{:S(2)}) collective-permute-start(bf16[256,384]{1,0:T(8,128)(2,1)S(1)} %get-tuple-element.113), channel_id=1, source_target_pairs={{0,10},{1,11},{2,12},{3,13},{4,14},{5,15},{6,0},{7,1},{8,2},{9,3},... | collective-permute-start | bytes 589832 | tf_op jit(solution)/shard_map/ppermute | solution.py:220
  75.6 31.0 %collective-permute-start.20 = (bf16[256,384]{1,0:T(8,128)(2,1)S(1)}, bf16[256,384]{1,0:T(8,128)(2,1)S(1)}, u32[]{:S(2)}, u32[]{:S(2)}) collective-permute-start(bf16[256,384]{1,0:T(8,128)(2,1)S(1)} %get-tuple-element.114), channel_id=1, source_target_pairs={{0,6},{1,7},{2,8},{3,9},{4,10},{5,11},{6,12},{7,13},{8,14},{9,15},... | collective-permute-start | bytes 589832 | tf_op jit(solution)/shard_map/ppermute | solution.py:220
  77.5 29.2 %collective-permute-start.21 = (bf16[256,384]{1,0:T(8,128)(2,1)S(1)}, bf16[256,384]{1,0:T(8,128)(2,1)S(1)}, u32[]{:S(2)}, u32[]{:S(2)}) collective-permute-start(bf16[256,384]{1,0:T(8,128)(2,1)S(1)} %get-tuple-element.115), channel_id=1, source_target_pairs={{0,4},{1,5},{2,6},{3,7},{4,8},{5,9},{6,10},{7,11},{8,12},{9,13},{1... | collective-permute-start | bytes 589832 | tf_op jit(solution)/shard_map/ppermute | solution.py:220
  79.9 26.7 %collective-permute-start.22 = (bf16[256,384]{1,0:T(8,128)(2,1)S(1)}, bf16[256,384]{1,0:T(8,128)(2,1)S(1)}, u32[]{:S(2)}, u32[]{:S(2)}) collective-permute-start(bf16[256,384]{1,0:T(8,128)(2,1)S(1)} %get-tuple-element.116), channel_id=1, source_target_pairs={{0,2},{1,3},{2,4},{3,5},{4,6},{5,7},{6,8},{7,9},{8,10},{9,11},{10,... | collective-permute-start | bytes 589832 | tf_op jit(solution)/shard_map/ppermute | solution.py:220
  84.1 25.9 %collective-permute-start.16 = (bf16[256,384]{1,0:T(8,128)(2,1)S(1)}, bf16[256,384]{1,0:T(8,128)(2,1)S(1)}, u32[]{:S(2)}, u32[]{:S(2)}) collective-permute-start(bf16[256,384]{1,0:T(8,128)(2,1)S(1)} %get-tuple-element.109), channel_id=1, source_target_pairs={{0,8},{1,9},{2,10},{3,11},{4,12},{5,13},{6,14},{7,15},{8,0},{9,1},... | collective-permute-start | bytes 589832 | tf_op jit(solution)/shard_map/ppermute | solution.py:220
